TPU v7x, 32 devices: a whole 2x2x4 slice. The times are simulated.
32 devices in a mesh: dp: 8 (over y, x, core), seq: 4 (over z).
Axes of the slice: x: 2, y: 2, z: 4, core: 2. Of those that a mesh axis runs over, the one named last changes fastest.
Arguments:
- tokens: bfloat16 [16, 1536, 768], P('dp', 'seq'), may hold values from -6 to 6
- teacher: bfloat16 [16, 1536, 768], P('dp', 'seq'), may hold values from -6 to 6
- teach_mask: int32 [16, 1536], P('dp', 'seq'), may hold values from 0 to 1
- lengths: int32 [16], replicated, may hold values from 1 to 1536, 18432 in all
- deal_group: int32 [16], replicated, may hold values from 0 to 7, as said below
- ln1_gain: bfloat16 [768], P('dp'), may hold values from 0.25 to 1.75
- ln1_bias: bfloat16 [768], P('dp'), may hold values from -3 to 3
- qkv_weight: bfloat16 [768, 2304], P('dp'), may hold values from -0.3125 to 0.3125
- out_weight: bfloat16 [768, 768], P('dp'), may hold values from -0.875 to 0.875
- ln2_gain: bfloat16 [768], P('dp'), may hold values from 0.25 to 1.75
- ln2_bias: bfloat16 [768], P('dp'), may hold values from -3 to 3
- up_weight: bfloat16 [768, 3072], P('dp'), may hold values from -0.21875 to 0.21875
- down_weight: bfloat16 [3072, 768], P('dp'), may hold values from -0.109375 to 0.109375
Outputs:
- activations: bfloat16 [16, 1536, 768], P('dp', 'seq')
- loss: float32 [], replicated
- input_grad: bfloat16 [16, 1536, 768], P('dp', 'seq')
- ln1_gain_grad: float32 [768], P('dp')
- ln1_bias_grad: float32 [768], P('dp')
- qkv_weight_grad: float32 [768, 2304], P('dp')
- out_weight_grad: float32 [768, 768], P('dp')
- ln2_gain_grad: float32 [768], P('dp')
- ln2_bias_grad: float32 [768], P('dp')
- up_weight_grad: float32 [768, 3072], P('dp')
- down_weight_grad: float32 [3072, 768], P('dp')
Inputs may be any that keep to these rules, and one draw needn't show every extreme that they name: Sequence 2 g + j (j = 0 or 1) goes to slot j of group deal_group[2 g + j] = g XOR mask_j, where mask_0 is one number of 0 to 7 and mask_1 = mask_0 XOR (7). The lengths add up to 18432 and one of them is 1536.
All inputs are finite; a program needn't handle non-finite values.
Results may differ from a plain program's by a relative error of at most 0.012.
The roundings to bfloat16 on the way count: a program that leaves them out, or rounds other values in their place, can miss the bound.
Values may be sent and summed in bfloat16 or wider, within the bound.
No kernel may reach another device: no remote copies, remote signals or barrier semaphores. Data moves between devices by JAX's collectives and lax.ppermute only.
A program may use at most 256 MiB of HBM per device.

v0:
```python
import math

import jax
import jax.numpy as jnp
from jax import lax
from jax.sharding import PartitionSpec as P

HEADS = 12
HEAD_DIM = 64


EPSILON = 1e-12
NEGATIVE = -1e30


def swapped(value, axis, stride):
    mask = 2**stride
    pairs = [(source, source ^ mask) for source in range(lax.axis_size(axis))]
    return lax.ppermute(value, axis, pairs)


def matmul_rows(left, right, form):
    return jnp.einsum(form, left, right, preferred_element_type=jnp.float32)


def norm_forward(values, gain, shift):
    center = values - jnp.mean(values, axis=-1, keepdims=True)
    inverse = lax.rsqrt(jnp.mean(center * center, axis=-1, keepdims=True) + EPSILON)
    unit_rows = center * inverse
    return (unit_rows * gain + shift, unit_rows, inverse)


def norm_backward(upstream, unit_rows, inverse, gain):
    scaled = upstream * gain
    first = jnp.mean(scaled, axis=-1, keepdims=True)
    second = jnp.mean(scaled * unit_rows, axis=-1, keepdims=True)
    result = inverse * (scaled - first - unit_rows * second)
    return (result, jnp.sum(upstream * unit_rows, axis=0), jnp.sum(upstream, axis=0))


def gelu_parts(values):
    cdf_part = 0.5 * (1.0 + jax.scipy.special.erf(values * (1.0 / math.sqrt(2.0))))
    density = jnp.exp(-0.5 * values * values) * (1.0 / math.sqrt(2.0 * math.pi))
    return (values * cdf_part, cdf_part + values * density)


def shards(
    tokens,
    teacher,
    teach_mask,
    lengths,
    deal_group,
    ln1_gain,
    ln1_bias,
    qkv_weight,
    out_weight,
    ln2_gain,
    ln2_bias,
    up_weight,
    down_weight,
):
    levels = lax.axis_size("dp").bit_length() - 1
    heads_way = lax.axis_size("seq")
    rows_slot = tokens.shape[1]
    model_width = tokens.shape[2]
    full_len = rows_slot * heads_way
    seq_count = lengths.shape[0]
    local_heads = HEADS // heads_way
    score_scale = 1.0 / math.sqrt(HEAD_DIM)
    block_rows = min(512, full_len)
    block_count = full_len // block_rows
    row_total = 2 * rows_slot
    deal_masks = deal_group[0:2]
    own_group = lax.axis_index("dp")
    sources = jnp.bitwise_xor(own_group, deal_masks) * 2 + jnp.arange(2, dtype=jnp.int32)
    picked = jnp.arange(seq_count, dtype=jnp.int32)[None, :] == sources[:, None]
    dealt_len = jnp.sum(jnp.where(picked, lengths[None, :], 0), axis=1)
    positions = lax.axis_index("seq") * rows_slot + jnp.arange(rows_slot, dtype=jnp.int32)
    valid_mask = ((positions[None, :] < dealt_len[:, None]) & (teach_mask == 1)).astype(jnp.float32)
    slot_pair = tokens
    for bit_level in range(levels):
        flagged = jnp.bitwise_and(jnp.right_shift(deal_masks[0], bit_level), 1) == 1
        outgoing = jnp.where(flagged, slot_pair[0], slot_pair[1])
        incoming = swapped(outgoing, "dp", bit_level)
        slot_pair = jnp.stack(
            [jnp.where(flagged, incoming, slot_pair[0]), jnp.where(flagged, slot_pair[1], incoming)]
        )
    gathered = (
        lax.all_gather(ln1_gain, "dp", axis=0, tiled=True),
        lax.all_gather(ln1_bias, "dp", axis=0, tiled=True),
        lax.all_gather(qkv_weight, "dp", axis=0, tiled=True),
        lax.all_gather(out_weight, "dp", axis=0, tiled=True),
        lax.all_gather(ln2_gain, "dp", axis=0, tiled=True),
        lax.all_gather(ln2_bias, "dp", axis=0, tiled=True),
        lax.all_gather(up_weight, "dp", axis=0, tiled=True),
        lax.all_gather(down_weight, "dp", axis=0, tiled=True),
    )
    gain_one, shift_one, w_qkv, w_out, gain_two, shift_two, w_up, w_down = gathered
    gain_one = gain_one.astype(jnp.float32)
    shift_one = shift_one.astype(jnp.float32)
    gain_two = gain_two.astype(jnp.float32)
    shift_two = shift_two.astype(jnp.float32)
    token_rows = slot_pair.reshape(row_total, model_width).astype(jnp.float32)
    normed, unit_one, inverse_one = norm_forward(token_rows, gain_one, shift_one)
    normed_low = normed.astype(jnp.bfloat16)
    qkv_rows = matmul_rows(normed_low, w_qkv, "rd,dc->rc").astype(jnp.bfloat16)
    spread = lax.all_to_all(
        qkv_rows.reshape(2, rows_slot, heads_way, -1),
        "seq",
        split_axis=2,
        concat_axis=1,
        tiled=True,
    )
    spread = spread.reshape(2, full_len, local_heads, 3, HEAD_DIM)
    queries = spread[:, :, :, 0]
    keys_all = spread[:, :, :, 1]
    values_all = spread[:, :, :, 2]
    key_keep = jnp.arange(full_len, dtype=jnp.int32)[None, :] < dealt_len[:, None]

    def scores_of(query_block):
        raw_scores = (
            jnp.einsum("sqhe,skhe->shqk", query_block, keys_all, preferred_element_type=jnp.float32)
            * score_scale
        )
        return jnp.where(key_keep[:, None, None, :], raw_scores, NEGATIVE)

    query_blocks = jnp.moveaxis(
        queries.reshape(2, block_count, block_rows, local_heads, HEAD_DIM), 1, 0
    )

    def forward_block(query_block):
        scores = scores_of(query_block)
        highest = jnp.max(scores, axis=-1, keepdims=True)
        exponent = jnp.exp(scores - highest)
        totals = jnp.sum(exponent, axis=-1, keepdims=True)
        probs_low = (exponent / totals).astype(jnp.bfloat16)
        mixed_out = jnp.einsum(
            "shqk,skhe->sqhe", probs_low, values_all, preferred_element_type=jnp.float32
        ).astype(jnp.bfloat16)
        return (mixed_out, (highest + jnp.log(totals))[..., 0])

    mixed_blocks, logsum_blocks = lax.map(forward_block, query_blocks)
    mixed_seq = jnp.moveaxis(mixed_blocks, 0, 1).reshape(2, full_len, 1, local_heads * HEAD_DIM)
    attn_back = lax.all_to_all(mixed_seq, "seq", split_axis=1, concat_axis=2, tiled=True)
    attn_rows = attn_back.reshape(row_total, model_width)
    middle = token_rows + matmul_rows(attn_rows, w_out, "rd,de->re")
    normed_two, unit_two, inverse_two = norm_forward(middle, gain_two, shift_two)
    low_two = normed_two.astype(jnp.bfloat16)
    hidden = matmul_rows(low_two, w_up, "rd,df->rf")
    active_value, active_slope = gelu_parts(hidden)
    active_low = active_value.astype(jnp.bfloat16)
    output = middle + matmul_rows(active_low, w_down, "rf,fd->rd")
    target_rows = teacher.reshape(row_total, model_width).astype(jnp.float32)
    valid_rows = valid_mask.reshape(row_total, 1)
    error_rows = output - target_rows
    squares = jnp.sum(valid_rows * error_rows * error_rows)
    total_sq, valid_count = lax.psum((squares, jnp.sum(valid_mask)), ("dp", "seq"))
    factor = seq_count * full_len * 1.0 / valid_count
    grad_out = valid_rows * (2.0 * factor) * error_rows
    grad_ff = grad_out.astype(jnp.bfloat16)
    down_grad = matmul_rows(active_low, grad_ff, "rf,rd->fd")
    grad_active = matmul_rows(grad_ff, w_down, "rd,fd->rf")
    grad_hidden = (grad_active * active_slope).astype(jnp.bfloat16)
    up_grad = matmul_rows(low_two, grad_hidden, "rd,rf->df")
    grad_norm_two = matmul_rows(grad_hidden, w_up, "rf,df->rd")
    grad_mid_norm, gain_two_grad, shift_two_grad = norm_backward(
        grad_norm_two, unit_two, inverse_two, gain_two
    )
    grad_middle = grad_out + grad_mid_norm
    grad_branch = grad_middle.astype(jnp.bfloat16)
    out_grad = matmul_rows(attn_rows, grad_branch, "rd,re->de")
    grad_attn = matmul_rows(grad_branch, w_out, "re,de->rd").astype(jnp.bfloat16)
    grad_spread = lax.all_to_all(
        grad_attn.reshape(2, rows_slot, heads_way, -1),
        "seq",
        split_axis=2,
        concat_axis=1,
        tiled=True,
    )
    grad_spread = grad_spread.reshape(2, block_count, block_rows, local_heads, HEAD_DIM)
    grad_blocks = jnp.moveaxis(grad_spread, 1, 0)

    def backward_block(carry, inputs):
        grad_keys, grad_values = carry
        query_block, grad_block, logsum_block = inputs
        scores = scores_of(query_block)
        probs_full = jnp.exp(scores - logsum_block[..., None])
        grad_values = grad_values + jnp.einsum(
            "shqk,sqhe->skhe",
            probs_full.astype(jnp.bfloat16),
            grad_block,
            preferred_element_type=jnp.float32,
        )
        grad_probs = jnp.einsum(
            "sqhe,skhe->shqk", grad_block, values_all, preferred_element_type=jnp.float32
        )
        row_delta = jnp.sum(probs_full * grad_probs, axis=-1, keepdims=True)
        grad_scores = (probs_full * (grad_probs - row_delta)).astype(jnp.bfloat16)
        grad_query = (
            jnp.einsum("shqk,skhe->sqhe", grad_scores, keys_all, preferred_element_type=jnp.float32)
            * score_scale
        )
        grad_keys = (
            grad_keys
            + jnp.einsum(
                "shqk,sqhe->skhe", grad_scores, query_block, preferred_element_type=jnp.float32
            )
            * score_scale
        )
        return ((grad_keys, grad_values), grad_query)

    zero_kv = jnp.zeros((2, full_len, local_heads, HEAD_DIM), jnp.float32)
    (grad_keys, grad_values), grad_query_blocks = lax.scan(
        backward_block, (zero_kv, zero_kv), (query_blocks, grad_blocks, logsum_blocks)
    )
    grad_queries = jnp.moveaxis(grad_query_blocks, 0, 1).reshape(2, full_len, local_heads, HEAD_DIM)
    grad_stack = jnp.stack([grad_queries, grad_keys, grad_values], axis=3).astype(jnp.bfloat16)
    grad_stack = grad_stack.reshape(2, full_len, 1, local_heads * 3 * HEAD_DIM)
    grad_qkv = lax.all_to_all(grad_stack, "seq", split_axis=1, concat_axis=2, tiled=True).reshape(
        row_total, 3 * model_width
    )
    qkv_grad = matmul_rows(normed_low, grad_qkv, "rd,rc->dc")
    grad_norm_one = matmul_rows(grad_qkv, w_qkv, "rc,dc->rd")
    grad_in_norm, gain_one_grad, shift_one_grad = norm_backward(
        grad_norm_one, unit_one, inverse_one, gain_one
    )
    grad_input = grad_middle + grad_in_norm
    loss = total_sq / (valid_count * model_width)
    pieces = (
        lax.psum_scatter(gain_one_grad, "dp", scatter_dimension=0, tiled=True),
        lax.psum_scatter(shift_one_grad, "dp", scatter_dimension=0, tiled=True),
        lax.psum_scatter(qkv_grad, "dp", scatter_dimension=0, tiled=True),
        lax.psum_scatter(out_grad, "dp", scatter_dimension=0, tiled=True),
        lax.psum_scatter(gain_two_grad, "dp", scatter_dimension=0, tiled=True),
        lax.psum_scatter(shift_two_grad, "dp", scatter_dimension=0, tiled=True),
        lax.psum_scatter(up_grad, "dp", scatter_dimension=0, tiled=True),
        lax.psum_scatter(down_grad, "dp", scatter_dimension=0, tiled=True),
    )
    owned = (
        lax.psum(pieces[0].astype(jnp.bfloat16), "seq").astype(jnp.float32),
        lax.psum(pieces[1].astype(jnp.bfloat16), "seq").astype(jnp.float32),
        lax.psum(pieces[2].astype(jnp.bfloat16), "seq").astype(jnp.float32),
        lax.psum(pieces[3].astype(jnp.bfloat16), "seq").astype(jnp.float32),
        lax.psum(pieces[4].astype(jnp.bfloat16), "seq").astype(jnp.float32),
        lax.psum(pieces[5].astype(jnp.bfloat16), "seq").astype(jnp.float32),
        lax.psum(pieces[6].astype(jnp.bfloat16), "seq").astype(jnp.float32),
        lax.psum(pieces[7].astype(jnp.bfloat16), "seq").astype(jnp.float32),
    )
    result_pair = output.reshape(2, rows_slot, model_width).astype(jnp.bfloat16)
    grad_pair = grad_input.reshape(2, rows_slot, model_width).astype(jnp.bfloat16)
    for bit_level in range(levels):
        flagged = jnp.bitwise_and(jnp.right_shift(deal_masks[0], bit_level), 1) == 1
        result_send = jnp.where(flagged, result_pair[0], result_pair[1])
        grad_send = jnp.where(flagged, grad_pair[0], grad_pair[1])
        result_got, grad_got = swapped((result_send, grad_send), "dp", bit_level)
        result_pair = jnp.stack(
            [
                jnp.where(flagged, result_got, result_pair[0]),
                jnp.where(flagged, result_pair[1], result_got),
            ]
        )
        grad_pair = jnp.stack(
            [jnp.where(flagged, grad_got, grad_pair[0]), jnp.where(flagged, grad_pair[1], grad_got)]
        )
    return (
        result_pair,
        loss,
        grad_pair,
        owned[0],
        owned[1],
        owned[2],
        owned[3],
        owned[4],
        owned[5],
        owned[6],
        owned[7],
    )


def solution(mesh):
    in_specs = (
        P("dp", "seq", None),
        P("dp", "seq", None),
        P("dp", "seq"),
        P(),
        P(),
        P("dp"),
        P("dp"),
        P("dp", None),
        P("dp", None),
        P("dp"),
        P("dp"),
        P("dp", None),
        P("dp", None),
    )
    out_specs = (
        P("dp", "seq", None),
        P(),
        P("dp", "seq", None),
        P("dp"),
        P("dp"),
        P("dp", None),
        P("dp", None),
        P("dp"),
        P("dp"),
        P("dp", None),
        P("dp", None),
    )
    return jax.shard_map(shards, mesh=mesh, in_specs=in_specs, out_specs=out_specs, check_vma=False)
```

profile of v0, /device:TPU:0, one launch (start us, length us, event | category | flops | bytes accessed | tf_op | source)
XLA Modules:
  0.0 1013.7 jit_solution(14657106016466862988)
XLA Ops:
  16.8 18.3 %collective-permute-done.1 = bf16[384,768]{0,1:T(8,128)(2,1)S(1)} collective-permute-done((bf16[384,768]{0,1:T(8,128)(2,1)S(1)}, bf16[384,768]{0,1:T(8,128)(2,1)S(1)}, u32[]{:S(2)}, u32[]{:S(2)}) %collective-permute-start.1) | collective-permute-done | bytes 589856 | tf_op jit(solution)/shard_map/ppermute | solution.py:19
  39.3 13.5 %all-reduce.10 = (bf16[768]{0:T(1024)(128)(2,1)S(1)}, bf16[768]{0:T(1024)(128)(2,1)S(1)}, bf16[768]{0:T(1024)(128)(2,1)}, bf16[768]{0:T(1024)(128)(2,1)}) all-reduce(bf16[768]{0:T(1024)(128)(2,1)S(1)} %dynamic-update-slice.1, bf16[768]{0:T(1024)(128)(2,1)S(1)} %dynamic-update-slice, ...), channel_id=1, replica_groups=mesh['dp'=8,'seq'=4] {'dp'}, use_global_device_ids=true, to_apply=%add.1 | all-reduce | flops 3072 | bytes 12288
  65.9 7.5 convolution_convert_fusion
  73.4 9.1 reshape.317
  82.5 11.4 %copy.122 = bf16[2,384,4,576]{1,0,3,2:T(2,128)(2,1)} copy(bf16[2,384,4,576]{3,2,1,0:T(4,128)(2,1)} %reshape.317) | data formatting | bytes 7077888 | tf_op jit(solution)/shard_map/reshape | solution.py:108
  100.1 75.7 %all-to-all-done = bf16[2,384,4,576]{1,0,3,2:T(2,128)(2,1)S(1)} async-done(((bf16[2,384,4,576]{1,0,3,2:T(2,128)(2,1)}), bf16[2,384,4,576]{1,0,3,2:T(2,128)(2,1)S(1)}, u32[]{:S(2)}, u32[]{:S(2)}) %all-to-all-start) | async-done | bytes 3538976 | tf_op jit(solution)/shard_map/all_to_all | solution.py:107
  193.5 90.8 %while.28 = (s32[]{:T(128)}, bf16[3,2,512,3,64]{2,4,3,1,0:T(8,128)(2,1)}, f32[3,2,3,512]{3,2,1,0:T(4,128)}, bf16[3,2,512,3,64]{2,4,3,1,0:T(8,128)(2,1)S(1)}, bf1...) while((s32[]{:T(128)}, ...), condition=%wide.region_6.7_spmd.clone, body=%wide.region_3.6_spmd.clone.sunk | while | flops 1264779264 | bytes 59911292 | solution.py:142
  194.3 8.0 fusion.116
  202.3 10.8 %fusion.117 = f32[2,3,512]{2,1,0:T(4,128)} fusion(f32[2,3,512,1536]{3,2,1,0:T(8,128)} %get-tuple-element.454, f32[2,3,512]{2,1,0:T(4,128)S(1)} %get-tuple-element.455, pred[2,1536]{1,0:T(4,128)(4,1)} %copy-done.19), kind=kLoop, calls=%fused_computation.6.clone.1 | loop fusion | flops 18871296 | bytes 18902016 | tf_op jit(solution)/shard_map/while/body/eval_jaxpr/reduce_sum | solution.py:135
  214.4 9.4 fusion.118
  224.5 8.0 fusion.116
  232.5 10.8 %fusion.117 = f32[2,3,512]{2,1,0:T(4,128)} fusion(f32[2,3,512,1536]{3,2,1,0:T(8,128)} %get-tuple-element.454, f32[2,3,512]{2,1,0:T(4,128)S(1)} %get-tuple-element.455, pred[2,1536]{1,0:T(4,128)(4,1)} %copy-done.19), kind=kLoop, calls=%fused_computation.6.clone.1 | loop fusion | flops 18871296 | bytes 18902016 | tf_op jit(solution)/shard_map/while/body/eval_jaxpr/reduce_sum | solution.py:135
  244.6 9.4 fusion.118
  254.8 8.0 fusion.116
  262.8 10.8 %fusion.117 = f32[2,3,512]{2,1,0:T(4,128)} fusion(f32[2,3,512,1536]{3,2,1,0:T(8,128)} %get-tuple-element.454, f32[2,3,512]{2,1,0:T(4,128)S(1)} %get-tuple-element.455, pred[2,1536]{1,0:T(4,128)(4,1)} %copy-done.19), kind=kLoop, calls=%fused_computation.6.clone.1 | loop fusion | flops 18871296 | bytes 18902016 | tf_op jit(solution)/shard_map/while/body/eval_jaxpr/reduce_sum | solution.py:135
  274.9 9.4 fusion.118
  290.0 7.3 reshape.318
  307.6 30.7 %all-to-all-done.1 = bf16[2,1536,1,192]{3,0,2,1:T(2,128)(2,1)} async-done(((bf16[2,1536,1,192]{3,0,2,1:T(2,128)(2,1)}), bf16[2,1536,1,192]{3,0,2,1:T(2,128)(2,1)}, u32[]{:S(2)}, u32[]{:S(2)}) %all-to-all-start.1) | async-done | bytes 1179680 | tf_op jit(solution)/shard_map/all_to_all | solution.py:144
  349.0 10.5 %multiply_convert_fusion.1 = (bf16[768,3072]{1,0:T(8,128)(2,1)}, f32[768,3072]{1,0:T(8,128)}) fusion(bf16[768,3072]{1,0:T(8,128)(2,1)} %all-gather.9.cloned.1.call-done, f32[768,768]{0,1:T(8,128)S(1)} %get-tuple-element.346, f32[768]{0:T(1024)S(1)} %convert_element_type.163, f32[768]{0:T(1024)S(1)} %convert_element_type.162, f32[768]{0:T(1024)S(1)} %add_rsqrt_fusion, ...), kind=kOutput, calls=%fused_computation.58 | convolution fusion | flops 3638624256 | bytes 21245952 | tf_op jit(solution)/shard_map/rd,df->rf/dot_general | solution.py:23
  359.5 10.9 %fusion.52 = (f32[]{:T(128)}, f32[768,768]{0,1:T(8,128)}, bf16[768,768]{0,1:T(8,128)(2,1)}) fusion(f32[768]{0:T(1024)} %mul.231, f32[768,768]{0,1:T(8,128)} %copy.125, f32[768,768]{0,1:T(8,128)S(1)} %get-tuple-element.346, bf16[768,3072]{1,0:T(8,128)(2,1)} %get-tuple-element.347, bf16[3072,768]{1,0:T(8,128)(2,1)} %all-gather.11.cloned.1.call-done), kind=kOutput, calls=%fused_computation.63 | convolution fusion | flops 3627417600 | bytes 17697796 | tf_op jit(solution)/shard_map/rf,fd->rd/dot_general | solution.py:23
  370.3 39.1 %all-reduce.8 = (f32[]{:T(128)}, f32[]{:T(128)}) all-reduce(f32[]{:T(128)} %get-tuple-element.319, f32[]{:T(128)} %get-tuple-element.317), channel_id=1, replica_groups=mesh['dp'=8,'seq'=4] {'dp','seq'}, use_global_device_ids=true, to_apply=%region_10.11 | all-reduce | flops 2 | bytes 16 | tf_op jit(solution)/shard_map/psum | solution.py:157
  410.8 9.9 fusion.51
  420.8 9.9 fusion.70
  443.4 8.7 fusion.60
  464.5 10.5 %fusion.63 = f32[768,3072]{1,0:T(8,128)} fusion(bf16[768,3072]{1,0:T(8,128)(2,1)} %copy-done.57, f32[768,768]{0,1:T(8,128)} %copy-done.4, f32[768]{0:T(1024)S(1)} %convert_element_type.163, f32[768]{0:T(1024)S(1)} %convert_element_type.162, f32[768]{0:T(1024)S(1)} %add_rsqrt_fusion, f32[768]{0:T(1024)S(1)} %broadcast_multiply_fusion.5), kind=kOutput, calls=%fused_computation.147 | convolution fusion | flops 3626827776 | bytes 16527360 | tf_op jit(solution)/shard_map/rd,rf->df/dot_general | solution.py:23
  475.1 18.0 %all-to-all-done.2 = bf16[2,384,4,192]{1,0,3,2:T(2,128)(2,1)} async-done(((bf16[2,384,4,192]{1,0,3,2:T(2,128)(2,1)}), bf16[2,384,4,192]{1,0,3,2:T(2,128)(2,1)}, u32[]{:S(2)}, u32[]{:S(2)}) %all-to-all-start.2) | async-done | bytes 1179680 | tf_op jit(solution)/shard_map/all_to_all | solution.py:173
  504.1 201.5 %while.29 = (s32[]{:T(128)}, f32[2,1536,3,64]{1,3,2,0:T(8,128)S(1)}, f32[2,1536,3,64]{1,3,2,0:T(8,128)}, bf16[3,2,512,3,64]{2,4,3,1,0:T(8,128)(2,1)}, bf16[3,2,5...) while((s32[]{:T(128)}, ...), condition=%wide.region_17.18_spmd.clone, body=%wide.region_15.17_spmd.clone.sunk | while | flops 3093823488 | bytes 208922960 | solution.py:213
  504.5 9.0 fusion.128
  515.0 13.8 %multiply_reduce_fusion.10 = (f32[2,3,512]{2,1,0:T(4,128)S(1)}, f32[2,3,512,1536]{3,2,1,0:T(8,128)}) fusion(f32[2,3,512,1536]{3,2,1,0:T(8,128)} %fusion.128, f32[2,3,512]{2,1,0:T(4,128)S(1)} %dynamic-slice_bitcast_fusion.2, pred[2,1536]{1,0:T(4,128)(4,1)S(1)} %iota_compare_fusion.5, bf16[2,1536,3,64]{1,3,2,0:T(8,128)(2,1)S(1)} %copy-done.2, ...), kind=kOutput, calls=%fused_computation.20.clone.1 | convolution fusion | flops 627569664 | bytes 39349760 | tf_op jit(solution)/shard_map/while/body/eval_jaxpr/sqhe,skhe->shqk/dot_general | solution.py:194
  528.8 17.6 %multiply_convert_fusion.6 = bf16[2,3,512,1536]{3,2,1,0:T(8,128)(2,1)} fusion(f32[2,3,512,1536]{3,2,1,0:T(8,128)} %get-tuple-element.466, f32[2,3,512,1536]{3,2,1,0:T(8,128)} %fusion.128, f32[2,3,512]{2,1,0:T(4,128)S(1)} %get-tuple-element.467, f32[2,3,512]{2,1,0:T(4,128)S(1)} %dynamic-slice_bitcast_fusion.2, pred[2,1536]{1,0:T(4,128)(4,1)S(1)} %iota_compare_fusion.5), kind=kLoop, calls=%fused_computation.19.clone.1 | loop fusion | flops 28311552 | bytes 47213568 | tf_op jit(solution)/shard_map/while/body/eval_jaxpr/convert_element_type | solution.py:198
  557.9 12.3 %fusion.130 = f32[2,1536,3,64]{1,3,2,0:T(8,128)} fusion(f32[2,3,512,1536]{3,2,1,0:T(8,128)} %fusion.128, f32[2,3,512]{2,1,0:T(4,128)S(1)} %dynamic-slice_bitcast_fusion.2, pred[2,1536]{1,0:T(4,128)(4,1)S(1)} %copy-done.21, f32[2,1536,3,64]{1,3,2,0:T(8,128)} %get-tuple-element.506, pred[]{:T(512)S(6)} %compare.3, ...), kind=kOutput, calls=%fused_computation.29.clone.1 | convolution fusion | flops 624033792 | bytes 24002048 | tf_op jit(solution)/shard_map/while/body/eval_jaxpr/shqk,sqhe->skhe/dot_general | solution.py:188
  570.2 11.9 %fusion.128 = f32[2,3,512,1536]{3,2,1,0:T(8,128)} fusion(bf16[2,1536,3,64]{1,3,2,0:T(8,128)(2,1)S(1)} %get-tuple-element.521, bf16[3,2,512,3,64]{2,4,3,1,0:T(8,128)(2,1)} %get-tuple-element.520, s32[]{:T(128)} %get-tuple-element.504), kind=kOutput, calls=%fused_computation.37.clone.1 | convolution fusion | flops 603979776 | bytes 20447744 | tf_op jit(solution)/shard_map/while/body/eval_jaxpr/sqhe,skhe->shqk/dot_general | solution.py:122
  583.6 14.5 %multiply_reduce_fusion.10 = (f32[2,3,512]{2,1,0:T(4,128)S(1)}, f32[2,3,512,1536]{3,2,1,0:T(8,128)}) fusion(f32[2,3,512,1536]{3,2,1,0:T(8,128)} %fusion.128, f32[2,3,512]{2,1,0:T(4,128)S(1)} %dynamic-slice_bitcast_fusion.2, pred[2,1536]{1,0:T(4,128)(4,1)S(1)} %iota_compare_fusion.5, bf16[2,1536,3,64]{1,3,2,0:T(8,128)(2,1)S(1)} %copy-done.2, ...), kind=kOutput, calls=%fused_computation.20.clone.1 | convolution fusion | flops 627569664 | bytes 39349760 | tf_op jit(solution)/shard_map/while/body/eval_jaxpr/sqhe,skhe->shqk/dot_general | solution.py:194
  598.0 18.0 %multiply_convert_fusion.6 = bf16[2,3,512,1536]{3,2,1,0:T(8,128)(2,1)} fusion(f32[2,3,512,1536]{3,2,1,0:T(8,128)} %get-tuple-element.466, f32[2,3,512,1536]{3,2,1,0:T(8,128)} %fusion.128, f32[2,3,512]{2,1,0:T(4,128)S(1)} %get-tuple-element.467, f32[2,3,512]{2,1,0:T(4,128)S(1)} %dynamic-slice_bitcast_fusion.2, pred[2,1536]{1,0:T(4,128)(4,1)S(1)} %iota_compare_fusion.5), kind=kLoop, calls=%fused_computation.19.clone.1 | loop fusion | flops 28311552 | bytes 47213568 | tf_op jit(solution)/shard_map/while/body/eval_jaxpr/convert_element_type | solution.py:198
  627.0 13.5 %fusion.130 = f32[2,1536,3,64]{1,3,2,0:T(8,128)} fusion(f32[2,3,512,1536]{3,2,1,0:T(8,128)} %fusion.128, f32[2,3,512]{2,1,0:T(4,128)S(1)} %dynamic-slice_bitcast_fusion.2, pred[2,1536]{1,0:T(4,128)(4,1)S(1)} %copy-done.21, f32[2,1536,3,64]{1,3,2,0:T(8,128)} %get-tuple-element.506, pred[]{:T(512)S(6)} %compare.3, ...), kind=kOutput, calls=%fused_computation.29.clone.1 | convolution fusion | flops 624033792 | bytes 24002048 | tf_op jit(solution)/shard_map/while/body/eval_jaxpr/shqk,sqhe->skhe/dot_general | solution.py:188
  640.5 9.1 fusion.128
  651.1 13.7 %multiply_reduce_fusion.10 = (f32[2,3,512]{2,1,0:T(4,128)S(1)}, f32[2,3,512,1536]{3,2,1,0:T(8,128)}) fusion(f32[2,3,512,1536]{3,2,1,0:T(8,128)} %fusion.128, f32[2,3,512]{2,1,0:T(4,128)S(1)} %dynamic-slice_bitcast_fusion.2, pred[2,1536]{1,0:T(4,128)(4,1)S(1)} %iota_compare_fusion.5, bf16[2,1536,3,64]{1,3,2,0:T(8,128)(2,1)S(1)} %copy-done.2, ...), kind=kOutput, calls=%fused_computation.20.clone.1 | convolution fusion | flops 627569664 | bytes 39349760 | tf_op jit(solution)/shard_map/while/body/eval_jaxpr/sqhe,skhe->shqk/dot_general | solution.py:194
  664.8 17.2 %multiply_convert_fusion.6 = bf16[2,3,512,1536]{3,2,1,0:T(8,128)(2,1)} fusion(f32[2,3,512,1536]{3,2,1,0:T(8,128)} %get-tuple-element.466, f32[2,3,512,1536]{3,2,1,0:T(8,128)} %fusion.128, f32[2,3,512]{2,1,0:T(4,128)S(1)} %get-tuple-element.467, f32[2,3,512]{2,1,0:T(4,128)S(1)} %dynamic-slice_bitcast_fusion.2, pred[2,1536]{1,0:T(4,128)(4,1)S(1)} %iota_compare_fusion.5), kind=kLoop, calls=%fused_computation.19.clone.1 | loop fusion | flops 28311552 | bytes 47213568 | tf_op jit(solution)/shard_map/while/body/eval_jaxpr/convert_element_type | solution.py:198
  692.7 12.7 %fusion.130 = f32[2,1536,3,64]{1,3,2,0:T(8,128)} fusion(f32[2,3,512,1536]{3,2,1,0:T(8,128)} %fusion.128, f32[2,3,512]{2,1,0:T(4,128)S(1)} %dynamic-slice_bitcast_fusion.2, pred[2,1536]{1,0:T(4,128)(4,1)S(1)} %copy-done.21, f32[2,1536,3,64]{1,3,2,0:T(8,128)} %get-tuple-element.506, pred[]{:T(512)S(6)} %compare.3, ...), kind=kOutput, calls=%fused_computation.29.clone.1 | convolution fusion | flops 624033792 | bytes 24002048 | tf_op jit(solution)/shard_map/while/body/eval_jaxpr/shqk,sqhe->skhe/dot_general | solution.py:188
  714.9 7.5 copy.112
  729.5 85.5 %all-to-all-done.3 = bf16[2,1536,1,576]{3,0,2,1:T(2,128)(2,1)} async-done(((bf16[2,1536,1,576]{3,0,2,1:T(2,128)(2,1)}), bf16[2,1536,1,576]{3,0,2,1:T(2,128)(2,1)}, u32[]{:S(2)}, u32[]{:S(2)}) %all-to-all-start.3) | async-done | bytes 3538976 | tf_op jit(solution)/shard_map/all_to_all | solution.py:219
  815.0 10.6 %copy.126 = bf16[2,4,384,1,576]{2,1,4,0,3:T(4,128)(2,1)S(1)} copy(bf16[2,4,384,1,576]{4,0,2,1,3:T(2,128)(2,1)} %bitcast.27) | data formatting | bytes 7077888 | tf_op jit(solution)/shard_map/all_to_all | solution.py:219
  838.9 8.6 fusion.69
  866.7 53.4 %reduce-scatter.5.cloned.1.call-done = f32[96,2304]{1,0:T(8,128)} async-done(((f32[768,2304]{1,0:T(8,128)}), f32[96,2304]{1,0:T(8,128)}) %reduce-scatter.5.cloned.1.call-update) | async-done | bytes 884752 | tf_op jit(solution)/shard_map/reduce_scatter | solution.py:232
  928.0 11.6 %collective-permute-done.5 = bf16[384,768]{0,1:T(8,128)(2,1)} collective-permute-done((bf16[384,768]{0,1:T(8,128)(2,1)}, bf16[384,768]{0,1:T(8,128)(2,1)}, u32[]{:S(2)}, u32[]{:S(2)}) %collective-permute-start.5) | collective-permute-done | bytes 589856 | tf_op jit(solution)/shard_map/ppermute | solution.py:19
  942.5 23.6 %all-reduce.9 = (bf16[768]{0:T(1024)(128)(2,1)S(1)}, bf16[768]{0:T(1024)(128)(2,1)S(1)}, bf16[768]{0:T(1024)(128)(2,1)S(1)}, bf16[768]{0:T(1024)(128)(2,1)S(1)}) all-reduce(f32[768]{0:T(1024)S(1)} %get-tuple-element.258, f32[768]{0:T(1024)S(1)} %copy-done.45, f32[768]{0:T(1024)S(1)} %copy-done.43, ...), channel_id=2, replica_groups=mesh['dp'=8,'seq'=4] {'dp'}, use_global_device_ids=true, to_apply=%region_21.22.clone | all-reduce | flops 3072 | bytes 18432
  966.4 12.4 %all-reduce.11 = (bf16[96]{0:T(256)(128)(2,1)S(1)}, bf16[96]{0:T(256)(128)(2,1)S(1)}, bf16[96]{0:T(256)(128)(2,1)S(1)}, bf16[96]{0:T(256)(128)(2,1)S(1)}) all-reduce(bf16[96]{0:T(256)(128)(2,1)S(1)} %dynamic-slice.19, bf16[96]{0:T(256)(128)(2,1)S(1)} %dynamic-slice.18, ...), channel_id=1, replica_groups=mesh['dp'=8,'seq'=4] {'seq'}, use_global_device_ids=true, to_apply=%region_22.23 | all-reduce | flops 384 | bytes 1536 | tf_op jit(solution)/shard_map/psum | solution.py:240
  983.7 16.0 %all-reduce.15.cloned.1.call-done = (bf16[96,2304]{1,0:T(8,128)(2,1)}, bf16[96,768]{1,0:T(8,128)(2,1)}, bf16[96,3072]{1,0:T(8,128)(2,1)}, bf16[384,768]{1,0:T(8,128)(2,1)}) async-done(((bf16[96,2304]{1,0:T(8,128)(2,1)}, bf16[96,768]{1,0:T(8,128)(2,1)}, bf16[96,3072]{1,0:T(8,128)(2,1)}, bf16[384,768]{1,0:T(8,128)(2,1)}), (bf16[96,2304]{1,0:T(8,128)(2,1)}, bf16[96,768]{1,0:T(8,128)(2,1)}, ...) | async-done | bytes 1769488 | tf_op jit(solution)/shard_map/psum | solution.py:242
  (317 shorter events, 224.7 us)
Async XLA Ops:
  7.2 58.6 %all-gather.5.cloned.1.call-start = ((), (), s32[]{:S(2)}) async-start(), calls=%async_computation.8 | async-start | bytes 3981312 | tf_op jit(solution)/shard_map/all_gather | solution.py:91
  7.9 337.2 %all-gather.7.cloned.1.call-start = ((), (), s32[]{:S(2)}) async-start(), calls=%async_computation.9 | async-start | bytes 1327104 | tf_op jit(solution)/shard_map/all_gather | solution.py:92
  8.7 340.3 %all-gather.9.cloned.1.call-start = ((), (), s32[]{:S(2)}) async-start(), calls=%async_computation.10 | async-start | bytes 5308416 | tf_op jit(solution)/shard_map/all_gather | solution.py:95
  11.4 2.2 collective-permute-start
  13.7 23.3 %copy-start.49 = (u32[32]{0:T(128)S(1)}, u32[32]{0:T(128)}, u32[]{:S(2)}) copy-start(u32[32]{0:T(128)} %constant.109) | copy-start | bytes 388
  13.8 24.5 %copy-start.50 = (bf16[96]{0:T(256)(128)(2,1)S(1)}, bf16[96]{0:T(256)(128)(2,1)}, u32[]{:S(2)}) copy-start(bf16[96]{0:T(256)(128)(2,1)} %param.22) | copy-start | bytes 580
  13.8 24.8 %copy-start.51 = (bf16[96]{0:T(256)(128)(2,1)S(1)}, bf16[96]{0:T(256)(128)(2,1)}, u32[]{:S(2)}) copy-start(bf16[96]{0:T(256)(128)(2,1)} %param.23) | copy-start | bytes 580
  13.8 25.0 %copy-start.52 = (bf16[96]{0:T(256)(128)(2,1)S(1)}, bf16[96]{0:T(256)(128)(2,1)}, u32[]{:S(2)}) copy-start(bf16[96]{0:T(256)(128)(2,1)} %param.26) | copy-start | bytes 580
  13.8 25.2 %copy-start.53 = (bf16[96]{0:T(256)(128)(2,1)S(1)}, bf16[96]{0:T(256)(128)(2,1)}, u32[]{:S(2)}) copy-start(bf16[96]{0:T(256)(128)(2,1)} %param.27) | copy-start | bytes 580
  13.8 21.3 %collective-permute-start.1 = (bf16[384,768]{0,1:T(8,128)(2,1)S(1)}, bf16[384,768]{0,1:T(8,128)(2,1)S(1)}, u32[]{:S(2)}, u32[]{:S(2)}) collective-permute-start(bf16[384,768]{0,1:T(8,128)(2,1)S(1)} %get-tuple-element.324), channel_id=1, source_target_pairs={{0,8},{4,12},{8,0},{12,4},{16,24},{20,28},{24,16},{28,20},{1,9},{5... | collective-permute-start | bytes 1769480 | tf_op jit(solution)/shard_map/ppermute | solution.py:19
  35.2 24.7 %collective-permute-start.2 = (bf16[384,768]{0,1:T(8,128)(2,1)S(1)}, bf16[384,768]{0,1:T(8,128)(2,1)S(1)}, u32[]{:S(2)}, u32[]{:S(2)}) collective-permute-start(bf16[384,768]{0,1:T(8,128)(2,1)S(1)} %broadcast_select_fusion.17), channel_id=1, source_target_pairs={{0,16},{4,20},{8,24},{12,28},{16,0},{20,4},{24,8},{28,12},{1,17},{... | collective-permute-start | bytes 1769480 | tf_op jit(solution)/shard_map/ppermute | solution.py:19
  52.8 13.0 %copy-start.29 = (f32[768]{0:T(1024)}, f32[768]{0:T(1024)S(1)}, u32[]{:S(2)}) copy-start(f32[768]{0:T(1024)S(1)} %convert_element_type.158) | copy-start | bytes 9220
  52.8 13.0 %copy-start.39 = (f32[768]{0:T(1024)}, f32[768]{0:T(1024)S(1)}, u32[]{:S(2)}) copy-start(f32[768]{0:T(1024)S(1)} %convert_element_type.159) | copy-start | bytes 9220
  65.8 7.6 copy-start.5
  93.8 82.0 %all-to-all-start = ((bf16[2,384,4,576]{1,0,3,2:T(2,128)(2,1)}), bf16[2,384,4,576]{1,0,3,2:T(2,128)(2,1)S(1)}, u32[]{:S(2)}, u32[]{:S(2)}) async-start(bf16[2,384,4,576]{1,0,3,2:T(2,128)(2,1)} %copy.122), calls=%async_computation | async-start | bytes 7077888 | tf_op jit(solution)/shard_map/all_to_all | solution.py:107
  98.8 260.7 %all-gather.11.cloned.1.call-start = ((), (), s32[]{:S(2)}) async-start(), calls=%async_computation.11 | async-start | bytes 5308416 | tf_op jit(solution)/shard_map/all_gather | solution.py:96
  194.2 8.0 copy-start.19
  224.5 8.0 copy-start.19
  254.8 8.0 copy-start.19
  284.3 13.1 %copy-start.1 = (bf16[2,1536,3,64]{1,3,2,0:T(8,128)(2,1)}, bf16[2,1536,3,64]{1,3,2,0:T(8,128)(2,1)S(1)}, u32[]{:S(2)}) copy-start(bf16[2,1536,3,64]{1,3,2,0:T(8,128)(2,1)S(1)} %get-tuple-element.545) | copy-start | bytes 3538948
  284.3 13.1 %copy-start.3 = (bf16[3,2,512,3,64]{2,4,3,1,0:T(8,128)(2,1)}, bf16[3,2,512,3,64]{2,4,3,1,0:T(8,128)(2,1)S(1)}, u32[]{:S(2)}) copy-start(bf16[3,2,512,3,64]{2,4,3,1,0:T(8,128)(2,1)S(1)} %get-tuple-element.546) | copy-start | bytes 3538948
  297.4 40.9 %all-to-all-start.1 = ((bf16[2,1536,1,192]{3,0,2,1:T(2,128)(2,1)}), bf16[2,1536,1,192]{3,0,2,1:T(2,128)(2,1)}, u32[]{:S(2)}, u32[]{:S(2)}) async-start(bf16[2,1536,1,192]{3,0,2,1:T(2,128)(2,1)} %reshape.318), calls=%async_computation.1 | async-start | bytes 3145728 | tf_op jit(solution)/shard_map/all_to_all | solution.py:144
  301.7 559.1 %reduce-scatter.7.cloned.1.call-start = ((), (), s32[]{:S(2)}) async-start(), calls=%async_computation.13 | async-start | bytes 2654208 | tf_op jit(solution)/shard_map/reduce_scatter | solution.py:233
  348.6 88.3 %copy-start.4 = (f32[768,768]{0,1:T(8,128)}, f32[768,768]{0,1:T(8,128)S(1)}, u32[]{:S(2)}) copy-start(f32[768,768]{0,1:T(8,128)S(1)} %get-tuple-element.346) | copy-start | bytes 7077892
  410.8 9.9 copy-start.41
  420.8 9.9 copy-start.57
  441.8 420.6 %reduce-scatter.11.cloned.1.call-start = ((), (), s32[]{:S(2)}) async-start(), calls=%async_computation.15 | async-start | bytes 10616832 | tf_op jit(solution)/shard_map/reduce_scatter | solution.py:237
  460.2 32.9 %all-to-all-start.2 = ((bf16[2,384,4,192]{1,0,3,2:T(2,128)(2,1)}), bf16[2,384,4,192]{1,0,3,2:T(2,128)(2,1)}, u32[]{:S(2)}, u32[]{:S(2)}) async-start(bf16[2,384,4,192]{1,0,3,2:T(2,128)(2,1)} %reshape.292), calls=%async_computation.2 | async-start | bytes 2359296 | tf_op jit(solution)/shard_map/all_to_all | solution.py:173
  464.5 400.1 %reduce-scatter.9.cloned.1.call-start = ((), (), s32[]{:S(2)}) async-start(), calls=%async_computation.14 | async-start | bytes 10616832 | tf_op jit(solution)/shard_map/reduce_scatter | solution.py:236
  504.5 10.5 %copy-start.2 = (bf16[2,1536,3,64]{1,3,2,0:T(8,128)(2,1)S(1)}, bf16[2,1536,3,64]{1,3,2,0:T(8,128)(2,1)}, u32[]{:S(2)}) copy-start(bf16[2,1536,3,64]{1,3,2,0:T(8,128)(2,1)} %get-tuple-element.524) | copy-start | bytes 3538948 | tf_op jit(solution)/shard_map/while
  515.0 13.8 %copy-start.20 = (pred[2,1536]{1,0:T(4,128)(4,1)}, pred[2,1536]{1,0:T(4,128)(4,1)S(1)}, u32[]{:S(2)}) copy-start(pred[2,1536]{1,0:T(4,128)(4,1)S(1)} %iota_compare_fusion.5) | copy-start | bytes 9220 | tf_op jit(solution)/shard_map/while
  546.4 7.3 copy-start
  546.4 7.5 copy-start.25
  570.2 13.4 %copy-start.2 = (bf16[2,1536,3,64]{1,3,2,0:T(8,128)(2,1)S(1)}, bf16[2,1536,3,64]{1,3,2,0:T(8,128)(2,1)}, u32[]{:S(2)}) copy-start(bf16[2,1536,3,64]{1,3,2,0:T(8,128)(2,1)} %get-tuple-element.524) | copy-start | bytes 3538948 | tf_op jit(solution)/shard_map/while
  583.6 14.5 %copy-start.20 = (pred[2,1536]{1,0:T(4,128)(4,1)}, pred[2,1536]{1,0:T(4,128)(4,1)S(1)}, u32[]{:S(2)}) copy-start(pred[2,1536]{1,0:T(4,128)(4,1)S(1)} %iota_compare_fusion.5) | copy-start | bytes 9220 | tf_op jit(solution)/shard_map/while
  616.0 7.0 copy-start.25
  640.5 10.6 %copy-start.2 = (bf16[2,1536,3,64]{1,3,2,0:T(8,128)(2,1)S(1)}, bf16[2,1536,3,64]{1,3,2,0:T(8,128)(2,1)}, u32[]{:S(2)}) copy-start(bf16[2,1536,3,64]{1,3,2,0:T(8,128)(2,1)} %get-tuple-element.524) | copy-start | bytes 3538948 | tf_op jit(solution)/shard_map/while
  651.0 13.7 %copy-start.20 = (pred[2,1536]{1,0:T(4,128)(4,1)}, pred[2,1536]{1,0:T(4,128)(4,1)S(1)}, u32[]{:S(2)}) copy-start(pred[2,1536]{1,0:T(4,128)(4,1)S(1)} %iota_compare_fusion.5) | copy-start | bytes 9220 | tf_op jit(solution)/shard_map/while
  682.0 6.8 copy-start.25
  722.5 92.5 %all-to-all-start.3 = ((bf16[2,1536,1,576]{3,0,2,1:T(2,128)(2,1)}), bf16[2,1536,1,576]{3,0,2,1:T(2,128)(2,1)}, u32[]{:S(2)}, u32[]{:S(2)}) async-start(bf16[2,1536,1,576]{3,0,2,1:T(2,128)(2,1)} %copy.112), calls=%async_computation.3 | async-start | bytes 7864320 | tf_op jit(solution)/shard_map/all_to_all | solution.py:219
  727.5 192.7 %reduce-scatter.5.cloned.1.call-start = ((), (), s32[]{:S(2)}) async-start(), calls=%async_computation.12 | async-start | bytes 7962624 | tf_op jit(solution)/shard_map/reduce_scatter | solution.py:232
  836.8 163.0 %all-reduce.15.cloned.1.call-start = ((), (), s32[]{:S(2)}) async-start(), calls=%async_computation.16 | async-start | bytes 3538944 | tf_op jit(solution)/shard_map/psum | solution.py:242
  838.9 16.8 %collective-permute-start.3 = (bf16[384,768]{0,1:T(8,128)(2,1)}, bf16[384,768]{0,1:T(8,128)(2,1)}, u32[]{:S(2)}, u32[]{:S(2)}) collective-permute-start(bf16[384,768]{0,1:T(8,128)(2,1)} %broadcast_select_fusion.5), channel_id=1, source_target_pairs={{0,4},{4,0},{8,12},{12,8},{16,20},{20,16},{24,28},{28,24},{1,5},{5... | collective-permute-start | bytes 1769480 | tf_op jit(solution)/shard_map/ppermute | solution.py:19
  855.2 4.0 collective-permute-start.6
  857.8 64.4 %collective-permute-start.4 = (bf16[384,768]{0,1:T(8,128)(2,1)}, bf16[384,768]{0,1:T(8,128)(2,1)S(1)}, u32[]{:S(2)}, u32[]{:S(2)}) collective-permute-start(bf16[384,768]{0,1:T(8,128)(2,1)} %get-tuple-element.321), channel_id=1, source_target_pairs={{0,8},{4,12},{8,0},{12,4},{16,24},{20,28},{24,16},{28,20},{1,9},{5... | collective-permute-start | bytes 1769480 | tf_op jit(solution)/shard_map/ppermute | solution.py:19
  860.2 64.4 %collective-permute-start.7 = (bf16[384,768]{0,1:T(8,128)(2,1)}, bf16[384,768]{0,1:T(8,128)(2,1)S(1)}, u32[]{:S(2)}, u32[]{:S(2)}) collective-permute-start(bf16[384,768]{0,1:T(8,128)(2,1)} %get-tuple-element.314), channel_id=1, source_target_pairs={{0,8},{4,12},{8,0},{12,4},{16,24},{20,28},{24,16},{28,20},{1,9},{5... | collective-permute-start | bytes 1769480 | tf_op jit(solution)/shard_map/ppermute | solution.py:19
  923.1 16.5 %collective-permute-start.5 = (bf16[384,768]{0,1:T(8,128)(2,1)}, bf16[384,768]{0,1:T(8,128)(2,1)}, u32[]{:S(2)}, u32[]{:S(2)}) collective-permute-start(bf16[384,768]{0,1:T(8,128)(2,1)} %broadcast_select_fusion.16), channel_id=1, source_target_pairs={{0,16},{4,20},{8,24},{12,28},{16,0},{20,4},{24,8},{28,12},{1,17},{... | collective-permute-start | bytes 1769480 | tf_op jit(solution)/shard_map/ppermute | solution.py:19
  925.5 55.4 %collective-permute-start.8 = (bf16[384,768]{0,1:T(8,128)(2,1)}, bf16[384,768]{0,1:T(8,128)(2,1)}, u32[]{:S(2)}, u32[]{:S(2)}) collective-permute-start(bf16[384,768]{0,1:T(8,128)(2,1)} %broadcast_select_fusion.15), channel_id=1, source_target_pairs={{0,16},{4,20},{8,24},{12,28},{16,0},{20,4},{24,8},{28,12},{1,17},{... | collective-permute-start | bytes 1769480 | tf_op jit(solution)/shard_map/ppermute | solution.py:19
  (46 other events, 152.5 us)
Sparse Core Ops, SparseCore 0:
  9.9 50.7 all-gather.4
  62.5 24.2 all-gather.6
  88.7 38.7 all-gather.8
  129.2 38.7 all-gather.10
  441.9 43.0 reduce-scatter.6
  488.3 76.8 reduce-scatter.10
  568.7 76.8 reduce-scatter.8
  836.9 83.2 reduce-scatter.4
  923.9 75.7 all-reduce.14
where the time goes:
time: 1020 us; the launch traced here: 1010 us
  waiting for transfers between devices  320 us (31%)
  matrix products  281 us (28%)
  local copies, waits for them, and re-layouts  140 us (14%)
  other arithmetic  134 us (13%)
  blocking collectives  88.7 us (9%)
  starting transfers between devices  29 us (3%)
  between operations  20.1 us (2%)
    dot_general x12, matrix products, matmul_rows(): return jnp.einsum(form, left, right, preferred_element_type=jnp.float32)  91.1 us
    all_to_all x1, waiting for transfers between devices, shards(): lax.all_to_all(grad_stack, 'seq', split_axis=1, concat_axis=2, tiled=True)  85.5 us
    all_to_all x1, waiting for transfers between devices, shards(): lax.all_to_all(qkv_rows.reshape(2, rows_slot, heads_way, -1), 'seq', spli...  75.7 us
    dot_general x6, matrix products, scores_of(): jnp.einsum('sqhe,skhe->shqk', query_block, keys_all, preferred_element_ty...  54 us
    reduce_scatter x1, waiting for transfers between devices, shards(): lax.psum_scatter(qkv_grad, 'dp', scatter_dimension=0, tiled=True)  53.4 us
    convert_element_type x3, other arithmetic, backward_block(): grad_scores = (probs_full * (grad_probs - row_delta)).astype(jnp.bfloat16)  52.8 us
    dot_general x3, matrix products, backward_block(): jnp.einsum('sqhe,skhe->shqk', grad_block, values_all, preferred_element_t...  42 us
    psum x1, blocking collectives, shards(): lax.psum((squares, jnp.sum(valid_mask)), ('dp', 'seq'))  39.1 us
  transfers between devices with their start and end apart: 22, of which 10 were waited for; matrix products, arithmetic and copies ran while one was open for 49% of the time, Pallas kernels for 0%

commit v1 on v0

v1 whole, which is shorter than its diff:
```python
import functools
import math

import jax
import jax.numpy as jnp
from jax import lax
from jax.experimental import pallas as pl
from jax.experimental.pallas import tpu as pltpu
from jax.sharding import Mesh
from jax.sharding import PartitionSpec as P

HEADS = 12
HEAD_DIM = 64
EPSILON = 1e-12
NEGATIVE = -1e30
SCALE = 1.0 / math.sqrt(HEAD_DIM)
AXES = ("pair", "core", "seq")
NT = (((1,), (1,)), ((), ()))
NN = (((1,), (0,)), ((), ()))
TN = (((0,), (0,)), ((), ()))
LOW = jnp.bfloat16
FULL = jnp.float32


def dot(left, right, form):
    return lax.dot_general(left, right, form, preferred_element_type=FULL)


def moved(value, target):
    pairs, cores, depth = (lax.axis_size(name) for name in AXES)
    links = []
    for p in range(pairs):
        for c in range(cores):
            for z in range(depth):
                q, e, w = target(p, c, z)
                links.append(((p * cores + c) * depth + z, (q * cores + e) * depth + w))
    return lax.ppermute(value, AXES, links)


def across_cores(value):
    return moved(value, lambda p, c, z: (p, 1 - c, z))


def across_pairs(value, bit):
    return moved(value, lambda p, c, z: (p ^ bit, c, z))


def across_depth(value, bit):
    return moved(value, lambda p, c, z: (p, c, z ^ bit))


def pair_bits():
    return [1 << level for level in range(lax.axis_size("pair").bit_length() - 1)]


def turned(stack):
    z = lax.axis_index("seq")
    got = []
    for step in range(2):
        piece = lax.dynamic_index_in_dim(stack, (z + step) % 2, 0, keepdims=False)
        got.append(moved(piece, lambda p, c, w: (p, w // 2, 2 * c + (w + step) % 2)))
    even = z % 2 == 0
    return jnp.stack([jnp.where(even, got[0], got[1]), jnp.where(even, got[1], got[0])])


def summed_everywhere(value):
    value = value + across_cores(value)
    for bit in pair_bits():
        value = value + across_pairs(value, bit)
    for level in range(lax.axis_size("seq").bit_length() - 1):
        value = value + across_depth(value, 1 << level)
    return value


def gathered_over_pairs(value):
    p = lax.axis_index("pair")
    rows, width = value.shape
    bits = pair_bits()
    count = 1 << len(bits)
    halves = []
    for which in range(2):
        order = bits if which == 0 else bits[::-1]
        current = value[which * rows // 2 : (which + 1) * rows // 2]
        for bit in order:
            other = across_pairs(current, bit)
            flag = jnp.bitwise_and(p, bit) != 0
            current = jnp.stack(
                [jnp.where(flag, other, current), jnp.where(flag, current, other)]
            )
        if which == 1:
            lead = tuple(range(len(bits)))[::-1]
            current = jnp.transpose(current, lead + (len(bits), len(bits) + 1))
        halves.append(current.reshape(count, rows // 2, width))
    return jnp.concatenate(halves, axis=1).reshape(count * rows, width)


def scattered_over_pairs(value):
    p = lax.axis_index("pair")
    bits = pair_bits()
    count = 1 << len(bits)
    rows, width = value.shape[0] // count, value.shape[1]
    blocks = value.reshape(count, rows, width)
    halves = []
    for which in range(2):
        order = bits if which == 0 else bits[::-1]
        current = blocks[:, which * rows // 2 : (which + 1) * rows // 2]
        current = current.reshape((2,) * len(bits) + (rows // 2, width))
        left = bits[::-1]
        for bit in order:
            axis = left.index(bit)
            mine = jnp.where(jnp.bitwise_and(p, bit) != 0, 1, 0)
            keep = lax.dynamic_index_in_dim(current, mine, axis, keepdims=False)
            send = lax.dynamic_index_in_dim(current, 1 - mine, axis, keepdims=False)
            current = keep + across_pairs(send, bit)
            left = [other for other in left if other != bit]
        halves.append(current)
    return jnp.concatenate(halves, axis=0)


def summed_over_depth(value):
    z = lax.axis_index("seq")
    current = value
    trail = []
    for level in range(lax.axis_size("seq").bit_length() - 1):
        bit = 1 << level
        mine = jnp.where(jnp.bitwise_and(z, bit) != 0, 1, 0)
        parts = current.reshape((2, current.shape[0] // 2) + current.shape[1:])
        keep = lax.dynamic_index_in_dim(parts, mine, 0, keepdims=False)
        send = lax.dynamic_index_in_dim(parts, 1 - mine, 0, keepdims=False)
        current = keep + across_depth(send, bit)
        trail.append((bit, mine))
    for bit, mine in trail[::-1]:
        other = across_depth(current, bit)
        first = jnp.where(mine == 0, current, other)
        second = jnp.where(mine == 0, other, current)
        current = jnp.concatenate([first, second], axis=0)
    return current


def keys_with_mask(k_ref, counts_ref, ka, rows):
    lane = lax.broadcasted_iota(jnp.int32, (rows, 128), 1)
    spot = lax.broadcasted_iota(jnp.int32, (rows, 128), 0)
    limit = jnp.where(spot < rows // 2, counts_ref[0], counts_ref[1] + rows // 2)
    bias = jnp.where(spot < limit, 0.0, NEGATIVE)
    k = k_ref[...].astype(FULL)
    ka[0] = jnp.where(lane < 64, k, jnp.where(lane == 64, bias, 0.0)).astype(LOW)
    ka[1] = jnp.where(lane >= 64, k, jnp.where(lane == 0, bias, 0.0)).astype(LOW)


def forward_kernel(counts_ref, q_ref, k_ref, v_ref, o_ref, lse_ref, ka, vt, *, rows, block):
    @pl.when(pl.program_id(1) == 0)
    def _():
        keys_with_mask(k_ref, counts_ref, ka, rows)
        vt[...] = v_ref[...].T

    lane = lax.broadcasted_iota(jnp.int32, (block, 128), 1)
    q = q_ref[...].astype(FULL) * SCALE
    mixed = []
    for h in range(2):
        mine = (lane < 64) if h == 0 else (lane >= 64)
        flag = lane == (64 if h == 0 else 0)
        qa = jnp.where(mine, q, jnp.where(flag, 1.0, 0.0)).astype(LOW)
        scores = dot(ka[h], qa, NT)
        highest = jnp.max(scores, axis=0, keepdims=True)
        exponent = jnp.exp(scores - highest)
        totals = jnp.sum(exponent, axis=0, keepdims=True)
        part = dot(vt[pl.ds(64 * h, 64), :], exponent.astype(LOW), NN)
        mixed.append(part * (1.0 / totals))
        lse_ref[0, pl.ds(h, 1), :] = highest + jnp.log(totals)
    o_ref[...] = jnp.concatenate(mixed, axis=0).T.astype(LOW)


def attention_forward(counts, qkv, block):
    rows, width = qkv.shape
    pairs = width // 384
    return pl.pallas_call(
        functools.partial(forward_kernel, rows=rows, block=block),
        grid_spec=pltpu.PrefetchScalarGridSpec(
            num_scalar_prefetch=1,
            grid=(pairs, rows // block),
            in_specs=[
                pl.BlockSpec((block, 128), lambda h, i, n: (i, h)),
                pl.BlockSpec((rows, 128), lambda h, i, n: (0, pairs + h)),
                pl.BlockSpec((rows, 128), lambda h, i, n: (0, 2 * pairs + h)),
            ],
            out_specs=[
                pl.BlockSpec((block, 128), lambda h, i, n: (i, h)),
                pl.BlockSpec((1, 2, block), lambda h, i, n: (h, 0, i)),
            ],
            scratch_shapes=[pltpu.VMEM((2, rows, 128), LOW), pltpu.VMEM((128, rows), LOW)],
        ),
        out_shape=[
            jax.ShapeDtypeStruct((rows, pairs * 128), LOW),
            jax.ShapeDtypeStruct((pairs, 2, rows), FULL),
        ],
        cost_estimate=pl.CostEstimate(
            flops=8 * pairs * rows * rows * 128,
            bytes_accessed=rows * width * 3,
            transcendentals=2 * pairs * rows * rows,
        ),
        name="attention_forward",
    )(counts, qkv, qkv, qkv)


def backward_kernel(
    counts_ref, q_ref, k_ref, v_ref, o_ref, g_ref, lse_ref, grad_ref,
    ka, va, kt, dk, dv, *, rows, block, steps, chunk, pairs,
):
    pair, step = pl.program_id(0), pl.program_id(1)

    @pl.when(step == 0)
    def _():
        keys_with_mask(k_ref, counts_ref, ka, rows)
        lane = lax.broadcasted_iota(jnp.int32, (rows, 128), 1)
        v = v_ref[...].astype(FULL)
        va[0] = jnp.where(lane < 64, v, 0.0).astype(LOW)
        va[1] = jnp.where(lane >= 64, v, 0.0).astype(LOW)
        kt[...] = k_ref[...].T
        dk[...] = jnp.zeros_like(dk)
        dv[...] = jnp.zeros_like(dv)

    lane = lax.broadcasted_iota(jnp.int32, (block, 128), 1)
    q = q_ref[...].astype(FULL)
    g = g_ref[...]
    wide = g.astype(FULL)
    product = (wide * o_ref[...].astype(FULL)).T
    scaled = q * SCALE
    columns = []
    for h in range(2):
        mine = (lane < 64) if h == 0 else (lane >= 64)
        flag = lane == (64 if h == 0 else 0)
        qa = jnp.where(mine, scaled, jnp.where(flag, 1.0, 0.0)).astype(LOW)
        qm = jnp.where(mine, q, 0.0).astype(LOW)
        gm = jnp.where(mine, wide, 0.0).astype(LOW)
        delta = jnp.sum(product[64 * h : 64 * h + 64], axis=0, keepdims=True)
        lse = lse_ref[0, pl.ds(h, 1), :]
        total = jnp.zeros((64, block), FULL)
        for c in range(rows // chunk):
            part = pl.ds(c * chunk, chunk)
            probs = jnp.exp(dot(ka[h, part, :], qa, NT) - lse)
            grad_probs = dot(va[h, part, :], g, NT)
            grad_scores = (probs * (grad_probs - delta)).astype(LOW)
            dv[part, :] += dot(probs.astype(LOW), gm, NN)
            dk[part, :] += dot(grad_scores, qm, NN)
            total = total + dot(kt[pl.ds(64 * h, 64), part], grad_scores, NN)
        columns.append(total)
    spot = pl.ds(pl.multiple_of(step * block, block), block)
    here = pl.multiple_of(pair * 128, 128)
    grad_ref[spot, pl.ds(here, 128)] = (jnp.concatenate(columns, axis=0).T * SCALE).astype(LOW)

    @pl.when(step == steps - 1)
    def _():
        grad_ref[:, pl.ds(here + pairs * 128, 128)] = (dk[...] * SCALE).astype(LOW)
        grad_ref[:, pl.ds(here + pairs * 256, 128)] = dv[...].astype(LOW)


def attention_backward(counts, qkv, mixed, grad, lse, block, chunk):
    rows, width = qkv.shape
    pairs = width // 384
    steps = rows // block
    return pl.pallas_call(
        functools.partial(
            backward_kernel, rows=rows, block=block, steps=steps, chunk=chunk, pairs=pairs
        ),
        grid_spec=pltpu.PrefetchScalarGridSpec(
            num_scalar_prefetch=1,
            grid=(pairs, steps),
            in_specs=[
                pl.BlockSpec((block, 128), lambda h, i, n: (i, h)),
                pl.BlockSpec((rows, 128), lambda h, i, n: (0, pairs + h)),
                pl.BlockSpec((rows, 128), lambda h, i, n: (0, 2 * pairs + h)),
                pl.BlockSpec((block, 128), lambda h, i, n: (i, h)),
                pl.BlockSpec((block, 128), lambda h, i, n: (i, h)),
                pl.BlockSpec((1, 2, block), lambda h, i, n: (h, 0, i)),
            ],
            out_specs=pl.BlockSpec((rows, width), lambda h, i, n: (0, 0)),
            scratch_shapes=[
                pltpu.VMEM((2, rows, 128), LOW),
                pltpu.VMEM((2, rows, 128), LOW),
                pltpu.VMEM((128, rows), LOW),
                pltpu.VMEM((rows, 128), FULL),
                pltpu.VMEM((rows, 128), FULL),
            ],
        ),
        out_shape=jax.ShapeDtypeStruct((rows, width), LOW),
        cost_estimate=pl.CostEstimate(
            flops=20 * pairs * rows * rows * 128,
            bytes_accessed=rows * width * 5,
            transcendentals=2 * pairs * rows * rows,
        ),
        name="attention_backward",
    )(counts, qkv, qkv, qkv, mixed, grad, lse)


def norm_parts(values):
    center = values - jnp.mean(values, axis=-1, keepdims=True)
    inverse = lax.rsqrt(jnp.mean(center * center, axis=-1, keepdims=True) + EPSILON)
    return center * inverse, inverse


def norm_backward(upstream, unit, inverse, gain):
    scaled = upstream * gain
    first = jnp.mean(scaled, axis=-1, keepdims=True)
    second = jnp.mean(scaled * unit, axis=-1, keepdims=True)
    result = inverse * (scaled - first - unit * second)
    return result, jnp.sum(upstream * unit, axis=0), jnp.sum(upstream, axis=0)


def gelu_parts(values):
    share = 0.5 * (1.0 + lax.erf(values * (1.0 / math.sqrt(2.0))))
    density = jnp.exp(-0.5 * values * values) * (1.0 / math.sqrt(2.0 * math.pi))
    return values * share, share + values * density


def shards(
    tokens, teacher, teach_mask, lengths, deal_group,
    ln1_gain, ln1_bias, qkv_weight, out_weight, ln2_gain, ln2_bias, up_weight, down_weight,
):
    pairs, cores, depth = (lax.axis_size(name) for name in AXES)
    p, c, z = (lax.axis_index(name) for name in AXES)
    groups = pairs * cores
    slot_rows, width = tokens.shape[1], tokens.shape[2]
    rows = 2 * slot_rows
    full_len = depth * slot_rows
    seq_count = lengths.shape[0]
    ff = up_weight.shape[1]
    own_rows = width // groups
    pair_rows = cores * own_rows
    half_width = width // 2
    half_ff = ff // 2
    is_first = c == 0

    def in_order(mine, other, axis):
        return jnp.concatenate(
            [jnp.where(is_first, mine, other), jnp.where(is_first, other, mine)], axis=axis
        )

    sequence = 2 * cores * p + z
    length = jnp.sum(jnp.where(jnp.arange(seq_count) == sequence, lengths, 0))
    base = c * rows
    counts = jnp.stack([length - base, length - (rows - base)])
    counts = jnp.clip(counts, 0, rows).astype(jnp.int32)

    x_rows = turned(tokens).reshape(rows, width)

    masks = deal_group[0:2]
    group = p * cores + c
    sources = jnp.bitwise_xor(group, masks) * 2 + jnp.arange(2, dtype=jnp.int32)
    picked = jnp.arange(seq_count, dtype=jnp.int32)[None, :] == sources[:, None]
    dealt_len = jnp.sum(jnp.where(picked, lengths[None, :], 0), axis=1)
    positions = z * slot_rows + jnp.arange(slot_rows, dtype=jnp.int32)
    live = (positions[None, :] < dealt_len[:, None]) & (teach_mask == 1)
    valid_count = summed_everywhere(jnp.full((8, 128), jnp.sum(live.astype(FULL))))[0, 0]

    heads_half = HEADS // 2
    shard = qkv_weight.reshape(own_rows, 2, heads_half, 3, HEAD_DIM)
    shard = jnp.transpose(shard, (1, 0, 3, 2, 4)).reshape(2, own_rows, 3 * half_width)
    keep = lax.dynamic_index_in_dim(shard, c, 0, keepdims=False)
    send = lax.dynamic_index_in_dim(shard, 1 - c, 0, keepdims=False)
    w_qkv = gathered_over_pairs(in_order(keep, across_cores(send), 0))

    block = ff // groups
    up_shard = up_weight.reshape(own_rows, pairs, cores, 2, block // 2)
    up_shard = jnp.transpose(up_shard, (2, 0, 3, 1, 4)).reshape(cores, own_rows, half_ff)
    out_shard = jnp.transpose(out_weight.reshape(own_rows, 2, half_width), (1, 0, 2))
    both = jnp.concatenate([up_shard, out_shard], axis=2)
    keep = lax.dynamic_index_in_dim(both, c, 0, keepdims=False)
    send = lax.dynamic_index_in_dim(both, 1 - c, 0, keepdims=False)
    both = in_order(keep, across_cores(send), 0)
    down_shard = jnp.concatenate([down_weight[: block // 2], down_weight[block // 2 :]], axis=1)
    mine = gathered_over_pairs(jnp.concatenate([both, down_shard], axis=1))
    other = across_cores(mine)

    def unpacked(stack):
        up = stack[:, :half_ff]
        out = stack[:, half_ff : half_ff + half_width]
        down = stack[:, half_ff + half_width :]
        return up, out, jnp.concatenate([down[:, :width], down[:, width:]], axis=0)

    up_mine, out_mine, down_mine = unpacked(mine)
    up_other, out_other, down_other = unpacked(other)
    w_out = in_order(out_mine, out_other, 1)

    vectors = jnp.stack([ln1_gain, ln1_bias, ln2_gain, ln2_bias])
    vectors = lax.all_gather(vectors, ("pair", "core"), axis=1, tiled=True).astype(FULL)
    gain_one, shift_one, gain_two, shift_two = vectors[0], vectors[1], vectors[2], vectors[3]

    mask_rows = jnp.pad(
        teach_mask.astype(LOW)[:, None, :], ((0, 0), (0, 15), (0, width - slot_rows))
    )
    slots = jnp.concatenate([teacher, mask_rows], axis=1)
    for level in range(groups.bit_length() - 1):
        flagged = jnp.bitwise_and(jnp.right_shift(masks[0], level), 1) == 1
        outgoing = jnp.where(flagged, slots[0], slots[1])
        incoming = across_cores(outgoing) if level == 0 else across_pairs(outgoing, 1 << (level - 1))
        slots = jnp.stack(
            [jnp.where(flagged, incoming, slots[0]), jnp.where(flagged, slots[1], incoming)]
        )
    goal = turned(slots)
    spots = base + jnp.arange(rows, dtype=jnp.int32)
    taught = goal[:, slot_rows, :slot_rows].reshape(rows)
    valid = ((spots < length) & (taught == 1)).astype(FULL)[:, None]
    goal = goal[:, :slot_rows].reshape(rows, width).astype(FULL)

    x_full = x_rows.astype(FULL)
    unit_one, inverse_one = norm_parts(x_full)
    norm_mine = (unit_one * gain_one + shift_one).astype(LOW)
    norm_one = jnp.concatenate([norm_mine, across_cores(norm_mine)], axis=0)
    qkv = dot(norm_one, w_qkv, NN).astype(LOW)
    mixed, lse = attention_forward(counts, qkv, 512)
    attended = in_order(mixed[:rows], across_cores(mixed[rows:]), 1)
    middle = x_full + dot(attended, w_out, NN)
    unit_two, inverse_two = norm_parts(middle)
    norm_two = (unit_two * gain_two + shift_two).astype(LOW)
    value_mine, slope_mine = gelu_parts(dot(norm_two, up_mine, NN))
    value_other, slope_other = gelu_parts(dot(norm_two, up_other, NN))
    active_mine = value_mine.astype(LOW)
    active_other = value_other.astype(LOW)
    output = middle + dot(active_mine, down_mine, NN) + dot(active_other, down_other, NN)
    activations = turned(output.astype(LOW).reshape(2, slot_rows, width))

    error = output - goal
    squares = jnp.sum(valid * error * error)
    factor = seq_count * full_len * 1.0 / valid_count
    grad_out = valid * (2.0 * factor) * error
    grad_ff = grad_out.astype(LOW)
    down_grad_mine = dot(active_mine, grad_ff, TN).astype(LOW)
    down_grad_other = dot(active_other, grad_ff, TN).astype(LOW)
    hidden_mine = (dot(grad_ff, down_mine, NT) * slope_mine).astype(LOW)
    hidden_other = (dot(grad_ff, down_other, NT) * slope_other).astype(LOW)
    up_grad_mine = dot(norm_two, hidden_mine, TN).astype(LOW)
    up_grad_other = dot(norm_two, hidden_other, TN).astype(LOW)
    grad_norm_two = dot(hidden_mine, up_mine, NT) + dot(hidden_other, up_other, NT)
    grad_mid, gain_two_grad, shift_two_grad = norm_backward(
        grad_norm_two, unit_two, inverse_two, gain_two
    )
    grad_middle = grad_out + grad_mid
    grad_branch = grad_middle.astype(LOW)
    out_grad = dot(attended, grad_branch, TN).astype(LOW)
    grad_attended = dot(grad_branch, w_out, NT).astype(LOW)
    keep = jnp.where(is_first, grad_attended[:, :half_width], grad_attended[:, half_width:])
    send = jnp.where(is_first, grad_attended[:, half_width:], grad_attended[:, :half_width])
    grad_mixed = jnp.concatenate([keep, across_cores(send)], axis=0)

    def packed(up, out, down):
        return jnp.concatenate([up, out, down[:width], down[width:]], axis=1)

    out_halves = jnp.stack([out_grad[:, :half_width], out_grad[:, half_width:]])
    out_keep = lax.dynamic_index_in_dim(out_halves, c, 0, keepdims=False)
    out_send = lax.dynamic_index_in_dim(out_halves, 1 - c, 0, keepdims=False)
    grads = packed(up_grad_mine, out_keep, down_grad_mine) + across_cores(
        packed(up_grad_other, out_send, down_grad_other)
    )
    grads = summed_over_depth(scattered_over_pairs(grads))

    grad_qkv = attention_backward(counts, qkv, mixed, grad_mixed, lse, 512, 512)
    partial = dot(grad_qkv, w_qkv, NT)
    grad_norm_one = partial[:rows] + across_cores(partial[rows:].astype(LOW)).astype(FULL)
    qkv_grad = dot(norm_one, grad_qkv, TN).astype(LOW)
    qkv_grad = summed_over_depth(scattered_over_pairs(qkv_grad))
    grad_in, gain_one_grad, shift_one_grad = norm_backward(
        grad_norm_one, unit_one, inverse_one, gain_one
    )
    input_grad = turned((grad_middle + grad_in).astype(LOW).reshape(2, slot_rows, width))

    small = jnp.stack(
        [
            gain_one_grad, shift_one_grad, gain_two_grad, shift_two_grad,
            jnp.full((width,), squares), jnp.zeros((width,)), jnp.zeros((width,)),
            jnp.zeros((width,)),
        ]
    )
    small = summed_everywhere(small)
    loss = small[4, 0] / (valid_count * width)
    own_small = lax.dynamic_slice_in_dim(small, group * own_rows, own_rows, 1)

    def own_block(stack, index):
        return lax.dynamic_slice_in_dim(stack, index * own_rows, own_rows, 0)

    wide = jnp.concatenate([grads[:, : half_ff + half_width], qkv_grad], axis=1)
    mine = own_block(wide, c)
    other = across_cores(own_block(wide, 1 - c))
    halves = jnp.stack([jnp.where(is_first, mine, other), jnp.where(is_first, other, mine)])
    halves = halves.astype(FULL)
    up_own = halves[:, :, :half_ff].reshape(cores, own_rows, 2, pairs, block // 2)
    up_own = jnp.transpose(up_own, (1, 3, 0, 2, 4)).reshape(own_rows, ff)
    out_own = jnp.transpose(halves[:, :, half_ff : half_ff + half_width], (1, 0, 2))
    out_own = out_own.reshape(own_rows, width)
    qkv_own = halves[:, :, half_ff + half_width :].reshape(2, own_rows, 3, heads_half, HEAD_DIM)
    qkv_own = jnp.transpose(qkv_own, (1, 0, 3, 2, 4)).reshape(own_rows, 3 * width)
    down_own = grads[:, half_ff + half_width :]
    down_own = jnp.concatenate([down_own[:, :width], down_own[:, width:]], axis=0).astype(FULL)
    return (
        activations, loss, input_grad, own_small[0], own_small[1], qkv_own, out_own,
        own_small[2], own_small[3], up_own, down_own,
    )


def solution(mesh):
    groups, depth = mesh.shape["dp"], mesh.shape["seq"]
    split = Mesh(mesh.devices.reshape(groups // 2, 2, depth), AXES)
    dp = ("pair", "core")
    rows3 = P(dp, "seq", None)
    in_specs = (
        rows3, rows3, P(dp, "seq"), P(), P(), P(dp), P(dp), P(dp, None), P(dp, None),
        P(dp), P(dp), P(dp, None), P(dp, None),
    )
    out_specs = (
        rows3, P(), rows3, P(dp), P(dp), P(dp, None), P(dp, None), P(dp), P(dp),
        P(dp, None), P(dp, None),
    )
    return jax.shard_map(shards, mesh=split, in_specs=in_specs, out_specs=out_specs, check_vma=False)
```

time: 1020 us -> 547 us (0.54)
  matrix products: 281 us -> 64.2 us
  waiting for transfers between devices: 320 us -> 197 us
  local copies, waits for them, and re-layouts: 140 us -> 45.2 us
  blocking collectives: 88.7 us -> 8.94 us
  Pallas kernels: 0 us -> 74 us
  other arithmetic: 134 us -> 63.5 us
  starting transfers between devices: 29 us -> 76.8 us
  between operations: 20.1 us -> 7.2 us
    dot_general x33 -> x18, matrix products: 281 us -> 64.2 us  [dot(): return lax.dot_general(left, right, form, preferred_element_type=FULL)]
    all_to_all x4 -> x0, waiting for transfers between devices: 210 us -> none  [the longest x1 85.5 us: shards(): lax.all_to_all(grad_stack, 'seq', split_axis=1, concat_axis=2, tiled=True)]
    ppermute x9 -> x54, waiting for transfers between devices: 38.6 us -> 197 us  [moved(): return lax.ppermute(value, AXES, links)]
    pallas_call x0 -> x2, Pallas kernels: none -> 74 us  [the longest x1 44.3 us: attention_backward(): pl.pallas_call(functools.partial(backward_kernel, rows=rows, block=block,...]
    ppermute x9 -> x54, starting transfers between devices: 9.91 us -> 76.8 us  [moved(): return lax.ppermute(value, AXES, links)]
    convert_element_type x23 -> x7, other arithmetic: 71.7 us -> 5.67 us  [the longest x1 2.72 us: shards(): (grad_middle + grad_in).astype(LOW).reshape(2, slot_rows, width)]
    reduce_scatter x4 -> x0, waiting for transfers between devices: 53.4 us -> none  [the longest x1 53.4 us: shards(): lax.psum_scatter(qkv_grad, 'dp', scatter_dimension=0, tiled=True)]
    psum x2 -> x0, blocking collectives: 51.5 us -> none  [the longest x1 39.1 us: shards(): lax.psum((squares, jnp.sum(valid_mask)), ('dp', 'seq'))]
  transfers between devices with their start and end apart: 22 -> 54, of which waited for: 10 -> 25; matrix products, arithmetic and copies ran while one was open for 49% -> 17% of each run, Pallas kernels for 0% -> 14%
where the time goes in v1:
time: 547 us; the launch traced here: 537 us
  waiting for transfers between devices  197 us (36%)
  starting transfers between devices  76.8 us (14%)
  Pallas kernels  74 us (14%)
  matrix products  64.2 us (12%)
  other arithmetic  63.5 us (12%)
  local copies, waits for them, and re-layouts  45.2 us (8%)
  blocking collectives  8.94 us (2%)
  between operations  7.2 us (1%)
    ppermute x54, waiting for transfers between devices, moved(): return lax.ppermute(value, AXES, links)  197 us
    ppermute x54, starting transfers between devices, moved(): return lax.ppermute(value, AXES, links)  76.8 us
    dot_general x18, matrix products, dot(): return lax.dot_general(left, right, form, preferred_element_type=FULL)  64.2 us
    pallas_call x1, Pallas kernels, attention_backward(): pl.pallas_call(functools.partial(backward_kernel, rows=rows, block=block,...  44.3 us
    pallas_call x1, Pallas kernels, attention_forward(): pl.pallas_call(functools.partial(forward_kernel, rows=rows, block=block),...  29.7 us
  transfers between devices with their start and end apart: 54, of which 25 were waited for; matrix products, arithmetic and copies ran while one was open for 17% of the time, Pallas kernels for 14%

profile of v1, /device:TPU:0, one launch (start us, length us, event | category | flops | bytes accessed | tf_op | source)
XLA Modules:
  0.0 537.4 jit_solution(6214486921616079143)
XLA Ops:
  4.6 6.1 %collective-permute-start = (bf16[384,768]{1,0:T(8,128)(2,1)}, bf16[384,768]{1,0:T(8,128)(2,1)}, u32[]{:S(2)}, u32[]{:S(2)}) collective-permute-start(bf16[384,768]{1,0:T(8,128)(2,1)} %get-tuple-element.153), channel_id=1, source_target_pairs={{0,0},{1,1},{2,4},{3,5},{4,2},{5,3},{6,6},{7,7},{8,8},{9,9},{10,12... | collective-permute-start | bytes 1769480 | tf_op jit(solution)/shard_map/ppermute | solution.py:37
  10.7 2.6 collective-permute-start.1
  20.9 8.9 %all-gather = bf16[8,96,4]{1,2,0:T(4,128)(2,1)S(1)} all-gather(bf16[1,96,4]{1,2,0:T(4,128)(2,1)S(1)} %maximum_bitcast_fusion.1), channel_id=1, replica_groups=mesh['pair'=4,'core'=2,'seq'=4] {'pair','core'}, dimensions={0}, use_global_device_ids=true | all-gather | bytes 6912 | tf_op jit(solution)/shard_map/all_gather | solution.py:385
  42.2 2.3 collective-permute-start.26
  52.0 4.5 collective-permute-done.4
  64.1 10.2 %collective-permute-done.10 = bf16[96,3456]{1,0:T(8,128)(2,1)S(1)} collective-permute-done((bf16[96,3456]{1,0:T(8,128)(2,1)S(1)}, bf16[96,3456]{1,0:T(8,128)(2,1)S(1)}, u32[]{:S(2)}, u32[]{:S(2)}) %collective-permute-start.10) | collective-permute-done | bytes 663584 | tf_op jit(solution)/shard_map/ppermute | solution.py:37
  84.2 28.1 %collective-permute-done.11 = bf16[2,96,3456]{2,1,0:T(8,128)(2,1)} collective-permute-done((bf16[2,96,3456]{2,1,0:T(8,128)(2,1)}, bf16[2,96,3456]{2,1,0:T(8,128)(2,1)}, u32[]{:S(2)}, u32[]{:S(2)}) %collective-permute-start.11) | collective-permute-done | bytes 1327136 | tf_op jit(solution)/shard_map/ppermute | solution.py:37
  114.7 27.1 %collective-permute-done.13 = bf16[2,96,3456]{2,1,0:T(8,128)(2,1)S(1)} collective-permute-done((bf16[2,96,3456]{2,1,0:T(8,128)(2,1)S(1)}, bf16[2,96,3456]{2,1,0:T(8,128)(2,1)S(1)}, u32[]{:S(2)}, u32[]{:S(2)}) %collective-permute-start.13) | collective-permute-done | bytes 1327136 | tf_op jit(solution)/shard_map/ppermute | solution.py:37
  142.5 2.8 pad_maximum_fusion
  150.6 6.0 %convolution_convert_fusion.q_ref.k_ref.v_ref = bf16[1536,1152]{1,0:T(8,128)(2,1)} fusion(bf16[768,1152]{1,0:T(8,128)(2,1)S(1)} %bitcast.313, bf16[768,768]{1,0:T(8,128)(2,1)S(1)} %collective-permute-done.2, bf16[768,768]{1,0:T(8,128)(2,1)S(1)} %fusion.22), kind=kOutput, calls=%fused_computation | convolution fusion | flops 2724397056 | bytes 7667712 | tf_op jit(solution)/shard_map/dot_general | solution.py:26
  156.6 29.7 %attention_forward.1 = (bf16[1536,384]{1,0:T(8,128)(2,1)}, f32[3,2,1536]{2,1,0:T(2,128)}) custom-call(s32[2]{0:T(128)} %add_clamp_fusion.counts_ref, bf16[1536,1152]{1,0:T(8,128)(2,1)} %convolution_convert_fusion.q_ref.k_ref.v_ref, bf16[1536,1152]{1,0:T(8,128)(2,1)} %convolution_convert_fusion.q_ref.k_ref.v_ref, ...), custom_call_target="tpu_custom_call" | custom-call | flops 7247757312 | bytes 5308416 | tf_op jit(solution)/shard_map/attention_forward/pallas_call | solution.py:176
  191.7 3.3 fusion.75
  196.0 9.0 %collective-permute-done.21 = bf16[400,768]{1,0:T(8,128)(2,1)S(1)} collective-permute-done((bf16[400,768]{1,0:T(8,128)(2,1)S(1)}, bf16[400,768]{1,0:T(8,128)(2,1)S(1)}, u32[]{:S(2)}, u32[]{:S(2)}) %collective-permute-start.21) | collective-permute-done | bytes 614432 | tf_op jit(solution)/shard_map/ppermute | solution.py:37
  210.2 5.1 multiply_convert_fusion.1
  217.3 4.0 multiply_convert_fusion
  227.2 3.5 convolution_convert_fusion.2
  230.7 5.3 fusion.5
  236.0 5.5 %fusion.11 = bf16[768,1536]{1,0:T(8,128)(2,1)S(1)} fusion(f32[768,1536]{1,0:T(8,128)S(1)} %get-tuple-element.186, bf16[768,768]{1,0:T(8,128)(2,1)S(1)} %get-tuple-element.187, bf16[768,768]{1,0:T(8,128)(2,1)S(1)} %get-tuple-element.101, bf16[768,768]{1,0:T(8,128)(2,1)S(1)} %get-tuple-element.100), kind=kOutput, calls=%fused_computation.17 | convolution fusion | flops 1828454400 | bytes 10616832 | tf_op jit(solution)/shard_map/dot_general | solution.py:26
  241.6 3.5 convolution_convert_fusion.3
  245.0 3.7 fusion.33
  248.7 4.2 multiply_reduce_fusion
  253.0 3.5 fusion.13
  267.4 2.8 pad_maximum_fusion.1
  270.2 10.2 %collective-permute-start.36 = (bf16[768,3456]{1,0:T(8,128)(2,1)}, bf16[768,3456]{1,0:T(8,128)(2,1)}, u32[]{:S(2)}, u32[]{:S(2)}) collective-permute-start(bf16[768,3456]{1,0:T(8,128)(2,1)} %pad_maximum_fusion.1), channel_id=1, source_target_pairs={{0,4},{1,5},{2,6},{3,7},{4,0},{5,1},{6,2},{7,3},{8,12},{9,13},{10,... | collective-permute-start | bytes 15925256 | tf_op jit(solution)/shard_map/ppermute | solution.py:37
  286.4 6.0 %collective-permute-start.15 = (bf16[384,768]{1,0:T(8,128)(2,1)}, bf16[384,768]{1,0:T(8,128)(2,1)}, u32[]{:S(2)}, u32[]{:S(2)}) collective-permute-start(bf16[384,768]{1,0:T(8,128)(2,1)} %get-tuple-element.149), channel_id=1, source_target_pairs={{0,0},{1,1},{2,4},{3,5},{4,2},{5,3},{6,6},{7,7},{8,8},{9,9},{10,12... | collective-permute-start | bytes 1769480 | tf_op jit(solution)/shard_map/ppermute | solution.py:37
  292.3 7.1 %collective-permute-start.16 = (bf16[384,768]{1,0:T(8,128)(2,1)}, bf16[384,768]{1,0:T(8,128)(2,1)}, u32[]{:S(2)}, u32[]{:S(2)}) collective-permute-start(bf16[384,768]{1,0:T(8,128)(2,1)} %get-tuple-element.150), channel_id=1, source_target_pairs={{0,1},{1,0},{2,5},{3,4},{4,3},{5,2},{6,7},{7,6},{8,9},{9,8},{10,13... | collective-permute-start | bytes 1769480 | tf_op jit(solution)/shard_map/ppermute | solution.py:37
  299.5 3.4 convolution_convert_fusion.5
  304.1 44.3 %attention_backward.1 = bf16[1536,1152]{1,0:T(8,128)(2,1)} custom-call(s32[2]{0:T(128)} %add_clamp_fusion.counts_ref, bf16[1536,1152]{1,0:T(8,128)(2,1)} %convolution_convert_fusion.q_ref.k_ref.v_ref, bf16[1536,1152]{1,0:T(8,128)(2,1)} %convolution_convert_fusion.q_ref.k_ref.v_ref, bf16[1536,1152]{1,0:T(8,128)(2,1)} %convolution_convert_fusion.q_ref.k_ref.v_ref, ...), custom_call_target="tpu_custom_call" | custom-call | flops 18119393280 | bytes 8847360 | tf_op jit(solution)/shard_map/attention_backward/pallas_call | solution.py:261
  348.4 6.1 %convolution_convert_fusion.1 = bf16[768,1152]{1,0:T(8,128)(2,1)S(1)} fusion(bf16[1536,1152]{1,0:T(8,128)(2,1)} %attention_backward.1, bf16[768,768]{1,0:T(8,128)(2,1)} %copy-done.58, bf16[768,768]{1,0:T(8,128)(2,1)} %copy-done.33), kind=kOutput, calls=%fused_computation.23 | convolution fusion | flops 2723512320 | bytes 7667712 | tf_op jit(solution)/shard_map/dot_general | solution.py:26
  354.5 3.3 fusion.82
  361.8 7.0 %collective-permute-done.45 = bf16[2,96,1152]{2,1,0:T(8,128)(2,1)S(1)} collective-permute-done((bf16[2,96,1152]{2,1,0:T(8,128)(2,1)S(1)}, bf16[2,96,1152]{2,1,0:T(8,128)(2,1)S(1)}, u32[]{:S(2)}, u32[]{:S(2)}) %collective-permute-start.45) | collective-permute-done | bytes 442400 | tf_op jit(solution)/shard_map/ppermute | solution.py:37
  371.1 3.7 collective-permute-done.46
  377.2 4.1 maximum_add_fusion
  383.1 3.8 collective-permute-start.50
  388.0 3.5 collective-permute-done.50
  394.4 14.7 %collective-permute-done.37 = bf16[2,96,3456]{2,1,0:T(8,128)(2,1)S(1)} collective-permute-done((bf16[2,96,3456]{2,1,0:T(8,128)(2,1)S(1)}, bf16[2,96,3456]{2,1,0:T(8,128)(2,1)S(1)}, u32[]{:S(2)}, u32[]{:S(2)}) %collective-permute-start.37) | collective-permute-done | bytes 1327136 | tf_op jit(solution)/shard_map/ppermute | solution.py:37
  409.6 15.3 %collective-permute-done.39 = bf16[2,96,3456]{2,1,0:T(8,128)(2,1)S(1)} collective-permute-done((bf16[2,96,3456]{2,1,0:T(8,128)(2,1)S(1)}, bf16[2,96,3456]{2,1,0:T(8,128)(2,1)S(1)}, u32[]{:S(2)}, u32[]{:S(2)}) %collective-permute-start.39) | collective-permute-done | bytes 1327136 | tf_op jit(solution)/shard_map/ppermute | solution.py:37
  426.7 9.8 %collective-permute-done.38 = bf16[96,3456]{1,0:T(8,128)(2,1)S(1)} collective-permute-done((bf16[96,3456]{1,0:T(8,128)(2,1)S(1)}, bf16[96,3456]{1,0:T(8,128)(2,1)S(1)}, u32[]{:S(2)}, u32[]{:S(2)}) %collective-permute-start.38) | collective-permute-done | bytes 663584 | tf_op jit(solution)/shard_map/ppermute | solution.py:37
  440.4 2.4 fusion.24
  454.0 4.9 collective-permute-start.42
  460.5 2.3 collective-permute-done.31
  462.8 8.4 %collective-permute-done.42 = bf16[48,3456]{1,0:T(8,128)(2,1)S(1)} collective-permute-done((bf16[48,3456]{1,0:T(8,128)(2,1)S(1)}, bf16[48,3456]{1,0:T(8,128)(2,1)S(1)}, u32[]{:S(2)}, u32[]{:S(2)}) %collective-permute-start.42) | collective-permute-done | bytes 331808 | tf_op jit(solution)/shard_map/ppermute | solution.py:37
  471.4 2.7 fusion.28
  474.1 3.0 collective-permute-start.33
  478.1 19.2 %collective-permute-done.33 = f32[8,768]{1,0:T(8,128)S(1)} collective-permute-done((f32[8,768]{1,0:T(8,128)S(1)}, f32[8,768]{1,0:T(8,128)S(1)}, u32[]{:S(2)}, u32[]{:S(2)}) %collective-permute-start.33) | collective-permute-done | bytes 24608 | tf_op jit(solution)/shard_map/ppermute | solution.py:37
  499.4 21.6 %collective-permute-done.44 = bf16[96,3456]{1,0:T(8,128)(2,1)S(1)} collective-permute-done((bf16[96,3456]{1,0:T(8,128)(2,1)S(1)}, bf16[96,3456]{1,0:T(8,128)(2,1)S(1)}, u32[]{:S(2)}, u32[]{:S(2)}) %collective-permute-start.44) | collective-permute-done | bytes 663584 | tf_op jit(solution)/shard_map/ppermute | solution.py:37
  525.9 2.4 reshape.251
  530.6 2.6 reshape.252
  (383 shorter events, 136.6 us)
Async XLA Ops:
  3.1 45.5 %collective-permute-start.3 = (bf16[96,1152]{1,0:T(8,128)(2,1)}, bf16[96,1152]{1,0:T(8,128)(2,1)S(1)}, u32[]{:S(2)}, u32[]{:S(2)}) collective-permute-start(bf16[96,1152]{1,0:T(8,128)(2,1)} %bitcast.18), channel_id=1, source_target_pairs={{0,4},{1,5},{2,6},{3,7},{4,0},{5,1},{6,2},{7,3},{8,12},{9,13},{10,... | collective-permute-start | bytes 663560 | tf_op jit(solution)/shard_map/ppermute | solution.py:37
  4.6 55.8 %collective-permute-start = (bf16[384,768]{1,0:T(8,128)(2,1)}, bf16[384,768]{1,0:T(8,128)(2,1)}, u32[]{:S(2)}, u32[]{:S(2)}) collective-permute-start(bf16[384,768]{1,0:T(8,128)(2,1)} %get-tuple-element.153), channel_id=1, source_target_pairs={{0,0},{1,1},{2,4},{3,5},{4,2},{5,3},{6,6},{7,7},{8,8},{9,9},{10,12... | collective-permute-start | bytes 1769480 | tf_op jit(solution)/shard_map/ppermute | solution.py:37
  10.7 51.2 %collective-permute-start.1 = (bf16[384,768]{1,0:T(8,128)(2,1)}, bf16[384,768]{1,0:T(8,128)(2,1)}, u32[]{:S(2)}, u32[]{:S(2)}) collective-permute-start(bf16[384,768]{1,0:T(8,128)(2,1)} %get-tuple-element.154), channel_id=1, source_target_pairs={{0,1},{1,0},{2,5},{3,4},{4,3},{5,2},{6,7},{7,6},{8,9},{9,8},{10,13... | collective-permute-start | bytes 1769480 | tf_op jit(solution)/shard_map/ppermute | solution.py:37
  16.4 33.8 %collective-permute-start.9 = (bf16[96,1920]{1,0:T(8,128)(2,1)}, bf16[96,1920]{1,0:T(8,128)(2,1)}, u32[]{:S(2)}, u32[]{:S(2)}) collective-permute-start(bf16[96,1920]{1,0:T(8,128)(2,1)} %fusion.54), channel_id=1, source_target_pairs={{0,4},{1,5},{2,6},{3,7},{4,0},{5,1},{6,2},{7,3},{8,12},{9,13},{10,... | collective-permute-start | bytes 1105928 | tf_op jit(solution)/shard_map/ppermute | solution.py:37
  17.9 11.9 %collective-permute-start.22 = (f32[8,128]{1,0:T(8,128)S(1)}, f32[8,128]{1,0:T(8,128)S(1)}, u32[]{:S(2)}, u32[]{:S(2)}) collective-permute-start(f32[8,128]{1,0:T(8,128)S(1)} %broadcast_in_dim.24), channel_id=1, source_target_pairs={{0,4},{1,5},{2,6},{3,7},{4,0},{5,1},{6,2},{7,3},{8,12},{9,13},{10,... | collective-permute-start | bytes 12296 | tf_op jit(solution)/shard_map/ppermute | solution.py:37
  42.2 4.5 collective-permute-start.26
  46.7 34.0 %collective-permute-start.17 = (bf16[400,768]{1,0:T(8,128)(2,1)}, bf16[400,768]{1,0:T(8,128)(2,1)}, u32[]{:S(2)}, u32[]{:S(2)}) collective-permute-start(bf16[400,768]{1,0:T(8,128)(2,1)} %broadcast_select_fusion.4), channel_id=1, source_target_pairs={{0,4},{1,5},{2,6},{3,7},{4,0},{5,1},{6,2},{7,3},{8,12},{9,13},{10,... | collective-permute-start | bytes 1843208 | tf_op jit(solution)/shard_map/ppermute | solution.py:37
  48.6 7.9 %collective-permute-start.4 = (bf16[96,1152]{1,0:T(8,128)(2,1)S(1)}, bf16[96,1152]{1,0:T(8,128)(2,1)S(1)}, u32[]{:S(2)}, u32[]{:S(2)}) collective-permute-start(bf16[96,1152]{1,0:T(8,128)(2,1)S(1)} %get-tuple-element.171), channel_id=1, source_target_pairs={{0,8},{1,9},{2,10},{3,11},{4,12},{5,13},{6,14},{7,15},{8,0},{9,1},... | collective-permute-start | bytes 663560 | tf_op jit(solution)/shard_map/ppermute | solution.py:37
  50.1 7.9 %collective-permute-start.6 = (bf16[96,1152]{1,0:T(8,128)(2,1)S(1)}, bf16[96,1152]{1,0:T(8,128)(2,1)S(1)}, u32[]{:S(2)}, u32[]{:S(2)}) collective-permute-start(bf16[96,1152]{1,0:T(8,128)(2,1)S(1)} %get-tuple-element.172), channel_id=1, source_target_pairs={{0,16},{1,17},{2,18},{3,19},{4,20},{5,21},{6,22},{7,23},{8,24},{9,... | collective-permute-start | bytes 663560 | tf_op jit(solution)/shard_map/ppermute | solution.py:37
  56.5 17.8 %collective-permute-start.10 = (bf16[96,3456]{1,0:T(8,128)(2,1)S(1)}, bf16[96,3456]{1,0:T(8,128)(2,1)S(1)}, u32[]{:S(2)}, u32[]{:S(2)}) collective-permute-start(bf16[96,3456]{1,0:T(8,128)(2,1)S(1)} %get-tuple-element.129), channel_id=1, source_target_pairs={{0,8},{1,9},{2,10},{3,11},{4,12},{5,13},{6,14},{7,15},{8,0},{9,1},... | collective-permute-start | bytes 1990664 | tf_op jit(solution)/shard_map/ppermute | solution.py:37
  58.0 17.8 %collective-permute-start.12 = (bf16[96,3456]{1,0:T(8,128)(2,1)S(1)}, bf16[96,3456]{1,0:T(8,128)(2,1)S(1)}, u32[]{:S(2)}, u32[]{:S(2)}) collective-permute-start(bf16[96,3456]{1,0:T(8,128)(2,1)S(1)} %get-tuple-element.130), channel_id=1, source_target_pairs={{0,16},{1,17},{2,18},{3,19},{4,20},{5,21},{6,22},{7,23},{8,24},{9,... | collective-permute-start | bytes 1990664 | tf_op jit(solution)/shard_map/ppermute | solution.py:37
  60.4 84.8 %collective-permute-start.5 = (bf16[2,96,1152]{2,1,0:T(8,128)(2,1)}, bf16[2,96,1152]{2,1,0:T(8,128)(2,1)}, u32[]{:S(2)}, u32[]{:S(2)}) collective-permute-start(bf16[2,96,1152]{2,1,0:T(8,128)(2,1)} %pad_maximum_fusion.32), channel_id=1, source_target_pairs={{0,16},{1,17},{2,18},{3,19},{4,20},{5,21},{6,22},{7,23},{8,24},{9,... | collective-permute-start | bytes 1327112 | tf_op jit(solution)/shard_map/ppermute | solution.py:37
  61.9 84.4 %collective-permute-start.7 = (bf16[2,96,1152]{2,1,0:T(8,128)(2,1)}, bf16[2,96,1152]{2,1,0:T(8,128)(2,1)}, u32[]{:S(2)}, u32[]{:S(2)}) collective-permute-start(bf16[2,96,1152]{2,1,0:T(8,128)(2,1)} %pad_maximum_fusion.33), channel_id=1, source_target_pairs={{0,8},{1,9},{2,10},{3,11},{4,12},{5,13},{6,14},{7,15},{8,0},{9,1},... | collective-permute-start | bytes 1327112 | tf_op jit(solution)/shard_map/ppermute | solution.py:37
  79.0 33.3 %collective-permute-start.11 = (bf16[2,96,3456]{2,1,0:T(8,128)(2,1)}, bf16[2,96,3456]{2,1,0:T(8,128)(2,1)}, u32[]{:S(2)}, u32[]{:S(2)}) collective-permute-start(bf16[2,96,3456]{2,1,0:T(8,128)(2,1)} %pad_maximum_fusion.15), channel_id=1, source_target_pairs={{0,16},{1,17},{2,18},{3,19},{4,20},{5,21},{6,22},{7,23},{8,24},{9,... | collective-permute-start | bytes 3981320 | tf_op jit(solution)/shard_map/ppermute | solution.py:37
  80.6 68.9 %collective-permute-start.2 = (bf16[768,768]{1,0:T(8,128)(2,1)S(1)}, bf16[768,768]{1,0:T(8,128)(2,1)S(1)}, u32[]{:S(2)}, u32[]{:S(2)}) collective-permute-start(bf16[768,768]{1,0:T(8,128)(2,1)S(1)} %fusion.22), channel_id=1, source_target_pairs={{0,4},{1,5},{2,6},{3,7},{4,0},{5,1},{6,2},{7,3},{8,12},{9,13},{10,... | collective-permute-start | bytes 3538952 | tf_op jit(solution)/shard_map/ppermute | solution.py:37
  82.5 65.5 %collective-permute-start.18 = (bf16[400,768]{1,0:T(8,128)(2,1)S(1)}, bf16[400,768]{1,0:T(8,128)(2,1)S(1)}, u32[]{:S(2)}, u32[]{:S(2)}) collective-permute-start(bf16[400,768]{1,0:T(8,128)(2,1)S(1)} %get-tuple-element.93), channel_id=1, source_target_pairs={{0,8},{1,9},{2,10},{3,11},{4,12},{5,13},{6,14},{7,15},{8,0},{9,1},... | collective-permute-start | bytes 1843208 | tf_op jit(solution)/shard_map/ppermute | solution.py:37
  112.3 29.5 %collective-permute-start.13 = (bf16[2,96,3456]{2,1,0:T(8,128)(2,1)S(1)}, bf16[2,96,3456]{2,1,0:T(8,128)(2,1)S(1)}, u32[]{:S(2)}, u32[]{:S(2)}) collective-permute-start(bf16[2,96,3456]{2,1,0:T(8,128)(2,1)S(1)} %pad_maximum_fusion.16), channel_id=1, source_target_pairs={{0,8},{1,9},{2,10},{3,11},{4,12},{5,13},{6,14},{7,15},{8,0},{9,1},... | collective-permute-start | bytes 3981320 | tf_op jit(solution)/shard_map/ppermute | solution.py:37
  145.2 61.4 %collective-permute-start.14 = (bf16[768,3456]{1,0:T(8,128)(2,1)}, bf16[768,3456]{1,0:T(8,128)(2,1)}, u32[]{:S(2)}, u32[]{:S(2)}) collective-permute-start(bf16[768,3456]{1,0:T(8,128)(2,1)} %bitcast.47), channel_id=1, source_target_pairs={{0,4},{1,5},{2,6},{3,7},{4,0},{5,1},{6,2},{7,3},{8,12},{9,13},{10,... | collective-permute-start | bytes 15925256 | tf_op jit(solution)/shard_map/ppermute | solution.py:37
  149.0 38.6 %collective-permute-start.19 = (bf16[400,768]{1,0:T(8,128)(2,1)}, bf16[400,768]{1,0:T(8,128)(2,1)}, u32[]{:S(2)}, u32[]{:S(2)}) collective-permute-start(bf16[400,768]{1,0:T(8,128)(2,1)} %broadcast_select_fusion.8), channel_id=1, source_target_pairs={{0,16},{1,17},{2,18},{3,19},{4,20},{5,21},{6,22},{7,23},{8,24},{9,... | collective-permute-start | bytes 1843208 | tf_op jit(solution)/shard_map/ppermute | solution.py:37
  187.4 7.7 %collective-permute-start.8 = (bf16[768,384]{1,0:T(8,128)(2,1)S(1)}, bf16[768,384]{1,0:T(8,128)(2,1)S(1)}, u32[]{:S(2)}, u32[]{:S(2)}) collective-permute-start(bf16[768,384]{1,0:T(8,128)(2,1)S(1)} %slice.170), channel_id=1, source_target_pairs={{0,4},{1,5},{2,6},{3,7},{4,0},{5,1},{6,2},{7,3},{8,12},{9,13},{10,... | collective-permute-start | bytes 1769480 | tf_op jit(solution)/shard_map/ppermute | solution.py:37
  189.4 6.6 %collective-permute-start.20 = (bf16[400,768]{1,0:T(8,128)(2,1)S(1)}, bf16[400,768]{1,0:T(8,128)(2,1)S(1)}, u32[]{:S(2)}, u32[]{:S(2)}) collective-permute-start(bf16[400,768]{1,0:T(8,128)(2,1)S(1)} %get-tuple-element.133), channel_id=1, source_target_pairs={{0,0},{1,1},{2,4},{3,5},{4,2},{5,3},{6,6},{7,7},{8,8},{9,9},{10,12... | collective-permute-start | bytes 1843208 | tf_op jit(solution)/shard_map/ppermute | solution.py:37
  190.1 14.9 %collective-permute-start.21 = (bf16[400,768]{1,0:T(8,128)(2,1)S(1)}, bf16[400,768]{1,0:T(8,128)(2,1)S(1)}, u32[]{:S(2)}, u32[]{:S(2)}) collective-permute-start(bf16[400,768]{1,0:T(8,128)(2,1)S(1)} %get-tuple-element.134), channel_id=1, source_target_pairs={{0,1},{1,0},{2,5},{3,4},{4,3},{5,2},{6,7},{7,6},{8,9},{9,8},{10,13... | collective-permute-start | bytes 1843208 | tf_op jit(solution)/shard_map/ppermute | solution.py:37
  270.2 106.9 %collective-permute-start.36 = (bf16[768,3456]{1,0:T(8,128)(2,1)}, bf16[768,3456]{1,0:T(8,128)(2,1)}, u32[]{:S(2)}, u32[]{:S(2)}) collective-permute-start(bf16[768,3456]{1,0:T(8,128)(2,1)} %pad_maximum_fusion.1), channel_id=1, source_target_pairs={{0,4},{1,5},{2,6},{3,7},{4,0},{5,1},{6,2},{7,3},{8,12},{9,13},{10,... | collective-permute-start | bytes 15925256 | tf_op jit(solution)/shard_map/ppermute | solution.py:37
  284.0 18.9 %collective-permute-start.27 = (bf16[768,384]{1,0:T(8,128)(2,1)S(1)}, bf16[768,384]{1,0:T(8,128)(2,1)S(1)}, u32[]{:S(2)}, u32[]{:S(2)}) collective-permute-start(bf16[768,384]{1,0:T(8,128)(2,1)S(1)} %get-tuple-element.146), channel_id=1, source_target_pairs={{0,4},{1,5},{2,6},{3,7},{4,0},{5,1},{6,2},{7,3},{8,12},{9,13},{10,... | collective-permute-start | bytes 1769480 | tf_op jit(solution)/shard_map/ppermute | solution.py:37
  286.4 74.0 %collective-permute-start.15 = (bf16[384,768]{1,0:T(8,128)(2,1)}, bf16[384,768]{1,0:T(8,128)(2,1)}, u32[]{:S(2)}, u32[]{:S(2)}) collective-permute-start(bf16[384,768]{1,0:T(8,128)(2,1)} %get-tuple-element.149), channel_id=1, source_target_pairs={{0,0},{1,1},{2,4},{3,5},{4,2},{5,3},{6,6},{7,7},{8,8},{9,9},{10,12... | collective-permute-start | bytes 1769480 | tf_op jit(solution)/shard_map/ppermute | solution.py:37
  292.3 68.1 %collective-permute-start.16 = (bf16[384,768]{1,0:T(8,128)(2,1)}, bf16[384,768]{1,0:T(8,128)(2,1)}, u32[]{:S(2)}, u32[]{:S(2)}) collective-permute-start(bf16[384,768]{1,0:T(8,128)(2,1)} %get-tuple-element.150), channel_id=1, source_target_pairs={{0,1},{1,0},{2,5},{3,4},{4,3},{5,2},{6,7},{7,6},{8,9},{9,8},{10,13... | collective-permute-start | bytes 1769480 | tf_op jit(solution)/shard_map/ppermute | solution.py:37
  358.0 10.7 %collective-permute-start.45 = (bf16[2,96,1152]{2,1,0:T(8,128)(2,1)S(1)}, bf16[2,96,1152]{2,1,0:T(8,128)(2,1)S(1)}, u32[]{:S(2)}, u32[]{:S(2)}) collective-permute-start(bf16[2,96,1152]{2,1,0:T(8,128)(2,1)S(1)} %dynamic-slice_bitcast_fusion.12), channel_id=1, source_target_pairs={{0,8},{1,9},{2,10},{3,11},{4,12},{5,13},{6,14},{7,15},{8,0},{9,1},... | collective-permute-start | bytes 1327112 | tf_op jit(solution)/shard_map/ppermute | solution.py:37
  359.6 11.2 %collective-permute-start.47 = (bf16[2,96,1152]{2,1,0:T(8,128)(2,1)S(1)}, bf16[2,96,1152]{2,1,0:T(8,128)(2,1)S(1)}, u32[]{:S(2)}, u32[]{:S(2)}) collective-permute-start(bf16[2,96,1152]{2,1,0:T(8,128)(2,1)S(1)} %dynamic-slice_bitcast_fusion.11), channel_id=1, source_target_pairs={{0,16},{1,17},{2,18},{3,19},{4,20},{5,21},{6,22},{7,23},{8,24},{9,... | collective-permute-start | bytes 1327112 | tf_op jit(solution)/shard_map/ppermute | solution.py:37
  360.3 80.0 %collective-permute-start.28 = (bf16[768,768]{1,0:T(8,128)(2,1)S(1)}, bf16[768,768]{1,0:T(8,128)(2,1)S(1)}, u32[]{:S(2)}, u32[]{:S(2)}) collective-permute-start(bf16[768,768]{1,0:T(8,128)(2,1)S(1)} %slice.323), channel_id=1, source_target_pairs={{0,4},{1,5},{2,6},{3,7},{4,0},{5,1},{6,2},{7,3},{8,12},{9,13},{10,... | collective-permute-start | bytes 3538952 | tf_op jit(solution)/shard_map/ppermute | solution.py:37
  368.9 6.0 %collective-permute-start.46 = (bf16[96,1152]{1,0:T(8,128)(2,1)S(1)}, bf16[96,1152]{1,0:T(8,128)(2,1)S(1)}, u32[]{:S(2)}, u32[]{:S(2)}) collective-permute-start(bf16[96,1152]{1,0:T(8,128)(2,1)S(1)} %dynamic-slice_bitcast_fusion.16), channel_id=1, source_target_pairs={{0,16},{1,17},{2,18},{3,19},{4,20},{5,21},{6,22},{7,23},{8,24},{9,... | collective-permute-start | bytes 663560 | tf_op jit(solution)/shard_map/ppermute | solution.py:37
  370.9 6.0 %collective-permute-start.48 = (bf16[96,1152]{1,0:T(8,128)(2,1)S(1)}, bf16[96,1152]{1,0:T(8,128)(2,1)S(1)}, u32[]{:S(2)}, u32[]{:S(2)}) collective-permute-start(bf16[96,1152]{1,0:T(8,128)(2,1)S(1)} %dynamic-slice_bitcast_fusion.15), channel_id=1, source_target_pairs={{0,8},{1,9},{2,10},{3,11},{4,12},{5,13},{6,14},{7,15},{8,0},{9,1},... | collective-permute-start | bytes 663560 | tf_op jit(solution)/shard_map/ppermute | solution.py:37
  377.0 6.0 %collective-permute-start.49 = (bf16[96,1152]{1,0:T(8,128)(2,1)S(1)}, bf16[96,1152]{1,0:T(8,128)(2,1)S(1)}, u32[]{:S(2)}, u32[]{:S(2)}) collective-permute-start(bf16[96,1152]{1,0:T(8,128)(2,1)S(1)} %dynamic-slice_bitcast_fusion.14), channel_id=1, source_target_pairs={{0,1},{1,0},{2,3},{3,2},{4,5},{5,4},{6,7},{7,6},{8,9},{9,8},{10,11... | collective-permute-start | bytes 663560 | tf_op jit(solution)/shard_map/ppermute | solution.py:37
  381.8 27.2 %collective-permute-start.37 = (bf16[2,96,3456]{2,1,0:T(8,128)(2,1)S(1)}, bf16[2,96,3456]{2,1,0:T(8,128)(2,1)S(1)}, u32[]{:S(2)}, u32[]{:S(2)}) collective-permute-start(bf16[2,96,3456]{2,1,0:T(8,128)(2,1)S(1)} %dynamic-slice_bitcast_fusion.1), channel_id=1, source_target_pairs={{0,8},{1,9},{2,10},{3,11},{4,12},{5,13},{6,14},{7,15},{8,0},{9,1},... | collective-permute-start | bytes 3981320 | tf_op jit(solution)/shard_map/ppermute | solution.py:37
  383.1 8.4 %collective-permute-start.50 = (bf16[48,1152]{1,0:T(8,128)(2,1)S(1)}, bf16[48,1152]{1,0:T(8,128)(2,1)S(1)}, u32[]{:S(2)}, u32[]{:S(2)}) collective-permute-start(bf16[48,1152]{1,0:T(8,128)(2,1)S(1)} %dynamic-slice_bitcast_fusion.17), channel_id=1, source_target_pairs={{0,2},{1,3},{2,0},{3,1},{4,6},{5,7},{6,4},{7,5},{8,10},{9,11},{10,... | collective-permute-start | bytes 331784 | tf_op jit(solution)/shard_map/ppermute | solution.py:37
  391.5 48.2 %collective-permute-start.51 = (bf16[48,1152]{1,0:T(8,128)(2,1)S(1)}, bf16[48,1152]{1,0:T(8,128)(2,1)S(1)}, u32[]{:S(2)}, u32[]{:S(2)}) collective-permute-start(bf16[48,1152]{1,0:T(8,128)(2,1)S(1)} %bitcast_add_fusion.12), channel_id=1, source_target_pairs={{0,2},{1,3},{2,0},{3,1},{4,6},{5,7},{6,4},{7,5},{8,10},{9,11},{10,... | collective-permute-start | bytes 331784 | tf_op jit(solution)/shard_map/ppermute | solution.py:37
  392.8 32.1 %collective-permute-start.39 = (bf16[2,96,3456]{2,1,0:T(8,128)(2,1)S(1)}, bf16[2,96,3456]{2,1,0:T(8,128)(2,1)S(1)}, u32[]{:S(2)}, u32[]{:S(2)}) collective-permute-start(bf16[2,96,3456]{2,1,0:T(8,128)(2,1)S(1)} %dynamic-slice_bitcast_fusion), channel_id=1, source_target_pairs={{0,16},{1,17},{2,18},{3,19},{4,20},{5,21},{6,22},{7,23},{8,24},{9,... | collective-permute-start | bytes 3981320 | tf_op jit(solution)/shard_map/ppermute | solution.py:37
  409.3 27.2 %collective-permute-start.38 = (bf16[96,3456]{1,0:T(8,128)(2,1)S(1)}, bf16[96,3456]{1,0:T(8,128)(2,1)S(1)}, u32[]{:S(2)}, u32[]{:S(2)}) collective-permute-start(bf16[96,3456]{1,0:T(8,128)(2,1)S(1)} %dynamic-slice_bitcast_fusion.4), channel_id=1, source_target_pairs={{0,16},{1,17},{2,18},{3,19},{4,20},{5,21},{6,22},{7,23},{8,24},{9,... | collective-permute-start | bytes 1990664 | tf_op jit(solution)/shard_map/ppermute | solution.py:37
  425.1 11.7 %collective-permute-start.40 = (bf16[96,3456]{1,0:T(8,128)(2,1)S(1)}, bf16[96,3456]{1,0:T(8,128)(2,1)S(1)}, u32[]{:S(2)}, u32[]{:S(2)}) collective-permute-start(bf16[96,3456]{1,0:T(8,128)(2,1)S(1)} %dynamic-slice_bitcast_fusion.3), channel_id=1, source_target_pairs={{0,8},{1,9},{2,10},{3,11},{4,12},{5,13},{6,14},{7,15},{8,0},{9,1},... | collective-permute-start | bytes 1990664 | tf_op jit(solution)/shard_map/ppermute | solution.py:37
  438.0 14.6 %collective-permute-start.41 = (bf16[96,3456]{1,0:T(8,128)(2,1)}, bf16[96,3456]{1,0:T(8,128)(2,1)}, u32[]{:S(2)}, u32[]{:S(2)}) collective-permute-start(bf16[96,3456]{1,0:T(8,128)(2,1)} %dynamic-slice_bitcast_fusion.2), channel_id=1, source_target_pairs={{0,1},{1,0},{2,3},{3,2},{4,5},{5,4},{6,7},{7,6},{8,9},{9,8},{10,11... | collective-permute-start | bytes 1990664 | tf_op jit(solution)/shard_map/ppermute | solution.py:37
  448.9 50.4 %collective-permute-start.52 = (bf16[96,1152]{1,0:T(8,128)(2,1)S(1)}, bf16[96,1152]{1,0:T(8,128)(2,1)S(1)}, u32[]{:S(2)}, u32[]{:S(2)}) collective-permute-start(bf16[96,1152]{1,0:T(8,128)(2,1)S(1)} %pad_maximum_fusion.35), channel_id=1, source_target_pairs={{0,1},{1,0},{2,3},{3,2},{4,5},{5,4},{6,7},{7,6},{8,9},{9,8},{10,11... | collective-permute-start | bytes 663560 | tf_op jit(solution)/shard_map/ppermute | solution.py:37
  450.1 8.8 %collective-permute-start.30 = (f32[8,768]{1,0:T(8,128)S(1)}, f32[8,768]{1,0:T(8,128)S(1)}, u32[]{:S(2)}, u32[]{:S(2)}) collective-permute-start(f32[8,768]{1,0:T(8,128)S(1)} %add.314), channel_id=1, source_target_pairs={{0,8},{1,9},{2,10},{3,11},{4,12},{5,13},{6,14},{7,15},{8,0},{9,1},... | collective-permute-start | bytes 73736 | tf_op jit(solution)/shard_map/ppermute | solution.py:37
  454.0 17.3 %collective-permute-start.42 = (bf16[48,3456]{1,0:T(8,128)(2,1)S(1)}, bf16[48,3456]{1,0:T(8,128)(2,1)S(1)}, u32[]{:S(2)}, u32[]{:S(2)}) collective-permute-start(bf16[48,3456]{1,0:T(8,128)(2,1)S(1)} %dynamic-slice_bitcast_fusion.13), channel_id=1, source_target_pairs={{0,2},{1,3},{2,0},{3,1},{4,6},{5,7},{6,4},{7,5},{8,10},{9,11},{10,... | collective-permute-start | bytes 995336 | tf_op jit(solution)/shard_map/ppermute | solution.py:37
  462.8 11.3 %collective-permute-start.32 = (f32[8,768]{1,0:T(8,128)S(1)}, f32[8,768]{1,0:T(8,128)S(1)}, u32[]{:S(2)}, u32[]{:S(2)}) collective-permute-start(f32[8,768]{1,0:T(8,128)S(1)} %add.316), channel_id=1, source_target_pairs={{0,1},{1,0},{2,3},{3,2},{4,5},{5,4},{6,7},{7,6},{8,9},{9,8},{10,11... | collective-permute-start | bytes 73736 | tf_op jit(solution)/shard_map/ppermute | solution.py:37
  471.3 27.3 %collective-permute-start.43 = (bf16[48,3456]{1,0:T(8,128)(2,1)S(1)}, bf16[48,3456]{1,0:T(8,128)(2,1)S(1)}, u32[]{:S(2)}, u32[]{:S(2)}) collective-permute-start(bf16[48,3456]{1,0:T(8,128)(2,1)S(1)} %bitcast_add_fusion.8), channel_id=1, source_target_pairs={{0,2},{1,3},{2,0},{3,1},{4,6},{5,7},{6,4},{7,5},{8,10},{9,11},{10,... | collective-permute-start | bytes 995336 | tf_op jit(solution)/shard_map/ppermute | solution.py:37
  474.1 23.2 %collective-permute-start.33 = (f32[8,768]{1,0:T(8,128)S(1)}, f32[8,768]{1,0:T(8,128)S(1)}, u32[]{:S(2)}, u32[]{:S(2)}) collective-permute-start(f32[8,768]{1,0:T(8,128)S(1)} %add.317), channel_id=1, source_target_pairs={{0,2},{1,3},{2,0},{3,1},{4,6},{5,7},{6,4},{7,5},{8,10},{9,11},{10,... | collective-permute-start | bytes 73736 | tf_op jit(solution)/shard_map/ppermute | solution.py:37
  477.2 44.5 %collective-permute-start.34 = (bf16[384,768]{1,0:T(8,128)(2,1)S(1)}, bf16[384,768]{1,0:T(8,128)(2,1)S(1)}, u32[]{:S(2)}, u32[]{:S(2)}) collective-permute-start(bf16[384,768]{1,0:T(8,128)(2,1)S(1)} %get-tuple-element.143), channel_id=1, source_target_pairs={{0,0},{1,1},{2,4},{3,5},{4,2},{5,3},{6,6},{7,7},{8,8},{9,9},{10,12... | collective-permute-start | bytes 1769480 | tf_op jit(solution)/shard_map/ppermute | solution.py:37
  478.0 43.6 %collective-permute-start.35 = (bf16[384,768]{1,0:T(8,128)(2,1)S(1)}, bf16[384,768]{1,0:T(8,128)(2,1)S(1)}, u32[]{:S(2)}, u32[]{:S(2)}) collective-permute-start(bf16[384,768]{1,0:T(8,128)(2,1)S(1)} %get-tuple-element.144), channel_id=1, source_target_pairs={{0,1},{1,0},{2,5},{3,4},{4,3},{5,2},{6,7},{7,6},{8,9},{9,8},{10,13... | collective-permute-start | bytes 1769480 | tf_op jit(solution)/shard_map/ppermute | solution.py:37
  498.7 22.3 %collective-permute-start.44 = (bf16[96,3456]{1,0:T(8,128)(2,1)S(1)}, bf16[96,3456]{1,0:T(8,128)(2,1)S(1)}, u32[]{:S(2)}, u32[]{:S(2)}) collective-permute-start(bf16[96,3456]{1,0:T(8,128)(2,1)S(1)} %pad_maximum_fusion.30), channel_id=1, source_target_pairs={{0,1},{1,0},{2,3},{3,2},{4,5},{5,4},{6,7},{7,6},{8,9},{9,8},{10,11... | collective-permute-start | bytes 1990664 | tf_op jit(solution)/shard_map/ppermute | solution.py:37
  (71 other events, 851.8 us)

commit v2 on v1

--- a/solution.py
+++ b/solution.py
@@ -74,6 +74,8 @@
 
 def gathered_over_pairs(value):
     p = lax.axis_index("pair")
+    if lax.axis_size("pair") <= 4:
+        return ([value] + [across_pairs(value, k) for k in range(1, lax.axis_size("pair"))], p)
     rows, width = value.shape
     bits = pair_bits()
     count = 1 << len(bits)
@@ -91,11 +93,29 @@
             lead = tuple(range(len(bits)))[::-1]
             current = jnp.transpose(current, lead + (len(bits), len(bits) + 1))
         halves.append(current.reshape(count, rows // 2, width))
-    return jnp.concatenate(halves, axis=1).reshape(count * rows, width)
+    return ([jnp.concatenate(halves, axis=1).reshape(count * rows, width)], None)
+
+
+def assembled(gathered):
+    pieces, p = gathered
+    if p is None:
+        return pieces[0]
+    rows, width = pieces[0].shape
+    whole = jnp.zeros((len(pieces) * rows, width), pieces[0].dtype)
+    for k, piece in enumerate(pieces):
+        whole = lax.dynamic_update_slice_in_dim(whole, piece, jnp.bitwise_xor(p, k) * rows, 0)
+    return whole
 
 
 def scattered_over_pairs(value):
     p = lax.axis_index("pair")
+    if lax.axis_size("pair") <= 4:
+        rows = value.shape[0] // lax.axis_size("pair")
+        pieces = []
+        for k in range(lax.axis_size("pair")):
+            piece = lax.dynamic_slice_in_dim(value, jnp.bitwise_xor(p, k) * rows, rows, 0)
+            pieces.append(across_pairs(piece, k) if k else piece)
+        return pieces
     bits = pair_bits()
     count = 1 << len(bits)
     rows, width = value.shape[0] // count, value.shape[1]
@@ -114,27 +134,37 @@
             current = keep + across_pairs(send, bit)
             left = [other for other in left if other != bit]
         halves.append(current)
-    return jnp.concatenate(halves, axis=0)
-
-
-def summed_over_depth(value):
-    z = lax.axis_index("seq")
-    current = value
-    trail = []
-    for level in range(lax.axis_size("seq").bit_length() - 1):
-        bit = 1 << level
-        mine = jnp.where(jnp.bitwise_and(z, bit) != 0, 1, 0)
-        parts = current.reshape((2, current.shape[0] // 2) + current.shape[1:])
-        keep = lax.dynamic_index_in_dim(parts, mine, 0, keepdims=False)
-        send = lax.dynamic_index_in_dim(parts, 1 - mine, 0, keepdims=False)
-        current = keep + across_depth(send, bit)
-        trail.append((bit, mine))
-    for bit, mine in trail[::-1]:
-        other = across_depth(current, bit)
-        first = jnp.where(mine == 0, current, other)
-        second = jnp.where(mine == 0, other, current)
-        current = jnp.concatenate([first, second], axis=0)
-    return current
+    return [jnp.concatenate(halves, axis=0)]
+
+
+def added(pieces):
+    total = pieces[0].astype(FULL)
+    for piece in pieces[1:]:
+        total = total + piece.astype(FULL)
+    return total.astype(LOW)
+
+
+def depth_flag(bit):
+    return jnp.where(jnp.bitwise_and(lax.axis_index("seq"), bit) != 0, 1, 0)
+
+
+def depth_halved(value, bit):
+    mine = depth_flag(bit)
+    parts = value.reshape((2, value.shape[0] // 2) + value.shape[1:])
+    keep = lax.dynamic_index_in_dim(parts, mine, 0, keepdims=False)
+    send = lax.dynamic_index_in_dim(parts, 1 - mine, 0, keepdims=False)
+    return [keep, across_depth(send, bit)]
+
+
+def depth_doubled(value, other, bit):
+    mine = depth_flag(bit)
+    return jnp.concatenate(
+        [jnp.where(mine == 0, value, other), jnp.where(mine == 0, other, value)], axis=0
+    )
+
+
+def tied(*values):
+    return lax.optimization_barrier(values)
 
 
 def keys_with_mask(k_ref, counts_ref, ka, rows):
@@ -179,9 +209,9 @@
             num_scalar_prefetch=1,
             grid=(pairs, rows // block),
             in_specs=[
-                pl.BlockSpec((block, 128), lambda h, i, n: (i, h)),
-                pl.BlockSpec((rows, 128), lambda h, i, n: (0, pairs + h)),
-                pl.BlockSpec((rows, 128), lambda h, i, n: (0, 2 * pairs + h)),
+                pl.BlockSpec((block, 128), lambda h, i, n: (i, 3 * h)),
+                pl.BlockSpec((rows, 128), lambda h, i, n: (0, 3 * h + 1)),
+                pl.BlockSpec((rows, 128), lambda h, i, n: (0, 3 * h + 2)),
             ],
             out_specs=[
                 pl.BlockSpec((block, 128), lambda h, i, n: (i, h)),
@@ -204,9 +234,9 @@
 
 def backward_kernel(
     counts_ref, q_ref, k_ref, v_ref, o_ref, g_ref, lse_ref, grad_ref,
-    ka, va, kt, dk, dv, *, rows, block, steps, chunk, pairs,
+    ka, va, kt, dk, dv, *, rows, block, steps, chunk,
 ):
-    pair, step = pl.program_id(0), pl.program_id(1)
+    step = pl.program_id(0)
 
     @pl.when(step == 0)
     def _():
@@ -245,35 +275,31 @@
             total = total + dot(kt[pl.ds(64 * h, 64), part], grad_scores, NN)
         columns.append(total)
     spot = pl.ds(pl.multiple_of(step * block, block), block)
-    here = pl.multiple_of(pair * 128, 128)
-    grad_ref[spot, pl.ds(here, 128)] = (jnp.concatenate(columns, axis=0).T * SCALE).astype(LOW)
+    grad_ref[spot, 0:128] = (jnp.concatenate(columns, axis=0).T * SCALE).astype(LOW)
 
     @pl.when(step == steps - 1)
     def _():
-        grad_ref[:, pl.ds(here + pairs * 128, 128)] = (dk[...] * SCALE).astype(LOW)
-        grad_ref[:, pl.ds(here + pairs * 256, 128)] = dv[...].astype(LOW)
-
-
-def attention_backward(counts, qkv, mixed, grad, lse, block, chunk):
-    rows, width = qkv.shape
-    pairs = width // 384
+        grad_ref[:, 128:256] = (dk[...] * SCALE).astype(LOW)
+        grad_ref[:, 256:384] = dv[...].astype(LOW)
+
+
+def attention_backward(counts, qkv, mixed, grad, lse, pair, block, chunk):
+    rows = qkv.shape[0]
     steps = rows // block
     return pl.pallas_call(
-        functools.partial(
-            backward_kernel, rows=rows, block=block, steps=steps, chunk=chunk, pairs=pairs
-        ),
+        functools.partial(backward_kernel, rows=rows, block=block, steps=steps, chunk=chunk),
         grid_spec=pltpu.PrefetchScalarGridSpec(
             num_scalar_prefetch=1,
-            grid=(pairs, steps),
+            grid=(steps,),
             in_specs=[
-                pl.BlockSpec((block, 128), lambda h, i, n: (i, h)),
-                pl.BlockSpec((rows, 128), lambda h, i, n: (0, pairs + h)),
-                pl.BlockSpec((rows, 128), lambda h, i, n: (0, 2 * pairs + h)),
-                pl.BlockSpec((block, 128), lambda h, i, n: (i, h)),
-                pl.BlockSpec((block, 128), lambda h, i, n: (i, h)),
-                pl.BlockSpec((1, 2, block), lambda h, i, n: (h, 0, i)),
+                pl.BlockSpec((block, 128), lambda i, n: (i, 3 * pair)),
+                pl.BlockSpec((rows, 128), lambda i, n: (0, 3 * pair + 1)),
+                pl.BlockSpec((rows, 128), lambda i, n: (0, 3 * pair + 2)),
+                pl.BlockSpec((block, 128), lambda i, n: (i, pair)),
+                pl.BlockSpec((block, 128), lambda i, n: (i, pair)),
+                pl.BlockSpec((1, 2, block), lambda i, n: (pair, 0, i)),
             ],
-            out_specs=pl.BlockSpec((rows, width), lambda h, i, n: (0, 0)),
+            out_specs=pl.BlockSpec((rows, 384), lambda i, n: (0, 0)),
             scratch_shapes=[
                 pltpu.VMEM((2, rows, 128), LOW),
                 pltpu.VMEM((2, rows, 128), LOW),
@@ -282,11 +308,11 @@
                 pltpu.VMEM((rows, 128), FULL),
             ],
         ),
-        out_shape=jax.ShapeDtypeStruct((rows, width), LOW),
+        out_shape=jax.ShapeDtypeStruct((rows, 384), LOW),
         cost_estimate=pl.CostEstimate(
-            flops=20 * pairs * rows * rows * 128,
-            bytes_accessed=rows * width * 5,
-            transcendentals=2 * pairs * rows * rows,
+            flops=20 * rows * rows * 128,
+            bytes_accessed=rows * 384 * 5,
+            transcendentals=2 * rows * rows,
         ),
         name="attention_backward",
     )(counts, qkv, qkv, qkv, mixed, grad, lse)
@@ -343,48 +369,38 @@
 
     x_rows = turned(tokens).reshape(rows, width)
 
+    heads_half = HEADS // 2
+    head_pairs = heads_half // 2
+    shard = qkv_weight.reshape(own_rows, 2, head_pairs, 2, 3, HEAD_DIM)
+    shard = jnp.transpose(shard, (1, 0, 2, 4, 3, 5)).reshape(2, own_rows, 3 * half_width)
+    vectors = jnp.stack([ln1_gain, ln1_bias, ln2_gain, ln2_bias], axis=1)
+    vectors = jnp.pad(vectors, ((0, 0), (0, 124)))
+    vectors = jnp.broadcast_to(vectors[None], (2, own_rows, 128))
+    shard = jnp.concatenate([shard, vectors], axis=2)
+    keep = lax.dynamic_index_in_dim(shard, c, 0, keepdims=False)
+    send = lax.dynamic_index_in_dim(shard, 1 - c, 0, keepdims=False)
+    w_qkv = assembled(gathered_over_pairs(in_order(keep, across_cores(send), 0)))
+    vectors = w_qkv[:, 3 * half_width :].T.astype(FULL)
+    w_qkv = w_qkv[:, : 3 * half_width]
+    gain_one, shift_one, gain_two, shift_two = vectors[0], vectors[1], vectors[2], vectors[3]
+
+    block = ff // groups
+
+    def unit_blocks(part):
+        return jnp.concatenate(
+            [up_weight[:, (2 * q + part) * block : (2 * q + part + 1) * block] for q in range(pairs)],
+            axis=1,
+        )
+
+    halves = [unit_blocks(0), unit_blocks(1)]
+    keep = jnp.where(is_first, halves[0], halves[1])
+    send = jnp.where(is_first, halves[1], halves[0])
+    up_pieces = gathered_over_pairs(in_order(keep, across_cores(send), 0))
+    down_pieces = gathered_over_pairs(down_weight)
+    out_pieces = gathered_over_pairs(out_weight)
+
     masks = deal_group[0:2]
     group = p * cores + c
-    sources = jnp.bitwise_xor(group, masks) * 2 + jnp.arange(2, dtype=jnp.int32)
-    picked = jnp.arange(seq_count, dtype=jnp.int32)[None, :] == sources[:, None]
-    dealt_len = jnp.sum(jnp.where(picked, lengths[None, :], 0), axis=1)
-    positions = z * slot_rows + jnp.arange(slot_rows, dtype=jnp.int32)
-    live = (positions[None, :] < dealt_len[:, None]) & (teach_mask == 1)
-    valid_count = summed_everywhere(jnp.full((8, 128), jnp.sum(live.astype(FULL))))[0, 0]
-
-    heads_half = HEADS // 2
-    shard = qkv_weight.reshape(own_rows, 2, heads_half, 3, HEAD_DIM)
-    shard = jnp.transpose(shard, (1, 0, 3, 2, 4)).reshape(2, own_rows, 3 * half_width)
-    keep = lax.dynamic_index_in_dim(shard, c, 0, keepdims=False)
-    send = lax.dynamic_index_in_dim(shard, 1 - c, 0, keepdims=False)
-    w_qkv = gathered_over_pairs(in_order(keep, across_cores(send), 0))
-
-    block = ff // groups
-    up_shard = up_weight.reshape(own_rows, pairs, cores, 2, block // 2)
-    up_shard = jnp.transpose(up_shard, (2, 0, 3, 1, 4)).reshape(cores, own_rows, half_ff)
-    out_shard = jnp.transpose(out_weight.reshape(own_rows, 2, half_width), (1, 0, 2))
-    both = jnp.concatenate([up_shard, out_shard], axis=2)
-    keep = lax.dynamic_index_in_dim(both, c, 0, keepdims=False)
-    send = lax.dynamic_index_in_dim(both, 1 - c, 0, keepdims=False)
-    both = in_order(keep, across_cores(send), 0)
-    down_shard = jnp.concatenate([down_weight[: block // 2], down_weight[block // 2 :]], axis=1)
-    mine = gathered_over_pairs(jnp.concatenate([both, down_shard], axis=1))
-    other = across_cores(mine)
-
-    def unpacked(stack):
-        up = stack[:, :half_ff]
-        out = stack[:, half_ff : half_ff + half_width]
-        down = stack[:, half_ff + half_width :]
-        return up, out, jnp.concatenate([down[:, :width], down[:, width:]], axis=0)
-
-    up_mine, out_mine, down_mine = unpacked(mine)
-    up_other, out_other, down_other = unpacked(other)
-    w_out = in_order(out_mine, out_other, 1)
-
-    vectors = jnp.stack([ln1_gain, ln1_bias, ln2_gain, ln2_bias])
-    vectors = lax.all_gather(vectors, ("pair", "core"), axis=1, tiled=True).astype(FULL)
-    gain_one, shift_one, gain_two, shift_two = vectors[0], vectors[1], vectors[2], vectors[3]
-
     mask_rows = jnp.pad(
         teach_mask.astype(LOW)[:, None, :], ((0, 0), (0, 15), (0, width - slot_rows))
     )
@@ -397,10 +413,13 @@
             [jnp.where(flagged, incoming, slots[0]), jnp.where(flagged, slots[1], incoming)]
         )
     goal = turned(slots)
-    spots = base + jnp.arange(rows, dtype=jnp.int32)
-    taught = goal[:, slot_rows, :slot_rows].reshape(rows)
-    valid = ((spots < length) & (taught == 1)).astype(FULL)[:, None]
-    goal = goal[:, :slot_rows].reshape(rows, width).astype(FULL)
+
+    sources = jnp.bitwise_xor(group, masks) * 2 + jnp.arange(2, dtype=jnp.int32)
+    picked = jnp.arange(seq_count, dtype=jnp.int32)[None, :] == sources[:, None]
+    dealt_len = jnp.sum(jnp.where(picked, lengths[None, :], 0), axis=1)
+    positions = z * slot_rows + jnp.arange(slot_rows, dtype=jnp.int32)
+    live = (positions[None, :] < dealt_len[:, None]) & (teach_mask == 1)
+    valid_count = summed_everywhere(jnp.full((8, 128), jnp.sum(live.astype(FULL))))[0, 0]
 
     x_full = x_rows.astype(FULL)
     unit_one, inverse_one = norm_parts(x_full)
@@ -408,60 +427,117 @@
     norm_one = jnp.concatenate([norm_mine, across_cores(norm_mine)], axis=0)
     qkv = dot(norm_one, w_qkv, NN).astype(LOW)
     mixed, lse = attention_forward(counts, qkv, 512)
+
+    flat, tree = jax.tree.flatten((up_pieces[0], down_pieces[0], out_pieces[0]))
+    *flat, mixed = tied(*flat, mixed)
+    up_list, down_list, out_list = jax.tree.unflatten(tree, flat)
+    w_up = assembled((up_list, up_pieces[1]))
+    w_down = assembled((down_list, down_pieces[1]))
+    out_mine = assembled((out_list, out_pieces[1])).reshape(pairs, own_rows, width)
+    out_other = across_cores(out_mine)
+    w_out = jnp.stack(
+        [jnp.where(is_first, out_mine, out_other), jnp.where(is_first, out_other, out_mine)], axis=1
+    ).reshape(width, width)
+
     attended = in_order(mixed[:rows], across_cores(mixed[rows:]), 1)
     middle = x_full + dot(attended, w_out, NN)
     unit_two, inverse_two = norm_parts(middle)
     norm_two = (unit_two * gain_two + shift_two).astype(LOW)
-    value_mine, slope_mine = gelu_parts(dot(norm_two, up_mine, NN))
-    value_other, slope_other = gelu_parts(dot(norm_two, up_other, NN))
-    active_mine = value_mine.astype(LOW)
-    active_other = value_other.astype(LOW)
-    output = middle + dot(active_mine, down_mine, NN) + dot(active_other, down_other, NN)
+    norm_other = across_cores(norm_two)
+
+    def expanded(low):
+        value, slope = gelu_parts(dot(low, w_up, NN))
+        return value.astype(LOW), slope.astype(LOW)
+
+    active_mine, slope_mine = expanded(norm_two)
+    active_other, slope_other = expanded(norm_other)
+    part_other = dot(active_other, w_down, NN).astype(LOW)
+    part_mine = dot(active_mine, w_down, NN)
+    output = middle + part_mine + across_cores(part_other).astype(FULL)
     activations = turned(output.astype(LOW).reshape(2, slot_rows, width))
 
-    error = output - goal
+    spots = base + jnp.arange(rows, dtype=jnp.int32)
+    taught = goal[:, slot_rows, :slot_rows].reshape(rows)
+    valid = ((spots < length) & (taught == 1)).astype(FULL)[:, None]
+    error = output - goal[:, :slot_rows].reshape(rows, width).astype(FULL)
     squares = jnp.sum(valid * error * error)
     factor = seq_count * full_len * 1.0 / valid_count
     grad_out = valid * (2.0 * factor) * error
     grad_ff = grad_out.astype(LOW)
-    down_grad_mine = dot(active_mine, grad_ff, TN).astype(LOW)
-    down_grad_other = dot(active_other, grad_ff, TN).astype(LOW)
-    hidden_mine = (dot(grad_ff, down_mine, NT) * slope_mine).astype(LOW)
-    hidden_other = (dot(grad_ff, down_other, NT) * slope_other).astype(LOW)
-    up_grad_mine = dot(norm_two, hidden_mine, TN).astype(LOW)
-    up_grad_other = dot(norm_two, hidden_other, TN).astype(LOW)
-    grad_norm_two = dot(hidden_mine, up_mine, NT) + dot(hidden_other, up_other, NT)
+    grad_ff_other = across_cores(grad_ff)
+    hidden_mine = (dot(grad_ff, w_down, NT) * slope_mine.astype(FULL)).astype(LOW)
+    hidden_other = (dot(grad_ff_other, w_down, NT) * slope_other.astype(FULL)).astype(LOW)
+    back_other = dot(hidden_other, w_up, NT).astype(LOW)
+    back_got = across_cores(back_other)
+    back_mine = dot(hidden_mine, w_up, NT)
+    down_grad = (dot(active_mine, grad_ff, TN) + dot(active_other, grad_ff_other, TN)).astype(LOW)
+    down_sum = scattered_over_pairs(down_grad)
     grad_mid, gain_two_grad, shift_two_grad = norm_backward(
-        grad_norm_two, unit_two, inverse_two, gain_two
+        back_mine + back_got.astype(FULL), unit_two, inverse_two, gain_two
     )
     grad_middle = grad_out + grad_mid
     grad_branch = grad_middle.astype(LOW)
-    out_grad = dot(attended, grad_branch, TN).astype(LOW)
     grad_attended = dot(grad_branch, w_out, NT).astype(LOW)
     keep = jnp.where(is_first, grad_attended[:, :half_width], grad_attended[:, half_width:])
     send = jnp.where(is_first, grad_attended[:, half_width:], grad_attended[:, :half_width])
     grad_mixed = jnp.concatenate([keep, across_cores(send)], axis=0)
-
-    def packed(up, out, down):
-        return jnp.concatenate([up, out, down[:width], down[width:]], axis=1)
-
-    out_halves = jnp.stack([out_grad[:, :half_width], out_grad[:, half_width:]])
-    out_keep = lax.dynamic_index_in_dim(out_halves, c, 0, keepdims=False)
-    out_send = lax.dynamic_index_in_dim(out_halves, 1 - c, 0, keepdims=False)
-    grads = packed(up_grad_mine, out_keep, down_grad_mine) + across_cores(
-        packed(up_grad_other, out_send, down_grad_other)
-    )
-    grads = summed_over_depth(scattered_over_pairs(grads))
-
-    grad_qkv = attention_backward(counts, qkv, mixed, grad_mixed, lse, 512, 512)
-    partial = dot(grad_qkv, w_qkv, NT)
-    grad_norm_one = partial[:rows] + across_cores(partial[rows:].astype(LOW)).astype(FULL)
-    qkv_grad = dot(norm_one, grad_qkv, TN).astype(LOW)
-    qkv_grad = summed_over_depth(scattered_over_pairs(qkv_grad))
+    up_grad = (dot(norm_two, hidden_mine, TN) + dot(norm_other, hidden_other, TN)).astype(LOW)
+    up_sum = scattered_over_pairs(up_grad)
+    out_grad = dot(attended, grad_branch, TN).astype(LOW).reshape(pairs, 2, own_rows, width)
+    out_keep = lax.dynamic_index_in_dim(out_grad, c, 1, keepdims=False)
+    out_send = lax.dynamic_index_in_dim(out_grad, 1 - c, 1, keepdims=False)
+    out_own = (out_keep + across_cores(out_send)).reshape(pairs * own_rows, width)
+    out_sum = scattered_over_pairs(out_own)
+
+    def attend(pair, gate):
+        return attention_backward(gate, qkv, mixed, grad_mixed, lse, pair, 512, 512)
+
+    def weight_part(grads):
+        return dot(norm_one, grads, TN).astype(LOW)
+
+    low_bit, high_bit = 1, depth // 2
+    *down_sum, gate = tied(*down_sum, counts)
+    down_step = depth_halved(added(down_sum), low_bit)
+    first = attend(0, gate)
+    flat, tree = jax.tree.flatten((down_step, up_sum, out_sum))
+    *flat, first, gate = tied(*flat, first, counts)
+    down_step, up_sum, out_sum = jax.tree.unflatten(tree, flat)
+    down_step = depth_halved(added(down_step), high_bit)
+    up_step = depth_halved(added(up_sum), low_bit)
+    out_step = depth_halved(added(out_sum), low_bit)
+    second = attend(1, gate)
+    flat, tree = jax.tree.flatten((down_step, up_step, out_step))
+    *flat, second, gate = tied(*flat, second, counts)
+    down_step, up_step, out_step = jax.tree.unflatten(tree, flat)
+    down_own = added(down_step)
+    down_got = across_depth(down_own, high_bit)
+    up_step = depth_halved(added(up_step), high_bit)
+    out_step = depth_halved(added(out_step), high_bit)
+    early = scattered_over_pairs(weight_part(jnp.concatenate([first, second], axis=1)))
+    third = attend(2, gate)
+    flat, tree = jax.tree.flatten((up_step, out_step, early))
+    *flat, third, down_own, down_got = tied(*flat, third, down_own, down_got)
+    up_step, out_step, early = jax.tree.unflatten(tree, flat)
+
+    partial = dot(jnp.concatenate([first, second, third], axis=1), w_qkv, NT)
+    back_got = across_cores(partial[rows:].astype(LOW))
+    late = scattered_over_pairs(weight_part(third))
+    grad_norm_one = partial[:rows] + back_got.astype(FULL)
     grad_in, gain_one_grad, shift_one_grad = norm_backward(
         grad_norm_one, unit_one, inverse_one, gain_one
     )
     input_grad = turned((grad_middle + grad_in).astype(LOW).reshape(2, slot_rows, width))
+
+    def finished(value):
+        value = depth_doubled(value, across_depth(value, high_bit), high_bit)
+        return depth_doubled(value, across_depth(value, low_bit), low_bit)
+
+    down_own = depth_doubled(down_own, down_got, high_bit)
+    down_own = depth_doubled(down_own, across_depth(down_own, low_bit), low_bit)
+    up_own = finished(added(up_step))
+    out_own = finished(added(out_step))
+    early = finished(added(depth_halved(added(depth_halved(added(early), low_bit)), high_bit)))
+    late = finished(added(depth_halved(added(depth_halved(added(late), low_bit)), high_bit)))
 
     small = jnp.stack(
         [
@@ -477,22 +553,20 @@
     def own_block(stack, index):
         return lax.dynamic_slice_in_dim(stack, index * own_rows, own_rows, 0)
 
-    wide = jnp.concatenate([grads[:, : half_ff + half_width], qkv_grad], axis=1)
-    mine = own_block(wide, c)
-    other = across_cores(own_block(wide, 1 - c))
-    halves = jnp.stack([jnp.where(is_first, mine, other), jnp.where(is_first, other, mine)])
-    halves = halves.astype(FULL)
-    up_own = halves[:, :, :half_ff].reshape(cores, own_rows, 2, pairs, block // 2)
-    up_own = jnp.transpose(up_own, (1, 3, 0, 2, 4)).reshape(own_rows, ff)
-    out_own = jnp.transpose(halves[:, :, half_ff : half_ff + half_width], (1, 0, 2))
-    out_own = out_own.reshape(own_rows, width)
-    qkv_own = halves[:, :, half_ff + half_width :].reshape(2, own_rows, 3, heads_half, HEAD_DIM)
-    qkv_own = jnp.transpose(qkv_own, (1, 0, 3, 2, 4)).reshape(own_rows, 3 * width)
-    down_own = grads[:, half_ff + half_width :]
-    down_own = jnp.concatenate([down_own[:, :width], down_own[:, width:]], axis=0).astype(FULL)
+    sums = jnp.concatenate([up_own, early, late], axis=1)
+    mine = own_block(sums, c)
+    other = across_cores(own_block(sums, 1 - c))
+    sides = [jnp.where(is_first, mine, other), jnp.where(is_first, other, mine)]
+    up_own = jnp.concatenate(
+        [side[:, q * block : (q + 1) * block] for q in range(pairs) for side in sides], axis=1
+    )
+    qkv_own = jnp.stack([side[:, half_ff:] for side in sides])
+    qkv_own = qkv_own.reshape(2, own_rows, head_pairs, 3, 2, HEAD_DIM)
+    qkv_own = jnp.transpose(qkv_own, (1, 0, 2, 4, 3, 5)).reshape(own_rows, 3 * width)
     return (
-        activations, loss, input_grad, own_small[0], own_small[1], qkv_own, out_own,
-        own_small[2], own_small[3], up_own, down_own,
+        activations, loss, input_grad, own_small[0], own_small[1], qkv_own.astype(FULL),
+        out_own.astype(FULL), own_small[2], own_small[3], up_own.astype(FULL),
+        down_own.astype(FULL),
     )
 
 

time: 547 us -> 512 us (0.936)
  waiting for transfers between devices: 197 us -> 153 us
  local copies, waits for them, and re-layouts: 45.2 us -> 75.6 us
  other arithmetic: 63.5 us -> 48.8 us
  starting transfers between devices: 76.8 us -> 87.6 us
  blocking collectives: 8.94 us -> 0 us
  matrix products: 64.2 us -> 55.3 us
  Pallas kernels: 74 us -> 79.6 us
    ppermute x54 -> x81, waiting for transfers between devices: 197 us -> 153 us  [moved(): return lax.ppermute(value, AXES, links)]
    dynamic_update_slice x0 -> x16, local copies, waits for them, and re-layouts: none -> 38.8 us  [assembled(): lax.dynamic_update_slice_in_dim(whole, piece, jnp.bitwise_xor(p, k) * row...]
    ppermute x54 -> x81, starting transfers between devices: 76.8 us -> 87.6 us  [moved(): return lax.ppermute(value, AXES, links)]
    another operation x16 -> x3, other arithmetic: 10.7 us -> 0.92 us  [the longest x1 0.73 us: shards(): vectors = jnp.stack([ln1_gain, ln1_bias, ln2_gain, ln2_bias], axis=1)]
    all_gather x1 -> x0, blocking collectives: 8.94 us -> none  [shards(): lax.all_gather(vectors, ('pair', 'core'), axis=1, tiled=True).astype(FULL)]
    dot_general x18 -> x19, matrix products: 64.2 us -> 55.3 us  [dot(): return lax.dot_general(left, right, form, preferred_element_type=FULL)]
    slice x13 -> x6, local copies, waits for them, and re-layouts: 9.77 us -> 1.6 us  [the longest x4 1.42 us: shards(): qkv_own = jnp.stack([side[:, half_ff:] for side in sides])]
    reshape x7 -> x0, local copies, waits for them, and re-layouts: 7.99 us -> none  [the longest x1 2.62 us: shards(): up_own = jnp.transpose(up_own, (1, 3, 0, 2, 4)).reshape(own_rows, ff)]
  transfers between devices with their start and end apart: 54 -> 81, of which waited for: 25 -> 28; matrix products, arithmetic and copies ran while one was open for 17% -> 29% of each run, Pallas kernels for 14% -> 16%
where the time goes in v2:
time: 512 us; the launch traced here: 507 us
  waiting for transfers between devices  153 us (30%)
  starting transfers between devices  87.6 us (17%)
  Pallas kernels  79.6 us (16%)
  local copies, waits for them, and re-layouts  75.6 us (15%)
  matrix products  55.3 us (11%)
  other arithmetic  48.8 us (10%)
  between operations  7.25 us (1%)
    ppermute x81, waiting for transfers between devices, moved(): return lax.ppermute(value, AXES, links)  153 us
    ppermute x81, starting transfers between devices, moved(): return lax.ppermute(value, AXES, links)  87.6 us
    dot_general x19, matrix products, dot(): return lax.dot_general(left, right, form, preferred_element_type=FULL)  55.3 us
    pallas_call x3, Pallas kernels, attention_backward(): pl.pallas_call(functools.partial(backward_kernel, rows=rows, block=block,...  49.9 us
    dynamic_update_slice x16, local copies, waits for them, and re-layouts, assembled(): lax.dynamic_update_slice_in_dim(whole, piece, jnp.bitwise_xor(p, k) * row...  38.8 us
    pallas_call x1, Pallas kernels, attention_forward(): pl.pallas_call(functools.partial(forward_kernel, rows=rows, block=block),...  29.6 us
  transfers between devices with their start and end apart: 81, of which 28 were waited for; matrix products, arithmetic and copies ran while one was open for 29% of the time, Pallas kernels for 16%

profile of v2, /device:TPU:0, one launch (start us, length us, event | category | flops | bytes accessed | tf_op | source)
XLA Modules:
  0.0 506.6 jit_solution(2683340417600047435)
XLA Ops:
  4.9 6.1 %collective-permute-start = (bf16[384,768]{1,0:T(8,128)(2,1)}, bf16[384,768]{1,0:T(8,128)(2,1)}, u32[]{:S(2)}, u32[]{:S(2)}) collective-permute-start(bf16[384,768]{1,0:T(8,128)(2,1)} %get-tuple-element.233), channel_id=1, source_target_pairs={{0,0},{1,1},{2,4},{3,5},{4,2},{5,3},{6,6},{7,7},{8,8},{9,9},{10,12... | collective-permute-start | bytes 1769480 | tf_op jit(solution)/shard_map/ppermute | solution.py:37
  11.0 2.6 collective-permute-start.1
  21.2 6.5 %collective-permute-done.29 = f32[8,128]{1,0:T(8,128)S(1)} collective-permute-done((f32[8,128]{1,0:T(8,128)S(1)}, f32[8,128]{1,0:T(8,128)S(1)}, u32[]{:S(2)}, u32[]{:S(2)}) %collective-permute-start.29) | collective-permute-done | bytes 4128 | tf_op jit(solution)/shard_map/ppermute | solution.py:37
  32.9 2.7 collective-permute-done.31
  36.4 3.8 collective-permute-done.32
  45.4 7.1 %dynamic_update_slice.48 = bf16[768,1280]{0,1:T(8,128)(2,1)} dynamic-update-slice(bf16[768,1280]{0,1:T(8,128)(2,1)} %broadcast_in_dim.31, bf16[192,1280]{0,1:T(8,128)(2,1)S(1)} %copy.83, s32[]{:T(128)S(6)} %select_n.482, s32[]{:T(128)} %constant.188.clone.1) | dynamic-update-slice | bytes 983044 | tf_op jit(solution)/shard_map/dynamic_update_slice | solution.py:106
  61.4 7.6 %dynamic_update_slice.49 = bf16[768,1280]{0,1:T(8,128)(2,1)} dynamic-update-slice(bf16[768,1280]{0,1:T(8,128)(2,1)} %dynamic_update_slice.48, bf16[192,1280]{0,1:T(8,128)(2,1)S(1)} %copy.84, s32[]{:T(128)S(6)} %select_n.483, s32[]{:T(128)} %constant.188.clone.1) | dynamic-update-slice | bytes 983044 | tf_op jit(solution)/shard_map/dynamic_update_slice | solution.py:106
  69.0 8.2 %collective-permute-done.14 = bf16[192,1280]{1,0:T(8,128)(2,1)} collective-permute-done((bf16[192,1280]{1,0:T(8,128)(2,1)S(1)}, bf16[192,1280]{1,0:T(8,128)(2,1)}, u32[]{:S(2)}, u32[]{:S(2)}) %collective-permute-start.14) | collective-permute-done | bytes 491552 | tf_op jit(solution)/shard_map/ppermute | solution.py:37
  78.5 6.6 %dynamic_update_slice.50 = bf16[768,1280]{0,1:T(8,128)(2,1)} dynamic-update-slice(bf16[768,1280]{0,1:T(8,128)(2,1)} %dynamic_update_slice.49, bf16[192,1280]{0,1:T(8,128)(2,1)S(1)} %copy.85, s32[]{:T(128)S(6)} %select_n.484, s32[]{:T(128)} %constant.188.clone.1) | dynamic-update-slice | bytes 983044 | tf_op jit(solution)/shard_map/dynamic_update_slice | solution.py:106
  88.0 6.9 %dynamic_update_slice.51 = bf16[768,1280]{0,1:T(8,128)(2,1)} dynamic-update-slice(bf16[768,1280]{0,1:T(8,128)(2,1)} %dynamic_update_slice.50, bf16[192,1280]{0,1:T(8,128)(2,1)S(1)} %copy.86, s32[]{:T(128)S(6)} %select_n.485, s32[]{:T(128)} %constant.188.clone.1) | dynamic-update-slice | bytes 983044 | tf_op jit(solution)/shard_map/dynamic_update_slice | solution.py:106
  103.4 11.5 %collective-permute-done.24 = bf16[400,768]{1,0:T(8,128)(2,1)S(1)} collective-permute-done((bf16[400,768]{1,0:T(8,128)(2,1)S(1)}, bf16[400,768]{1,0:T(8,128)(2,1)S(1)}, u32[]{:S(2)}, u32[]{:S(2)}) %collective-permute-start.24) | collective-permute-done | bytes 614432 | tf_op jit(solution)/shard_map/ppermute | solution.py:37
  118.6 5.9 %convolution_convert_fusion.q_ref.k_ref.v_ref = bf16[1536,1152]{1,0:T(8,128)(2,1)} fusion(bf16[768,1280]{0,1:T(8,128)(2,1)S(1)} %copy-done.10, bf16[768,768]{1,0:T(8,128)(2,1)S(1)} %collective-permute-done.16, bf16[768,768]{1,0:T(8,128)(2,1)S(1)} %fusion.30), kind=kOutput, calls=%fused_computation | convolution fusion | flops 2724397056 | bytes 7667712 | tf_op jit(solution)/shard_map/dot_general | solution.py:26
  131.0 29.6 %attention_forward.1 = (bf16[1536,384]{1,0:T(8,128)(2,1)}, f32[3,2,1536]{2,1,0:T(2,128)}) custom-call(s32[2]{0:T(128)} %add_clamp_fusion.counts_ref, bf16[1536,1152]{1,0:T(8,128)(2,1)} %convolution_convert_fusion.q_ref.k_ref.v_ref, bf16[1536,1152]{1,0:T(8,128)(2,1)} %convolution_convert_fusion.q_ref.k_ref.v_ref, ...), custom_call_target="tpu_custom_call" | custom-call | flops 7247757312 | bytes 5308416 | tf_op jit(solution)/shard_map/attention_forward/pallas_call | solution.py:206
  160.6 4.6 collective-permute-done.5
  166.3 11.9 %collective-permute-done.25 = bf16[400,768]{1,0:T(8,128)(2,1)} collective-permute-done((bf16[400,768]{1,0:T(8,128)(2,1)}, bf16[400,768]{1,0:T(8,128)(2,1)}, u32[]{:S(2)}, u32[]{:S(2)}) %collective-permute-start.25) | collective-permute-done | bytes 614432 | tf_op jit(solution)/shard_map/ppermute | solution.py:37
  181.6 3.4 collective-permute-start.17
  199.4 3.9 multiply_convert_fusion.2
  203.3 3.0 convolution_convert_fusion.4
  212.2 4.2 multiply_convert_fusion.3
  216.4 3.5 multiply_convert_fusion.4
  222.4 4.0 multiply_convert_fusion.1
  228.5 4.2 multiply_convert_fusion
  245.2 8.4 %collective-permute-done.34 = bf16[384,768]{1,0:T(8,128)(2,1)S(1)} collective-permute-done((bf16[384,768]{1,0:T(8,128)(2,1)S(1)}, bf16[384,768]{1,0:T(8,128)(2,1)S(1)}, u32[]{:S(2)}, u32[]{:S(2)}) %collective-permute-start.34) | collective-permute-done | bytes 589856 | tf_op jit(solution)/shard_map/ppermute | solution.py:37
  254.5 11.6 %collective-permute-done.35 = bf16[384,768]{1,0:T(8,128)(2,1)S(1)} collective-permute-done((bf16[384,768]{1,0:T(8,128)(2,1)S(1)}, bf16[384,768]{1,0:T(8,128)(2,1)S(1)}, u32[]{:S(2)}, u32[]{:S(2)}) %collective-permute-start.35) | collective-permute-done | bytes 589856 | tf_op jit(solution)/shard_map/ppermute | solution.py:37
  266.9 2.6 multiply_reduce_fusion
  269.5 2.7 fusion.17
  280.6 5.5 %collective-permute-start.22 = (bf16[384,768]{1,0:T(8,128)(2,1)}, bf16[384,768]{1,0:T(8,128)(2,1)}, u32[]{:S(2)}, u32[]{:S(2)}) collective-permute-start(bf16[384,768]{1,0:T(8,128)(2,1)} %get-tuple-element.228), channel_id=1, source_target_pairs={{0,1},{1,0},{2,5},{3,4},{4,3},{5,2},{6,7},{7,6},{8,9},{9,8},{10,13... | collective-permute-start | bytes 1769480 | tf_op jit(solution)/shard_map/ppermute | solution.py:37
  287.3 16.7 %attention_backward.3 = bf16[1536,384]{1,0:T(8,128)(2,1)} custom-call(s32[2]{0:T(128)} %add_clamp_fusion.counts_ref, bf16[1536,1152]{1,0:T(8,128)(2,1)} %convolution_convert_fusion.q_ref.k_ref.v_ref, bf16[1536,1152]{1,0:T(8,128)(2,1)} %convolution_convert_fusion.q_ref.k_ref.v_ref, bf16[1536,1152]{1,0:T(8,128)(2,1)} %convolution_convert_fusion.q_ref.k_ref.v_ref, ...), custom_call_target="tpu_custom_call" | custom-call | flops 6039797760 | bytes 2949120 | tf_op jit(solution)/shard_map/attention_backward/pallas_call | solution.py:289
  312.5 7.0 %collective-permute-done.40 = bf16[192,1536]{1,0:T(8,128)(2,1)S(1)} collective-permute-done((bf16[192,1536]{1,0:T(8,128)(2,1)}, bf16[192,1536]{1,0:T(8,128)(2,1)S(1)}, u32[]{:S(2)}, u32[]{:S(2)}) %collective-permute-start.40) | collective-permute-done | bytes 589856 | tf_op jit(solution)/shard_map/ppermute | solution.py:37
  319.5 3.0 collective-permute-done.43
  322.5 3.4 collective-permute-done.44
  333.1 16.8 %attention_backward.4 = bf16[1536,384]{1,0:T(8,128)(2,1)} custom-call(s32[2]{0:T(128)} %add_clamp_fusion.counts_ref, bf16[1536,1152]{1,0:T(8,128)(2,1)} %convolution_convert_fusion.q_ref.k_ref.v_ref, bf16[1536,1152]{1,0:T(8,128)(2,1)} %convolution_convert_fusion.q_ref.k_ref.v_ref, bf16[1536,1152]{1,0:T(8,128)(2,1)} %convolution_convert_fusion.q_ref.k_ref.v_ref, ...), custom_call_target="tpu_custom_call" | custom-call | flops 6039797760 | bytes 2949120 | tf_op jit(solution)/shard_map/attention_backward/pallas_call | solution.py:289
  351.9 4.0 fusion.39
  362.6 2.7 collective-permute-done.51
  367.4 16.4 %attention_backward.5 = bf16[1536,384]{1,0:T(8,128)(2,1)} custom-call(s32[2]{0:T(128)} %add_clamp_fusion.counts_ref, bf16[1536,1152]{1,0:T(8,128)(2,1)} %convolution_convert_fusion.q_ref.k_ref.v_ref, bf16[1536,1152]{1,0:T(8,128)(2,1)} %convolution_convert_fusion.q_ref.k_ref.v_ref, bf16[1536,1152]{1,0:T(8,128)(2,1)} %convolution_convert_fusion.q_ref.k_ref.v_ref, ...), custom_call_target="tpu_custom_call" | custom-call | flops 6039797760 | bytes 2949120 | tf_op jit(solution)/shard_map/attention_backward/pallas_call | solution.py:289
  385.1 3.9 collective-permute-start.80
  390.5 3.0 collective-permute-start.78
  393.5 4.8 fusion.10
  410.9 7.7 %collective-permute-done.73 = bf16[96,384]{1,0:T(8,128)(2,1)S(1)} collective-permute-done((bf16[96,384]{1,0:T(8,128)(2,1)S(1)}, bf16[96,384]{1,0:T(8,128)(2,1)S(1)}, u32[]{:S(2)}, u32[]{:S(2)}) %collective-permute-start.73) | collective-permute-done | bytes 73760 | tf_op jit(solution)/shard_map/ppermute | solution.py:37
  418.9 4.7 collective-permute-done.74
  423.7 6.4 %collective-permute-done.67 = bf16[48,768]{1,0:T(8,128)(2,1)S(1)} collective-permute-done((bf16[48,768]{1,0:T(8,128)(2,1)S(1)}, bf16[48,768]{1,0:T(8,128)(2,1)S(1)}, u32[]{:S(2)}, u32[]{:S(2)}) %collective-permute-start.67) | collective-permute-done | bytes 73760 | tf_op jit(solution)/shard_map/ppermute | solution.py:37
  430.2 5.2 %collective-permute-done.75 = bf16[48,384]{1,0:T(8,128)(2,1)S(1)} collective-permute-done((bf16[48,384]{1,0:T(8,128)(2,1)S(1)}, bf16[48,384]{1,0:T(8,128)(2,1)S(1)}, u32[]{:S(2)}, u32[]{:S(2)}) %collective-permute-start.75) | collective-permute-done | bytes 36896 | tf_op jit(solution)/shard_map/ppermute | solution.py:37
  435.4 5.4 %collective-permute-done.68 = bf16[48,768]{1,0:T(8,128)(2,1)S(1)} collective-permute-done((bf16[48,768]{1,0:T(8,128)(2,1)S(1)}, bf16[48,768]{1,0:T(8,128)(2,1)S(1)}, u32[]{:S(2)}, u32[]{:S(2)}) %collective-permute-start.68) | collective-permute-done | bytes 73760 | tf_op jit(solution)/shard_map/ppermute | solution.py:37
  440.8 4.3 collective-permute-done.76
  445.3 5.0 collective-permute-done.69
  463.3 2.9 fusion.36
  474.7 19.7 %collective-permute-done.60 = f32[8,768]{1,0:T(8,128)S(1)} collective-permute-done((f32[8,768]{1,0:T(8,128)S(1)}, f32[8,768]{1,0:T(8,128)S(1)}, u32[]{:S(2)}, u32[]{:S(2)}) %collective-permute-start.60) | collective-permute-done | bytes 24608 | tf_op jit(solution)/shard_map/ppermute | solution.py:37
  497.6 3.9 collective-permute-done.61
  (469 shorter events, 173.9 us)
Async XLA Ops:
  3.2 38.8 %collective-permute-start.12 = (bf16[96,1280]{1,0:T(8,128)(2,1)S(1)}, bf16[96,1280]{1,0:T(8,128)(2,1)S(1)}, u32[]{:S(2)}, u32[]{:S(2)}) collective-permute-start(bf16[96,1280]{1,0:T(8,128)(2,1)S(1)} %bitcast.250), channel_id=1, source_target_pairs={{0,4},{1,5},{2,6},{3,7},{4,0},{5,1},{6,2},{7,3},{8,12},{9,13},{10,... | collective-permute-start | bytes 737288 | tf_op jit(solution)/shard_map/ppermute | solution.py:37
  4.9 47.6 %collective-permute-start = (bf16[384,768]{1,0:T(8,128)(2,1)}, bf16[384,768]{1,0:T(8,128)(2,1)}, u32[]{:S(2)}, u32[]{:S(2)}) collective-permute-start(bf16[384,768]{1,0:T(8,128)(2,1)} %get-tuple-element.233), channel_id=1, source_target_pairs={{0,0},{1,1},{2,4},{3,5},{4,2},{5,3},{6,6},{7,7},{8,8},{9,9},{10,12... | collective-permute-start | bytes 1769480 | tf_op jit(solution)/shard_map/ppermute | solution.py:37
  11.0 42.9 %collective-permute-start.1 = (bf16[384,768]{1,0:T(8,128)(2,1)}, bf16[384,768]{1,0:T(8,128)(2,1)}, u32[]{:S(2)}, u32[]{:S(2)}) collective-permute-start(bf16[384,768]{1,0:T(8,128)(2,1)} %get-tuple-element.234), channel_id=1, source_target_pairs={{0,1},{1,0},{2,5},{3,4},{4,3},{5,2},{6,7},{7,6},{8,9},{9,8},{10,13... | collective-permute-start | bytes 1769480 | tf_op jit(solution)/shard_map/ppermute | solution.py:37
  13.6 115.1 %collective-permute-start.6 = (bf16[384,768]{1,0:T(8,128)(2,1)}, bf16[384,768]{1,0:T(8,128)(2,1)}, u32[]{:S(2)}, u32[]{:S(2)}) collective-permute-start(bf16[384,768]{1,0:T(8,128)(2,1)} %param.25), channel_id=1, source_target_pairs={{0,8},{1,9},{2,10},{3,11},{4,12},{5,13},{6,14},{7,15},{8,0},{9,1},... | collective-permute-start | bytes 1769480 | tf_op jit(solution)/shard_map/ppermute | solution.py:37
  40.2 56.9 %collective-permute-start.23 = (bf16[400,768]{1,0:T(8,128)(2,1)}, bf16[400,768]{1,0:T(8,128)(2,1)}, u32[]{:S(2)}, u32[]{:S(2)}) collective-permute-start(bf16[400,768]{1,0:T(8,128)(2,1)} %broadcast_select_fusion.2), channel_id=1, source_target_pairs={{0,4},{1,5},{2,6},{3,7},{4,0},{5,1},{6,2},{7,3},{8,12},{9,13},{10,... | collective-permute-start | bytes 1843208 | tf_op jit(solution)/shard_map/ppermute | solution.py:37
  42.4 16.1 %collective-permute-start.13 = (bf16[192,1280]{1,0:T(8,128)(2,1)S(1)}, bf16[192,1280]{1,0:T(8,128)(2,1)S(1)}, u32[]{:S(2)}, u32[]{:S(2)}) collective-permute-start(bf16[192,1280]{1,0:T(8,128)(2,1)S(1)} %pad_maximum_fusion.14), channel_id=1, source_target_pairs={{0,8},{1,9},{2,10},{3,11},{4,12},{5,13},{6,14},{7,15},{8,0},{9,1},... | collective-permute-start | bytes 1474568 | tf_op jit(solution)/shard_map/ppermute | solution.py:37
  52.5 24.7 %collective-permute-start.14 = (bf16[192,1280]{1,0:T(8,128)(2,1)S(1)}, bf16[192,1280]{1,0:T(8,128)(2,1)}, u32[]{:S(2)}, u32[]{:S(2)}) collective-permute-start(bf16[192,1280]{1,0:T(8,128)(2,1)S(1)} %pad_maximum_fusion.14), channel_id=1, source_target_pairs={{0,16},{1,17},{2,18},{3,19},{4,20},{5,21},{6,22},{7,23},{8,24},{9,... | collective-permute-start | bytes 1474568 | tf_op jit(solution)/shard_map/ppermute | solution.py:37
  53.8 31.3 %collective-permute-start.15 = (bf16[192,1280]{1,0:T(8,128)(2,1)S(1)}, bf16[192,1280]{1,0:T(8,128)(2,1)}, u32[]{:S(2)}, u32[]{:S(2)}) collective-permute-start(bf16[192,1280]{1,0:T(8,128)(2,1)S(1)} %pad_maximum_fusion.14), channel_id=1, source_target_pairs={{0,24},{1,25},{2,26},{3,27},{4,28},{5,29},{6,30},{7,31},{8,16},{9,... | collective-permute-start | bytes 1474568 | tf_op jit(solution)/shard_map/ppermute | solution.py:37
  59.3 71.0 %collective-permute-start.7 = (bf16[384,768]{1,0:T(8,128)(2,1)}, bf16[384,768]{1,0:T(8,128)(2,1)}, u32[]{:S(2)}, u32[]{:S(2)}) collective-permute-start(bf16[384,768]{1,0:T(8,128)(2,1)} %param.25), channel_id=1, source_target_pairs={{0,16},{1,17},{2,18},{3,19},{4,20},{5,21},{6,22},{7,23},{8,24},{9,... | collective-permute-start | bytes 1769480 | tf_op jit(solution)/shard_map/ppermute | solution.py:37
  77.2 21.7 %collective-permute-start.2 = (bf16[96,1536]{1,0:T(8,128)(2,1)}, bf16[96,1536]{1,0:T(8,128)(2,1)}, u32[]{:S(2)}, u32[]{:S(2)}) collective-permute-start(bf16[96,1536]{1,0:T(8,128)(2,1)} %broadcast_select_fusion.19), channel_id=1, source_target_pairs={{0,4},{1,5},{2,6},{3,7},{4,0},{5,1},{6,2},{7,3},{8,12},{9,13},{10,... | collective-permute-start | bytes 884744 | tf_op jit(solution)/shard_map/ppermute | solution.py:37
  85.1 39.3 %collective-permute-start.10 = (bf16[96,768]{1,0:T(8,128)(2,1)}, bf16[96,768]{1,0:T(8,128)(2,1)S(1)}, u32[]{:S(2)}, u32[]{:S(2)}) collective-permute-start(bf16[96,768]{1,0:T(8,128)(2,1)} %param.21), channel_id=1, source_target_pairs={{0,16},{1,17},{2,18},{3,19},{4,20},{5,21},{6,22},{7,23},{8,24},{9,... | collective-permute-start | bytes 442376 | tf_op jit(solution)/shard_map/ppermute | solution.py:37
  97.0 20.3 %collective-permute-start.16 = (bf16[768,768]{1,0:T(8,128)(2,1)S(1)}, bf16[768,768]{1,0:T(8,128)(2,1)S(1)}, u32[]{:S(2)}, u32[]{:S(2)}) collective-permute-start(bf16[768,768]{1,0:T(8,128)(2,1)S(1)} %fusion.30), channel_id=1, source_target_pairs={{0,4},{1,5},{2,6},{3,7},{4,0},{5,1},{6,2},{7,3},{8,12},{9,13},{10,... | collective-permute-start | bytes 3538952 | tf_op jit(solution)/shard_map/ppermute | solution.py:37
  98.9 16.1 %collective-permute-start.24 = (bf16[400,768]{1,0:T(8,128)(2,1)S(1)}, bf16[400,768]{1,0:T(8,128)(2,1)S(1)}, u32[]{:S(2)}, u32[]{:S(2)}) collective-permute-start(bf16[400,768]{1,0:T(8,128)(2,1)S(1)} %get-tuple-element.191), channel_id=1, source_target_pairs={{0,8},{1,9},{2,10},{3,11},{4,12},{5,13},{6,14},{7,15},{8,0},{9,1},... | collective-permute-start | bytes 1843208 | tf_op jit(solution)/shard_map/ppermute | solution.py:37
  124.4 36.1 %collective-permute-start.8 = (bf16[384,768]{1,0:T(8,128)(2,1)}, bf16[384,768]{1,0:T(8,128)(2,1)}, u32[]{:S(2)}, u32[]{:S(2)}) collective-permute-start(bf16[384,768]{1,0:T(8,128)(2,1)} %param.25), channel_id=1, source_target_pairs={{0,24},{1,25},{2,26},{3,27},{4,28},{5,29},{6,30},{7,31},{8,16},{9,... | collective-permute-start | bytes 1769480 | tf_op jit(solution)/shard_map/ppermute | solution.py:37
  126.1 34.5 %collective-permute-start.3 = (bf16[192,1536]{1,0:T(8,128)(2,1)}, bf16[192,1536]{1,0:T(8,128)(2,1)}, u32[]{:S(2)}, u32[]{:S(2)}) collective-permute-start(bf16[192,1536]{1,0:T(8,128)(2,1)} %pad_maximum_fusion.13), channel_id=1, source_target_pairs={{0,8},{1,9},{2,10},{3,11},{4,12},{5,13},{6,14},{7,15},{8,0},{9,1},... | collective-permute-start | bytes 1769480 | tf_op jit(solution)/shard_map/ppermute | solution.py:37
  127.5 33.1 %collective-permute-start.4 = (bf16[192,1536]{1,0:T(8,128)(2,1)}, bf16[192,1536]{1,0:T(8,128)(2,1)}, u32[]{:S(2)}, u32[]{:S(2)}) collective-permute-start(bf16[192,1536]{1,0:T(8,128)(2,1)} %pad_maximum_fusion.13), channel_id=1, source_target_pairs={{0,16},{1,17},{2,18},{3,19},{4,20},{5,21},{6,22},{7,23},{8,24},{9,... | collective-permute-start | bytes 1769480 | tf_op jit(solution)/shard_map/ppermute | solution.py:37
  128.7 36.5 %collective-permute-start.5 = (bf16[192,1536]{1,0:T(8,128)(2,1)}, bf16[192,1536]{1,0:T(8,128)(2,1)}, u32[]{:S(2)}, u32[]{:S(2)}) collective-permute-start(bf16[192,1536]{1,0:T(8,128)(2,1)} %pad_maximum_fusion.13), channel_id=1, source_target_pairs={{0,24},{1,25},{2,26},{3,27},{4,28},{5,29},{6,30},{7,31},{8,16},{9,... | collective-permute-start | bytes 1769480 | tf_op jit(solution)/shard_map/ppermute | solution.py:37
  130.3 47.9 %collective-permute-start.25 = (bf16[400,768]{1,0:T(8,128)(2,1)}, bf16[400,768]{1,0:T(8,128)(2,1)}, u32[]{:S(2)}, u32[]{:S(2)}) collective-permute-start(bf16[400,768]{1,0:T(8,128)(2,1)} %broadcast_select_fusion.6), channel_id=1, source_target_pairs={{0,16},{1,17},{2,18},{3,19},{4,20},{5,21},{6,22},{7,23},{8,24},{9,... | collective-permute-start | bytes 1843208 | tf_op jit(solution)/shard_map/ppermute | solution.py:37
  166.3 21.1 %collective-permute-start.18 = (bf16[4,96,768]{2,1,0:T(8,128)(2,1)S(1)}, bf16[4,96,768]{2,1,0:T(8,128)(2,1)S(1)}, u32[]{:S(2)}, u32[]{:S(2)}) collective-permute-start(bf16[4,96,768]{2,1,0:T(8,128)(2,1)S(1)} %bitcast.225), channel_id=1, source_target_pairs={{0,4},{1,5},{2,6},{3,7},{4,0},{5,1},{6,2},{7,3},{8,12},{9,13},{10,... | collective-permute-start | bytes 1769480 | tf_op jit(solution)/shard_map/ppermute | solution.py:37
  179.9 26.5 %collective-permute-start.26 = (bf16[400,768]{1,0:T(8,128)(2,1)S(1)}, bf16[400,768]{1,0:T(8,128)(2,1)S(1)}, u32[]{:S(2)}, u32[]{:S(2)}) collective-permute-start(bf16[400,768]{1,0:T(8,128)(2,1)S(1)} %get-tuple-element.211), channel_id=1, source_target_pairs={{0,0},{1,1},{2,4},{3,5},{4,2},{5,3},{6,6},{7,7},{8,8},{9,9},{10,12... | collective-permute-start | bytes 1843208 | tf_op jit(solution)/shard_map/ppermute | solution.py:37
  181.2 25.3 %collective-permute-start.27 = (bf16[400,768]{1,0:T(8,128)(2,1)S(1)}, bf16[400,768]{1,0:T(8,128)(2,1)S(1)}, u32[]{:S(2)}, u32[]{:S(2)}) collective-permute-start(bf16[400,768]{1,0:T(8,128)(2,1)S(1)} %get-tuple-element.212), channel_id=1, source_target_pairs={{0,1},{1,0},{2,5},{3,4},{4,3},{5,2},{6,7},{7,6},{8,9},{9,8},{10,13... | collective-permute-start | bytes 1843208 | tf_op jit(solution)/shard_map/ppermute | solution.py:37
  234.7 32.2 %collective-permute-start.41 = (bf16[768,768]{1,0:T(8,128)(2,1)S(1)}, bf16[768,768]{1,0:T(8,128)(2,1)S(1)}, u32[]{:S(2)}, u32[]{:S(2)}) collective-permute-start(bf16[768,768]{1,0:T(8,128)(2,1)S(1)} %convolution_convert_fusion.3), channel_id=1, source_target_pairs={{0,4},{1,5},{2,6},{3,7},{4,0},{5,1},{6,2},{7,3},{8,12},{9,13},{10,... | collective-permute-start | bytes 3538952 | tf_op jit(solution)/shard_map/ppermute | solution.py:37
  237.3 16.3 %collective-permute-start.34 = (bf16[384,768]{1,0:T(8,128)(2,1)S(1)}, bf16[384,768]{1,0:T(8,128)(2,1)S(1)}, u32[]{:S(2)}, u32[]{:S(2)}) collective-permute-start(bf16[384,768]{1,0:T(8,128)(2,1)S(1)} %get-tuple-element.203), channel_id=1, source_target_pairs={{0,8},{1,9},{2,10},{3,11},{4,12},{5,13},{6,14},{7,15},{8,0},{9,1},... | collective-permute-start | bytes 1769480 | tf_op jit(solution)/shard_map/ppermute | solution.py:37
  238.2 27.9 %collective-permute-start.35 = (bf16[384,768]{1,0:T(8,128)(2,1)S(1)}, bf16[384,768]{1,0:T(8,128)(2,1)S(1)}, u32[]{:S(2)}, u32[]{:S(2)}) collective-permute-start(bf16[384,768]{1,0:T(8,128)(2,1)S(1)} %get-tuple-element.202), channel_id=1, source_target_pairs={{0,16},{1,17},{2,18},{3,19},{4,20},{5,21},{6,22},{7,23},{8,24},{9,... | collective-permute-start | bytes 1769480 | tf_op jit(solution)/shard_map/ppermute | solution.py:37
  239.6 27.0 %collective-permute-start.36 = (bf16[384,768]{1,0:T(8,128)(2,1)S(1)}, bf16[384,768]{1,0:T(8,128)(2,1)S(1)}, u32[]{:S(2)}, u32[]{:S(2)}) collective-permute-start(bf16[384,768]{1,0:T(8,128)(2,1)S(1)} %get-tuple-element.201), channel_id=1, source_target_pairs={{0,24},{1,25},{2,26},{3,27},{4,28},{5,29},{6,30},{7,31},{8,16},{9,... | collective-permute-start | bytes 1769480 | tf_op jit(solution)/shard_map/ppermute | solution.py:37
  244.4 62.1 %collective-permute-start.38 = (bf16[192,1536]{1,0:T(8,128)(2,1)}, bf16[192,1536]{1,0:T(8,128)(2,1)}, u32[]{:S(2)}, u32[]{:S(2)}) collective-permute-start(bf16[192,1536]{1,0:T(8,128)(2,1)} %get-tuple-element.199), channel_id=1, source_target_pairs={{0,8},{1,9},{2,10},{3,11},{4,12},{5,13},{6,14},{7,15},{8,0},{9,1},... | collective-permute-start | bytes 1769480 | tf_op jit(solution)/shard_map/ppermute | solution.py:37
  253.6 53.0 %collective-permute-start.39 = (bf16[192,1536]{1,0:T(8,128)(2,1)}, bf16[192,1536]{1,0:T(8,128)(2,1)}, u32[]{:S(2)}, u32[]{:S(2)}) collective-permute-start(bf16[192,1536]{1,0:T(8,128)(2,1)} %get-tuple-element.198), channel_id=1, source_target_pairs={{0,16},{1,17},{2,18},{3,19},{4,20},{5,21},{6,22},{7,23},{8,24},{9,... | collective-permute-start | bytes 1769480 | tf_op jit(solution)/shard_map/ppermute | solution.py:37
  276.6 27.3 %collective-permute-start.42 = (bf16[4,96,768]{2,1,0:T(8,128)(2,1)}, bf16[4,96,768]{2,1,0:T(8,128)(2,1)}, u32[]{:S(2)}, u32[]{:S(2)}) collective-permute-start(bf16[4,96,768]{2,1,0:T(8,128)(2,1)} %dynamic-slice_bitcast_fusion.2), channel_id=1, source_target_pairs={{0,4},{1,5},{2,6},{3,7},{4,0},{5,1},{6,2},{7,3},{8,12},{9,13},{10,... | collective-permute-start | bytes 1769480 | tf_op jit(solution)/shard_map/ppermute | solution.py:37
  278.9 29.2 %collective-permute-start.21 = (bf16[384,768]{1,0:T(8,128)(2,1)}, bf16[384,768]{1,0:T(8,128)(2,1)S(1)}, u32[]{:S(2)}, u32[]{:S(2)}) collective-permute-start(bf16[384,768]{1,0:T(8,128)(2,1)} %get-tuple-element.227), channel_id=1, source_target_pairs={{0,0},{1,1},{2,4},{3,5},{4,2},{5,3},{6,6},{7,7},{8,8},{9,9},{10,12... | collective-permute-start | bytes 1769480 | tf_op jit(solution)/shard_map/ppermute | solution.py:37
  280.6 28.1 %collective-permute-start.22 = (bf16[384,768]{1,0:T(8,128)(2,1)}, bf16[384,768]{1,0:T(8,128)(2,1)}, u32[]{:S(2)}, u32[]{:S(2)}) collective-permute-start(bf16[384,768]{1,0:T(8,128)(2,1)} %get-tuple-element.228), channel_id=1, source_target_pairs={{0,1},{1,0},{2,5},{3,4},{4,3},{5,2},{6,7},{7,6},{8,9},{9,8},{10,13... | collective-permute-start | bytes 1769480 | tf_op jit(solution)/shard_map/ppermute | solution.py:37
  308.1 17.8 %collective-permute-start.44 = (bf16[96,768]{1,0:T(8,128)(2,1)S(1)}, bf16[96,768]{1,0:T(8,128)(2,1)S(1)}, u32[]{:S(2)}, u32[]{:S(2)}) collective-permute-start(bf16[96,768]{1,0:T(8,128)(2,1)S(1)} %get-tuple-element.249), channel_id=1, source_target_pairs={{0,16},{1,17},{2,18},{3,19},{4,20},{5,21},{6,22},{7,23},{8,24},{9,... | collective-permute-start | bytes 442376 | tf_op jit(solution)/shard_map/ppermute | solution.py:37
  308.8 17.1 %collective-permute-start.45 = (bf16[96,768]{1,0:T(8,128)(2,1)S(1)}, bf16[96,768]{1,0:T(8,128)(2,1)S(1)}, u32[]{:S(2)}, u32[]{:S(2)}) collective-permute-start(bf16[96,768]{1,0:T(8,128)(2,1)S(1)} %get-tuple-element.248), channel_id=1, source_target_pairs={{0,24},{1,25},{2,26},{3,27},{4,28},{5,29},{6,30},{7,31},{8,16},{9,... | collective-permute-start | bytes 442376 | tf_op jit(solution)/shard_map/ppermute | solution.py:37
  326.6 23.3 %collective-permute-start.49 = (bf16[48,768]{1,0:T(8,128)(2,1)}, bf16[48,768]{1,0:T(8,128)(2,1)S(1)}, u32[]{:S(2)}, u32[]{:S(2)}) collective-permute-start(bf16[48,768]{1,0:T(8,128)(2,1)} %get-tuple-element.280), channel_id=1, source_target_pairs={{0,1},{1,0},{2,3},{3,2},{4,5},{5,4},{6,7},{7,6},{8,9},{9,8},{10,11... | collective-permute-start | bytes 221192 | tf_op jit(solution)/shard_map/ppermute | solution.py:37
  329.2 20.7 %collective-permute-start.48 = (bf16[96,1536]{1,0:T(8,128)(2,1)S(1)}, bf16[96,1536]{1,0:T(8,128)(2,1)S(1)}, u32[]{:S(2)}, u32[]{:S(2)}) collective-permute-start(bf16[96,1536]{1,0:T(8,128)(2,1)S(1)} %get-tuple-element.246), channel_id=1, source_target_pairs={{0,1},{1,0},{2,3},{3,2},{4,5},{5,4},{6,7},{7,6},{8,9},{9,8},{10,11... | collective-permute-start | bytes 884744 | tf_op jit(solution)/shard_map/ppermute | solution.py:37
  331.1 18.9 %collective-permute-start.47 = (bf16[96,768]{1,0:T(8,128)(2,1)}, bf16[96,768]{1,0:T(8,128)(2,1)}, u32[]{:S(2)}, u32[]{:S(2)}) collective-permute-start(bf16[96,768]{1,0:T(8,128)(2,1)} %get-tuple-element.272), channel_id=1, source_target_pairs={{0,2},{1,3},{2,0},{3,1},{4,6},{5,7},{6,4},{7,5},{8,10},{9,11},{10,... | collective-permute-start | bytes 442376 | tf_op jit(solution)/shard_map/ppermute | solution.py:37
  350.9 33.0 %collective-permute-start.55 = (bf16[96,768]{1,0:T(8,128)(2,1)S(1)}, bf16[96,768]{1,0:T(8,128)(2,1)}, u32[]{:S(2)}, u32[]{:S(2)}) collective-permute-start(bf16[96,768]{1,0:T(8,128)(2,1)S(1)} %add_convert_fusion.10), channel_id=1, source_target_pairs={{0,2},{1,3},{2,0},{3,1},{4,6},{5,7},{6,4},{7,5},{8,10},{9,11},{10,... | collective-permute-start | bytes 442376 | tf_op jit(solution)/shard_map/ppermute | solution.py:37
  356.9 27.0 %collective-permute-start.52 = (bf16[192,768]{1,0:T(8,128)(2,1)}, bf16[192,768]{1,0:T(8,128)(2,1)}, u32[]{:S(2)}, u32[]{:S(2)}) collective-permute-start(bf16[192,768]{1,0:T(8,128)(2,1)} %get-tuple-element.221), channel_id=1, source_target_pairs={{0,8},{1,9},{2,10},{3,11},{4,12},{5,13},{6,14},{7,15},{8,0},{9,1},... | collective-permute-start | bytes 884744 | tf_op jit(solution)/shard_map/ppermute | solution.py:37
  358.2 25.7 %collective-permute-start.53 = (bf16[192,768]{1,0:T(8,128)(2,1)}, bf16[192,768]{1,0:T(8,128)(2,1)}, u32[]{:S(2)}, u32[]{:S(2)}) collective-permute-start(bf16[192,768]{1,0:T(8,128)(2,1)} %get-tuple-element.220), channel_id=1, source_target_pairs={{0,16},{1,17},{2,18},{3,19},{4,20},{5,21},{6,22},{7,23},{8,24},{9,... | collective-permute-start | bytes 884744 | tf_op jit(solution)/shard_map/ppermute | solution.py:37
  358.9 25.1 %collective-permute-start.54 = (bf16[192,768]{1,0:T(8,128)(2,1)}, bf16[192,768]{1,0:T(8,128)(2,1)}, u32[]{:S(2)}, u32[]{:S(2)}) collective-permute-start(bf16[192,768]{1,0:T(8,128)(2,1)} %get-tuple-element.219), channel_id=1, source_target_pairs={{0,24},{1,25},{2,26},{3,27},{4,28},{5,29},{6,30},{7,31},{8,16},{9,... | collective-permute-start | bytes 884744 | tf_op jit(solution)/shard_map/ppermute | solution.py:37
  365.3 18.6 %collective-permute-start.50 = (bf16[48,1536]{1,0:T(8,128)(2,1)S(1)}, bf16[48,1536]{1,0:T(8,128)(2,1)S(1)}, u32[]{:S(2)}, u32[]{:S(2)}) collective-permute-start(bf16[48,1536]{1,0:T(8,128)(2,1)S(1)} %get-tuple-element.270), channel_id=1, source_target_pairs={{0,2},{1,3},{2,0},{3,1},{4,6},{5,7},{6,4},{7,5},{8,10},{9,11},{10,... | collective-permute-start | bytes 442376 | tf_op jit(solution)/shard_map/ppermute | solution.py:37
  385.1 66.3 %collective-permute-start.80 = (bf16[192,768]{1,0:T(8,128)(2,1)S(1)}, bf16[192,768]{1,0:T(8,128)(2,1)S(1)}, u32[]{:S(2)}, u32[]{:S(2)}) collective-permute-start(bf16[192,768]{1,0:T(8,128)(2,1)S(1)} %pad_maximum_fusion.18), channel_id=1, source_target_pairs={{0,1},{1,0},{2,3},{3,2},{4,5},{5,4},{6,7},{7,6},{8,9},{9,8},{10,11... | collective-permute-start | bytes 884744 | tf_op jit(solution)/shard_map/ppermute | solution.py:37
  390.4 20.0 %collective-permute-start.66 = (bf16[96,768]{1,0:T(8,128)(2,1)S(1)}, bf16[96,768]{1,0:T(8,128)(2,1)S(1)}, u32[]{:S(2)}, u32[]{:S(2)}) collective-permute-start(bf16[96,768]{1,0:T(8,128)(2,1)S(1)} %dynamic-slice_bitcast_fusion.11), channel_id=1, source_target_pairs={{0,1},{1,0},{2,3},{3,2},{4,5},{5,4},{6,7},{7,6},{8,9},{9,8},{10,11... | collective-permute-start | bytes 442376 | tf_op jit(solution)/shard_map/ppermute | solution.py:37
  405.0 48.5 %collective-permute-start.56 = (bf16[768,768]{1,0:T(8,128)(2,1)S(1)}, bf16[768,768]{1,0:T(8,128)(2,1)S(1)}, u32[]{:S(2)}, u32[]{:S(2)}) collective-permute-start(bf16[768,768]{1,0:T(8,128)(2,1)S(1)} %slice.249), channel_id=1, source_target_pairs={{0,4},{1,5},{2,6},{3,7},{4,0},{5,1},{6,2},{7,3},{8,12},{9,13},{10,... | collective-permute-start | bytes 3538952 | tf_op jit(solution)/shard_map/ppermute | solution.py:37
  406.6 44.0 %collective-permute-start.79 = (bf16[48,768]{1,0:T(8,128)(2,1)S(1)}, bf16[48,768]{1,0:T(8,128)(2,1)S(1)}, u32[]{:S(2)}, u32[]{:S(2)}) collective-permute-start(bf16[48,768]{1,0:T(8,128)(2,1)S(1)} %pad_maximum_fusion.21), channel_id=1, source_target_pairs={{0,1},{1,0},{2,3},{3,2},{4,5},{5,4},{6,7},{7,6},{8,9},{9,8},{10,11... | collective-permute-start | bytes 221192 | tf_op jit(solution)/shard_map/ppermute | solution.py:37
  408.6 36.6 %collective-permute-start.65 = (bf16[96,1536]{1,0:T(8,128)(2,1)S(1)}, bf16[96,1536]{1,0:T(8,128)(2,1)S(1)}, u32[]{:S(2)}, u32[]{:S(2)}) collective-permute-start(bf16[96,1536]{1,0:T(8,128)(2,1)S(1)} %pad_maximum_fusion.17), channel_id=1, source_target_pairs={{0,1},{1,0},{2,3},{3,2},{4,5},{5,4},{6,7},{7,6},{8,9},{9,8},{10,11... | collective-permute-start | bytes 884744 | tf_op jit(solution)/shard_map/ppermute | solution.py:37
  469.4 34.7 %collective-permute-start.62 = (bf16[384,768]{1,0:T(8,128)(2,1)}, bf16[384,768]{1,0:T(8,128)(2,1)S(1)}, u32[]{:S(2)}, u32[]{:S(2)}) collective-permute-start(bf16[384,768]{1,0:T(8,128)(2,1)} %get-tuple-element.217), channel_id=1, source_target_pairs={{0,0},{1,1},{2,4},{3,5},{4,2},{5,3},{6,6},{7,7},{8,8},{9,9},{10,12... | collective-permute-start | bytes 1769480 | tf_op jit(solution)/shard_map/ppermute | solution.py:37
  471.1 33.0 %collective-permute-start.63 = (bf16[384,768]{1,0:T(8,128)(2,1)}, bf16[384,768]{1,0:T(8,128)(2,1)S(1)}, u32[]{:S(2)}, u32[]{:S(2)}) collective-permute-start(bf16[384,768]{1,0:T(8,128)(2,1)} %get-tuple-element.218), channel_id=1, source_target_pairs={{0,1},{1,0},{2,5},{3,4},{4,3},{5,2},{6,7},{7,6},{8,9},{9,8},{10,13... | collective-permute-start | bytes 1769480 | tf_op jit(solution)/shard_map/ppermute | solution.py:37
  471.1 23.2 %collective-permute-start.60 = (f32[8,768]{1,0:T(8,128)S(1)}, f32[8,768]{1,0:T(8,128)S(1)}, u32[]{:S(2)}, u32[]{:S(2)}) collective-permute-start(f32[8,768]{1,0:T(8,128)S(1)} %add.440), channel_id=1, source_target_pairs={{0,1},{1,0},{2,3},{3,2},{4,5},{5,4},{6,7},{7,6},{8,9},{9,8},{10,11... | collective-permute-start | bytes 73736 | tf_op jit(solution)/shard_map/ppermute | solution.py:37
  (107 other events, 936.1 us)

commit v3 on v2

--- a/solution.py
+++ b/solution.py
@@ -53,23 +53,31 @@
     return [1 << level for level in range(lax.axis_size("pair").bit_length() - 1)]
 
 
-def turned(stack):
+def turned_parts(stack):
     z = lax.axis_index("seq")
     got = []
     for step in range(2):
         piece = lax.dynamic_index_in_dim(stack, (z + step) % 2, 0, keepdims=False)
         got.append(moved(piece, lambda p, c, w: (p, w // 2, 2 * c + (w + step) % 2)))
-    even = z % 2 == 0
+    return got
+
+
+def turned_settled(got):
+    even = lax.axis_index("seq") % 2 == 0
     return jnp.stack([jnp.where(even, got[0], got[1]), jnp.where(even, got[1], got[0])])
 
 
-def summed_everywhere(value):
-    value = value + across_cores(value)
-    for bit in pair_bits():
-        value = value + across_pairs(value, bit)
-    for level in range(lax.axis_size("seq").bit_length() - 1):
-        value = value + across_depth(value, 1 << level)
-    return value
+def turned(stack):
+    return turned_settled(turned_parts(stack))
+
+
+def sum_steps():
+    depth_steps = [
+        functools.partial(across_depth, bit=1 << level)
+        for level in range(lax.axis_size("seq").bit_length() - 1)
+    ]
+    pair_steps = [functools.partial(across_pairs, bit=bit) for bit in pair_bits()]
+    return depth_steps, [across_cores] + pair_steps
 
 
 def gathered_over_pairs(value):
@@ -96,15 +104,57 @@
     return ([jnp.concatenate(halves, axis=1).reshape(count * rows, width)], None)
 
 
-def assembled(gathered):
+def place_kernel(p_ref, *refs, segments, pairs, outs):
+    pieces, results, done = refs[:pairs], refs[pairs : pairs + outs], refs[-1]
+    copies = []
+    for k in range(pairs):
+        spot = jnp.bitwise_xor(p_ref[0], k)
+        for index, row, rows, column, width, target in segments:
+            copies.append(
+                pltpu.make_async_copy(
+                    pieces[k].at[pl.ds(row, rows), pl.ds(column, width)],
+                    results[index].at[
+                        pl.ds(pl.multiple_of(spot * rows, 16), rows), pl.ds(target, width)
+                    ],
+                    done.at[len(copies)],
+                )
+            )
+    for copy in copies:
+        copy.start()
+    for copy in copies:
+        copy.wait()
+
+
+def placed(gathered, segments):
     pieces, p = gathered
+    pairs = lax.axis_size("pair")
+    outs = 1 + max(segment[0] for segment in segments)
     if p is None:
-        return pieces[0]
-    rows, width = pieces[0].shape
-    whole = jnp.zeros((len(pieces) * rows, width), pieces[0].dtype)
-    for k, piece in enumerate(pieces):
-        whole = lax.dynamic_update_slice_in_dim(whole, piece, jnp.bitwise_xor(p, k) * rows, 0)
-    return whole
+        stack = pieces[0].reshape(pairs, -1, pieces[0].shape[1])
+        results = []
+        for index in range(outs):
+            parts = [
+                stack[:, row : row + rows, column : column + width].reshape(pairs * rows, width)
+                for which, row, rows, column, width, _ in segments
+                if which == index
+            ]
+            results.append(jnp.concatenate(parts, axis=1))
+        return results
+    shapes = []
+    for index in range(outs):
+        mine = [segment for segment in segments if segment[0] == index]
+        shapes.append(
+            jax.ShapeDtypeStruct((pairs * mine[0][2], sum(part[4] for part in mine)), LOW)
+        )
+    anywhere = pl.BlockSpec(memory_space=pl.ANY)
+    return pl.pallas_call(
+        functools.partial(place_kernel, segments=segments, pairs=pairs, outs=outs),
+        in_specs=[pl.BlockSpec(memory_space=pltpu.SMEM)] + [anywhere] * pairs,
+        out_specs=[anywhere] * outs,
+        out_shape=shapes,
+        scratch_shapes=[pltpu.SemaphoreType.DMA((pairs * len(segments),))],
+        name="place",
+    )(p.astype(jnp.int32).reshape(1), *pieces)
 
 
 def scattered_over_pairs(value):
@@ -223,11 +273,7 @@
             jax.ShapeDtypeStruct((rows, pairs * 128), LOW),
             jax.ShapeDtypeStruct((pairs, 2, rows), FULL),
         ],
-        cost_estimate=pl.CostEstimate(
-            flops=8 * pairs * rows * rows * 128,
-            bytes_accessed=rows * width * 3,
-            transcendentals=2 * pairs * rows * rows,
-        ),
+        cost_estimate=pl.CostEstimate(flops=1, bytes_accessed=1, transcendentals=0),
         name="attention_forward",
     )(counts, qkv, qkv, qkv)
 
@@ -309,11 +355,7 @@
             ],
         ),
         out_shape=jax.ShapeDtypeStruct((rows, 384), LOW),
-        cost_estimate=pl.CostEstimate(
-            flops=20 * rows * rows * 128,
-            bytes_accessed=rows * 384 * 5,
-            transcendentals=2 * rows * rows,
-        ),
+        cost_estimate=pl.CostEstimate(flops=1, bytes_accessed=1, transcendentals=0),
         name="attention_backward",
     )(counts, qkv, qkv, qkv, mixed, grad, lse)
 
@@ -367,22 +409,50 @@
     counts = jnp.stack([length - base, length - (rows - base)])
     counts = jnp.clip(counts, 0, rows).astype(jnp.int32)
 
-    x_rows = turned(tokens).reshape(rows, width)
-
     heads_half = HEADS // 2
     head_pairs = heads_half // 2
+    wide_half = 3 * half_width
     shard = qkv_weight.reshape(own_rows, 2, head_pairs, 2, 3, HEAD_DIM)
-    shard = jnp.transpose(shard, (1, 0, 2, 4, 3, 5)).reshape(2, own_rows, 3 * half_width)
+    shard = jnp.transpose(shard, (1, 0, 2, 4, 3, 5)).reshape(2, own_rows, wide_half)
     vectors = jnp.stack([ln1_gain, ln1_bias, ln2_gain, ln2_bias], axis=1)
     vectors = jnp.pad(vectors, ((0, 0), (0, 124)))
     vectors = jnp.broadcast_to(vectors[None], (2, own_rows, 128))
     shard = jnp.concatenate([shard, vectors], axis=2)
     keep = lax.dynamic_index_in_dim(shard, c, 0, keepdims=False)
     send = lax.dynamic_index_in_dim(shard, 1 - c, 0, keepdims=False)
-    w_qkv = assembled(gathered_over_pairs(in_order(keep, across_cores(send), 0)))
-    vectors = w_qkv[:, 3 * half_width :].T.astype(FULL)
-    w_qkv = w_qkv[:, : 3 * half_width]
-    gain_one, shift_one, gain_two, shift_two = vectors[0], vectors[1], vectors[2], vectors[3]
+    qkv_shard = in_order(keep, across_cores(send), 0)
+    qkv_pieces = gathered_over_pairs(qkv_shard)
+
+    x_rows = turned(tokens).reshape(rows, width)
+
+    masks = deal_group[0:2]
+    group = p * cores + c
+    sources = jnp.bitwise_xor(group, masks) * 2 + jnp.arange(2, dtype=jnp.int32)
+    picked = jnp.arange(seq_count, dtype=jnp.int32)[None, :] == sources[:, None]
+    dealt_len = jnp.sum(jnp.where(picked, lengths[None, :], 0), axis=1)
+    positions = z * slot_rows + jnp.arange(slot_rows, dtype=jnp.int32)
+    live = (positions[None, :] < dealt_len[:, None]) & (teach_mask == 1)
+    tally = jnp.full((8, 128), jnp.sum(live.astype(FULL)))
+    tally = tally + across_cores(tally)
+
+    mask_rows = jnp.pad(
+        teach_mask.astype(LOW)[:, None, :], ((0, 0), (0, 15), (0, width - slot_rows))
+    )
+    slots = jnp.concatenate([teacher, mask_rows], axis=1)
+
+    def dealt(slots, level):
+        flagged = jnp.bitwise_and(jnp.right_shift(masks[0], level), 1) == 1
+        outgoing = jnp.where(flagged, slots[0], slots[1])
+        incoming = across_cores(outgoing) if level == 0 else across_pairs(outgoing, 1 << (level - 1))
+        return [flagged, slots, incoming]
+
+    def settled(flagged, slots, incoming):
+        return jnp.stack(
+            [jnp.where(flagged, incoming, slots[0]), jnp.where(flagged, slots[1], incoming)]
+        )
+
+    levels = groups.bit_length() - 1
+    deal = dealt(slots, 0)
 
     block = ff // groups
 
@@ -392,54 +462,58 @@
             axis=1,
         )
 
-    halves = [unit_blocks(0), unit_blocks(1)]
-    keep = jnp.where(is_first, halves[0], halves[1])
-    send = jnp.where(is_first, halves[1], halves[0])
-    up_pieces = gathered_over_pairs(in_order(keep, across_cores(send), 0))
-    down_pieces = gathered_over_pairs(down_weight)
-    out_pieces = gathered_over_pairs(out_weight)
-
-    masks = deal_group[0:2]
-    group = p * cores + c
-    mask_rows = jnp.pad(
-        teach_mask.astype(LOW)[:, None, :], ((0, 0), (0, 15), (0, width - slot_rows))
-    )
-    slots = jnp.concatenate([teacher, mask_rows], axis=1)
-    for level in range(groups.bit_length() - 1):
-        flagged = jnp.bitwise_and(jnp.right_shift(masks[0], level), 1) == 1
-        outgoing = jnp.where(flagged, slots[0], slots[1])
-        incoming = across_cores(outgoing) if level == 0 else across_pairs(outgoing, 1 << (level - 1))
-        slots = jnp.stack(
-            [jnp.where(flagged, incoming, slots[0]), jnp.where(flagged, slots[1], incoming)]
-        )
-    goal = turned(slots)
-
-    sources = jnp.bitwise_xor(group, masks) * 2 + jnp.arange(2, dtype=jnp.int32)
-    picked = jnp.arange(seq_count, dtype=jnp.int32)[None, :] == sources[:, None]
-    dealt_len = jnp.sum(jnp.where(picked, lengths[None, :], 0), axis=1)
-    positions = z * slot_rows + jnp.arange(slot_rows, dtype=jnp.int32)
-    live = (positions[None, :] < dealt_len[:, None]) & (teach_mask == 1)
-    valid_count = summed_everywhere(jnp.full((8, 128), jnp.sum(live.astype(FULL))))[0, 0]
+    up_parts = [unit_blocks(0), unit_blocks(1)]
+    keep = jnp.where(is_first, up_parts[0], up_parts[1])
+    send = jnp.where(is_first, up_parts[1], up_parts[0])
+    got = across_cores(jnp.concatenate([send[:, :width], send[:, width:], out_weight], axis=0))
+    up_shard = in_order(keep, jnp.concatenate([got[:own_rows], got[own_rows : 2 * own_rows]], axis=1), 0)
+    out_shard = in_order(out_weight, got[2 * own_rows :], 0)
+    payload = jnp.concatenate(
+        [down_weight, up_shard[:, :width], up_shard[:, width:], out_shard], axis=0
+    )
+    down_rows = down_weight.shape[0]
+    payload_plan = (
+        (0, 0, down_rows, 0, width, 0),
+        (1, down_rows, pair_rows, 0, width, 0),
+        (1, down_rows + pair_rows, pair_rows, 0, width, width),
+        (2, down_rows + 2 * pair_rows, pair_rows, 0, width, 0),
+    )
+    deal, tally = tied(deal, tally)
+    x_rows, payload = tied(x_rows, payload)
+    tally_steps = sum_steps()
+    tally = tally + tally_steps[1][1](tally)
+    deal = dealt(settled(*deal), 1)
+    payload_pieces = gathered_over_pairs(payload)
 
     x_full = x_rows.astype(FULL)
     unit_one, inverse_one = norm_parts(x_full)
+    w_qkv, vectors = placed(
+        qkv_pieces,
+        ((0, 0, pair_rows, 0, wide_half, 0), (1, 0, pair_rows, wide_half, 128, 0)),
+    )
+    pick = lax.broadcasted_iota(jnp.int32, (8, 128), 0) == lax.broadcasted_iota(jnp.int32, (8, 128), 1)
+    vectors = dot(pick.astype(LOW), vectors, NT)
+    gain_one, shift_one, gain_two, shift_two = vectors[0], vectors[1], vectors[2], vectors[3]
     norm_mine = (unit_one * gain_one + shift_one).astype(LOW)
     norm_one = jnp.concatenate([norm_mine, across_cores(norm_mine)], axis=0)
+    norm_one, tally = tied(norm_one, tally)
+    for step in tally_steps[1][2:]:
+        tally = tally + step(tally)
     qkv = dot(norm_one, w_qkv, NN).astype(LOW)
+    qkv, deal, tally = tied(qkv, deal, tally)
+    for level in range(2, levels):
+        deal = dealt(settled(*deal), level)
+    tally = tally + tally_steps[0][0](tally)
     mixed, lse = attention_forward(counts, qkv, 512)
 
-    flat, tree = jax.tree.flatten((up_pieces[0], down_pieces[0], out_pieces[0]))
-    *flat, mixed = tied(*flat, mixed)
-    up_list, down_list, out_list = jax.tree.unflatten(tree, flat)
-    w_up = assembled((up_list, up_pieces[1]))
-    w_down = assembled((down_list, down_pieces[1]))
-    out_mine = assembled((out_list, out_pieces[1])).reshape(pairs, own_rows, width)
-    out_other = across_cores(out_mine)
-    w_out = jnp.stack(
-        [jnp.where(is_first, out_mine, out_other), jnp.where(is_first, out_other, out_mine)], axis=1
-    ).reshape(width, width)
-
-    attended = in_order(mixed[:rows], across_cores(mixed[rows:]), 1)
+    mixed, payload_pieces, deal, tally = tied(mixed, payload_pieces, deal, tally)
+    mixed_got = across_cores(mixed[rows:])
+    goal = turned(settled(*deal))
+    for step in tally_steps[0][1:]:
+        tally = tally + step(tally)
+    w_down, w_up, w_out = placed(payload_pieces, payload_plan)
+
+    attended = in_order(mixed[:rows], mixed_got, 1)
     middle = x_full + dot(attended, w_out, NN)
     unit_two, inverse_two = norm_parts(middle)
     norm_two = (unit_two * gain_two + shift_two).astype(LOW)
@@ -454,8 +528,9 @@
     part_other = dot(active_other, w_down, NN).astype(LOW)
     part_mine = dot(active_mine, w_down, NN)
     output = middle + part_mine + across_cores(part_other).astype(FULL)
-    activations = turned(output.astype(LOW).reshape(2, slot_rows, width))
-
+
+    output, goal, tally = tied(output, goal, tally)
+    valid_count = tally[0, 0]
     spots = base + jnp.arange(rows, dtype=jnp.int32)
     taught = goal[:, slot_rows, :slot_rows].reshape(rows)
     valid = ((spots < length) & (taught == 1)).astype(FULL)[:, None]
@@ -465,13 +540,16 @@
     grad_out = valid * (2.0 * factor) * error
     grad_ff = grad_out.astype(LOW)
     grad_ff_other = across_cores(grad_ff)
+    output_moved = turned_parts(output.astype(LOW).reshape(2, slot_rows, width))
     hidden_mine = (dot(grad_ff, w_down, NT) * slope_mine.astype(FULL)).astype(LOW)
+    down_grad = (dot(active_mine, grad_ff, TN) + dot(active_other, grad_ff_other, TN)).astype(LOW)
+    down_grad, grad_ff_other, hidden_mine = tied(down_grad, grad_ff_other, hidden_mine)
+    down_sum = scattered_over_pairs(down_grad)
     hidden_other = (dot(grad_ff_other, w_down, NT) * slope_other.astype(FULL)).astype(LOW)
     back_other = dot(hidden_other, w_up, NT).astype(LOW)
     back_got = across_cores(back_other)
     back_mine = dot(hidden_mine, w_up, NT)
-    down_grad = (dot(active_mine, grad_ff, TN) + dot(active_other, grad_ff_other, TN)).astype(LOW)
-    down_sum = scattered_over_pairs(down_grad)
+    up_grad = (dot(norm_two, hidden_mine, TN) + dot(norm_other, hidden_other, TN)).astype(LOW)
     grad_mid, gain_two_grad, shift_two_grad = norm_backward(
         back_mine + back_got.astype(FULL), unit_two, inverse_two, gain_two
     )
@@ -480,14 +558,10 @@
     grad_attended = dot(grad_branch, w_out, NT).astype(LOW)
     keep = jnp.where(is_first, grad_attended[:, :half_width], grad_attended[:, half_width:])
     send = jnp.where(is_first, grad_attended[:, half_width:], grad_attended[:, :half_width])
-    grad_mixed = jnp.concatenate([keep, across_cores(send)], axis=0)
-    up_grad = (dot(norm_two, hidden_mine, TN) + dot(norm_other, hidden_other, TN)).astype(LOW)
-    up_sum = scattered_over_pairs(up_grad)
-    out_grad = dot(attended, grad_branch, TN).astype(LOW).reshape(pairs, 2, own_rows, width)
-    out_keep = lax.dynamic_index_in_dim(out_grad, c, 1, keepdims=False)
-    out_send = lax.dynamic_index_in_dim(out_grad, 1 - c, 1, keepdims=False)
-    out_own = (out_keep + across_cores(out_send)).reshape(pairs * own_rows, width)
-    out_sum = scattered_over_pairs(out_own)
+    mixed_grad_got = across_cores(send)
+    out_grad = dot(attended, grad_branch, TN).astype(LOW)
+    rest_sum = scattered_over_pairs(jnp.concatenate([up_grad, out_grad], axis=1))
+    grad_mixed = jnp.concatenate([keep, mixed_grad_got], axis=0)
 
     def attend(pair, gate):
         return attention_backward(gate, qkv, mixed, grad_mixed, lse, pair, 512, 512)
@@ -496,77 +570,92 @@
         return dot(norm_one, grads, TN).astype(LOW)
 
     low_bit, high_bit = 1, depth // 2
-    *down_sum, gate = tied(*down_sum, counts)
+    first = attend(0, counts)
+    first, down_sum, output_moved, gate = tied(first, down_sum, output_moved, counts)
+    activations = turned_settled(output_moved)
     down_step = depth_halved(added(down_sum), low_bit)
-    first = attend(0, gate)
-    flat, tree = jax.tree.flatten((down_step, up_sum, out_sum))
-    *flat, first, gate = tied(*flat, first, counts)
-    down_step, up_sum, out_sum = jax.tree.unflatten(tree, flat)
+    second = attend(1, gate)
+    second, first, down_step, rest_sum, gate = tied(second, first, down_step, rest_sum, counts)
     down_step = depth_halved(added(down_step), high_bit)
-    up_step = depth_halved(added(up_sum), low_bit)
-    out_step = depth_halved(added(out_sum), low_bit)
-    second = attend(1, gate)
-    flat, tree = jax.tree.flatten((down_step, up_step, out_step))
-    *flat, second, gate = tied(*flat, second, counts)
-    down_step, up_step, out_step = jax.tree.unflatten(tree, flat)
-    down_own = added(down_step)
-    down_got = across_depth(down_own, high_bit)
-    up_step = depth_halved(added(up_step), high_bit)
-    out_step = depth_halved(added(out_step), high_bit)
+    rest_step = depth_halved(added(rest_sum), low_bit)
     early = scattered_over_pairs(weight_part(jnp.concatenate([first, second], axis=1)))
     third = attend(2, gate)
-    flat, tree = jax.tree.flatten((up_step, out_step, early))
-    *flat, third, down_own, down_got = tied(*flat, third, down_own, down_got)
-    up_step, out_step, early = jax.tree.unflatten(tree, flat)
+    third, first, second, down_step, rest_step, early = tied(
+        third, first, second, down_step, rest_step, early
+    )
 
     partial = dot(jnp.concatenate([first, second, third], axis=1), w_qkv, NT)
     back_got = across_cores(partial[rows:].astype(LOW))
     late = scattered_over_pairs(weight_part(third))
+    down_own = added(down_step)
+    down_got = across_depth(down_own, high_bit)
+    rest_step = depth_halved(added(rest_step), high_bit)
+    early = added(early)
     grad_norm_one = partial[:rows] + back_got.astype(FULL)
     grad_in, gain_one_grad, shift_one_grad = norm_backward(
         grad_norm_one, unit_one, inverse_one, gain_one
     )
-    input_grad = turned((grad_middle + grad_in).astype(LOW).reshape(2, slot_rows, width))
-
-    def finished(value):
-        value = depth_doubled(value, across_depth(value, high_bit), high_bit)
-        return depth_doubled(value, across_depth(value, low_bit), low_bit)
-
+    grad_rows = (grad_middle + grad_in).astype(LOW)
+
+    row_index = lax.broadcasted_iota(jnp.int32, (8, width), 0)
+    small = jnp.zeros((8, width), FULL)
+    for index, value in enumerate(
+        [gain_one_grad, shift_one_grad, gain_two_grad, shift_two_grad, jnp.full((width,), squares)]
+    ):
+        small = jnp.where(row_index == index, value[None, :], small)
+    depth_steps, plane_steps = sum_steps()
+    for step in depth_steps:
+        small = small + step(small)
+    grad_rows, small, down_got, rest_step, late = tied(grad_rows, small, down_got, rest_step, late)
+    input_moved = turned_parts(grad_rows.reshape(2, slot_rows, width))
+
+    qkv_step = depth_halved(jnp.concatenate([early, added(late)], axis=1), low_bit)
     down_own = depth_doubled(down_own, down_got, high_bit)
-    down_own = depth_doubled(down_own, across_depth(down_own, low_bit), low_bit)
-    up_own = finished(added(up_step))
-    out_own = finished(added(out_step))
-    early = finished(added(depth_halved(added(depth_halved(added(early), low_bit)), high_bit)))
-    late = finished(added(depth_halved(added(depth_halved(added(late), low_bit)), high_bit)))
-
-    small = jnp.stack(
-        [
-            gain_one_grad, shift_one_grad, gain_two_grad, shift_two_grad,
-            jnp.full((width,), squares), jnp.zeros((width,)), jnp.zeros((width,)),
-            jnp.zeros((width,)),
-        ]
-    )
-    small = summed_everywhere(small)
+    down_got = across_depth(down_own, low_bit)
+    rest_own = added(rest_step)
+    rest_got = across_depth(rest_own, high_bit)
+    small = small + plane_steps[0](small)
+    qkv_step, down_got, rest_got, small = tied(qkv_step, down_got, rest_got, small)
+    qkv_step = depth_halved(added(qkv_step), high_bit)
+    rest_own = depth_doubled(rest_own, rest_got, high_bit)
+    rest_got = across_depth(rest_own, low_bit)
+    small = small + plane_steps[1](small)
+    down_own = depth_doubled(down_own, down_got, low_bit)
+    qkv_step, rest_got, small = tied(qkv_step, rest_got, small)
+    qkv_own = added(qkv_step)
+    qkv_got = across_depth(qkv_own, high_bit)
+    rest_own = depth_doubled(rest_own, rest_got, low_bit)
+
+    def own_block(stack, index):
+        return lax.dynamic_slice_in_dim(stack, index * own_rows, own_rows, 0)
+
+    rest_mine = own_block(rest_own, c)
+    rest_other = across_cores(own_block(rest_own, 1 - c))
+    for step in plane_steps[2:]:
+        small = small + step(small)
+    qkv_got, rest_other, small = tied(qkv_got, rest_other, small)
+    qkv_own = depth_doubled(qkv_own, qkv_got, high_bit)
+    qkv_own = depth_doubled(qkv_own, across_depth(qkv_own, low_bit), low_bit)
+    qkv_mine = own_block(qkv_own, c)
+    qkv_other = across_cores(own_block(qkv_own, 1 - c))
+    qkv_other, input_moved = tied(qkv_other, input_moved)
+    input_grad = turned_settled(input_moved)
+
     loss = small[4, 0] / (valid_count * width)
     own_small = lax.dynamic_slice_in_dim(small, group * own_rows, own_rows, 1)
-
-    def own_block(stack, index):
-        return lax.dynamic_slice_in_dim(stack, index * own_rows, own_rows, 0)
-
-    sums = jnp.concatenate([up_own, early, late], axis=1)
-    mine = own_block(sums, c)
-    other = across_cores(own_block(sums, 1 - c))
-    sides = [jnp.where(is_first, mine, other), jnp.where(is_first, other, mine)]
+    out_own = rest_mine[:, half_ff:].astype(FULL) + rest_other[:, half_ff:].astype(FULL)
+    sides = [jnp.where(is_first, rest_mine, rest_other), jnp.where(is_first, rest_other, rest_mine)]
     up_own = jnp.concatenate(
         [side[:, q * block : (q + 1) * block] for q in range(pairs) for side in sides], axis=1
     )
-    qkv_own = jnp.stack([side[:, half_ff:] for side in sides])
+    qkv_own = jnp.stack(
+        [jnp.where(is_first, qkv_mine, qkv_other), jnp.where(is_first, qkv_other, qkv_mine)]
+    )
     qkv_own = qkv_own.reshape(2, own_rows, head_pairs, 3, 2, HEAD_DIM)
     qkv_own = jnp.transpose(qkv_own, (1, 0, 2, 4, 3, 5)).reshape(own_rows, 3 * width)
     return (
         activations, loss, input_grad, own_small[0], own_small[1], qkv_own.astype(FULL),
-        out_own.astype(FULL), own_small[2], own_small[3], up_own.astype(FULL),
-        down_own.astype(FULL),
+        out_own, own_small[2], own_small[3], up_own.astype(FULL), down_own.astype(FULL),
     )
 
 

time: 512 us -> 762 us (1.49)
  Pallas kernels: 79.6 us -> 321 us
  other arithmetic: 48.8 us -> 78.6 us
  local copies, waits for them, and re-layouts: 75.6 us -> 52.2 us
  starting transfers between devices: 87.6 us -> 72.3 us
  matrix products: 55.3 us -> 66.4 us
    pallas_call x0 -> x2, Pallas kernels: none -> 241 us  [placed(): pl.pallas_call(functools.partial(place_kernel, segments=segments, pairs=p...]
    dynamic_update_slice x16 -> x0, local copies, waits for them, and re-layouts: 38.8 us -> none  [assembled(): lax.dynamic_update_slice_in_dim(whole, piece, jnp.bitwise_xor(p, k) * row...]
    dynamic_slice x1 -> x6, local copies, waits for them, and re-layouts: 0.05 us -> 19.7 us  [turned_parts(): piece = lax.dynamic_index_in_dim(stack, (z + step) % 2, 0, keepdims=False)]
    ppermute x81 -> x63, starting transfers between devices: 87.6 us -> 72.3 us  [moved(): return lax.ppermute(value, AXES, links)]
    dot_general x19 -> x20, matrix products: 55.3 us -> 66.4 us  [dot(): return lax.dot_general(left, right, form, preferred_element_type=FULL)]
    concatenate x2 -> x6, other arithmetic: 1.21 us -> 10.1 us  [the longest x1 3.54 us: shards(): jnp.concatenate([up_grad, out_grad], axis=1)]
    ppermute x81 -> x63, waiting for transfers between devices: 153 us -> 159 us  [moved(): return lax.ppermute(value, AXES, links)]
  transfers between devices with their start and end apart: 81 -> 63, of which waited for: 28 -> 16; matrix products, arithmetic and copies ran while one was open for 29% -> 18% of each run, Pallas kernels for 16% -> 42%
where the time goes in v3:
time: 762 us; the launch traced here: 756 us
  Pallas kernels  321 us (42%)
  waiting for transfers between devices  159 us (21%)
  other arithmetic  78.6 us (10%)
  starting transfers between devices  72.3 us (9%)
  matrix products  66.4 us (9%)
  local copies, waits for them, and re-layouts  52.2 us (7%)
    pallas_call x2, Pallas kernels, placed(): pl.pallas_call(functools.partial(place_kernel, segments=segments, pairs=p...  241 us
    ppermute x63, waiting for transfers between devices, moved(): return lax.ppermute(value, AXES, links)  159 us
    ppermute x63, starting transfers between devices, moved(): return lax.ppermute(value, AXES, links)  72.3 us
    dot_general x20, matrix products, dot(): return lax.dot_general(left, right, form, preferred_element_type=FULL)  66.4 us
    pallas_call x3, Pallas kernels, attention_backward(): pl.pallas_call(functools.partial(backward_kernel, rows=rows, block=block,...  50.3 us
    pallas_call x1, Pallas kernels, attention_forward(): pl.pallas_call(functools.partial(forward_kernel, rows=rows, block=block),...  29.6 us
    dynamic_slice x6, local copies, waits for them, and re-layouts, turned_parts(): piece = lax.dynamic_index_in_dim(stack, (z + step) % 2, 0, keepdims=False)  19.7 us
  transfers between devices with their start and end apart: 63, of which 16 were waited for; matrix products, arithmetic and copies ran while one was open for 18% of the time, Pallas kernels for 42%

profile of v3, /device:TPU:0, one launch (start us, length us, event | category | flops | bytes accessed | tf_op | source)
XLA Modules:
  0.0 756.3 jit_solution(4884683951778081915)
XLA Ops:
  4.6 6.1 collective-permute-start
  10.7 2.6 collective-permute-start.1
  37.4 8.4 %collective-permute-done.5.refs_2_ = bf16[192,1280]{1,0:T(8,128)(2,1)} collective-permute-done((bf16[192,1280]{1,0:T(8,128)(2,1)S(1)}, bf16[192,1280]{1,0:T(8,128)(2,1)}, u32[]{:S(2)}, u32[]{:S(2)}) %collective-permute-start.5) | collective-permute-done | bytes 491552 | tf_op jit(solution)/shard_map/ppermute | solution.py:37
  46.6 60.7 %place.2 = (bf16[768,1152]{1,0:T(8,128)(2,1)}, bf16[768,128]{1,0:T(8,128)(2,1)}) custom-call(s32[1]{0:T(128)} %bitcast.7.p_ref, bf16[192,1280]{1,0:T(8,128)(2,1)} %copy-done.13, bf16[192,1280]{1,0:T(8,128)(2,1)} %collective-permute-done.4.refs_1_, bf16[192,1280]{1,0:T(8,128)(2,1)} %collective-permute-done.5.refs_2_, bf16[192,1280]{1,0:T(8,128)(2,1)} %copy-done.41), custom_call_target="tpu_custom_call" | custom-call | tf_op jit(solution)/shard_map/place/pallas_call | solution.py:150
  120.4 60.3 %collective-permute-done.10 = f32[8,128]{1,0:T(8,128)S(1)} collective-permute-done((f32[8,128]{1,0:T(8,128)S(1)}, f32[8,128]{1,0:T(8,128)S(1)}, u32[]{:S(2)}, u32[]{:S(2)}) %collective-permute-start.10) | collective-permute-done | bytes 4128 | tf_op jit(solution)/shard_map/ppermute | solution.py:37
  184.8 4.7 convolution_convert_fusion.q_ref.k_ref.v_ref
  189.6 6.4 collective-permute-done.11
  202.5 29.6 %attention_forward.1 = (bf16[1536,384]{1,0:T(8,128)(2,1)}, f32[3,2,1536]{2,1,0:T(2,128)}) custom-call(s32[2]{0:T(128)} %add_clamp_fusion.counts_ref, bf16[1536,1152]{1,0:T(8,128)(2,1)} %convolution_convert_fusion.q_ref.k_ref.v_ref, bf16[1536,1152]{1,0:T(8,128)(2,1)} %convolution_convert_fusion.q_ref.k_ref.v_ref, ...), custom_call_target="tpu_custom_call" | custom-call | flops 1 | bytes 1 | tf_op jit(solution)/shard_map/attention_forward/pallas_call | solution.py:256
  235.0 179.9 %place.3 = (bf16[1536,768]{1,0:T(8,128)(2,1)}, bf16[768,1536]{1,0:T(8,128)(2,1)}, bf16[768,768]{1,0:T(8,128)(2,1)}) custom-call(s32[1]{0:T(128)} %bitcast.30.p_ref, bf16[960,768]{1,0:T(8,128)(2,1)} %select_dynamic-update-slice_fusion.refs_0_, bf16[960,768]{1,0:T(8,128)(2,1)} %collective-permute-done.13.refs_1_, ...), custom_call_target="tpu_custom_call" | custom-call | tf_op jit(solution)/shard_map/place/pallas_call | solution.py:150
  421.7 4.2 multiply_convert_fusion.2
  426.0 3.1 convolution_convert_fusion.4
  430.9 6.4 collective-permute-start.21
  438.9 25.1 %collective-permute-done.23 = f32[8,128]{1,0:T(8,128)} collective-permute-done((f32[8,128]{1,0:T(8,128)}, f32[8,128]{1,0:T(8,128)}, u32[]{:S(2)}, u32[]{:S(2)}) %collective-permute-start.23) | collective-permute-done | bytes 4128 | tf_op jit(solution)/shard_map/ppermute | solution.py:37
  465.2 6.8 multiply_convert_fusion.3
  474.9 4.9 convert_add_fusion.2
  488.4 2.8 bitcast_convert_fusion
  491.2 3.4 copy.130
  494.6 2.9 multiply_convert_fusion.4
  497.6 3.9 fusion.91
  501.5 4.2 multiply_convert_fusion.1
  507.9 4.4 multiply_convert_fusion
  521.7 3.5 add_convert_fusion
  525.2 3.3 multiply_reduce_fusion
  528.5 3.1 fusion.32
  535.0 4.2 convolution_convert_fusion.1
  539.2 3.4 constant_dynamic-slice_fusion.11
  542.6 4.5 copy.112
  547.1 6.0 collective-permute-start.30
  553.1 3.2 copy.113
  556.5 3.5 fusion.41
  565.7 16.6 %attention_backward.3 = bf16[1536,384]{1,0:T(8,128)(2,1)} custom-call(s32[2]{0:T(128)} %add_clamp_fusion.counts_ref, bf16[1536,1152]{1,0:T(8,128)(2,1)} %convolution_convert_fusion.q_ref.k_ref.v_ref, bf16[1536,1152]{1,0:T(8,128)(2,1)} %convolution_convert_fusion.q_ref.k_ref.v_ref, bf16[1536,1152]{1,0:T(8,128)(2,1)} %convolution_convert_fusion.q_ref.k_ref.v_ref, ...), custom_call_target="tpu_custom_call" | custom-call | flops 1 | bytes 1 | tf_op jit(solution)/shard_map/attention_backward/pallas_call | solution.py:335
  588.6 17.0 %attention_backward.4 = bf16[1536,384]{1,0:T(8,128)(2,1)} custom-call(s32[2]{0:T(128)} %add_clamp_fusion.counts_ref, bf16[1536,1152]{1,0:T(8,128)(2,1)} %convolution_convert_fusion.q_ref.k_ref.v_ref, bf16[1536,1152]{1,0:T(8,128)(2,1)} %convolution_convert_fusion.q_ref.k_ref.v_ref, bf16[1536,1152]{1,0:T(8,128)(2,1)} %convolution_convert_fusion.q_ref.k_ref.v_ref, ...), custom_call_target="tpu_custom_call" | custom-call | flops 1 | bytes 1 | tf_op jit(solution)/shard_map/attention_backward/pallas_call | solution.py:335
  605.7 4.0 fusion.37
  621.7 16.7 %attention_backward.5 = bf16[1536,384]{1,0:T(8,128)(2,1)} custom-call(s32[2]{0:T(128)} %add_clamp_fusion.counts_ref, bf16[1536,1152]{1,0:T(8,128)(2,1)} %convolution_convert_fusion.q_ref.k_ref.v_ref, bf16[1536,1152]{1,0:T(8,128)(2,1)} %convolution_convert_fusion.q_ref.k_ref.v_ref, bf16[1536,1152]{1,0:T(8,128)(2,1)} %convolution_convert_fusion.q_ref.k_ref.v_ref, ...), custom_call_target="tpu_custom_call" | custom-call | flops 1 | bytes 1 | tf_op jit(solution)/shard_map/attention_backward/pallas_call | solution.py:335
  638.5 2.8 convolution_convert_fusion.5
  644.9 3.2 fusion.10
  650.4 2.8 collective-permute-start.45
  659.3 4.1 collective-permute-done.42
  665.2 5.6 collective-permute-done.43
  672.2 8.3 %collective-permute-done.44 = bf16[96,768]{1,0:T(8,128)(2,1)S(1)} collective-permute-done((bf16[96,768]{1,0:T(8,128)(2,1)S(1)}, bf16[96,768]{1,0:T(8,128)(2,1)S(1)}, u32[]{:S(2)}, u32[]{:S(2)}) %collective-permute-start.44) | collective-permute-done | bytes 147488 | tf_op jit(solution)/shard_map/ppermute | solution.py:37
  682.1 3.4 collective-permute-start.50
  687.9 2.4 constant_dynamic-slice_fusion.1
  690.3 3.0 copy.117
  695.0 3.2 copy.118
  703.8 3.9 collective-permute-start.53
  708.9 20.1 %collective-permute-done.53 = bf16[48,1152]{1,0:T(8,128)(2,1)S(1)} collective-permute-done((bf16[48,1152]{1,0:T(8,128)(2,1)S(1)}, bf16[48,1152]{1,0:T(8,128)(2,1)S(1)}, u32[]{:S(2)}, u32[]{:S(2)}) %collective-permute-start.53) | collective-permute-done | bytes 110624 | tf_op jit(solution)/shard_map/ppermute | solution.py:37
  735.0 6.0 collective-permute-done.56
  744.8 5.0 collective-permute-done.59
  (421 shorter events, 155.7 us)
Async XLA Ops:
  2.9 19.4 %collective-permute-start.2 = (bf16[288,768]{1,0:T(8,128)(2,1)}, bf16[288,768]{1,0:T(8,128)(2,1)}, u32[]{:S(2)}, u32[]{:S(2)}) collective-permute-start(bf16[288,768]{1,0:T(8,128)(2,1)} %pad_maximum_fusion.12), channel_id=1, source_target_pairs={{0,4},{1,5},{2,6},{3,7},{4,0},{5,1},{6,2},{7,3},{8,12},{9,13},{10,... | collective-permute-start | bytes 1327112 | tf_op jit(solution)/shard_map/ppermute | solution.py:37
  4.6 25.2 %collective-permute-start = (bf16[384,768]{1,0:T(8,128)(2,1)}, bf16[384,768]{1,0:T(8,128)(2,1)}, u32[]{:S(2)}, u32[]{:S(2)}) collective-permute-start(bf16[384,768]{1,0:T(8,128)(2,1)} %get-tuple-element.286), channel_id=1, source_target_pairs={{0,0},{1,1},{2,4},{3,5},{4,2},{5,3},{6,6},{7,7},{8,8},{9,9},{10,12... | collective-permute-start | bytes 1769480 | tf_op jit(solution)/shard_map/ppermute | solution.py:37
  10.7 21.9 %collective-permute-start.1 = (bf16[384,768]{1,0:T(8,128)(2,1)}, bf16[384,768]{1,0:T(8,128)(2,1)}, u32[]{:S(2)}, u32[]{:S(2)}) collective-permute-start(bf16[384,768]{1,0:T(8,128)(2,1)} %get-tuple-element.287), channel_id=1, source_target_pairs={{0,1},{1,0},{2,5},{3,4},{4,3},{5,2},{6,7},{7,6},{8,9},{9,8},{10,13... | collective-permute-start | bytes 1769480 | tf_op jit(solution)/shard_map/ppermute | solution.py:37
  18.2 99.8 %collective-permute-start.8 = (bf16[400,768]{1,0:T(8,128)(2,1)}, bf16[400,768]{1,0:T(8,128)(2,1)}, u32[]{:S(2)}, u32[]{:S(2)}) collective-permute-start(bf16[400,768]{1,0:T(8,128)(2,1)} %fusion.49), channel_id=1, source_target_pairs={{0,4},{1,5},{2,6},{3,7},{4,0},{5,1},{6,2},{7,3},{8,12},{9,13},{10,... | collective-permute-start | bytes 1843208 | tf_op jit(solution)/shard_map/ppermute | solution.py:37
  20.8 16.6 %collective-permute-start.4 = (bf16[192,1280]{1,0:T(8,128)(2,1)S(1)}, bf16[192,1280]{1,0:T(8,128)(2,1)}, u32[]{:S(2)}, u32[]{:S(2)}) collective-permute-start(bf16[192,1280]{1,0:T(8,128)(2,1)S(1)} %pad_maximum_fusion.11.refs_0_), channel_id=1, source_target_pairs={{0,8},{1,9},{2,10},{3,11},{4,12},{5,13},{6,14},{7,15},{8,0},{9,1},... | collective-permute-start | bytes 1474568 | tf_op jit(solution)/shard_map/ppermute | solution.py:37
  22.4 23.5 %collective-permute-start.5 = (bf16[192,1280]{1,0:T(8,128)(2,1)S(1)}, bf16[192,1280]{1,0:T(8,128)(2,1)}, u32[]{:S(2)}, u32[]{:S(2)}) collective-permute-start(bf16[192,1280]{1,0:T(8,128)(2,1)S(1)} %pad_maximum_fusion.11.refs_0_), channel_id=1, source_target_pairs={{0,16},{1,17},{2,18},{3,19},{4,20},{5,21},{6,22},{7,23},{8,24},{9,... | collective-permute-start | bytes 1474568 | tf_op jit(solution)/shard_map/ppermute | solution.py:37
  29.8 16.0 %collective-permute-start.6 = (bf16[192,1280]{1,0:T(8,128)(2,1)S(1)}, bf16[192,1280]{1,0:T(8,128)(2,1)S(1)}, u32[]{:S(2)}, u32[]{:S(2)}) collective-permute-start(bf16[192,1280]{1,0:T(8,128)(2,1)S(1)} %pad_maximum_fusion.11.refs_0_), channel_id=1, source_target_pairs={{0,24},{1,25},{2,26},{3,27},{4,28},{5,29},{6,30},{7,31},{8,16},{9,... | collective-permute-start | bytes 1474568 | tf_op jit(solution)/shard_map/ppermute | solution.py:37
  110.6 71.3 %collective-permute-start.7 = (bf16[768,768]{0,1:T(8,128)(2,1)}, bf16[768,768]{0,1:T(8,128)(2,1)}, u32[]{:S(2)}, u32[]{:S(2)}) collective-permute-start(bf16[768,768]{0,1:T(8,128)(2,1)} %fusion.24), channel_id=1, source_target_pairs={{0,4},{1,5},{2,6},{3,7},{4,0},{5,1},{6,2},{7,3},{8,12},{9,13},{10,... | collective-permute-start | bytes 3538952 | tf_op jit(solution)/shard_map/ppermute | solution.py:37
  114.4 118.3 %collective-permute-start.13 = (bf16[960,768]{1,0:T(8,128)(2,1)}, bf16[960,768]{1,0:T(8,128)(2,1)}, u32[]{:S(2)}, u32[]{:S(2)}) collective-permute-start(bf16[960,768]{1,0:T(8,128)(2,1)} %select_dynamic-update-slice_fusion.refs_0_), channel_id=1, source_target_pairs={{0,8},{1,9},{2,10},{3,11},{4,12},{5,13},{6,14},{7,15},{8,0},{9,1},... | collective-permute-start | bytes 4423688 | tf_op jit(solution)/shard_map/ppermute | solution.py:37
  115.6 117.2 %collective-permute-start.14 = (bf16[960,768]{1,0:T(8,128)(2,1)}, bf16[960,768]{1,0:T(8,128)(2,1)}, u32[]{:S(2)}, u32[]{:S(2)}) collective-permute-start(bf16[960,768]{1,0:T(8,128)(2,1)} %select_dynamic-update-slice_fusion.refs_0_), channel_id=1, source_target_pairs={{0,16},{1,17},{2,18},{3,19},{4,20},{5,21},{6,22},{7,23},{8,24},{9,... | collective-permute-start | bytes 4423688 | tf_op jit(solution)/shard_map/ppermute | solution.py:37
  116.5 116.2 %collective-permute-start.15 = (bf16[960,768]{1,0:T(8,128)(2,1)}, bf16[960,768]{1,0:T(8,128)(2,1)}, u32[]{:S(2)}, u32[]{:S(2)}) collective-permute-start(bf16[960,768]{1,0:T(8,128)(2,1)} %select_dynamic-update-slice_fusion.refs_0_), channel_id=1, source_target_pairs={{0,24},{1,25},{2,26},{3,27},{4,28},{5,29},{6,30},{7,31},{8,16},{9,... | collective-permute-start | bytes 4423688 | tf_op jit(solution)/shard_map/ppermute | solution.py:37
  118.0 62.8 %collective-permute-start.10 = (f32[8,128]{1,0:T(8,128)S(1)}, f32[8,128]{1,0:T(8,128)S(1)}, u32[]{:S(2)}, u32[]{:S(2)}) collective-permute-start(f32[8,128]{1,0:T(8,128)S(1)} %broadcast_add_fusion), channel_id=1, source_target_pairs={{0,8},{1,9},{2,10},{3,11},{4,12},{5,13},{6,14},{7,15},{8,0},{9,1},... | collective-permute-start | bytes 12296 | tf_op jit(solution)/shard_map/ppermute | solution.py:37
  180.8 15.1 %collective-permute-start.11 = (bf16[400,768]{1,0:T(8,128)(2,1)S(1)}, bf16[400,768]{1,0:T(8,128)(2,1)S(1)}, u32[]{:S(2)}, u32[]{:S(2)}) collective-permute-start(bf16[400,768]{1,0:T(8,128)(2,1)S(1)} %get-tuple-element.261), channel_id=1, source_target_pairs={{0,8},{1,9},{2,10},{3,11},{4,12},{5,13},{6,14},{7,15},{8,0},{9,1},... | collective-permute-start | bytes 1843208 | tf_op jit(solution)/shard_map/ppermute | solution.py:37
  196.9 35.9 %collective-permute-start.16 = (bf16[400,768]{1,0:T(8,128)(2,1)}, bf16[400,768]{1,0:T(8,128)(2,1)S(1)}, u32[]{:S(2)}, u32[]{:S(2)}) collective-permute-start(bf16[400,768]{1,0:T(8,128)(2,1)} %get-tuple-element.258), channel_id=1, source_target_pairs={{0,16},{1,17},{2,18},{3,19},{4,20},{5,21},{6,22},{7,23},{8,24},{9,... | collective-permute-start | bytes 1843208 | tf_op jit(solution)/shard_map/ppermute | solution.py:37
  200.9 31.3 %collective-permute-start.17 = (f32[8,128]{1,0:T(8,128)S(1)}, f32[8,128]{1,0:T(8,128)S(1)}, u32[]{:S(2)}, u32[]{:S(2)}) collective-permute-start(f32[8,128]{1,0:T(8,128)S(1)} %add.328), channel_id=1, source_target_pairs={{0,1},{1,0},{2,3},{3,2},{4,5},{5,4},{6,7},{7,6},{8,9},{9,8},{10,11... | collective-permute-start | bytes 12296 | tf_op jit(solution)/shard_map/ppermute | solution.py:37
  235.0 180.0 %collective-permute-start.18 = (bf16[768,384]{1,0:T(8,128)(2,1)}, bf16[768,384]{1,0:T(8,128)(2,1)}, u32[]{:S(2)}, u32[]{:S(2)}) collective-permute-start(bf16[768,384]{1,0:T(8,128)(2,1)} %slice.191), channel_id=1, source_target_pairs={{0,4},{1,5},{2,6},{3,7},{4,0},{5,1},{6,2},{7,3},{8,12},{9,13},{10,... | collective-permute-start | bytes 1769480 | tf_op jit(solution)/shard_map/ppermute | solution.py:37
  429.0 45.3 %collective-permute-start.20 = (bf16[768,768]{0,1:T(8,128)(2,1)}, bf16[768,768]{0,1:T(8,128)(2,1)}, u32[]{:S(2)}, u32[]{:S(2)}) collective-permute-start(bf16[768,768]{0,1:T(8,128)(2,1)} %convolution_convert_fusion.4), channel_id=1, source_target_pairs={{0,4},{1,5},{2,6},{3,7},{4,0},{5,1},{6,2},{7,3},{8,12},{9,13},{10,... | collective-permute-start | bytes 3538952 | tf_op jit(solution)/shard_map/ppermute | solution.py:37
  430.9 41.1 %collective-permute-start.21 = (bf16[400,768]{1,0:T(8,128)(2,1)}, bf16[400,768]{1,0:T(8,128)(2,1)}, u32[]{:S(2)}, u32[]{:S(2)}) collective-permute-start(bf16[400,768]{1,0:T(8,128)(2,1)} %get-tuple-element.268), channel_id=1, source_target_pairs={{0,0},{1,1},{2,4},{3,5},{4,2},{5,3},{6,6},{7,7},{8,8},{9,9},{10,12... | collective-permute-start | bytes 1843208 | tf_op jit(solution)/shard_map/ppermute | solution.py:37
  437.3 34.7 %collective-permute-start.22 = (bf16[400,768]{1,0:T(8,128)(2,1)}, bf16[400,768]{1,0:T(8,128)(2,1)}, u32[]{:S(2)}, u32[]{:S(2)}) collective-permute-start(bf16[400,768]{1,0:T(8,128)(2,1)} %get-tuple-element.269), channel_id=1, source_target_pairs={{0,1},{1,0},{2,5},{3,4},{4,3},{5,2},{6,7},{7,6},{8,9},{9,8},{10,13... | collective-permute-start | bytes 1843208 | tf_op jit(solution)/shard_map/ppermute | solution.py:37
  438.9 25.1 %collective-permute-start.23 = (f32[8,128]{1,0:T(8,128)}, f32[8,128]{1,0:T(8,128)}, u32[]{:S(2)}, u32[]{:S(2)}) collective-permute-start(f32[8,128]{1,0:T(8,128)} %add.329), channel_id=1, source_target_pairs={{0,2},{1,3},{2,0},{3,1},{4,6},{5,7},{6,4},{7,5},{8,10},{9,11},{10,... | collective-permute-start | bytes 12296 | tf_op jit(solution)/shard_map/ppermute | solution.py:37
  514.3 10.8 %collective-permute-start.25 = (bf16[768,768]{0,1:T(8,128)(2,1)S(1)}, bf16[768,768]{0,1:T(8,128)(2,1)S(1)}, u32[]{:S(2)}, u32[]{:S(2)}) collective-permute-start(bf16[768,768]{0,1:T(8,128)(2,1)S(1)} %convolution_convert_fusion.3), channel_id=1, source_target_pairs={{0,4},{1,5},{2,6},{3,7},{4,0},{5,1},{6,2},{7,3},{8,12},{9,13},{10,... | collective-permute-start | bytes 3538952 | tf_op jit(solution)/shard_map/ppermute | solution.py:37
  516.2 40.2 %collective-permute-start.27 = (bf16[384,768]{1,0:T(8,128)(2,1)}, bf16[384,768]{1,0:T(8,128)(2,1)}, u32[]{:S(2)}, u32[]{:S(2)}) collective-permute-start(bf16[384,768]{1,0:T(8,128)(2,1)} %get-tuple-element.254), channel_id=1, source_target_pairs={{0,8},{1,9},{2,10},{3,11},{4,12},{5,13},{6,14},{7,15},{8,0},{9,1},... | collective-permute-start | bytes 1769480 | tf_op jit(solution)/shard_map/ppermute | solution.py:37
  516.7 43.3 %collective-permute-start.28 = (bf16[384,768]{1,0:T(8,128)(2,1)}, bf16[384,768]{1,0:T(8,128)(2,1)}, u32[]{:S(2)}, u32[]{:S(2)}) collective-permute-start(bf16[384,768]{1,0:T(8,128)(2,1)} %get-tuple-element.253), channel_id=1, source_target_pairs={{0,16},{1,17},{2,18},{3,19},{4,20},{5,21},{6,22},{7,23},{8,24},{9,... | collective-permute-start | bytes 1769480 | tf_op jit(solution)/shard_map/ppermute | solution.py:37
  517.8 42.8 %collective-permute-start.29 = (bf16[384,768]{1,0:T(8,128)(2,1)}, bf16[384,768]{1,0:T(8,128)(2,1)}, u32[]{:S(2)}, u32[]{:S(2)}) collective-permute-start(bf16[384,768]{1,0:T(8,128)(2,1)} %get-tuple-element.252), channel_id=1, source_target_pairs={{0,24},{1,25},{2,26},{3,27},{4,28},{5,29},{6,30},{7,31},{8,16},{9,... | collective-permute-start | bytes 1769480 | tf_op jit(solution)/shard_map/ppermute | solution.py:37
  534.1 27.5 %collective-permute-start.26 = (bf16[768,384]{1,0:T(8,128)(2,1)}, bf16[768,384]{1,0:T(8,128)(2,1)}, u32[]{:S(2)}, u32[]{:S(2)}) collective-permute-start(bf16[768,384]{1,0:T(8,128)(2,1)} %get-tuple-element.283), channel_id=1, source_target_pairs={{0,4},{1,5},{2,6},{3,7},{4,0},{5,1},{6,2},{7,3},{8,12},{9,13},{10,... | collective-permute-start | bytes 1769480 | tf_op jit(solution)/shard_map/ppermute | solution.py:37
  547.1 35.2 %collective-permute-start.30 = (bf16[384,768]{1,0:T(8,128)(2,1)}, bf16[384,768]{1,0:T(8,128)(2,1)}, u32[]{:S(2)}, u32[]{:S(2)}) collective-permute-start(bf16[384,768]{1,0:T(8,128)(2,1)} %bitcast.41), channel_id=1, source_target_pairs={{0,0},{1,1},{2,4},{3,5},{4,2},{5,3},{6,6},{7,7},{8,8},{9,9},{10,12... | collective-permute-start | bytes 1769480 | tf_op jit(solution)/shard_map/ppermute | solution.py:37
  556.3 26.0 %collective-permute-start.31 = (bf16[384,768]{1,0:T(8,128)(2,1)}, bf16[384,768]{1,0:T(8,128)(2,1)S(1)}, u32[]{:S(2)}, u32[]{:S(2)}) collective-permute-start(bf16[384,768]{1,0:T(8,128)(2,1)} %bitcast.42), channel_id=1, source_target_pairs={{0,1},{1,0},{2,5},{3,4},{4,3},{5,2},{6,7},{7,6},{8,9},{9,8},{10,13... | collective-permute-start | bytes 1769480 | tf_op jit(solution)/shard_map/ppermute | solution.py:37
  560.0 45.6 %collective-permute-start.33 = (bf16[192,2304]{1,0:T(8,128)(2,1)}, bf16[192,2304]{1,0:T(8,128)(2,1)}, u32[]{:S(2)}, u32[]{:S(2)}) collective-permute-start(bf16[192,2304]{1,0:T(8,128)(2,1)} %get-tuple-element.249), channel_id=1, source_target_pairs={{0,8},{1,9},{2,10},{3,11},{4,12},{5,13},{6,14},{7,15},{8,0},{9,1},... | collective-permute-start | bytes 2654216 | tf_op jit(solution)/shard_map/ppermute | solution.py:37
  560.6 45.0 %collective-permute-start.34 = (bf16[192,2304]{1,0:T(8,128)(2,1)}, bf16[192,2304]{1,0:T(8,128)(2,1)}, u32[]{:S(2)}, u32[]{:S(2)}) collective-permute-start(bf16[192,2304]{1,0:T(8,128)(2,1)} %get-tuple-element.250), channel_id=1, source_target_pairs={{0,16},{1,17},{2,18},{3,19},{4,20},{5,21},{6,22},{7,23},{8,24},{9,... | collective-permute-start | bytes 2654216 | tf_op jit(solution)/shard_map/ppermute | solution.py:37
  561.7 43.9 %collective-permute-start.35 = (bf16[192,2304]{1,0:T(8,128)(2,1)}, bf16[192,2304]{1,0:T(8,128)(2,1)}, u32[]{:S(2)}, u32[]{:S(2)}) collective-permute-start(bf16[192,2304]{1,0:T(8,128)(2,1)} %get-tuple-element.247), channel_id=1, source_target_pairs={{0,24},{1,25},{2,26},{3,27},{4,28},{5,29},{6,30},{7,31},{8,16},{9,... | collective-permute-start | bytes 2654216 | tf_op jit(solution)/shard_map/ppermute | solution.py:37
  585.0 20.6 %collective-permute-start.32 = (bf16[192,768]{1,0:T(8,128)(2,1)}, bf16[192,768]{1,0:T(8,128)(2,1)}, u32[]{:S(2)}, u32[]{:S(2)}) collective-permute-start(bf16[192,768]{1,0:T(8,128)(2,1)} %get-tuple-element.302), channel_id=1, source_target_pairs={{0,1},{1,0},{2,3},{3,2},{4,5},{5,4},{6,7},{7,6},{8,9},{9,8},{10,11... | collective-permute-start | bytes 884744 | tf_op jit(solution)/shard_map/ppermute | solution.py:37
  610.7 27.7 %collective-permute-start.38 = (bf16[192,768]{1,0:T(8,128)(2,1)}, bf16[192,768]{1,0:T(8,128)(2,1)}, u32[]{:S(2)}, u32[]{:S(2)}) collective-permute-start(bf16[192,768]{1,0:T(8,128)(2,1)} %get-tuple-element.276), channel_id=1, source_target_pairs={{0,8},{1,9},{2,10},{3,11},{4,12},{5,13},{6,14},{7,15},{8,0},{9,1},... | collective-permute-start | bytes 884744 | tf_op jit(solution)/shard_map/ppermute | solution.py:37
  611.2 27.2 %collective-permute-start.39 = (bf16[192,768]{1,0:T(8,128)(2,1)}, bf16[192,768]{1,0:T(8,128)(2,1)}, u32[]{:S(2)}, u32[]{:S(2)}) collective-permute-start(bf16[192,768]{1,0:T(8,128)(2,1)} %get-tuple-element.275), channel_id=1, source_target_pairs={{0,16},{1,17},{2,18},{3,19},{4,20},{5,21},{6,22},{7,23},{8,24},{9,... | collective-permute-start | bytes 884744 | tf_op jit(solution)/shard_map/ppermute | solution.py:37
  612.3 26.1 %collective-permute-start.40 = (bf16[192,768]{1,0:T(8,128)(2,1)}, bf16[192,768]{1,0:T(8,128)(2,1)}, u32[]{:S(2)}, u32[]{:S(2)}) collective-permute-start(bf16[192,768]{1,0:T(8,128)(2,1)} %get-tuple-element.274), channel_id=1, source_target_pairs={{0,24},{1,25},{2,26},{3,27},{4,28},{5,29},{6,30},{7,31},{8,16},{9,... | collective-permute-start | bytes 884744 | tf_op jit(solution)/shard_map/ppermute | solution.py:37
  617.3 21.1 %collective-permute-start.37 = (bf16[96,2304]{1,0:T(8,128)(2,1)}, bf16[96,2304]{1,0:T(8,128)(2,1)}, u32[]{:S(2)}, u32[]{:S(2)}) collective-permute-start(bf16[96,2304]{1,0:T(8,128)(2,1)} %get-tuple-element.290), channel_id=1, source_target_pairs={{0,1},{1,0},{2,3},{3,2},{4,5},{5,4},{6,7},{7,6},{8,9},{9,8},{10,11... | collective-permute-start | bytes 1327112 | tf_op jit(solution)/shard_map/ppermute | solution.py:37
  619.3 19.1 %collective-permute-start.36 = (bf16[96,768]{1,0:T(8,128)(2,1)}, bf16[96,768]{1,0:T(8,128)(2,1)}, u32[]{:S(2)}, u32[]{:S(2)}) collective-permute-start(bf16[96,768]{1,0:T(8,128)(2,1)} %get-tuple-element.326), channel_id=1, source_target_pairs={{0,2},{1,3},{2,0},{3,1},{4,6},{5,7},{6,4},{7,5},{8,10},{9,11},{10,... | collective-permute-start | bytes 442376 | tf_op jit(solution)/shard_map/ppermute | solution.py:37
  641.4 30.8 %collective-permute-start.46 = (bf16[192,384]{1,0:T(8,128)(2,1)S(1)}, bf16[192,384]{1,0:T(8,128)(2,1)S(1)}, u32[]{:S(2)}, u32[]{:S(2)}) collective-permute-start(bf16[192,384]{1,0:T(8,128)(2,1)S(1)} %get-tuple-element.300), channel_id=1, source_target_pairs={{0,8},{1,9},{2,10},{3,11},{4,12},{5,13},{6,14},{7,15},{8,0},{9,1},... | collective-permute-start | bytes 442376 | tf_op jit(solution)/shard_map/ppermute | solution.py:37
  642.0 30.2 %collective-permute-start.47 = (bf16[192,384]{1,0:T(8,128)(2,1)S(1)}, bf16[192,384]{1,0:T(8,128)(2,1)S(1)}, u32[]{:S(2)}, u32[]{:S(2)}) collective-permute-start(bf16[192,384]{1,0:T(8,128)(2,1)S(1)} %get-tuple-element.299), channel_id=1, source_target_pairs={{0,16},{1,17},{2,18},{3,19},{4,20},{5,21},{6,22},{7,23},{8,24},{9,... | collective-permute-start | bytes 442376 | tf_op jit(solution)/shard_map/ppermute | solution.py:37
  643.1 29.1 %collective-permute-start.48 = (bf16[192,384]{1,0:T(8,128)(2,1)S(1)}, bf16[192,384]{1,0:T(8,128)(2,1)S(1)}, u32[]{:S(2)}, u32[]{:S(2)}) collective-permute-start(bf16[192,384]{1,0:T(8,128)(2,1)S(1)} %get-tuple-element.298), channel_id=1, source_target_pairs={{0,24},{1,25},{2,26},{3,27},{4,28},{5,29},{6,30},{7,31},{8,16},{9,... | collective-permute-start | bytes 442376 | tf_op jit(solution)/shard_map/ppermute | solution.py:37
  650.4 30.2 %collective-permute-start.45 = (bf16[48,2304]{1,0:T(8,128)(2,1)S(1)}, bf16[48,2304]{1,0:T(8,128)(2,1)S(1)}, u32[]{:S(2)}, u32[]{:S(2)}) collective-permute-start(bf16[48,2304]{1,0:T(8,128)(2,1)S(1)} %get-tuple-element.320), channel_id=1, source_target_pairs={{0,2},{1,3},{2,0},{3,1},{4,6},{5,7},{6,4},{7,5},{8,10},{9,11},{10,... | collective-permute-start | bytes 663560 | tf_op jit(solution)/shard_map/ppermute | solution.py:37
  681.3 19.7 %collective-permute-start.51 = (bf16[48,2304]{1,0:T(8,128)(2,1)}, bf16[48,2304]{1,0:T(8,128)(2,1)}, u32[]{:S(2)}, u32[]{:S(2)}) collective-permute-start(bf16[48,2304]{1,0:T(8,128)(2,1)} %add_convert_fusion.9), channel_id=1, source_target_pairs={{0,2},{1,3},{2,0},{3,1},{4,6},{5,7},{6,4},{7,5},{8,10},{9,11},{10,... | collective-permute-start | bytes 663560 | tf_op jit(solution)/shard_map/ppermute | solution.py:37
  682.1 18.8 %collective-permute-start.50 = (bf16[192,768]{1,0:T(8,128)(2,1)}, bf16[192,768]{1,0:T(8,128)(2,1)}, u32[]{:S(2)}, u32[]{:S(2)}) collective-permute-start(bf16[192,768]{1,0:T(8,128)(2,1)} %pad_maximum_fusion.19), channel_id=1, source_target_pairs={{0,1},{1,0},{2,3},{3,2},{4,5},{5,4},{6,7},{7,6},{8,9},{9,8},{10,11... | collective-permute-start | bytes 884744 | tf_op jit(solution)/shard_map/ppermute | solution.py:37
  686.4 14.5 %collective-permute-start.49 = (bf16[96,1152]{1,0:T(8,128)(2,1)}, bf16[96,1152]{1,0:T(8,128)(2,1)}, u32[]{:S(2)}, u32[]{:S(2)}) collective-permute-start(bf16[96,1152]{1,0:T(8,128)(2,1)} %get-tuple-element.318), channel_id=1, source_target_pairs={{0,1},{1,0},{2,3},{3,2},{4,5},{5,4},{6,7},{7,6},{8,9},{9,8},{10,11... | collective-permute-start | bytes 663560 | tf_op jit(solution)/shard_map/ppermute | solution.py:37
  687.6 10.6 %collective-permute-start.52 = (f32[8,768]{1,0:T(8,128)}, f32[8,768]{1,0:T(8,128)}, u32[]{:S(2)}, u32[]{:S(2)}) collective-permute-start(f32[8,768]{1,0:T(8,128)} %fusion.126), channel_id=1, source_target_pairs={{0,4},{1,5},{2,6},{3,7},{4,0},{5,1},{6,2},{7,3},{8,12},{9,13},{10,... | collective-permute-start | bytes 73736 | tf_op jit(solution)/shard_map/ppermute | solution.py:37
  693.3 57.3 %collective-permute-start.61 = (bf16[384,768]{1,0:T(8,128)(2,1)}, bf16[384,768]{1,0:T(8,128)(2,1)S(1)}, u32[]{:S(2)}, u32[]{:S(2)}) collective-permute-start(bf16[384,768]{1,0:T(8,128)(2,1)} %bitcast.64), channel_id=1, source_target_pairs={{0,0},{1,1},{2,4},{3,5},{4,2},{5,3},{6,6},{7,7},{8,8},{9,9},{10,12... | collective-permute-start | bytes 1769480 | tf_op jit(solution)/shard_map/ppermute | solution.py:37
  698.2 52.4 %collective-permute-start.62 = (bf16[384,768]{1,0:T(8,128)(2,1)}, bf16[384,768]{1,0:T(8,128)(2,1)S(1)}, u32[]{:S(2)}, u32[]{:S(2)}) collective-permute-start(bf16[384,768]{1,0:T(8,128)(2,1)} %bitcast.65), channel_id=1, source_target_pairs={{0,1},{1,0},{2,5},{3,4},{4,3},{5,2},{6,7},{7,6},{8,9},{9,8},{10,13... | collective-permute-start | bytes 1769480 | tf_op jit(solution)/shard_map/ppermute | solution.py:37
  702.7 28.5 %collective-permute-start.54 = (bf16[96,2304]{1,0:T(8,128)(2,1)S(1)}, bf16[96,2304]{1,0:T(8,128)(2,1)S(1)}, u32[]{:S(2)}, u32[]{:S(2)}) collective-permute-start(bf16[96,2304]{1,0:T(8,128)(2,1)S(1)} %pad_maximum_fusion.14), channel_id=1, source_target_pairs={{0,1},{1,0},{2,3},{3,2},{4,5},{5,4},{6,7},{7,6},{8,9},{9,8},{10,11... | collective-permute-start | bytes 1327112 | tf_op jit(solution)/shard_map/ppermute | solution.py:37
  703.8 25.1 %collective-permute-start.53 = (bf16[48,1152]{1,0:T(8,128)(2,1)S(1)}, bf16[48,1152]{1,0:T(8,128)(2,1)S(1)}, u32[]{:S(2)}, u32[]{:S(2)}) collective-permute-start(bf16[48,1152]{1,0:T(8,128)(2,1)S(1)} %get-tuple-element.332), channel_id=1, source_target_pairs={{0,2},{1,3},{2,0},{3,1},{4,6},{5,7},{6,4},{7,5},{8,10},{9,11},{10,... | collective-permute-start | bytes 331784 | tf_op jit(solution)/shard_map/ppermute | solution.py:37
  (95 other events, 947.3 us)

commit v4 on v3

--- a/solution.py
+++ b/solution.py
@@ -5,6 +5,7 @@
 import jax.numpy as jnp
 from jax import lax
 from jax.experimental import pallas as pl
+from jax.experimental.layout import Layout, with_layout_constraint
 from jax.experimental.pallas import tpu as pltpu
 from jax.sharding import Mesh
 from jax.sharding import PartitionSpec as P
@@ -26,6 +27,10 @@
     return lax.dot_general(left, right, form, preferred_element_type=FULL)
 
 
+def row_major(value):
+    return with_layout_constraint(value, Layout(major_to_minor=tuple(range(value.ndim))))
+
+
 def moved(value, target):
     pairs, cores, depth = (lax.axis_size(name) for name in AXES)
     links = []
@@ -83,7 +88,9 @@
 def gathered_over_pairs(value):
     p = lax.axis_index("pair")
     if lax.axis_size("pair") <= 4:
-        return ([value] + [across_pairs(value, k) for k in range(1, lax.axis_size("pair"))], p)
+        count = lax.axis_size("pair")
+        layout = tuple((k, k, 0, 0, value.shape[0]) for k in range(count))
+        return [value] + [across_pairs(value, k) for k in range(1, count)], p, layout
     rows, width = value.shape
     bits = pair_bits()
     count = 1 << len(bits)
@@ -101,32 +108,47 @@
             lead = tuple(range(len(bits)))[::-1]
             current = jnp.transpose(current, lead + (len(bits), len(bits) + 1))
         halves.append(current.reshape(count, rows // 2, width))
-    return ([jnp.concatenate(halves, axis=1).reshape(count * rows, width)], None)
-
-
-def place_kernel(p_ref, *refs, segments, pairs, outs):
-    pieces, results, done = refs[:pairs], refs[pairs : pairs + outs], refs[-1]
-    copies = []
-    for k in range(pairs):
+    return [jnp.concatenate(halves, axis=1).reshape(count * rows, width)], None, ()
+
+
+def halves_first(value):
+    if lax.axis_size("pair") != 4:
+        return value, None
+    rows = value.shape[0] // 2
+    return value, (across_pairs(value[:rows], 1), across_pairs(value[rows:], 2))
+
+
+def halves_second(state):
+    value, near = state
+    if near is None:
+        return gathered_over_pairs(value)
+    rows = value.shape[0] // 2
+    upper = across_pairs(jnp.concatenate([value[:rows], near[0]], axis=0), 2)
+    lower = across_pairs(jnp.concatenate([value[rows:], near[1]], axis=0), 1)
+    layout = (
+        (0, 0, 0, 0, 2 * rows),
+        (1, 1, 0, 0, rows), (1, 4, 0, rows, rows),
+        (2, 3, 0, 0, rows), (2, 2, 0, rows, rows),
+        (3, 3, rows, 0, rows), (3, 4, rows, rows, rows),
+    )
+    return [value, near[0], near[1], upper, lower], lax.axis_index("pair"), layout
+
+
+def place_kernel(p_ref, *refs, segments, layout, count):
+    sources, results = refs[:count], refs[count:]
+    for k, source, origin, first, size in layout:
         spot = jnp.bitwise_xor(p_ref[0], k)
         for index, row, rows, column, width, target in segments:
-            copies.append(
-                pltpu.make_async_copy(
-                    pieces[k].at[pl.ds(row, rows), pl.ds(column, width)],
-                    results[index].at[
-                        pl.ds(pl.multiple_of(spot * rows, 16), rows), pl.ds(target, width)
-                    ],
-                    done.at[len(copies)],
-                )
-            )
-    for copy in copies:
-        copy.start()
-    for copy in copies:
-        copy.wait()
+            low, high = max(row, first), min(row + rows, first + size)
+            if low < high:
+                start = pl.multiple_of(spot * rows + (low - row), 16)
+                results[index][pl.ds(start, high - low), target : target + width] = sources[source][
+                    low - first + origin : high - first + origin, column : column + width
+                ]
 
 
 def placed(gathered, segments):
-    pieces, p = gathered
+    pieces, p, layout = gathered
     pairs = lax.axis_size("pair")
     outs = 1 + max(segment[0] for segment in segments)
     if p is None:
@@ -146,13 +168,12 @@
         shapes.append(
             jax.ShapeDtypeStruct((pairs * mine[0][2], sum(part[4] for part in mine)), LOW)
         )
-    anywhere = pl.BlockSpec(memory_space=pl.ANY)
+    local = pl.BlockSpec(memory_space=pltpu.VMEM)
     return pl.pallas_call(
-        functools.partial(place_kernel, segments=segments, pairs=pairs, outs=outs),
-        in_specs=[pl.BlockSpec(memory_space=pltpu.SMEM)] + [anywhere] * pairs,
-        out_specs=[anywhere] * outs,
+        functools.partial(place_kernel, segments=segments, layout=layout, count=len(pieces)),
+        in_specs=[pl.BlockSpec(memory_space=pltpu.SMEM)] + [local] * len(pieces),
+        out_specs=[local] * outs,
         out_shape=shapes,
-        scratch_shapes=[pltpu.SemaphoreType.DMA((pairs * len(segments),))],
         name="place",
     )(p.astype(jnp.int32).reshape(1), *pieces)
 
@@ -478,12 +499,11 @@
         (1, down_rows + pair_rows, pair_rows, 0, width, width),
         (2, down_rows + 2 * pair_rows, pair_rows, 0, width, 0),
     )
-    deal, tally = tied(deal, tally)
-    x_rows, payload = tied(x_rows, payload)
-    tally_steps = sum_steps()
-    tally = tally + tally_steps[1][1](tally)
-    deal = dealt(settled(*deal), 1)
-    payload_pieces = gathered_over_pairs(payload)
+    depth_steps, plane_steps = sum_steps()
+    for step in plane_steps[1:]:
+        tally = tally + step(tally)
+    x_rows, payload, tally = tied(x_rows, payload, tally)
+    payload_first = halves_first(payload)
 
     x_full = x_rows.astype(FULL)
     unit_one, inverse_one = norm_parts(x_full)
@@ -496,22 +516,23 @@
     gain_one, shift_one, gain_two, shift_two = vectors[0], vectors[1], vectors[2], vectors[3]
     norm_mine = (unit_one * gain_one + shift_one).astype(LOW)
     norm_one = jnp.concatenate([norm_mine, across_cores(norm_mine)], axis=0)
-    norm_one, tally = tied(norm_one, tally)
-    for step in tally_steps[1][2:]:
-        tally = tally + step(tally)
+    norm_one, tally, deal = tied(norm_one, tally, deal)
+    deal = dealt(settled(*deal), 1)
+    tally = tally + depth_steps[0](tally)
     qkv = dot(norm_one, w_qkv, NN).astype(LOW)
-    qkv, deal, tally = tied(qkv, deal, tally)
+    qkv, deal, tally, payload_first = tied(qkv, deal, tally, payload_first)
+    payload_pieces = halves_second(payload_first)
     for level in range(2, levels):
         deal = dealt(settled(*deal), level)
-    tally = tally + tally_steps[0][0](tally)
+    for step in depth_steps[1:]:
+        tally = tally + step(tally)
     mixed, lse = attention_forward(counts, qkv, 512)
 
-    mixed, payload_pieces, deal, tally = tied(mixed, payload_pieces, deal, tally)
+    sources, *place_args = payload_pieces
+    mixed, sources, deal, tally = tied(mixed, sources, deal, tally)
     mixed_got = across_cores(mixed[rows:])
     goal = turned(settled(*deal))
-    for step in tally_steps[0][1:]:
-        tally = tally + step(tally)
-    w_down, w_up, w_out = placed(payload_pieces, payload_plan)
+    w_down, w_up, w_out = placed((sources, *place_args), payload_plan)
 
     attended = in_order(mixed[:rows], mixed_got, 1)
     middle = x_full + dot(attended, w_out, NN)
@@ -525,8 +546,8 @@
 
     active_mine, slope_mine = expanded(norm_two)
     active_other, slope_other = expanded(norm_other)
-    part_other = dot(active_other, w_down, NN).astype(LOW)
-    part_mine = dot(active_mine, w_down, NN)
+    part_other = row_major(dot(active_other, w_down, NN).astype(LOW))
+    part_mine = row_major(dot(active_mine, w_down, NN))
     output = middle + part_mine + across_cores(part_other).astype(FULL)
 
     output, goal, tally = tied(output, goal, tally)
@@ -584,18 +605,19 @@
         third, first, second, down_step, rest_step, early
     )
 
-    partial = dot(jnp.concatenate([first, second, third], axis=1), w_qkv, NT)
+    partial = row_major(dot(jnp.concatenate([first, second, third], axis=1), w_qkv, NT))
     back_got = across_cores(partial[rows:].astype(LOW))
-    late = scattered_over_pairs(weight_part(third))
+    early = depth_halved(added(early), low_bit)
+    rest_step = depth_halved(added(rest_step), high_bit)
     down_own = added(down_step)
     down_got = across_depth(down_own, high_bit)
-    rest_step = depth_halved(added(rest_step), high_bit)
-    early = added(early)
+    late = scattered_over_pairs(weight_part(third))
     grad_norm_one = partial[:rows] + back_got.astype(FULL)
     grad_in, gain_one_grad, shift_one_grad = norm_backward(
         grad_norm_one, unit_one, inverse_one, gain_one
     )
-    grad_rows = (grad_middle + grad_in).astype(LOW)
+    grad_rows = row_major((grad_middle + grad_in).astype(LOW))
+    input_moved = turned_parts(grad_rows.reshape(2, slot_rows, width))
 
     row_index = lax.broadcasted_iota(jnp.int32, (8, width), 0)
     small = jnp.zeros((8, width), FULL)
@@ -603,43 +625,44 @@
         [gain_one_grad, shift_one_grad, gain_two_grad, shift_two_grad, jnp.full((width,), squares)]
     ):
         small = jnp.where(row_index == index, value[None, :], small)
-    depth_steps, plane_steps = sum_steps()
-    for step in depth_steps:
-        small = small + step(small)
-    grad_rows, small, down_got, rest_step, late = tied(grad_rows, small, down_got, rest_step, late)
-    input_moved = turned_parts(grad_rows.reshape(2, slot_rows, width))
-
-    qkv_step = depth_halved(jnp.concatenate([early, added(late)], axis=1), low_bit)
+    small = small + plane_steps[0](small)
+
+    late = depth_halved(added(late), low_bit)
+    rest_own = added(rest_step)
+    rest_got = across_depth(rest_own, high_bit)
+    late, early, rest_got, small, down_got, near = tied(
+        late, early, rest_got, small, down_got, input_moved[0]
+    )
     down_own = depth_doubled(down_own, down_got, high_bit)
     down_got = across_depth(down_own, low_bit)
-    rest_own = added(rest_step)
-    rest_got = across_depth(rest_own, high_bit)
-    small = small + plane_steps[0](small)
-    qkv_step, down_got, rest_got, small = tied(qkv_step, down_got, rest_got, small)
-    qkv_step = depth_halved(added(qkv_step), high_bit)
+    qkv_step = depth_halved(jnp.concatenate([added(early), added(late)], axis=1), high_bit)
     rest_own = depth_doubled(rest_own, rest_got, high_bit)
     rest_got = across_depth(rest_own, low_bit)
     small = small + plane_steps[1](small)
+    qkv_step, small, down_got, far = tied(qkv_step, small, down_got, input_moved[1])
+    input_grad = turned_settled([near, far])
     down_own = depth_doubled(down_own, down_got, low_bit)
-    qkv_step, rest_got, small = tied(qkv_step, rest_got, small)
     qkv_own = added(qkv_step)
     qkv_got = across_depth(qkv_own, high_bit)
+    for step in plane_steps[2:]:
+        small = small + step(small)
+    qkv_got, rest_got, small = tied(qkv_got, rest_got, small)
+    qkv_own = depth_doubled(qkv_own, qkv_got, high_bit)
+    qkv_got = across_depth(qkv_own, low_bit)
     rest_own = depth_doubled(rest_own, rest_got, low_bit)
+    small = small + depth_steps[0](small)
 
     def own_block(stack, index):
         return lax.dynamic_slice_in_dim(stack, index * own_rows, own_rows, 0)
 
     rest_mine = own_block(rest_own, c)
     rest_other = across_cores(own_block(rest_own, 1 - c))
-    for step in plane_steps[2:]:
-        small = small + step(small)
     qkv_got, rest_other, small = tied(qkv_got, rest_other, small)
-    qkv_own = depth_doubled(qkv_own, qkv_got, high_bit)
-    qkv_own = depth_doubled(qkv_own, across_depth(qkv_own, low_bit), low_bit)
+    qkv_own = depth_doubled(qkv_own, qkv_got, low_bit)
     qkv_mine = own_block(qkv_own, c)
     qkv_other = across_cores(own_block(qkv_own, 1 - c))
-    qkv_other, input_moved = tied(qkv_other, input_moved)
-    input_grad = turned_settled(input_moved)
+    for step in depth_steps[1:]:
+        small = small + step(small)
 
     loss = small[4, 0] / (valid_count * width)
     own_small = lax.dynamic_slice_in_dim(small, group * own_rows, own_rows, 1)

time: 762 us -> 441 us (0.58)
  Pallas kernels: 321 us -> 88.4 us
  waiting for transfers between devices: 159 us -> 118 us
  local copies, waits for them, and re-layouts: 52.2 us -> 25.9 us
  other arithmetic: 78.6 us -> 54.3 us
    pallas_call x2, Pallas kernels: 241 us -> 8.58 us  [placed(): pl.pallas_call(functools.partial(place_kernel, segments=segments, layout=...]
    ppermute x63 -> x65, waiting for transfers between devices: 159 us -> 118 us  [moved(): return lax.ppermute(value, AXES, links)]
    dynamic_slice x6 -> x0, local copies, waits for them, and re-layouts: 19.7 us -> none  [turned_parts(): piece = lax.dynamic_index_in_dim(stack, (z + step) % 2, 0, keepdims=False)]
    ppermute x63 -> x65, starting transfers between devices: 72.3 us -> 79 us  [moved(): return lax.ppermute(value, AXES, links)]
  transfers between devices with their start and end apart: 63 -> 65, of which waited for: 16 -> 22; matrix products, arithmetic and copies ran while one was open for 18% -> 19% of each run, Pallas kernels for 42% -> 20%
where the time goes in v4:
time: 441 us; the launch traced here: 434 us
  waiting for transfers between devices  118 us (27%)
  Pallas kernels  88.4 us (20%)
  starting transfers between devices  79 us (18%)
  matrix products  61.2 us (14%)
  other arithmetic  54.3 us (12%)
  local copies, waits for them, and re-layouts  25.9 us (6%)
  between operations  7.42 us (2%)
    ppermute x65, waiting for transfers between devices, moved(): return lax.ppermute(value, AXES, links)  118 us
    ppermute x65, starting transfers between devices, moved(): return lax.ppermute(value, AXES, links)  79 us
    dot_general x20, matrix products, dot(): return lax.dot_general(left, right, form, preferred_element_type=FULL)  61.2 us
    pallas_call x3, Pallas kernels, attention_backward(): pl.pallas_call(functools.partial(backward_kernel, rows=rows, block=block,...  50.2 us
    pallas_call x1, Pallas kernels, attention_forward(): pl.pallas_call(functools.partial(forward_kernel, rows=rows, block=block),...  29.6 us
  transfers between devices with their start and end apart: 65, of which 22 were waited for; matrix products, arithmetic and copies ran while one was open for 19% of the time, Pallas kernels for 20%

profile of v4, /device:TPU:0, one launch (start us, length us, event | category | flops | bytes accessed | tf_op | source)
XLA Modules:
  0.0 434.3 jit_solution(7336063551510565797)
XLA Ops:
  4.6 5.9 %collective-permute-start = (bf16[384,768]{1,0:T(8,128)(2,1)}, bf16[384,768]{1,0:T(8,128)(2,1)}, u32[]{:S(2)}, u32[]{:S(2)}) collective-permute-start(bf16[384,768]{1,0:T(8,128)(2,1)} %get-tuple-element.286), channel_id=1, source_target_pairs={{0,0},{1,1},{2,4},{3,5},{4,2},{5,3},{6,6},{7,7},{8,8},{9,9},{10,12... | collective-permute-start | bytes 1769480 | tf_op jit(solution)/shard_map/ppermute | solution.py:42
  10.5 2.6 collective-permute-start.1
  34.1 4.6 %collective-permute-done.7.refs_1_ = bf16[192,1280]{1,0:T(8,128)(2,1)S(1)} collective-permute-done((bf16[192,1280]{1,0:T(8,128)(2,1)S(1)}, bf16[192,1280]{1,0:T(8,128)(2,1)S(1)}, u32[]{:S(2)}, u32[]{:S(2)}) %collective-permute-start.7) | collective-permute-done | bytes 491552 | tf_op jit(solution)/shard_map/ppermute | solution.py:42
  38.8 9.4 %collective-permute-done.8.refs_2_ = bf16[192,1280]{1,0:T(8,128)(2,1)S(1)} collective-permute-done((bf16[192,1280]{1,0:T(8,128)(2,1)S(1)}, bf16[192,1280]{1,0:T(8,128)(2,1)S(1)}, u32[]{:S(2)}, u32[]{:S(2)}) %collective-permute-start.8) | collective-permute-done | bytes 491552 | tf_op jit(solution)/shard_map/ppermute | solution.py:42
  49.8 2.9 place.2
  60.6 4.8 %convolution_convert_fusion.q_ref.k_ref.v_ref = bf16[1536,1152]{1,0:T(8,128)(2,1)} fusion(bf16[1536,768]{1,0:T(8,128)(2,1)S(1)} %pad_maximum_fusion, bf16[768,1152]{1,0:T(8,128)(2,1)S(1)} %copy-done.64), kind=kOutput, calls=%fused_computation | convolution fusion | flops 2719678464 | bytes 7667712 | tf_op jit(solution)/shard_map/dot_general | solution.py:27
  65.6 9.9 %collective-permute-done.14.refs_1_ = bf16[480,768]{1,0:T(8,128)(2,1)S(1)} collective-permute-done((bf16[480,768]{1,0:T(8,128)(2,1)S(1)}, bf16[480,768]{1,0:T(8,128)(2,1)S(1)}, u32[]{:S(2)}, u32[]{:S(2)}) %collective-permute-start.14) | collective-permute-done | bytes 737312 | tf_op jit(solution)/shard_map/ppermute | solution.py:42
  75.4 12.2 %collective-permute-done.12 = bf16[400,768]{1,0:T(8,128)(2,1)S(1)} collective-permute-done((bf16[400,768]{1,0:T(8,128)(2,1)S(1)}, bf16[400,768]{1,0:T(8,128)(2,1)S(1)}, u32[]{:S(2)}, u32[]{:S(2)}) %collective-permute-start.12) | collective-permute-done | bytes 614432 | tf_op jit(solution)/shard_map/ppermute | solution.py:42
  96.3 2.2 collective-permute-start.19
  99.6 29.6 %attention_forward.1 = (bf16[1536,384]{1,0:T(8,128)(2,1)}, f32[3,2,1536]{2,1,0:T(2,128)}) custom-call(s32[2]{0:T(128)} %add_clamp_fusion.counts_ref, bf16[1536,1152]{1,0:T(8,128)(2,1)} %convolution_convert_fusion.q_ref.k_ref.v_ref, bf16[1536,1152]{1,0:T(8,128)(2,1)} %convolution_convert_fusion.q_ref.k_ref.v_ref, ...), custom_call_target="tpu_custom_call" | custom-call | flops 1 | bytes 1 | tf_op jit(solution)/shard_map/attention_forward/pallas_call | solution.py:277
  129.9 7.2 %collective-permute-done.18 = bf16[400,768]{1,0:T(8,128)(2,1)S(1)} collective-permute-done((bf16[400,768]{1,0:T(8,128)(2,1)}, bf16[400,768]{1,0:T(8,128)(2,1)S(1)}, u32[]{:S(2)}, u32[]{:S(2)}) %collective-permute-start.18) | collective-permute-done | bytes 614432 | tf_op jit(solution)/shard_map/ppermute | solution.py:42
  137.1 2.2 slice.207
  139.3 5.7 %place.3 = (bf16[1536,768]{1,0:T(8,128)(2,1)}, bf16[768,1536]{1,0:T(8,128)(2,1)}, bf16[768,768]{1,0:T(8,128)(2,1)}) custom-call(s32[1]{0:T(128)} %bitcast.7.p_ref, bf16[960,768]{1,0:T(8,128)(2,1)} %copy-done.1, bf16[480,768]{1,0:T(8,128)(2,1)} %copy-done.7, bf16[480,768]{1,0:T(8,128)(2,1)} %copy-done.8, bf16[960,768]{1,0:T(8,128)(2,1)} %collective-permute-done.16.refs_3_, ...), custom_call_target="tpu_custom_call" | custom-call | tf_op jit(solution)/shard_map/place/pallas_call | solution.py:172
  149.8 2.4 collective-permute-done.21
  152.1 3.9 multiply_convert_fusion.2
  156.1 3.0 convolution_convert_fusion.4
  161.0 6.8 %collective-permute-start.23 = (bf16[400,768]{1,0:T(8,128)(2,1)}, bf16[400,768]{1,0:T(8,128)(2,1)}, u32[]{:S(2)}, u32[]{:S(2)}) collective-permute-start(bf16[400,768]{1,0:T(8,128)(2,1)} %get-tuple-element.268), channel_id=1, source_target_pairs={{0,0},{1,1},{2,4},{3,5},{4,2},{5,3},{6,6},{7,7},{8,8},{9,9},{10,12... | collective-permute-start | bytes 1843208 | tf_op jit(solution)/shard_map/ppermute | solution.py:42
  168.3 6.3 %multiply_convert_fusion.3 = (bf16[768,1536]{1,0:T(8,128)(2,1)S(1)}, f32[768,1536]{1,0:T(8,128)}) fusion(bf16[768,768]{1,0:T(8,128)(2,1)} %copy-done.19, bf16[768,1536]{1,0:T(8,128)(2,1)} %get-tuple-element.123), kind=kOutput, calls=%fused_computation.23 | convolution fusion | flops 1817837568 | bytes 10616832 | tf_op jit(solution)/shard_map/dot_general | solution.py:27
  174.7 16.7 %collective-permute-done.24 = bf16[400,768]{1,0:T(8,128)(2,1)} collective-permute-done((bf16[400,768]{1,0:T(8,128)(2,1)}, bf16[400,768]{1,0:T(8,128)(2,1)}, u32[]{:S(2)}, u32[]{:S(2)}) %collective-permute-start.24) | collective-permute-done | bytes 614432 | tf_op jit(solution)/shard_map/ppermute | solution.py:42
  192.9 4.7 %convert_add_fusion.2 = f32[768,768]{1,0:T(8,128)} fusion(bf16[768,768]{1,0:T(8,128)(2,1)} %collective-permute-done.22, f32[768,768]{1,0:T(8,128)S(1)} %get-tuple-element.338, bf16[768,1536]{1,0:T(8,128)(2,1)S(1)} %get-tuple-element.341, bf16[1536,768]{1,0:T(8,128)(2,1)S(1)} %copy-done.62), kind=kOutput, calls=%fused_computation.69 | convolution fusion | flops 1813708800 | bytes 10616832 | tf_op jit(solution)/shard_map/dot_general | solution.py:27
  205.0 2.4 multiply_convert_fusion.4
  207.5 3.9 fusion.94
  211.5 4.0 multiply_convert_fusion.1
  215.5 2.3 add_convert_fusion.1
  217.8 4.0 multiply_convert_fusion
  231.0 2.2 add_convert_fusion
  233.2 3.2 multiply_reduce_fusion
  236.5 3.0 fusion.32
  245.9 2.2 collective-permute-start.32
  249.6 5.1 %collective-permute-done.29 = bf16[384,768]{1,0:T(8,128)(2,1)S(1)} collective-permute-done((bf16[384,768]{1,0:T(8,128)(2,1)S(1)}, bf16[384,768]{1,0:T(8,128)(2,1)S(1)}, u32[]{:S(2)}, u32[]{:S(2)}) %collective-permute-start.29) | collective-permute-done | bytes 589856 | tf_op jit(solution)/shard_map/ppermute | solution.py:42
  259.3 16.6 %attention_backward.3 = bf16[1536,384]{1,0:T(8,128)(2,1)} custom-call(s32[2]{0:T(128)} %add_clamp_fusion.counts_ref, bf16[1536,1152]{1,0:T(8,128)(2,1)} %convolution_convert_fusion.q_ref.k_ref.v_ref, bf16[1536,1152]{1,0:T(8,128)(2,1)} %convolution_convert_fusion.q_ref.k_ref.v_ref, bf16[1536,1152]{1,0:T(8,128)(2,1)} %convolution_convert_fusion.q_ref.k_ref.v_ref, ...), custom_call_target="tpu_custom_call" | custom-call | flops 1 | bytes 1 | tf_op jit(solution)/shard_map/attention_backward/pallas_call | solution.py:356
  278.6 2.6 collective-permute-start.33
  283.4 16.8 %attention_backward.4 = bf16[1536,384]{1,0:T(8,128)(2,1)} custom-call(s32[2]{0:T(128)} %add_clamp_fusion.counts_ref, bf16[1536,1152]{1,0:T(8,128)(2,1)} %convolution_convert_fusion.q_ref.k_ref.v_ref, bf16[1536,1152]{1,0:T(8,128)(2,1)} %convolution_convert_fusion.q_ref.k_ref.v_ref, bf16[1536,1152]{1,0:T(8,128)(2,1)} %convolution_convert_fusion.q_ref.k_ref.v_ref, ...), custom_call_target="tpu_custom_call" | custom-call | flops 1 | bytes 1 | tf_op jit(solution)/shard_map/attention_backward/pallas_call | solution.py:356
  300.3 4.0 fusion.37
  313.8 3.1 collective-permute-start.37
  319.1 16.8 %attention_backward.5 = bf16[1536,384]{1,0:T(8,128)(2,1)} custom-call(s32[2]{0:T(128)} %add_clamp_fusion.counts_ref, bf16[1536,1152]{1,0:T(8,128)(2,1)} %convolution_convert_fusion.q_ref.k_ref.v_ref, bf16[1536,1152]{1,0:T(8,128)(2,1)} %convolution_convert_fusion.q_ref.k_ref.v_ref, bf16[1536,1152]{1,0:T(8,128)(2,1)} %convolution_convert_fusion.q_ref.k_ref.v_ref, ...), custom_call_target="tpu_custom_call" | custom-call | flops 1 | bytes 1 | tf_op jit(solution)/shard_map/attention_backward/pallas_call | solution.py:356
  336.1 2.8 convolution_convert_fusion.5
  338.9 3.3 fusion.10
  351.0 2.9 collective-permute-start.47
  360.3 2.4 collective-permute-done.47
  364.7 2.3 collective-permute-start.56
  367.0 24.6 %collective-permute-done.48 = bf16[48,2304]{1,0:T(8,128)(2,1)S(1)} collective-permute-done((bf16[48,2304]{1,0:T(8,128)(2,1)S(1)}, bf16[48,2304]{1,0:T(8,128)(2,1)S(1)}, u32[]{:S(2)}, u32[]{:S(2)}) %collective-permute-start.48) | collective-permute-done | bytes 221216 | tf_op jit(solution)/shard_map/ppermute | solution.py:42
  391.7 2.6 collective-permute-start.54
  396.6 4.9 %collective-permute-done.53 = bf16[48,1152]{1,0:T(8,128)(2,1)S(1)} collective-permute-done((bf16[48,1152]{1,0:T(8,128)(2,1)S(1)}, bf16[48,1152]{1,0:T(8,128)(2,1)S(1)}, u32[]{:S(2)}, u32[]{:S(2)}) %collective-permute-start.53) | collective-permute-done | bytes 110624 | tf_op jit(solution)/shard_map/ppermute | solution.py:42
  404.2 3.0 collective-permute-start.57
  407.4 5.5 %collective-permute-done.57 = bf16[48,1152]{1,0:T(8,128)(2,1)S(1)} collective-permute-done((bf16[48,1152]{1,0:T(8,128)(2,1)S(1)}, bf16[48,1152]{1,0:T(8,128)(2,1)S(1)}, u32[]{:S(2)}, u32[]{:S(2)}) %collective-permute-start.57) | collective-permute-done | bytes 110624 | tf_op jit(solution)/shard_map/ppermute | solution.py:42
  418.5 4.1 collective-permute-done.62
  423.9 2.8 collective-permute-start.63
  (416 shorter events, 130.3 us)
Async XLA Ops:
  3.0 24.7 %collective-permute-start.2 = (bf16[288,768]{1,0:T(8,128)(2,1)}, bf16[288,768]{1,0:T(8,128)(2,1)}, u32[]{:S(2)}, u32[]{:S(2)}) collective-permute-start(bf16[288,768]{1,0:T(8,128)(2,1)} %pad_maximum_fusion.14), channel_id=1, source_target_pairs={{0,4},{1,5},{2,6},{3,7},{4,0},{5,1},{6,2},{7,3},{8,12},{9,13},{10,... | collective-permute-start | bytes 1327112 | tf_op jit(solution)/shard_map/ppermute | solution.py:42
  4.6 26.8 %collective-permute-start = (bf16[384,768]{1,0:T(8,128)(2,1)}, bf16[384,768]{1,0:T(8,128)(2,1)}, u32[]{:S(2)}, u32[]{:S(2)}) collective-permute-start(bf16[384,768]{1,0:T(8,128)(2,1)} %get-tuple-element.286), channel_id=1, source_target_pairs={{0,0},{1,1},{2,4},{3,5},{4,2},{5,3},{6,6},{7,7},{8,8},{9,9},{10,12... | collective-permute-start | bytes 1769480 | tf_op jit(solution)/shard_map/ppermute | solution.py:42
  10.5 20.9 %collective-permute-start.1 = (bf16[384,768]{1,0:T(8,128)(2,1)}, bf16[384,768]{1,0:T(8,128)(2,1)}, u32[]{:S(2)}, u32[]{:S(2)}) collective-permute-start(bf16[384,768]{1,0:T(8,128)(2,1)} %get-tuple-element.287), channel_id=1, source_target_pairs={{0,1},{1,0},{2,5},{3,4},{4,3},{5,2},{6,7},{7,6},{8,9},{9,8},{10,13... | collective-permute-start | bytes 1769480 | tf_op jit(solution)/shard_map/ppermute | solution.py:42
  24.6 14.2 %collective-permute-start.7 = (bf16[192,1280]{1,0:T(8,128)(2,1)S(1)}, bf16[192,1280]{1,0:T(8,128)(2,1)S(1)}, u32[]{:S(2)}, u32[]{:S(2)}) collective-permute-start(bf16[192,1280]{1,0:T(8,128)(2,1)S(1)} %pad_maximum_fusion.13.refs_0_), channel_id=1, source_target_pairs={{0,8},{1,9},{2,10},{3,11},{4,12},{5,13},{6,14},{7,15},{8,0},{9,1},... | collective-permute-start | bytes 1474568 | tf_op jit(solution)/shard_map/ppermute | solution.py:42
  26.2 22.0 %collective-permute-start.8 = (bf16[192,1280]{1,0:T(8,128)(2,1)S(1)}, bf16[192,1280]{1,0:T(8,128)(2,1)S(1)}, u32[]{:S(2)}, u32[]{:S(2)}) collective-permute-start(bf16[192,1280]{1,0:T(8,128)(2,1)S(1)} %pad_maximum_fusion.13.refs_0_), channel_id=1, source_target_pairs={{0,16},{1,17},{2,18},{3,19},{4,20},{5,21},{6,22},{7,23},{8,24},{9,... | collective-permute-start | bytes 1474568 | tf_op jit(solution)/shard_map/ppermute | solution.py:42
  27.7 20.5 %collective-permute-start.9 = (bf16[192,1280]{1,0:T(8,128)(2,1)S(1)}, bf16[192,1280]{1,0:T(8,128)(2,1)S(1)}, u32[]{:S(2)}, u32[]{:S(2)}) collective-permute-start(bf16[192,1280]{1,0:T(8,128)(2,1)S(1)} %pad_maximum_fusion.13.refs_0_), channel_id=1, source_target_pairs={{0,24},{1,25},{2,26},{3,27},{4,28},{5,29},{6,30},{7,31},{8,16},{9,... | collective-permute-start | bytes 1474568 | tf_op jit(solution)/shard_map/ppermute | solution.py:42
  56.0 19.4 %collective-permute-start.14 = (bf16[480,768]{1,0:T(8,128)(2,1)S(1)}, bf16[480,768]{1,0:T(8,128)(2,1)S(1)}, u32[]{:S(2)}, u32[]{:S(2)}) collective-permute-start(bf16[480,768]{1,0:T(8,128)(2,1)S(1)} %get-tuple-element.265), channel_id=1, source_target_pairs={{0,8},{1,9},{2,10},{3,11},{4,12},{5,13},{6,14},{7,15},{8,0},{9,1},... | collective-permute-start | bytes 2211848 | tf_op jit(solution)/shard_map/ppermute | solution.py:42
  56.5 18.9 %collective-permute-start.15 = (bf16[480,768]{1,0:T(8,128)(2,1)S(1)}, bf16[480,768]{1,0:T(8,128)(2,1)S(1)}, u32[]{:S(2)}, u32[]{:S(2)}) collective-permute-start(bf16[480,768]{1,0:T(8,128)(2,1)S(1)} %get-tuple-element.264), channel_id=1, source_target_pairs={{0,16},{1,17},{2,18},{3,19},{4,20},{5,21},{6,22},{7,23},{8,24},{9,... | collective-permute-start | bytes 2211848 | tf_op jit(solution)/shard_map/ppermute | solution.py:42
  59.3 28.3 %collective-permute-start.12 = (bf16[400,768]{1,0:T(8,128)(2,1)S(1)}, bf16[400,768]{1,0:T(8,128)(2,1)S(1)}, u32[]{:S(2)}, u32[]{:S(2)}) collective-permute-start(bf16[400,768]{1,0:T(8,128)(2,1)S(1)} %get-tuple-element.257), channel_id=1, source_target_pairs={{0,8},{1,9},{2,10},{3,11},{4,12},{5,13},{6,14},{7,15},{8,0},{9,1},... | collective-permute-start | bytes 1843208 | tf_op jit(solution)/shard_map/ppermute | solution.py:42
  88.9 48.2 %collective-permute-start.17 = (bf16[960,768]{1,0:T(8,128)(2,1)}, bf16[960,768]{1,0:T(8,128)(2,1)}, u32[]{:S(2)}, u32[]{:S(2)}) collective-permute-start(bf16[960,768]{1,0:T(8,128)(2,1)} %pad_maximum_fusion.2), channel_id=1, source_target_pairs={{0,8},{1,9},{2,10},{3,11},{4,12},{5,13},{6,14},{7,15},{8,0},{9,1},... | collective-permute-start | bytes 4423688 | tf_op jit(solution)/shard_map/ppermute | solution.py:42
  90.7 46.4 %collective-permute-start.16 = (bf16[960,768]{1,0:T(8,128)(2,1)}, bf16[960,768]{1,0:T(8,128)(2,1)}, u32[]{:S(2)}, u32[]{:S(2)}) collective-permute-start(bf16[960,768]{1,0:T(8,128)(2,1)} %pad_maximum_fusion.1), channel_id=1, source_target_pairs={{0,16},{1,17},{2,18},{3,19},{4,20},{5,21},{6,22},{7,23},{8,24},{9,... | collective-permute-start | bytes 4423688 | tf_op jit(solution)/shard_map/ppermute | solution.py:42
  93.3 43.8 %collective-permute-start.18 = (bf16[400,768]{1,0:T(8,128)(2,1)}, bf16[400,768]{1,0:T(8,128)(2,1)S(1)}, u32[]{:S(2)}, u32[]{:S(2)}) collective-permute-start(bf16[400,768]{1,0:T(8,128)(2,1)} %get-tuple-element.254), channel_id=1, source_target_pairs={{0,16},{1,17},{2,18},{3,19},{4,20},{5,21},{6,22},{7,23},{8,24},{9,... | collective-permute-start | bytes 1843208 | tf_op jit(solution)/shard_map/ppermute | solution.py:42
  96.3 33.0 %collective-permute-start.19 = (f32[8,128]{1,0:T(8,128)S(1)}, f32[8,128]{1,0:T(8,128)S(1)}, u32[]{:S(2)}, u32[]{:S(2)}) collective-permute-start(f32[8,128]{1,0:T(8,128)S(1)} %add.334), channel_id=1, source_target_pairs={{0,2},{1,3},{2,0},{3,1},{4,6},{5,7},{6,4},{7,5},{8,10},{9,11},{10,... | collective-permute-start | bytes 12296 | tf_op jit(solution)/shard_map/ppermute | solution.py:42
  159.1 33.8 %collective-permute-start.22 = (bf16[768,768]{1,0:T(8,128)(2,1)}, bf16[768,768]{1,0:T(8,128)(2,1)}, u32[]{:S(2)}, u32[]{:S(2)}) collective-permute-start(bf16[768,768]{1,0:T(8,128)(2,1)} %convolution_convert_fusion.4), channel_id=1, source_target_pairs={{0,4},{1,5},{2,6},{3,7},{4,0},{5,1},{6,2},{7,3},{8,12},{9,13},{10,... | collective-permute-start | bytes 3538952 | tf_op jit(solution)/shard_map/ppermute | solution.py:42
  161.0 13.7 %collective-permute-start.23 = (bf16[400,768]{1,0:T(8,128)(2,1)}, bf16[400,768]{1,0:T(8,128)(2,1)}, u32[]{:S(2)}, u32[]{:S(2)}) collective-permute-start(bf16[400,768]{1,0:T(8,128)(2,1)} %get-tuple-element.268), channel_id=1, source_target_pairs={{0,0},{1,1},{2,4},{3,5},{4,2},{5,3},{6,6},{7,7},{8,8},{9,9},{10,12... | collective-permute-start | bytes 1843208 | tf_op jit(solution)/shard_map/ppermute | solution.py:42
  167.8 23.6 %collective-permute-start.24 = (bf16[400,768]{1,0:T(8,128)(2,1)}, bf16[400,768]{1,0:T(8,128)(2,1)}, u32[]{:S(2)}, u32[]{:S(2)}) collective-permute-start(bf16[400,768]{1,0:T(8,128)(2,1)} %get-tuple-element.269), channel_id=1, source_target_pairs={{0,1},{1,0},{2,5},{3,4},{4,3},{5,2},{6,7},{7,6},{8,9},{9,8},{10,13... | collective-permute-start | bytes 1843208 | tf_op jit(solution)/shard_map/ppermute | solution.py:42
  207.4 8.1 %collective-permute-start.25 = (bf16[768,768]{1,0:T(8,128)(2,1)S(1)}, bf16[768,768]{1,0:T(8,128)(2,1)S(1)}, u32[]{:S(2)}, u32[]{:S(2)}) collective-permute-start(bf16[768,768]{1,0:T(8,128)(2,1)S(1)} %multiply_convert_fusion.4), channel_id=1, source_target_pairs={{0,4},{1,5},{2,6},{3,7},{4,0},{5,1},{6,2},{7,3},{8,12},{9,13},{10,... | collective-permute-start | bytes 3538952 | tf_op jit(solution)/shard_map/ppermute | solution.py:42
  223.9 9.3 %collective-permute-start.26 = (bf16[768,768]{1,0:T(8,128)(2,1)S(1)}, bf16[768,768]{1,0:T(8,128)(2,1)S(1)}, u32[]{:S(2)}, u32[]{:S(2)}) collective-permute-start(bf16[768,768]{1,0:T(8,128)(2,1)S(1)} %convolution_convert_fusion.3), channel_id=1, source_target_pairs={{0,4},{1,5},{2,6},{3,7},{4,0},{5,1},{6,2},{7,3},{8,12},{9,13},{10,... | collective-permute-start | bytes 3538952 | tf_op jit(solution)/shard_map/ppermute | solution.py:42
  225.4 20.4 %collective-permute-start.28 = (bf16[384,768]{1,0:T(8,128)(2,1)S(1)}, bf16[384,768]{1,0:T(8,128)(2,1)S(1)}, u32[]{:S(2)}, u32[]{:S(2)}) collective-permute-start(bf16[384,768]{1,0:T(8,128)(2,1)S(1)} %get-tuple-element.250), channel_id=1, source_target_pairs={{0,8},{1,9},{2,10},{3,11},{4,12},{5,13},{6,14},{7,15},{8,0},{9,1},... | collective-permute-start | bytes 1769480 | tf_op jit(solution)/shard_map/ppermute | solution.py:42
  227.0 27.6 %collective-permute-start.29 = (bf16[384,768]{1,0:T(8,128)(2,1)S(1)}, bf16[384,768]{1,0:T(8,128)(2,1)S(1)}, u32[]{:S(2)}, u32[]{:S(2)}) collective-permute-start(bf16[384,768]{1,0:T(8,128)(2,1)S(1)} %get-tuple-element.249), channel_id=1, source_target_pairs={{0,16},{1,17},{2,18},{3,19},{4,20},{5,21},{6,22},{7,23},{8,24},{9,... | collective-permute-start | bytes 1769480 | tf_op jit(solution)/shard_map/ppermute | solution.py:42
  228.5 26.1 %collective-permute-start.30 = (bf16[384,768]{1,0:T(8,128)(2,1)S(1)}, bf16[384,768]{1,0:T(8,128)(2,1)S(1)}, u32[]{:S(2)}, u32[]{:S(2)}) collective-permute-start(bf16[384,768]{1,0:T(8,128)(2,1)S(1)} %get-tuple-element.248), channel_id=1, source_target_pairs={{0,24},{1,25},{2,26},{3,27},{4,28},{5,29},{6,30},{7,31},{8,16},{9,... | collective-permute-start | bytes 1769480 | tf_op jit(solution)/shard_map/ppermute | solution.py:42
  240.7 15.9 %collective-permute-start.27 = (bf16[768,384]{1,0:T(8,128)(2,1)S(1)}, bf16[768,384]{1,0:T(8,128)(2,1)S(1)}, u32[]{:S(2)}, u32[]{:S(2)}) collective-permute-start(bf16[768,384]{1,0:T(8,128)(2,1)S(1)} %get-tuple-element.283), channel_id=1, source_target_pairs={{0,4},{1,5},{2,6},{3,7},{4,0},{5,1},{6,2},{7,3},{8,12},{9,13},{10,... | collective-permute-start | bytes 1769480 | tf_op jit(solution)/shard_map/ppermute | solution.py:42
  244.1 31.7 %collective-permute-start.31 = (bf16[384,768]{1,0:T(8,128)(2,1)}, bf16[384,768]{1,0:T(8,128)(2,1)S(1)}, u32[]{:S(2)}, u32[]{:S(2)}) collective-permute-start(bf16[384,768]{1,0:T(8,128)(2,1)} %get-tuple-element.281), channel_id=1, source_target_pairs={{0,0},{1,1},{2,4},{3,5},{4,2},{5,3},{6,6},{7,7},{8,8},{9,9},{10,12... | collective-permute-start | bytes 1769480 | tf_op jit(solution)/shard_map/ppermute | solution.py:42
  245.9 30.0 %collective-permute-start.32 = (bf16[384,768]{1,0:T(8,128)(2,1)}, bf16[384,768]{1,0:T(8,128)(2,1)}, u32[]{:S(2)}, u32[]{:S(2)}) collective-permute-start(bf16[384,768]{1,0:T(8,128)(2,1)} %get-tuple-element.280), channel_id=1, source_target_pairs={{0,1},{1,0},{2,5},{3,4},{4,3},{5,2},{6,7},{7,6},{8,9},{9,8},{10,13... | collective-permute-start | bytes 1769480 | tf_op jit(solution)/shard_map/ppermute | solution.py:42
  254.6 45.6 %collective-permute-start.34 = (bf16[192,2304]{1,0:T(8,128)(2,1)}, bf16[192,2304]{1,0:T(8,128)(2,1)}, u32[]{:S(2)}, u32[]{:S(2)}) collective-permute-start(bf16[192,2304]{1,0:T(8,128)(2,1)} %get-tuple-element.245), channel_id=1, source_target_pairs={{0,8},{1,9},{2,10},{3,11},{4,12},{5,13},{6,14},{7,15},{8,0},{9,1},... | collective-permute-start | bytes 2654216 | tf_op jit(solution)/shard_map/ppermute | solution.py:42
  254.6 45.6 %collective-permute-start.35 = (bf16[192,2304]{1,0:T(8,128)(2,1)}, bf16[192,2304]{1,0:T(8,128)(2,1)}, u32[]{:S(2)}, u32[]{:S(2)}) collective-permute-start(bf16[192,2304]{1,0:T(8,128)(2,1)} %get-tuple-element.246), channel_id=1, source_target_pairs={{0,16},{1,17},{2,18},{3,19},{4,20},{5,21},{6,22},{7,23},{8,24},{9,... | collective-permute-start | bytes 2654216 | tf_op jit(solution)/shard_map/ppermute | solution.py:42
  256.7 43.6 %collective-permute-start.36 = (bf16[192,2304]{1,0:T(8,128)(2,1)}, bf16[192,2304]{1,0:T(8,128)(2,1)}, u32[]{:S(2)}, u32[]{:S(2)}) collective-permute-start(bf16[192,2304]{1,0:T(8,128)(2,1)} %get-tuple-element.243), channel_id=1, source_target_pairs={{0,24},{1,25},{2,26},{3,27},{4,28},{5,29},{6,30},{7,31},{8,16},{9,... | collective-permute-start | bytes 2654216 | tf_op jit(solution)/shard_map/ppermute | solution.py:42
  278.6 21.7 %collective-permute-start.33 = (bf16[192,768]{1,0:T(8,128)(2,1)}, bf16[192,768]{1,0:T(8,128)(2,1)}, u32[]{:S(2)}, u32[]{:S(2)}) collective-permute-start(bf16[192,768]{1,0:T(8,128)(2,1)} %get-tuple-element.301), channel_id=1, source_target_pairs={{0,1},{1,0},{2,3},{3,2},{4,5},{5,4},{6,7},{7,6},{8,9},{9,8},{10,11... | collective-permute-start | bytes 884744 | tf_op jit(solution)/shard_map/ppermute | solution.py:42
  305.3 30.6 %collective-permute-start.39 = (bf16[192,768]{1,0:T(8,128)(2,1)}, bf16[192,768]{1,0:T(8,128)(2,1)}, u32[]{:S(2)}, u32[]{:S(2)}) collective-permute-start(bf16[192,768]{1,0:T(8,128)(2,1)} %get-tuple-element.276), channel_id=1, source_target_pairs={{0,8},{1,9},{2,10},{3,11},{4,12},{5,13},{6,14},{7,15},{8,0},{9,1},... | collective-permute-start | bytes 884744 | tf_op jit(solution)/shard_map/ppermute | solution.py:42
  305.5 30.5 %collective-permute-start.40 = (bf16[192,768]{1,0:T(8,128)(2,1)}, bf16[192,768]{1,0:T(8,128)(2,1)}, u32[]{:S(2)}, u32[]{:S(2)}) collective-permute-start(bf16[192,768]{1,0:T(8,128)(2,1)} %get-tuple-element.275), channel_id=1, source_target_pairs={{0,16},{1,17},{2,18},{3,19},{4,20},{5,21},{6,22},{7,23},{8,24},{9,... | collective-permute-start | bytes 884744 | tf_op jit(solution)/shard_map/ppermute | solution.py:42
  307.4 28.6 %collective-permute-start.41 = (bf16[192,768]{1,0:T(8,128)(2,1)}, bf16[192,768]{1,0:T(8,128)(2,1)}, u32[]{:S(2)}, u32[]{:S(2)}) collective-permute-start(bf16[192,768]{1,0:T(8,128)(2,1)} %get-tuple-element.274), channel_id=1, source_target_pairs={{0,24},{1,25},{2,26},{3,27},{4,28},{5,29},{6,30},{7,31},{8,16},{9,... | collective-permute-start | bytes 884744 | tf_op jit(solution)/shard_map/ppermute | solution.py:42
  312.0 24.0 %collective-permute-start.38 = (bf16[96,2304]{1,0:T(8,128)(2,1)}, bf16[96,2304]{1,0:T(8,128)(2,1)}, u32[]{:S(2)}, u32[]{:S(2)}) collective-permute-start(bf16[96,2304]{1,0:T(8,128)(2,1)} %get-tuple-element.290), channel_id=1, source_target_pairs={{0,1},{1,0},{2,3},{3,2},{4,5},{5,4},{6,7},{7,6},{8,9},{9,8},{10,11... | collective-permute-start | bytes 1327112 | tf_op jit(solution)/shard_map/ppermute | solution.py:42
  313.8 22.2 %collective-permute-start.37 = (bf16[96,768]{1,0:T(8,128)(2,1)}, bf16[96,768]{1,0:T(8,128)(2,1)}, u32[]{:S(2)}, u32[]{:S(2)}) collective-permute-start(bf16[96,768]{1,0:T(8,128)(2,1)} %get-tuple-element.323), channel_id=1, source_target_pairs={{0,2},{1,3},{2,0},{3,1},{4,6},{5,7},{6,4},{7,5},{8,10},{9,11},{10,... | collective-permute-start | bytes 442376 | tf_op jit(solution)/shard_map/ppermute | solution.py:42
  342.4 13.8 %collective-permute-start.49 = (bf16[768,768]{1,0:T(8,128)(2,1)S(1)}, bf16[768,768]{1,0:T(8,128)(2,1)S(1)}, u32[]{:S(2)}, u32[]{:S(2)}) collective-permute-start(bf16[768,768]{1,0:T(8,128)(2,1)S(1)} %slice.335), channel_id=1, source_target_pairs={{0,4},{1,5},{2,6},{3,7},{4,0},{5,1},{6,2},{7,3},{8,12},{9,13},{10,... | collective-permute-start | bytes 3538952 | tf_op jit(solution)/shard_map/ppermute | solution.py:42
  344.1 20.7 %collective-permute-start.51 = (bf16[96,768]{1,0:T(8,128)(2,1)S(1)}, bf16[96,768]{1,0:T(8,128)(2,1)S(1)}, u32[]{:S(2)}, u32[]{:S(2)}) collective-permute-start(bf16[96,768]{1,0:T(8,128)(2,1)S(1)} %add_convert_fusion.9), channel_id=1, source_target_pairs={{0,2},{1,3},{2,0},{3,1},{4,6},{5,7},{6,4},{7,5},{8,10},{9,11},{10,... | collective-permute-start | bytes 442376 | tf_op jit(solution)/shard_map/ppermute | solution.py:42
  344.4 9.5 %collective-permute-start.43 = (bf16[192,384]{1,0:T(8,128)(2,1)S(1)}, bf16[192,384]{1,0:T(8,128)(2,1)S(1)}, u32[]{:S(2)}, u32[]{:S(2)}) collective-permute-start(bf16[192,384]{1,0:T(8,128)(2,1)S(1)} %get-tuple-element.300), channel_id=1, source_target_pairs={{0,16},{1,17},{2,18},{3,19},{4,20},{5,21},{6,22},{7,23},{8,24},{9,... | collective-permute-start | bytes 442376 | tf_op jit(solution)/shard_map/ppermute | solution.py:42
  346.1 7.8 %collective-permute-start.44 = (bf16[192,384]{1,0:T(8,128)(2,1)S(1)}, bf16[192,384]{1,0:T(8,128)(2,1)S(1)}, u32[]{:S(2)}, u32[]{:S(2)}) collective-permute-start(bf16[192,384]{1,0:T(8,128)(2,1)S(1)} %get-tuple-element.299), channel_id=1, source_target_pairs={{0,24},{1,25},{2,26},{3,27},{4,28},{5,29},{6,30},{7,31},{8,16},{9,... | collective-permute-start | bytes 442376 | tf_op jit(solution)/shard_map/ppermute | solution.py:42
  351.0 11.8 %collective-permute-start.47 = (bf16[48,2304]{1,0:T(8,128)(2,1)S(1)}, bf16[48,2304]{1,0:T(8,128)(2,1)S(1)}, u32[]{:S(2)}, u32[]{:S(2)}) collective-permute-start(bf16[48,2304]{1,0:T(8,128)(2,1)S(1)} %dynamic-slice_bitcast_fusion.10), channel_id=1, source_target_pairs={{0,2},{1,3},{2,0},{3,1},{4,6},{5,7},{6,4},{7,5},{8,10},{9,11},{10,... | collective-permute-start | bytes 663560 | tf_op jit(solution)/shard_map/ppermute | solution.py:42
  353.9 13.1 %collective-permute-start.46 = (bf16[96,768]{1,0:T(8,128)(2,1)S(1)}, bf16[96,768]{1,0:T(8,128)(2,1)S(1)}, u32[]{:S(2)}, u32[]{:S(2)}) collective-permute-start(bf16[96,768]{1,0:T(8,128)(2,1)S(1)} %get-tuple-element.321), channel_id=1, source_target_pairs={{0,1},{1,0},{2,3},{3,2},{4,5},{5,4},{6,7},{7,6},{8,9},{9,8},{10,11... | collective-permute-start | bytes 442376 | tf_op jit(solution)/shard_map/ppermute | solution.py:42
  354.1 12.9 %collective-permute-start.45 = (bf16[96,384]{1,0:T(8,128)(2,1)S(1)}, bf16[96,384]{1,0:T(8,128)(2,1)S(1)}, u32[]{:S(2)}, u32[]{:S(2)}) collective-permute-start(bf16[96,384]{1,0:T(8,128)(2,1)S(1)} %get-tuple-element.331), channel_id=1, source_target_pairs={{0,1},{1,0},{2,3},{3,2},{4,5},{5,4},{6,7},{7,6},{8,9},{9,8},{10,11... | collective-permute-start | bytes 221192 | tf_op jit(solution)/shard_map/ppermute | solution.py:42
  358.8 32.7 %collective-permute-start.52 = (bf16[384,768]{1,0:T(8,128)(2,1)S(1)}, bf16[384,768]{1,0:T(8,128)(2,1)S(1)}, u32[]{:S(2)}, u32[]{:S(2)}) collective-permute-start(bf16[384,768]{1,0:T(8,128)(2,1)S(1)} %get-tuple-element.273), channel_id=1, source_target_pairs={{0,0},{1,1},{2,4},{3,5},{4,2},{5,3},{6,6},{7,7},{8,8},{9,9},{10,12... | collective-permute-start | bytes 1769480 | tf_op jit(solution)/shard_map/ppermute | solution.py:42
  364.0 27.6 %collective-permute-start.48 = (bf16[48,2304]{1,0:T(8,128)(2,1)S(1)}, bf16[48,2304]{1,0:T(8,128)(2,1)S(1)}, u32[]{:S(2)}, u32[]{:S(2)}) collective-permute-start(bf16[48,2304]{1,0:T(8,128)(2,1)S(1)} %fusion.56), channel_id=1, source_target_pairs={{0,2},{1,3},{2,0},{3,1},{4,6},{5,7},{6,4},{7,5},{8,10},{9,11},{10,... | collective-permute-start | bytes 663560 | tf_op jit(solution)/shard_map/ppermute | solution.py:42
  364.7 31.9 %collective-permute-start.56 = (bf16[384,768]{1,0:T(8,128)(2,1)S(1)}, bf16[384,768]{1,0:T(8,128)(2,1)S(1)}, u32[]{:S(2)}, u32[]{:S(2)}) collective-permute-start(bf16[384,768]{1,0:T(8,128)(2,1)S(1)} %get-tuple-element.272), channel_id=1, source_target_pairs={{0,1},{1,0},{2,5},{3,4},{4,3},{5,2},{6,7},{7,6},{8,9},{9,8},{10,13... | collective-permute-start | bytes 1769480 | tf_op jit(solution)/shard_map/ppermute | solution.py:42
  391.6 11.6 %collective-permute-start.55 = (bf16[192,768]{1,0:T(8,128)(2,1)S(1)}, bf16[192,768]{1,0:T(8,128)(2,1)S(1)}, u32[]{:S(2)}, u32[]{:S(2)}) collective-permute-start(bf16[192,768]{1,0:T(8,128)(2,1)S(1)} %pad_maximum_fusion.20), channel_id=1, source_target_pairs={{0,1},{1,0},{2,3},{3,2},{4,5},{5,4},{6,7},{7,6},{8,9},{9,8},{10,11... | collective-permute-start | bytes 884744 | tf_op jit(solution)/shard_map/ppermute | solution.py:42
  394.9 18.7 %collective-permute-start.58 = (bf16[96,2304]{1,0:T(8,128)(2,1)S(1)}, bf16[96,2304]{1,0:T(8,128)(2,1)S(1)}, u32[]{:S(2)}, u32[]{:S(2)}) collective-permute-start(bf16[96,2304]{1,0:T(8,128)(2,1)S(1)} %pad_maximum_fusion.15), channel_id=1, source_target_pairs={{0,1},{1,0},{2,3},{3,2},{4,5},{5,4},{6,7},{7,6},{8,9},{9,8},{10,11... | collective-permute-start | bytes 1327112 | tf_op jit(solution)/shard_map/ppermute | solution.py:42
  404.2 8.8 %collective-permute-start.57 = (bf16[48,1152]{1,0:T(8,128)(2,1)S(1)}, bf16[48,1152]{1,0:T(8,128)(2,1)S(1)}, u32[]{:S(2)}, u32[]{:S(2)}) collective-permute-start(bf16[48,1152]{1,0:T(8,128)(2,1)S(1)} %add_convert_fusion.11), channel_id=1, source_target_pairs={{0,2},{1,3},{2,0},{3,1},{4,6},{5,7},{6,4},{7,5},{8,10},{9,11},{10,... | collective-permute-start | bytes 331784 | tf_op jit(solution)/shard_map/ppermute | solution.py:42
  414.0 8.6 %collective-permute-start.61 = (bf16[96,2304]{1,0:T(8,128)(2,1)S(1)}, bf16[96,2304]{1,0:T(8,128)(2,1)S(1)}, u32[]{:S(2)}, u32[]{:S(2)}) collective-permute-start(bf16[96,2304]{1,0:T(8,128)(2,1)S(1)} %fusion.55), channel_id=1, source_target_pairs={{0,4},{1,5},{2,6},{3,7},{4,0},{5,1},{6,2},{7,3},{8,12},{9,13},{10,... | collective-permute-start | bytes 1327112 | tf_op jit(solution)/shard_map/ppermute | solution.py:42
  414.2 8.4 %collective-permute-start.60 = (bf16[96,1152]{1,0:T(8,128)(2,1)S(1)}, bf16[96,1152]{1,0:T(8,128)(2,1)S(1)}, u32[]{:S(2)}, u32[]{:S(2)}) collective-permute-start(bf16[96,1152]{1,0:T(8,128)(2,1)S(1)} %pad_maximum_fusion.22), channel_id=1, source_target_pairs={{0,1},{1,0},{2,3},{3,2},{4,5},{5,4},{6,7},{7,6},{8,9},{9,8},{10,11... | collective-permute-start | bytes 663560 | tf_op jit(solution)/shard_map/ppermute | solution.py:42
  (94 other events, 542.4 us)

commit v5 on v4

--- a/solution.py
+++ b/solution.py
@@ -65,6 +65,15 @@
         piece = lax.dynamic_index_in_dim(stack, (z + step) % 2, 0, keepdims=False)
         got.append(moved(piece, lambda p, c, w: (p, w // 2, 2 * c + (w + step) % 2)))
     return got
+
+
+def turned_piece(stack, step):
+    piece = lax.dynamic_index_in_dim(stack, (lax.axis_index("seq") + step) % 2, 0, keepdims=False)
+    return [piece[: piece.shape[0] // 2], piece[piece.shape[0] // 2 :]]
+
+
+def turned_send(piece, step):
+    return moved(piece, lambda p, c, w: (p, w // 2, 2 * c + (w + step) % 2))
 
 
 def turned_settled(got):
@@ -442,7 +451,6 @@
     keep = lax.dynamic_index_in_dim(shard, c, 0, keepdims=False)
     send = lax.dynamic_index_in_dim(shard, 1 - c, 0, keepdims=False)
     qkv_shard = in_order(keep, across_cores(send), 0)
-    qkv_pieces = gathered_over_pairs(qkv_shard)
 
     x_rows = turned(tokens).reshape(rows, width)
 
@@ -502,8 +510,10 @@
     depth_steps, plane_steps = sum_steps()
     for step in plane_steps[1:]:
         tally = tally + step(tally)
-    x_rows, payload, tally = tied(x_rows, payload, tally)
     payload_first = halves_first(payload)
+    qkv_shard, payload_first = tied(qkv_shard, payload_first)
+    qkv_pieces = gathered_over_pairs(qkv_shard)
+    x_rows, tally = tied(x_rows, tally)
 
     x_full = x_rows.astype(FULL)
     unit_one, inverse_one = norm_parts(x_full)
@@ -516,14 +526,12 @@
     gain_one, shift_one, gain_two, shift_two = vectors[0], vectors[1], vectors[2], vectors[3]
     norm_mine = (unit_one * gain_one + shift_one).astype(LOW)
     norm_one = jnp.concatenate([norm_mine, across_cores(norm_mine)], axis=0)
-    norm_one, tally, deal = tied(norm_one, tally, deal)
-    deal = dealt(settled(*deal), 1)
+    norm_one, tally, payload_first = tied(norm_one, tally, payload_first)
+    payload_pieces = halves_second(payload_first)
     tally = tally + depth_steps[0](tally)
     qkv = dot(norm_one, w_qkv, NN).astype(LOW)
-    qkv, deal, tally, payload_first = tied(qkv, deal, tally, payload_first)
-    payload_pieces = halves_second(payload_first)
-    for level in range(2, levels):
-        deal = dealt(settled(*deal), level)
+    qkv, deal, tally = tied(qkv, deal, tally)
+    deal = dealt(settled(*deal), 1)
     for step in depth_steps[1:]:
         tally = tally + step(tally)
     mixed, lse = attention_forward(counts, qkv, 512)
@@ -531,7 +539,8 @@
     sources, *place_args = payload_pieces
     mixed, sources, deal, tally = tied(mixed, sources, deal, tally)
     mixed_got = across_cores(mixed[rows:])
-    goal = turned(settled(*deal))
+    for level in range(2, levels):
+        deal = dealt(settled(*deal), level)
     w_down, w_up, w_out = placed((sources, *place_args), payload_plan)
 
     attended = in_order(mixed[:rows], mixed_got, 1)
@@ -545,6 +554,8 @@
         return value.astype(LOW), slope.astype(LOW)
 
     active_mine, slope_mine = expanded(norm_two)
+    active_mine, slope_mine, deal = tied(active_mine, slope_mine, deal)
+    goal = turned(settled(*deal))
     active_other, slope_other = expanded(norm_other)
     part_other = row_major(dot(active_other, w_down, NN).astype(LOW))
     part_mine = row_major(dot(active_mine, w_down, NN))
@@ -617,7 +628,9 @@
         grad_norm_one, unit_one, inverse_one, gain_one
     )
     grad_rows = row_major((grad_middle + grad_in).astype(LOW))
-    input_moved = turned_parts(grad_rows.reshape(2, slot_rows, width))
+    grad_rows = grad_rows.reshape(2, slot_rows, width)
+    parts = turned_piece(grad_rows, 0) + turned_piece(grad_rows, 1)
+    sent = [turned_send(parts[0], 0)]
 
     row_index = lax.broadcasted_iota(jnp.int32, (8, width), 0)
     small = jnp.zeros((8, width), FULL)
@@ -630,39 +643,44 @@
     late = depth_halved(added(late), low_bit)
     rest_own = added(rest_step)
     rest_got = across_depth(rest_own, high_bit)
-    late, early, rest_got, small, down_got, near = tied(
-        late, early, rest_got, small, down_got, input_moved[0]
-    )
+    late, early, small, parts[1] = tied(late, early, small, parts[1])
+    qkv_step = depth_halved(jnp.concatenate([added(early), added(late)], axis=1), high_bit)
+    sent.append(turned_send(parts[1], 0))
+    small = small + plane_steps[1](small)
+    qkv_step, small, rest_got, down_got, sent[0], parts[2] = tied(
+        qkv_step, small, rest_got, down_got, sent[0], parts[2]
+    )
+    qkv_own = added(qkv_step)
+    qkv_got = across_depth(qkv_own, high_bit)
+    sent.append(turned_send(parts[2], 1))
+    rest_own = depth_doubled(rest_own, rest_got, high_bit)
+    rest_got = across_depth(rest_own, low_bit)
     down_own = depth_doubled(down_own, down_got, high_bit)
     down_got = across_depth(down_own, low_bit)
-    qkv_step = depth_halved(jnp.concatenate([added(early), added(late)], axis=1), high_bit)
-    rest_own = depth_doubled(rest_own, rest_got, high_bit)
-    rest_got = across_depth(rest_own, low_bit)
-    small = small + plane_steps[1](small)
-    qkv_step, small, down_got, far = tied(qkv_step, small, down_got, input_moved[1])
-    input_grad = turned_settled([near, far])
-    down_own = depth_doubled(down_own, down_got, low_bit)
-    qkv_own = added(qkv_step)
-    qkv_got = across_depth(qkv_own, high_bit)
     for step in plane_steps[2:]:
         small = small + step(small)
-    qkv_got, rest_got, small = tied(qkv_got, rest_got, small)
+    qkv_got, small, sent[1], parts[3] = tied(qkv_got, small, sent[1], parts[3])
     qkv_own = depth_doubled(qkv_own, qkv_got, high_bit)
     qkv_got = across_depth(qkv_own, low_bit)
+    sent.append(turned_send(parts[3], 1))
+    small = small + depth_steps[0](small)
+    qkv_got, rest_got, down_got, small, sent[2] = tied(qkv_got, rest_got, down_got, small, sent[2])
     rest_own = depth_doubled(rest_own, rest_got, low_bit)
-    small = small + depth_steps[0](small)
+    down_own = depth_doubled(down_own, down_got, low_bit)
 
     def own_block(stack, index):
         return lax.dynamic_slice_in_dim(stack, index * own_rows, own_rows, 0)
 
     rest_mine = own_block(rest_own, c)
     rest_other = across_cores(own_block(rest_own, 1 - c))
-    qkv_got, rest_other, small = tied(qkv_got, rest_other, small)
     qkv_own = depth_doubled(qkv_own, qkv_got, low_bit)
     qkv_mine = own_block(qkv_own, c)
     qkv_other = across_cores(own_block(qkv_own, 1 - c))
     for step in depth_steps[1:]:
         small = small + step(small)
+    input_grad = turned_settled(
+        [jnp.concatenate(sent[0:2], axis=0), jnp.concatenate(sent[2:4], axis=0)]
+    )
 
     loss = small[4, 0] / (valid_count * width)
     own_small = lax.dynamic_slice_in_dim(small, group * own_rows, own_rows, 1)

time: 441 us -> 455 us (1.032)
  waiting for transfers between devices: 118 us -> 127 us
  starting transfers between devices: 79 us -> 86 us
  matrix products: 61.2 us -> 54.5 us
    ppermute x65 -> x67, waiting for transfers between devices: 118 us -> 127 us  [moved(): return lax.ppermute(value, AXES, links)]
    ppermute x65 -> x67, starting transfers between devices: 79 us -> 86 us  [moved(): return lax.ppermute(value, AXES, links)]
    dot_general x20, matrix products: 61.2 us -> 54.5 us  [dot(): return lax.dot_general(left, right, form, preferred_element_type=FULL)]
  transfers between devices with their start and end apart: 65 -> 67, of which waited for: 22 -> 18; matrix products, arithmetic and copies ran while one was open for 19% -> 18% of each run, Pallas kernels for 20% -> 19%
where the time goes in v5:
time: 455 us; the launch traced here: 449 us
  waiting for transfers between devices  127 us (28%)
  Pallas kernels  88.4 us (19%)
  starting transfers between devices  86 us (19%)
  other arithmetic  57.9 us (13%)
  matrix products  54.5 us (12%)
  local copies, waits for them, and re-layouts  27.1 us (6%)
  between operations  7.34 us (2%)
    ppermute x67, waiting for transfers between devices, moved(): return lax.ppermute(value, AXES, links)  127 us
    ppermute x67, starting transfers between devices, moved(): return lax.ppermute(value, AXES, links)  86 us
    dot_general x20, matrix products, dot(): return lax.dot_general(left, right, form, preferred_element_type=FULL)  54.5 us
    pallas_call x3, Pallas kernels, attention_backward(): pl.pallas_call(functools.partial(backward_kernel, rows=rows, block=block,...  50.2 us
    pallas_call x1, Pallas kernels, attention_forward(): pl.pallas_call(functools.partial(forward_kernel, rows=rows, block=block),...  29.6 us
  transfers between devices with their start and end apart: 67, of which 18 were waited for; matrix products, arithmetic and copies ran while one was open for 18% of the time, Pallas kernels for 19%

profile of v5, /device:TPU:0, one launch (start us, length us, event | category | flops | bytes accessed | tf_op | source)
XLA Modules:
  0.0 448.5 jit_solution(13329363003310122355)
XLA Ops:
  0.8 2.4 dynamic-slice_bitcast_fusion.3
  3.1 6.1 %collective-permute-start = (bf16[384,768]{1,0:T(8,128)(2,1)}, bf16[384,768]{1,0:T(8,128)(2,1)}, u32[]{:S(2)}, u32[]{:S(2)}) collective-permute-start(bf16[384,768]{1,0:T(8,128)(2,1)} %get-tuple-element.312), channel_id=1, source_target_pairs={{0,0},{1,1},{2,4},{3,5},{4,2},{5,3},{6,6},{7,7},{8,8},{9,9},{10,12... | collective-permute-start | bytes 1769480 | tf_op jit(solution)/shard_map/ppermute | solution.py:42
  9.2 3.1 collective-permute-start.1
  34.1 12.0 %collective-permute-done.7.refs_1_ = bf16[480,768]{1,0:T(8,128)(2,1)S(1)} collective-permute-done((bf16[480,768]{1,0:T(8,128)(2,1)S(1)}, bf16[480,768]{1,0:T(8,128)(2,1)S(1)}, u32[]{:S(2)}, u32[]{:S(2)}) %collective-permute-start.7) | collective-permute-done | bytes 737312 | tf_op jit(solution)/shard_map/ppermute | solution.py:42
  51.4 10.1 %collective-permute-done.9.refs_1_ = bf16[192,1280]{1,0:T(8,128)(2,1)S(1)} collective-permute-done((bf16[192,1280]{1,0:T(8,128)(2,1)S(1)}, bf16[192,1280]{1,0:T(8,128)(2,1)S(1)}, u32[]{:S(2)}, u32[]{:S(2)}) %collective-permute-start.9) | collective-permute-done | bytes 491552 | tf_op jit(solution)/shard_map/ppermute | solution.py:42
  61.5 6.3 %collective-permute-done.10.refs_2_ = bf16[192,1280]{1,0:T(8,128)(2,1)S(1)} collective-permute-done((bf16[192,1280]{1,0:T(8,128)(2,1)S(1)}, bf16[192,1280]{1,0:T(8,128)(2,1)S(1)}, u32[]{:S(2)}, u32[]{:S(2)}) %collective-permute-start.10) | collective-permute-done | bytes 491552 | tf_op jit(solution)/shard_map/ppermute | solution.py:42
  70.2 2.9 place.2
  81.9 2.3 pad_maximum_fusion.2
  85.7 4.8 %convolution_convert_fusion.q_ref.k_ref.v_ref = bf16[1536,1152]{1,0:T(8,128)(2,1)} fusion(bf16[1536,768]{1,0:T(8,128)(2,1)S(1)} %pad_maximum_fusion, bf16[768,1152]{1,0:T(8,128)(2,1)S(1)} %copy-done.65), kind=kOutput, calls=%fused_computation | convolution fusion | flops 2719678464 | bytes 7667712 | tf_op jit(solution)/shard_map/dot_general | solution.py:27
  94.6 2.6 collective-permute-start.18
  98.4 29.6 %attention_forward.1 = (bf16[1536,384]{1,0:T(8,128)(2,1)}, f32[3,2,1536]{2,1,0:T(2,128)}) custom-call(s32[2]{0:T(128)} %add_clamp_fusion.counts_ref, bf16[1536,1152]{1,0:T(8,128)(2,1)} %convolution_convert_fusion.q_ref.k_ref.v_ref, bf16[1536,1152]{1,0:T(8,128)(2,1)} %convolution_convert_fusion.q_ref.k_ref.v_ref, ...), custom_call_target="tpu_custom_call" | custom-call | flops 1 | bytes 1 | tf_op jit(solution)/shard_map/attention_forward/pallas_call | solution.py:286
  128.6 2.8 collective-permute-done.17
  131.4 2.2 slice.231
  133.7 5.7 %place.3 = (bf16[1536,768]{1,0:T(8,128)(2,1)}, bf16[768,1536]{1,0:T(8,128)(2,1)}, bf16[768,768]{1,0:T(8,128)(2,1)}) custom-call(s32[1]{0:T(128)} %bitcast.7.p_ref, bf16[960,768]{1,0:T(8,128)(2,1)} %copy-done.5, bf16[480,768]{1,0:T(8,128)(2,1)} %copy-done.7, bf16[480,768]{1,0:T(8,128)(2,1)} %collective-permute-done.8.refs_2_, ...), custom_call_target="tpu_custom_call" | custom-call | tf_op jit(solution)/shard_map/place/pallas_call | solution.py:181
  145.6 5.1 %fusion.4 = (bf16[768,1536]{1,0:T(8,128)(2,1)}, bf16[768,1536]{1,0:T(8,128)(2,1)}) fusion(bf16[768,768]{1,0:T(8,128)(2,1)S(1)} %add_convert_fusion.2, bf16[768,1536]{1,0:T(8,128)(2,1)S(1)} %copy-done.60), kind=kOutput, calls=%fused_computation.11 | convolution fusion | flops 1824915456 | bytes 8257536 | tf_op jit(solution)/shard_map/dot_general | solution.py:27
  150.6 9.8 %collective-permute-done.20 = bf16[400,768]{1,0:T(8,128)(2,1)S(1)} collective-permute-done((bf16[400,768]{1,0:T(8,128)(2,1)S(1)}, bf16[400,768]{1,0:T(8,128)(2,1)S(1)}, u32[]{:S(2)}, u32[]{:S(2)}) %collective-permute-start.20) | collective-permute-done | bytes 614432 | tf_op jit(solution)/shard_map/ppermute | solution.py:42
  160.6 3.9 multiply_convert_fusion.2
  164.4 3.0 convolution_convert_fusion.4
  168.9 6.6 %collective-permute-start.23 = (bf16[400,768]{1,0:T(8,128)(2,1)}, bf16[400,768]{1,0:T(8,128)(2,1)}, u32[]{:S(2)}, u32[]{:S(2)}) collective-permute-start(bf16[400,768]{1,0:T(8,128)(2,1)} %get-tuple-element.292), channel_id=1, source_target_pairs={{0,0},{1,1},{2,4},{3,5},{4,2},{5,3},{6,6},{7,7},{8,8},{9,9},{10,12... | collective-permute-start | bytes 1843208 | tf_op jit(solution)/shard_map/ppermute | solution.py:42
  177.2 20.9 %collective-permute-done.24 = bf16[400,768]{1,0:T(8,128)(2,1)} collective-permute-done((bf16[400,768]{1,0:T(8,128)(2,1)}, bf16[400,768]{1,0:T(8,128)(2,1)}, u32[]{:S(2)}, u32[]{:S(2)}) %collective-permute-start.24) | collective-permute-done | bytes 614432 | tf_op jit(solution)/shard_map/ppermute | solution.py:42
  199.6 4.7 %convert_add_fusion.2 = f32[768,768]{1,0:T(8,128)} fusion(bf16[768,768]{1,0:T(8,128)(2,1)} %collective-permute-done.22, f32[768,768]{1,0:T(8,128)S(1)} %get-tuple-element.366, bf16[768,1536]{1,0:T(8,128)(2,1)S(1)} %copy-done.73, bf16[1536,768]{1,0:T(8,128)(2,1)S(1)} %copy-done.63), kind=kOutput, calls=%fused_computation.69 | convolution fusion | flops 1813708800 | bytes 10616832 | tf_op jit(solution)/shard_map/dot_general | solution.py:27
  211.6 2.4 multiply_convert_fusion.4
  220.1 2.2 add_convert_fusion.1
  222.4 4.4 multiply_convert_fusion
  235.8 2.2 add_convert_fusion
  238.1 3.2 multiply_reduce_fusion
  241.3 2.8 fusion.32
  248.7 5.9 %collective-permute-start.31 = (bf16[384,768]{1,0:T(8,128)(2,1)}, bf16[384,768]{1,0:T(8,128)(2,1)}, u32[]{:S(2)}, u32[]{:S(2)}) collective-permute-start(bf16[384,768]{1,0:T(8,128)(2,1)} %get-tuple-element.307), channel_id=1, source_target_pairs={{0,0},{1,1},{2,4},{3,5},{4,2},{5,3},{6,6},{7,7},{8,8},{9,9},{10,12... | collective-permute-start | bytes 1769480 | tf_op jit(solution)/shard_map/ppermute | solution.py:42
  255.5 4.1 collective-permute-start.32
  265.7 16.8 %attention_backward.3 = bf16[1536,384]{1,0:T(8,128)(2,1)} custom-call(s32[2]{0:T(128)} %add_clamp_fusion.counts_ref, bf16[1536,1152]{1,0:T(8,128)(2,1)} %convolution_convert_fusion.q_ref.k_ref.v_ref, bf16[1536,1152]{1,0:T(8,128)(2,1)} %convolution_convert_fusion.q_ref.k_ref.v_ref, bf16[1536,1152]{1,0:T(8,128)(2,1)} %convolution_convert_fusion.q_ref.k_ref.v_ref, ...), custom_call_target="tpu_custom_call" | custom-call | flops 1 | bytes 1 | tf_op jit(solution)/shard_map/attention_backward/pallas_call | solution.py:365
  284.9 2.7 collective-permute-start.33
  288.1 16.6 %attention_backward.4 = bf16[1536,384]{1,0:T(8,128)(2,1)} custom-call(s32[2]{0:T(128)} %add_clamp_fusion.counts_ref, bf16[1536,1152]{1,0:T(8,128)(2,1)} %convolution_convert_fusion.q_ref.k_ref.v_ref, bf16[1536,1152]{1,0:T(8,128)(2,1)} %convolution_convert_fusion.q_ref.k_ref.v_ref, bf16[1536,1152]{1,0:T(8,128)(2,1)} %convolution_convert_fusion.q_ref.k_ref.v_ref, ...), custom_call_target="tpu_custom_call" | custom-call | flops 1 | bytes 1 | tf_op jit(solution)/shard_map/attention_backward/pallas_call | solution.py:365
  304.8 2.3 add_convert_fusion.3
  308.1 2.1 fusion.37
  312.7 2.1 collective-permute-start.41
  315.6 3.1 collective-permute-start.37
  319.7 16.8 %attention_backward.5 = bf16[1536,384]{1,0:T(8,128)(2,1)} custom-call(s32[2]{0:T(128)} %add_clamp_fusion.counts_ref, bf16[1536,1152]{1,0:T(8,128)(2,1)} %convolution_convert_fusion.q_ref.k_ref.v_ref, bf16[1536,1152]{1,0:T(8,128)(2,1)} %convolution_convert_fusion.q_ref.k_ref.v_ref, bf16[1536,1152]{1,0:T(8,128)(2,1)} %convolution_convert_fusion.q_ref.k_ref.v_ref, ...), custom_call_target="tpu_custom_call" | custom-call | flops 1 | bytes 1 | tf_op jit(solution)/shard_map/attention_backward/pallas_call | solution.py:365
  336.6 2.8 convolution_convert_fusion.5
  344.5 3.3 fusion.10
  354.1 2.1 collective-permute-start.45
  356.2 12.0 %collective-permute-done.51 = bf16[48,2304]{1,0:T(8,128)(2,1)S(1)} collective-permute-done((bf16[48,2304]{1,0:T(8,128)(2,1)S(1)}, bf16[48,2304]{1,0:T(8,128)(2,1)S(1)}, u32[]{:S(2)}, u32[]{:S(2)}) %collective-permute-start.51) | collective-permute-done | bytes 221216 | tf_op jit(solution)/shard_map/ppermute | solution.py:42
  373.4 4.3 collective-permute-start.49
  379.0 2.6 collective-permute-done.50
  382.3 11.5 %collective-permute-done.49 = bf16[48,1152]{1,0:T(8,128)(2,1)S(1)} collective-permute-done((bf16[48,1152]{1,0:T(8,128)(2,1)S(1)}, bf16[48,1152]{1,0:T(8,128)(2,1)S(1)}, u32[]{:S(2)}, u32[]{:S(2)}) %collective-permute-start.49) | collective-permute-done | bytes 110624 | tf_op jit(solution)/shard_map/ppermute | solution.py:42
  398.8 2.9 collective-permute-done.55
  403.2 2.1 collective-permute-start.61
  406.4 21.1 %collective-permute-done.61 = f32[8,768]{1,0:T(8,128)S(1)} collective-permute-done((f32[8,768]{1,0:T(8,128)S(1)}, f32[8,768]{1,0:T(8,128)S(1)}, u32[]{:S(2)}, u32[]{:S(2)}) %collective-permute-start.61) | collective-permute-done | bytes 24608 | tf_op jit(solution)/shard_map/ppermute | solution.py:42
  430.3 6.1 %collective-permute-done.64 = bf16[192,768]{1,0:T(8,128)(2,1)S(1)} collective-permute-done((bf16[192,768]{1,0:T(8,128)(2,1)S(1)}, bf16[192,768]{1,0:T(8,128)(2,1)S(1)}, u32[]{:S(2)}, u32[]{:S(2)}) %collective-permute-start.64) | collective-permute-done | bytes 294944 | tf_op jit(solution)/shard_map/ppermute | solution.py:42
  (420 shorter events, 134.1 us)
Async XLA Ops:
  3.1 29.1 %collective-permute-start = (bf16[384,768]{1,0:T(8,128)(2,1)}, bf16[384,768]{1,0:T(8,128)(2,1)}, u32[]{:S(2)}, u32[]{:S(2)}) collective-permute-start(bf16[384,768]{1,0:T(8,128)(2,1)} %get-tuple-element.312), channel_id=1, source_target_pairs={{0,0},{1,1},{2,4},{3,5},{4,2},{5,3},{6,6},{7,7},{8,8},{9,9},{10,12... | collective-permute-start | bytes 1769480 | tf_op jit(solution)/shard_map/ppermute | solution.py:42
  9.2 23.0 %collective-permute-start.1 = (bf16[384,768]{1,0:T(8,128)(2,1)}, bf16[384,768]{1,0:T(8,128)(2,1)}, u32[]{:S(2)}, u32[]{:S(2)}) collective-permute-start(bf16[384,768]{1,0:T(8,128)(2,1)} %get-tuple-element.313), channel_id=1, source_target_pairs={{0,1},{1,0},{2,5},{3,4},{4,3},{5,2},{6,7},{7,6},{8,9},{9,8},{10,13... | collective-permute-start | bytes 1769480 | tf_op jit(solution)/shard_map/ppermute | solution.py:42
  29.1 17.0 %collective-permute-start.7 = (bf16[480,768]{1,0:T(8,128)(2,1)S(1)}, bf16[480,768]{1,0:T(8,128)(2,1)S(1)}, u32[]{:S(2)}, u32[]{:S(2)}) collective-permute-start(bf16[480,768]{1,0:T(8,128)(2,1)S(1)} %get-tuple-element.352), channel_id=1, source_target_pairs={{0,8},{1,9},{2,10},{3,11},{4,12},{5,13},{6,14},{7,15},{8,0},{9,1},... | collective-permute-start | bytes 2211848 | tf_op jit(solution)/shard_map/ppermute | solution.py:42
  30.6 16.7 %collective-permute-start.8 = (bf16[480,768]{1,0:T(8,128)(2,1)S(1)}, bf16[480,768]{1,0:T(8,128)(2,1)}, u32[]{:S(2)}, u32[]{:S(2)}) collective-permute-start(bf16[480,768]{1,0:T(8,128)(2,1)S(1)} %get-tuple-element.351), channel_id=1, source_target_pairs={{0,16},{1,17},{2,18},{3,19},{4,20},{5,21},{6,22},{7,23},{8,24},{9,... | collective-permute-start | bytes 2211848 | tf_op jit(solution)/shard_map/ppermute | solution.py:42
  47.4 14.1 %collective-permute-start.9 = (bf16[192,1280]{1,0:T(8,128)(2,1)S(1)}, bf16[192,1280]{1,0:T(8,128)(2,1)S(1)}, u32[]{:S(2)}, u32[]{:S(2)}) collective-permute-start(bf16[192,1280]{1,0:T(8,128)(2,1)S(1)} %pad_maximum_fusion.19.refs_0_), channel_id=1, source_target_pairs={{0,8},{1,9},{2,10},{3,11},{4,12},{5,13},{6,14},{7,15},{8,0},{9,1},... | collective-permute-start | bytes 1474568 | tf_op jit(solution)/shard_map/ppermute | solution.py:42
  47.9 19.9 %collective-permute-start.10 = (bf16[192,1280]{1,0:T(8,128)(2,1)S(1)}, bf16[192,1280]{1,0:T(8,128)(2,1)S(1)}, u32[]{:S(2)}, u32[]{:S(2)}) collective-permute-start(bf16[192,1280]{1,0:T(8,128)(2,1)S(1)} %pad_maximum_fusion.19.refs_0_), channel_id=1, source_target_pairs={{0,16},{1,17},{2,18},{3,19},{4,20},{5,21},{6,22},{7,23},{8,24},{9,... | collective-permute-start | bytes 1474568 | tf_op jit(solution)/shard_map/ppermute | solution.py:42
  49.4 19.9 %collective-permute-start.11 = (bf16[192,1280]{1,0:T(8,128)(2,1)S(1)}, bf16[192,1280]{1,0:T(8,128)(2,1)S(1)}, u32[]{:S(2)}, u32[]{:S(2)}) collective-permute-start(bf16[192,1280]{1,0:T(8,128)(2,1)S(1)} %pad_maximum_fusion.19.refs_0_), channel_id=1, source_target_pairs={{0,24},{1,25},{2,26},{3,27},{4,28},{5,29},{6,30},{7,31},{8,16},{9,... | collective-permute-start | bytes 1474568 | tf_op jit(solution)/shard_map/ppermute | solution.py:42
  75.7 14.9 %collective-permute-start.13 = (bf16[400,768]{1,0:T(8,128)(2,1)S(1)}, bf16[400,768]{1,0:T(8,128)(2,1)S(1)}, u32[]{:S(2)}, u32[]{:S(2)}) collective-permute-start(bf16[400,768]{1,0:T(8,128)(2,1)S(1)} %fusion.49), channel_id=1, source_target_pairs={{0,4},{1,5},{2,6},{3,7},{4,0},{5,1},{6,2},{7,3},{8,12},{9,13},{10,... | collective-permute-start | bytes 1843208 | tf_op jit(solution)/shard_map/ppermute | solution.py:42
  80.3 51.1 %collective-permute-start.15 = (bf16[960,768]{1,0:T(8,128)(2,1)}, bf16[960,768]{1,0:T(8,128)(2,1)}, u32[]{:S(2)}, u32[]{:S(2)}) collective-permute-start(bf16[960,768]{1,0:T(8,128)(2,1)} %pad_maximum_fusion.1), channel_id=1, source_target_pairs={{0,16},{1,17},{2,18},{3,19},{4,20},{5,21},{6,22},{7,23},{8,24},{9,... | collective-permute-start | bytes 4423688 | tf_op jit(solution)/shard_map/ppermute | solution.py:42
  84.3 47.2 %collective-permute-start.16 = (bf16[960,768]{1,0:T(8,128)(2,1)}, bf16[960,768]{1,0:T(8,128)(2,1)}, u32[]{:S(2)}, u32[]{:S(2)}) collective-permute-start(bf16[960,768]{1,0:T(8,128)(2,1)} %pad_maximum_fusion.2), channel_id=1, source_target_pairs={{0,8},{1,9},{2,10},{3,11},{4,12},{5,13},{6,14},{7,15},{8,0},{9,1},... | collective-permute-start | bytes 4423688 | tf_op jit(solution)/shard_map/ppermute | solution.py:42
  91.5 39.9 %collective-permute-start.17 = (bf16[400,768]{1,0:T(8,128)(2,1)}, bf16[400,768]{1,0:T(8,128)(2,1)S(1)}, u32[]{:S(2)}, u32[]{:S(2)}) collective-permute-start(bf16[400,768]{1,0:T(8,128)(2,1)} %get-tuple-element.283), channel_id=1, source_target_pairs={{0,8},{1,9},{2,10},{3,11},{4,12},{5,13},{6,14},{7,15},{8,0},{9,1},... | collective-permute-start | bytes 1843208 | tf_op jit(solution)/shard_map/ppermute | solution.py:42
  94.6 33.4 %collective-permute-start.18 = (f32[8,128]{1,0:T(8,128)S(1)}, f32[8,128]{1,0:T(8,128)S(1)}, u32[]{:S(2)}, u32[]{:S(2)}) collective-permute-start(f32[8,128]{1,0:T(8,128)S(1)} %add.334), channel_id=1, source_target_pairs={{0,2},{1,3},{2,0},{3,1},{4,6},{5,7},{6,4},{7,5},{8,10},{9,11},{10,... | collective-permute-start | bytes 12296 | tf_op jit(solution)/shard_map/ppermute | solution.py:42
  143.2 17.4 %collective-permute-start.21 = (bf16[768,768]{1,0:T(8,128)(2,1)S(1)}, bf16[768,768]{1,0:T(8,128)(2,1)S(1)}, u32[]{:S(2)}, u32[]{:S(2)}) collective-permute-start(bf16[768,768]{1,0:T(8,128)(2,1)S(1)} %add_convert_fusion.2), channel_id=1, source_target_pairs={{0,4},{1,5},{2,6},{3,7},{4,0},{5,1},{6,2},{7,3},{8,12},{9,13},{10,... | collective-permute-start | bytes 3538952 | tf_op jit(solution)/shard_map/ppermute | solution.py:42
  144.1 16.3 %collective-permute-start.20 = (bf16[400,768]{1,0:T(8,128)(2,1)S(1)}, bf16[400,768]{1,0:T(8,128)(2,1)S(1)}, u32[]{:S(2)}, u32[]{:S(2)}) collective-permute-start(bf16[400,768]{1,0:T(8,128)(2,1)S(1)} %get-tuple-element.280), channel_id=1, source_target_pairs={{0,16},{1,17},{2,18},{3,19},{4,20},{5,21},{6,22},{7,23},{8,24},{9,... | collective-permute-start | bytes 1843208 | tf_op jit(solution)/shard_map/ppermute | solution.py:42
  167.4 32.1 %collective-permute-start.22 = (bf16[768,768]{1,0:T(8,128)(2,1)}, bf16[768,768]{1,0:T(8,128)(2,1)}, u32[]{:S(2)}, u32[]{:S(2)}) collective-permute-start(bf16[768,768]{1,0:T(8,128)(2,1)} %convolution_convert_fusion.4), channel_id=1, source_target_pairs={{0,4},{1,5},{2,6},{3,7},{4,0},{5,1},{6,2},{7,3},{8,12},{9,13},{10,... | collective-permute-start | bytes 3538952 | tf_op jit(solution)/shard_map/ppermute | solution.py:42
  175.5 22.6 %collective-permute-start.24 = (bf16[400,768]{1,0:T(8,128)(2,1)}, bf16[400,768]{1,0:T(8,128)(2,1)}, u32[]{:S(2)}, u32[]{:S(2)}) collective-permute-start(bf16[400,768]{1,0:T(8,128)(2,1)} %get-tuple-element.293), channel_id=1, source_target_pairs={{0,1},{1,0},{2,5},{3,4},{4,3},{5,2},{6,7},{7,6},{8,9},{9,8},{10,13... | collective-permute-start | bytes 1843208 | tf_op jit(solution)/shard_map/ppermute | solution.py:42
  230.3 24.4 %collective-permute-start.28 = (bf16[384,768]{1,0:T(8,128)(2,1)S(1)}, bf16[384,768]{1,0:T(8,128)(2,1)S(1)}, u32[]{:S(2)}, u32[]{:S(2)}) collective-permute-start(bf16[384,768]{1,0:T(8,128)(2,1)S(1)} %get-tuple-element.276), channel_id=1, source_target_pairs={{0,8},{1,9},{2,10},{3,11},{4,12},{5,13},{6,14},{7,15},{8,0},{9,1},... | collective-permute-start | bytes 1769480 | tf_op jit(solution)/shard_map/ppermute | solution.py:42
  231.7 29.3 %collective-permute-start.29 = (bf16[384,768]{1,0:T(8,128)(2,1)S(1)}, bf16[384,768]{1,0:T(8,128)(2,1)S(1)}, u32[]{:S(2)}, u32[]{:S(2)}) collective-permute-start(bf16[384,768]{1,0:T(8,128)(2,1)S(1)} %get-tuple-element.275), channel_id=1, source_target_pairs={{0,16},{1,17},{2,18},{3,19},{4,20},{5,21},{6,22},{7,23},{8,24},{9,... | collective-permute-start | bytes 1769480 | tf_op jit(solution)/shard_map/ppermute | solution.py:42
  232.4 30.1 %collective-permute-start.30 = (bf16[384,768]{1,0:T(8,128)(2,1)S(1)}, bf16[384,768]{1,0:T(8,128)(2,1)S(1)}, u32[]{:S(2)}, u32[]{:S(2)}) collective-permute-start(bf16[384,768]{1,0:T(8,128)(2,1)S(1)} %get-tuple-element.274), channel_id=1, source_target_pairs={{0,24},{1,25},{2,26},{3,27},{4,28},{5,29},{6,30},{7,31},{8,16},{9,... | collective-permute-start | bytes 1769480 | tf_op jit(solution)/shard_map/ppermute | solution.py:42
  245.4 17.7 %collective-permute-start.27 = (bf16[768,384]{1,0:T(8,128)(2,1)S(1)}, bf16[768,384]{1,0:T(8,128)(2,1)S(1)}, u32[]{:S(2)}, u32[]{:S(2)}) collective-permute-start(bf16[768,384]{1,0:T(8,128)(2,1)S(1)} %get-tuple-element.309), channel_id=1, source_target_pairs={{0,4},{1,5},{2,6},{3,7},{4,0},{5,1},{6,2},{7,3},{8,12},{9,13},{10,... | collective-permute-start | bytes 1769480 | tf_op jit(solution)/shard_map/ppermute | solution.py:42
  248.7 33.7 %collective-permute-start.31 = (bf16[384,768]{1,0:T(8,128)(2,1)}, bf16[384,768]{1,0:T(8,128)(2,1)}, u32[]{:S(2)}, u32[]{:S(2)}) collective-permute-start(bf16[384,768]{1,0:T(8,128)(2,1)} %get-tuple-element.307), channel_id=1, source_target_pairs={{0,0},{1,1},{2,4},{3,5},{4,2},{5,3},{6,6},{7,7},{8,8},{9,9},{10,12... | collective-permute-start | bytes 1769480 | tf_op jit(solution)/shard_map/ppermute | solution.py:42
  255.5 26.9 %collective-permute-start.32 = (bf16[384,768]{1,0:T(8,128)(2,1)}, bf16[384,768]{1,0:T(8,128)(2,1)}, u32[]{:S(2)}, u32[]{:S(2)}) collective-permute-start(bf16[384,768]{1,0:T(8,128)(2,1)} %get-tuple-element.306), channel_id=1, source_target_pairs={{0,1},{1,0},{2,5},{3,4},{4,3},{5,2},{6,7},{7,6},{8,9},{9,8},{10,13... | collective-permute-start | bytes 1769480 | tf_op jit(solution)/shard_map/ppermute | solution.py:42
  261.0 43.8 %collective-permute-start.34 = (bf16[192,2304]{1,0:T(8,128)(2,1)}, bf16[192,2304]{1,0:T(8,128)(2,1)}, u32[]{:S(2)}, u32[]{:S(2)}) collective-permute-start(bf16[192,2304]{1,0:T(8,128)(2,1)} %get-tuple-element.271), channel_id=1, source_target_pairs={{0,8},{1,9},{2,10},{3,11},{4,12},{5,13},{6,14},{7,15},{8,0},{9,1},... | collective-permute-start | bytes 2654216 | tf_op jit(solution)/shard_map/ppermute | solution.py:42
  262.5 42.3 %collective-permute-start.35 = (bf16[192,2304]{1,0:T(8,128)(2,1)}, bf16[192,2304]{1,0:T(8,128)(2,1)}, u32[]{:S(2)}, u32[]{:S(2)}) collective-permute-start(bf16[192,2304]{1,0:T(8,128)(2,1)} %get-tuple-element.272), channel_id=1, source_target_pairs={{0,16},{1,17},{2,18},{3,19},{4,20},{5,21},{6,22},{7,23},{8,24},{9,... | collective-permute-start | bytes 2654216 | tf_op jit(solution)/shard_map/ppermute | solution.py:42
  263.1 41.7 %collective-permute-start.36 = (bf16[192,2304]{1,0:T(8,128)(2,1)S(1)}, bf16[192,2304]{1,0:T(8,128)(2,1)}, u32[]{:S(2)}, u32[]{:S(2)}) collective-permute-start(bf16[192,2304]{1,0:T(8,128)(2,1)S(1)} %get-tuple-element.269), channel_id=1, source_target_pairs={{0,24},{1,25},{2,26},{3,27},{4,28},{5,29},{6,30},{7,31},{8,16},{9,... | collective-permute-start | bytes 2654216 | tf_op jit(solution)/shard_map/ppermute | solution.py:42
  284.9 19.8 %collective-permute-start.33 = (bf16[192,768]{1,0:T(8,128)(2,1)}, bf16[192,768]{1,0:T(8,128)(2,1)S(1)}, u32[]{:S(2)}, u32[]{:S(2)}) collective-permute-start(bf16[192,768]{1,0:T(8,128)(2,1)} %get-tuple-element.327), channel_id=1, source_target_pairs={{0,1},{1,0},{2,3},{3,2},{4,5},{5,4},{6,7},{7,6},{8,9},{9,8},{10,11... | collective-permute-start | bytes 884744 | tf_op jit(solution)/shard_map/ppermute | solution.py:42
  308.1 28.5 %collective-permute-start.38 = (bf16[96,2304]{1,0:T(8,128)(2,1)}, bf16[96,2304]{1,0:T(8,128)(2,1)}, u32[]{:S(2)}, u32[]{:S(2)}) collective-permute-start(bf16[96,2304]{1,0:T(8,128)(2,1)} %get-tuple-element.316), channel_id=1, source_target_pairs={{0,1},{1,0},{2,3},{3,2},{4,5},{5,4},{6,7},{7,6},{8,9},{9,8},{10,11... | collective-permute-start | bytes 1327112 | tf_op jit(solution)/shard_map/ppermute | solution.py:42
  311.3 25.3 %collective-permute-start.39 = (bf16[192,768]{1,0:T(8,128)(2,1)}, bf16[192,768]{1,0:T(8,128)(2,1)}, u32[]{:S(2)}, u32[]{:S(2)}) collective-permute-start(bf16[192,768]{1,0:T(8,128)(2,1)} %get-tuple-element.302), channel_id=1, source_target_pairs={{0,8},{1,9},{2,10},{3,11},{4,12},{5,13},{6,14},{7,15},{8,0},{9,1},... | collective-permute-start | bytes 884744 | tf_op jit(solution)/shard_map/ppermute | solution.py:42
  312.1 24.5 %collective-permute-start.40 = (bf16[192,768]{1,0:T(8,128)(2,1)}, bf16[192,768]{1,0:T(8,128)(2,1)}, u32[]{:S(2)}, u32[]{:S(2)}) collective-permute-start(bf16[192,768]{1,0:T(8,128)(2,1)} %get-tuple-element.301), channel_id=1, source_target_pairs={{0,16},{1,17},{2,18},{3,19},{4,20},{5,21},{6,22},{7,23},{8,24},{9,... | collective-permute-start | bytes 884744 | tf_op jit(solution)/shard_map/ppermute | solution.py:42
  312.7 23.9 %collective-permute-start.41 = (bf16[192,768]{1,0:T(8,128)(2,1)}, bf16[192,768]{1,0:T(8,128)(2,1)}, u32[]{:S(2)}, u32[]{:S(2)}) collective-permute-start(bf16[192,768]{1,0:T(8,128)(2,1)} %get-tuple-element.300), channel_id=1, source_target_pairs={{0,24},{1,25},{2,26},{3,27},{4,28},{5,29},{6,30},{7,31},{8,16},{9,... | collective-permute-start | bytes 884744 | tf_op jit(solution)/shard_map/ppermute | solution.py:42
  315.6 20.9 %collective-permute-start.37 = (bf16[96,768]{1,0:T(8,128)(2,1)}, bf16[96,768]{1,0:T(8,128)(2,1)}, u32[]{:S(2)}, u32[]{:S(2)}) collective-permute-start(bf16[96,768]{1,0:T(8,128)(2,1)} %get-tuple-element.349), channel_id=1, source_target_pairs={{0,2},{1,3},{2,0},{3,1},{4,6},{5,7},{6,4},{7,5},{8,10},{9,11},{10,... | collective-permute-start | bytes 442376 | tf_op jit(solution)/shard_map/ppermute | solution.py:42
  339.7 13.2 %collective-permute-start.43 = (bf16[192,384]{1,0:T(8,128)(2,1)S(1)}, bf16[192,384]{1,0:T(8,128)(2,1)S(1)}, u32[]{:S(2)}, u32[]{:S(2)}) collective-permute-start(bf16[192,384]{1,0:T(8,128)(2,1)S(1)} %get-tuple-element.326), channel_id=1, source_target_pairs={{0,16},{1,17},{2,18},{3,19},{4,20},{5,21},{6,22},{7,23},{8,24},{9,... | collective-permute-start | bytes 442376 | tf_op jit(solution)/shard_map/ppermute | solution.py:42
  344.4 28.9 %collective-permute-start.46 = (bf16[96,768]{1,0:T(8,128)(2,1)S(1)}, bf16[96,768]{1,0:T(8,128)(2,1)S(1)}, u32[]{:S(2)}, u32[]{:S(2)}) collective-permute-start(bf16[96,768]{1,0:T(8,128)(2,1)S(1)} %get-tuple-element.347), channel_id=1, source_target_pairs={{0,1},{1,0},{2,3},{3,2},{4,5},{5,4},{6,7},{7,6},{8,9},{9,8},{10,11... | collective-permute-start | bytes 442376 | tf_op jit(solution)/shard_map/ppermute | solution.py:42
  348.0 20.4 %collective-permute-start.47 = (bf16[768,768]{1,0:T(8,128)(2,1)S(1)}, bf16[768,768]{1,0:T(8,128)(2,1)S(1)}, u32[]{:S(2)}, u32[]{:S(2)}) collective-permute-start(bf16[768,768]{1,0:T(8,128)(2,1)S(1)} %slice.368), channel_id=1, source_target_pairs={{0,4},{1,5},{2,6},{3,7},{4,0},{5,1},{6,2},{7,3},{8,12},{9,13},{10,... | collective-permute-start | bytes 3538952 | tf_op jit(solution)/shard_map/ppermute | solution.py:42
  351.0 17.2 %collective-permute-start.51 = (bf16[48,2304]{1,0:T(8,128)(2,1)S(1)}, bf16[48,2304]{1,0:T(8,128)(2,1)S(1)}, u32[]{:S(2)}, u32[]{:S(2)}) collective-permute-start(bf16[48,2304]{1,0:T(8,128)(2,1)S(1)} %dynamic-slice_bitcast_fusion.12), channel_id=1, source_target_pairs={{0,2},{1,3},{2,0},{3,1},{4,6},{5,7},{6,4},{7,5},{8,10},{9,11},{10,... | collective-permute-start | bytes 663560 | tf_op jit(solution)/shard_map/ppermute | solution.py:42
  352.9 29.4 %collective-permute-start.53 = (bf16[96,768]{1,0:T(8,128)(2,1)S(1)}, bf16[96,768]{1,0:T(8,128)(2,1)S(1)}, u32[]{:S(2)}, u32[]{:S(2)}) collective-permute-start(bf16[96,768]{1,0:T(8,128)(2,1)S(1)} %add_convert_fusion.8), channel_id=1, source_target_pairs={{0,2},{1,3},{2,0},{3,1},{4,6},{5,7},{6,4},{7,5},{8,10},{9,11},{10,... | collective-permute-start | bytes 442376 | tf_op jit(solution)/shard_map/ppermute | solution.py:42
  354.1 19.2 %collective-permute-start.45 = (bf16[96,384]{1,0:T(8,128)(2,1)S(1)}, bf16[96,384]{1,0:T(8,128)(2,1)S(1)}, u32[]{:S(2)}, u32[]{:S(2)}) collective-permute-start(bf16[96,384]{1,0:T(8,128)(2,1)S(1)} %get-tuple-element.359), channel_id=1, source_target_pairs={{0,1},{1,0},{2,3},{3,2},{4,5},{5,4},{6,7},{7,6},{8,9},{9,8},{10,11... | collective-permute-start | bytes 221192 | tf_op jit(solution)/shard_map/ppermute | solution.py:42
  368.3 14.0 %collective-permute-start.52 = (bf16[48,2304]{1,0:T(8,128)(2,1)S(1)}, bf16[48,2304]{1,0:T(8,128)(2,1)S(1)}, u32[]{:S(2)}, u32[]{:S(2)}) collective-permute-start(bf16[48,2304]{1,0:T(8,128)(2,1)S(1)} %fusion.56), channel_id=1, source_target_pairs={{0,2},{1,3},{2,0},{3,1},{4,6},{5,7},{6,4},{7,5},{8,10},{9,11},{10,... | collective-permute-start | bytes 663560 | tf_op jit(solution)/shard_map/ppermute | solution.py:42
  371.9 21.9 %collective-permute-start.54 = (bf16[192,768]{1,0:T(8,128)(2,1)S(1)}, bf16[192,768]{1,0:T(8,128)(2,1)S(1)}, u32[]{:S(2)}, u32[]{:S(2)}) collective-permute-start(bf16[192,768]{1,0:T(8,128)(2,1)S(1)} %get-tuple-element.299), channel_id=1, source_target_pairs={{0,0},{1,1},{2,4},{3,5},{4,2},{5,3},{6,6},{7,7},{8,8},{9,9},{10,12... | collective-permute-start | bytes 884744 | tf_op jit(solution)/shard_map/ppermute | solution.py:42
  373.4 20.3 %collective-permute-start.49 = (bf16[48,1152]{1,0:T(8,128)(2,1)S(1)}, bf16[48,1152]{1,0:T(8,128)(2,1)S(1)}, u32[]{:S(2)}, u32[]{:S(2)}) collective-permute-start(bf16[48,1152]{1,0:T(8,128)(2,1)S(1)} %get-tuple-element.357), channel_id=1, source_target_pairs={{0,2},{1,3},{2,0},{3,1},{4,6},{5,7},{6,4},{7,5},{8,10},{9,11},{10,... | collective-permute-start | bytes 331784 | tf_op jit(solution)/shard_map/ppermute | solution.py:42
  381.6 17.2 %collective-permute-start.57 = (bf16[192,768]{1,0:T(8,128)(2,1)S(1)}, bf16[192,768]{1,0:T(8,128)(2,1)S(1)}, u32[]{:S(2)}, u32[]{:S(2)}) collective-permute-start(bf16[192,768]{1,0:T(8,128)(2,1)S(1)} %get-tuple-element.185), channel_id=1, source_target_pairs={{0,0},{1,1},{2,4},{3,5},{4,2},{5,3},{6,6},{7,7},{8,8},{9,9},{10,12... | collective-permute-start | bytes 884744 | tf_op jit(solution)/shard_map/ppermute | solution.py:42
  394.5 33.1 %collective-permute-start.59 = (bf16[96,2304]{1,0:T(8,128)(2,1)S(1)}, bf16[96,2304]{1,0:T(8,128)(2,1)S(1)}, u32[]{:S(2)}, u32[]{:S(2)}) collective-permute-start(bf16[96,2304]{1,0:T(8,128)(2,1)S(1)} %pad_maximum_fusion.21), channel_id=1, source_target_pairs={{0,1},{1,0},{2,3},{3,2},{4,5},{5,4},{6,7},{7,6},{8,9},{9,8},{10,11... | collective-permute-start | bytes 1327112 | tf_op jit(solution)/shard_map/ppermute | solution.py:42
  395.6 31.9 %collective-permute-start.60 = (bf16[192,768]{1,0:T(8,128)(2,1)S(1)}, bf16[192,768]{1,0:T(8,128)(2,1)S(1)}, u32[]{:S(2)}, u32[]{:S(2)}) collective-permute-start(bf16[192,768]{1,0:T(8,128)(2,1)S(1)} %pad_maximum_fusion.26), channel_id=1, source_target_pairs={{0,1},{1,0},{2,3},{3,2},{4,5},{5,4},{6,7},{7,6},{8,9},{9,8},{10,11... | collective-permute-start | bytes 884744 | tf_op jit(solution)/shard_map/ppermute | solution.py:42
  397.8 29.8 %collective-permute-start.62 = (bf16[192,768]{1,0:T(8,128)(2,1)S(1)}, bf16[192,768]{1,0:T(8,128)(2,1)S(1)}, u32[]{:S(2)}, u32[]{:S(2)}) collective-permute-start(bf16[192,768]{1,0:T(8,128)(2,1)S(1)} %get-tuple-element.190), channel_id=1, source_target_pairs={{0,1},{1,0},{2,5},{3,4},{4,3},{5,2},{6,7},{7,6},{8,9},{9,8},{10,13... | collective-permute-start | bytes 884744 | tf_op jit(solution)/shard_map/ppermute | solution.py:42
  401.8 25.8 %collective-permute-start.58 = (bf16[96,1152]{1,0:T(8,128)(2,1)S(1)}, bf16[96,1152]{1,0:T(8,128)(2,1)S(1)}, u32[]{:S(2)}, u32[]{:S(2)}) collective-permute-start(bf16[96,1152]{1,0:T(8,128)(2,1)S(1)} %pad_maximum_fusion.28), channel_id=1, source_target_pairs={{0,1},{1,0},{2,3},{3,2},{4,5},{5,4},{6,7},{7,6},{8,9},{9,8},{10,11... | collective-permute-start | bytes 663560 | tf_op jit(solution)/shard_map/ppermute | solution.py:42
  403.2 24.3 %collective-permute-start.61 = (f32[8,768]{1,0:T(8,128)S(1)}, f32[8,768]{1,0:T(8,128)S(1)}, u32[]{:S(2)}, u32[]{:S(2)}) collective-permute-start(f32[8,768]{1,0:T(8,128)S(1)} %add.386), channel_id=1, source_target_pairs={{0,1},{1,0},{2,3},{3,2},{4,5},{5,4},{6,7},{7,6},{8,9},{9,8},{10,11... | collective-permute-start | bytes 73736 | tf_op jit(solution)/shard_map/ppermute | solution.py:42
  427.9 12.7 %collective-permute-start.65 = (bf16[96,1152]{1,0:T(8,128)(2,1)S(1)}, bf16[96,1152]{1,0:T(8,128)(2,1)S(1)}, u32[]{:S(2)}, u32[]{:S(2)}) collective-permute-start(bf16[96,1152]{1,0:T(8,128)(2,1)S(1)} %fusion.60), channel_id=1, source_target_pairs={{0,4},{1,5},{2,6},{3,7},{4,0},{5,1},{6,2},{7,3},{8,12},{9,13},{10,... | collective-permute-start | bytes 663560 | tf_op jit(solution)/shard_map/ppermute | solution.py:42
  430.1 12.7 %collective-permute-start.66 = (bf16[96,2304]{1,0:T(8,128)(2,1)S(1)}, bf16[96,2304]{1,0:T(8,128)(2,1)}, u32[]{:S(2)}, u32[]{:S(2)}) collective-permute-start(bf16[96,2304]{1,0:T(8,128)(2,1)S(1)} %fusion.54), channel_id=1, source_target_pairs={{0,4},{1,5},{2,6},{3,7},{4,0},{5,1},{6,2},{7,3},{8,12},{9,13},{10,... | collective-permute-start | bytes 1327112 | tf_op jit(solution)/shard_map/ppermute | solution.py:42
  (96 other events, 611.4 us)

commit v6 on v4

--- a/solution.py
+++ b/solution.py
@@ -109,29 +109,6 @@
             current = jnp.transpose(current, lead + (len(bits), len(bits) + 1))
         halves.append(current.reshape(count, rows // 2, width))
     return [jnp.concatenate(halves, axis=1).reshape(count * rows, width)], None, ()
-
-
-def halves_first(value):
-    if lax.axis_size("pair") != 4:
-        return value, None
-    rows = value.shape[0] // 2
-    return value, (across_pairs(value[:rows], 1), across_pairs(value[rows:], 2))
-
-
-def halves_second(state):
-    value, near = state
-    if near is None:
-        return gathered_over_pairs(value)
-    rows = value.shape[0] // 2
-    upper = across_pairs(jnp.concatenate([value[:rows], near[0]], axis=0), 2)
-    lower = across_pairs(jnp.concatenate([value[rows:], near[1]], axis=0), 1)
-    layout = (
-        (0, 0, 0, 0, 2 * rows),
-        (1, 1, 0, 0, rows), (1, 4, 0, rows, rows),
-        (2, 3, 0, 0, rows), (2, 2, 0, rows, rows),
-        (3, 3, rows, 0, rows), (3, 4, rows, rows, rows),
-    )
-    return [value, near[0], near[1], upper, lower], lax.axis_index("pair"), layout
 
 
 def place_kernel(p_ref, *refs, segments, layout, count):
@@ -442,7 +419,6 @@
     keep = lax.dynamic_index_in_dim(shard, c, 0, keepdims=False)
     send = lax.dynamic_index_in_dim(shard, 1 - c, 0, keepdims=False)
     qkv_shard = in_order(keep, across_cores(send), 0)
-    qkv_pieces = gathered_over_pairs(qkv_shard)
 
     x_rows = turned(tokens).reshape(rows, width)
 
@@ -474,6 +450,12 @@
 
     levels = groups.bit_length() - 1
     deal = dealt(slots, 0)
+    deal, tally = tied(deal, tally)
+    depth_steps, plane_steps = sum_steps()
+    tally = tally + plane_steps[1](tally)
+    deal = dealt(settled(*deal), 1)
+    qkv_shard, deal, tally = tied(qkv_shard, deal, tally)
+    qkv_pieces = gathered_over_pairs(qkv_shard)
 
     block = ff // groups
 
@@ -499,11 +481,12 @@
         (1, down_rows + pair_rows, pair_rows, 0, width, width),
         (2, down_rows + 2 * pair_rows, pair_rows, 0, width, 0),
     )
-    depth_steps, plane_steps = sum_steps()
-    for step in plane_steps[1:]:
+    for step in plane_steps[2:]:
         tally = tally + step(tally)
-    x_rows, payload, tally = tied(x_rows, payload, tally)
-    payload_first = halves_first(payload)
+    x_rows, payload, tally, deal = tied(x_rows, payload, tally, deal)
+    for level in range(2, levels):
+        deal = dealt(settled(*deal), level)
+    tally = tally + depth_steps[0](tally)
 
     x_full = x_rows.astype(FULL)
     unit_one, inverse_one = norm_parts(x_full)
@@ -515,23 +498,20 @@
     vectors = dot(pick.astype(LOW), vectors, NT)
     gain_one, shift_one, gain_two, shift_two = vectors[0], vectors[1], vectors[2], vectors[3]
     norm_mine = (unit_one * gain_one + shift_one).astype(LOW)
-    norm_one = jnp.concatenate([norm_mine, across_cores(norm_mine)], axis=0)
-    norm_one, tally, deal = tied(norm_one, tally, deal)
-    deal = dealt(settled(*deal), 1)
-    tally = tally + depth_steps[0](tally)
-    qkv = dot(norm_one, w_qkv, NN).astype(LOW)
-    qkv, deal, tally, payload_first = tied(qkv, deal, tally, payload_first)
-    payload_pieces = halves_second(payload_first)
-    for level in range(2, levels):
-        deal = dealt(settled(*deal), level)
+    norm_got = across_cores(norm_mine)
+    norm_got, deal, payload, tally = tied(norm_got, deal, payload, tally)
+    goal_moved = turned_parts(settled(*deal))
+    payload_pieces = gathered_over_pairs(payload)
+    norm_one = jnp.concatenate([norm_mine, norm_got], axis=0)
     for step in depth_steps[1:]:
         tally = tally + step(tally)
+    qkv = dot(norm_one, w_qkv, NN).astype(LOW)
     mixed, lse = attention_forward(counts, qkv, 512)
 
     sources, *place_args = payload_pieces
-    mixed, sources, deal, tally = tied(mixed, sources, deal, tally)
+    mixed, sources, goal_moved, tally = tied(mixed, sources, goal_moved, tally)
     mixed_got = across_cores(mixed[rows:])
-    goal = turned(settled(*deal))
+    goal = turned_settled(goal_moved)
     w_down, w_up, w_out = placed((sources, *place_args), payload_plan)
 
     attended = in_order(mixed[:rows], mixed_got, 1)
@@ -630,39 +610,39 @@
     late = depth_halved(added(late), low_bit)
     rest_own = added(rest_step)
     rest_got = across_depth(rest_own, high_bit)
-    late, early, rest_got, small, down_got, near = tied(
-        late, early, rest_got, small, down_got, input_moved[0]
-    )
+    late, early, small = tied(late, early, small)
+    qkv_step = depth_halved(jnp.concatenate([added(early), added(late)], axis=1), high_bit)
+    small = small + depth_steps[0](small)
+    qkv_step, small, rest_got, down_got, near = tied(
+        qkv_step, small, rest_got, down_got, input_moved[0]
+    )
+    qkv_own = added(qkv_step)
+    qkv_got = across_depth(qkv_own, high_bit)
+    for step in depth_steps[1:]:
+        small = small + step(small)
+    rest_own = depth_doubled(rest_own, rest_got, high_bit)
+    rest_got = across_depth(rest_own, low_bit)
     down_own = depth_doubled(down_own, down_got, high_bit)
     down_got = across_depth(down_own, low_bit)
-    qkv_step = depth_halved(jnp.concatenate([added(early), added(late)], axis=1), high_bit)
-    rest_own = depth_doubled(rest_own, rest_got, high_bit)
-    rest_got = across_depth(rest_own, low_bit)
-    small = small + plane_steps[1](small)
-    qkv_step, small, down_got, far = tied(qkv_step, small, down_got, input_moved[1])
-    input_grad = turned_settled([near, far])
-    down_own = depth_doubled(down_own, down_got, low_bit)
-    qkv_own = added(qkv_step)
-    qkv_got = across_depth(qkv_own, high_bit)
-    for step in plane_steps[2:]:
-        small = small + step(small)
-    qkv_got, rest_got, small = tied(qkv_got, rest_got, small)
+    qkv_got, small, far = tied(qkv_got, small, input_moved[1])
     qkv_own = depth_doubled(qkv_own, qkv_got, high_bit)
     qkv_got = across_depth(qkv_own, low_bit)
+    small = small + plane_steps[1](small)
+    qkv_got, rest_got, down_got, small = tied(qkv_got, rest_got, down_got, small)
     rest_own = depth_doubled(rest_own, rest_got, low_bit)
-    small = small + depth_steps[0](small)
+    down_own = depth_doubled(down_own, down_got, low_bit)
 
     def own_block(stack, index):
         return lax.dynamic_slice_in_dim(stack, index * own_rows, own_rows, 0)
 
     rest_mine = own_block(rest_own, c)
     rest_other = across_cores(own_block(rest_own, 1 - c))
-    qkv_got, rest_other, small = tied(qkv_got, rest_other, small)
     qkv_own = depth_doubled(qkv_own, qkv_got, low_bit)
     qkv_mine = own_block(qkv_own, c)
     qkv_other = across_cores(own_block(qkv_own, 1 - c))
-    for step in depth_steps[1:]:
+    for step in plane_steps[2:]:
         small = small + step(small)
+    input_grad = turned_settled([near, far])
 
     loss = small[4, 0] / (valid_count * width)
     own_small = lax.dynamic_slice_in_dim(small, group * own_rows, own_rows, 1)

time: 441 us -> 442 us (level)
  waiting for transfers between devices: 118 us -> 108 us
  starting transfers between devices: 79 us -> 88.3 us
    ppermute x65 -> x64, waiting for transfers between devices: 118 us -> 108 us  [moved(): return lax.ppermute(value, AXES, links)]
    ppermute x65 -> x64, starting transfers between devices: 79 us -> 88.3 us  [moved(): return lax.ppermute(value, AXES, links)]
    unnamed x165 -> x155, local copies, waits for them, and re-layouts: 7.22 us -> 10.3 us
  transfers between devices with their start and end apart: 65 -> 64, of which waited for: 22 -> 20; matrix products, arithmetic and copies ran while one was open for 19% -> 19% of each run, Pallas kernels for 20% -> 20%
where the time goes in v6:
time: 442 us; the launch traced here: 435 us
  waiting for transfers between devices  108 us (24%)
  Pallas kernels  88.7 us (20%)
  starting transfers between devices  88.3 us (20%)
  matrix products  61.4 us (14%)
  other arithmetic  54.1 us (12%)
  local copies, waits for them, and re-layouts  28.2 us (6%)
  between operations  7.11 us (2%)
    ppermute x64, waiting for transfers between devices, moved(): return lax.ppermute(value, AXES, links)  108 us
    ppermute x64, starting transfers between devices, moved(): return lax.ppermute(value, AXES, links)  88.3 us
    dot_general x20, matrix products, dot(): return lax.dot_general(left, right, form, preferred_element_type=FULL)  61.4 us
    pallas_call x3, Pallas kernels, attention_backward(): pl.pallas_call(functools.partial(backward_kernel, rows=rows, block=block,...  50.5 us
    pallas_call x1, Pallas kernels, attention_forward(): pl.pallas_call(functools.partial(forward_kernel, rows=rows, block=block),...  29.6 us
    unnamed x155, local copies, waits for them, and re-layouts  10.3 us
  transfers between devices with their start and end apart: 64, of which 20 were waited for; matrix products, arithmetic and copies ran while one was open for 19% of the time, Pallas kernels for 20%

profile of v6, /device:TPU:0, one launch (start us, length us, event | category | flops | bytes accessed | tf_op | source)
XLA Modules:
  0.0 435.5 jit_solution(5984974538867800565)
XLA Ops:
  8.7 2.3 dynamic-slice_bitcast_fusion.5
  11.1 5.9 %collective-permute-start = (bf16[384,768]{1,0:T(8,128)(2,1)}, bf16[384,768]{1,0:T(8,128)(2,1)}, u32[]{:S(2)}, u32[]{:S(2)}) collective-permute-start(bf16[384,768]{1,0:T(8,128)(2,1)} %get-tuple-element.286), channel_id=1, source_target_pairs={{0,0},{1,1},{2,4},{3,5},{4,2},{5,3},{6,6},{7,7},{8,8},{9,9},{10,12... | collective-permute-start | bytes 1769480 | tf_op jit(solution)/shard_map/ppermute | solution.py:42
  19.1 3.1 collective-permute-start.1
  31.9 9.9 %collective-permute-done.1 = bf16[384,768]{1,0:T(8,128)(2,1)S(1)} collective-permute-done((bf16[384,768]{1,0:T(8,128)(2,1)}, bf16[384,768]{1,0:T(8,128)(2,1)S(1)}, u32[]{:S(2)}, u32[]{:S(2)}) %collective-permute-start.1) | collective-permute-done | bytes 589856 | tf_op jit(solution)/shard_map/ppermute | solution.py:42
  48.8 2.9 collective-permute-start.11
  53.9 13.8 %collective-permute-done.10.refs_2_ = bf16[192,1280]{1,0:T(8,128)(2,1)S(1)} collective-permute-done((bf16[192,1280]{1,0:T(8,128)(2,1)S(1)}, bf16[192,1280]{1,0:T(8,128)(2,1)S(1)}, u32[]{:S(2)}, u32[]{:S(2)}) %collective-permute-start.10) | collective-permute-done | bytes 491552 | tf_op jit(solution)/shard_map/ppermute | solution.py:42
  69.7 2.9 place.2
  75.6 5.2 %collective-permute-start.14 = (f32[8,128]{1,0:T(8,128)S(1)}, f32[8,128]{1,0:T(8,128)S(1)}, u32[]{:S(2)}, u32[]{:S(2)}) collective-permute-start(f32[8,128]{1,0:T(8,128)S(1)} %add.329), channel_id=1, source_target_pairs={{0,1},{1,0},{2,3},{3,2},{4,5},{5,4},{6,7},{7,6},{8,9},{9,8},{10,11... | collective-permute-start | bytes 12296 | tf_op jit(solution)/shard_map/ppermute | solution.py:42
  82.5 8.9 %collective-permute-done.13 = bf16[400,768]{1,0:T(8,128)(2,1)S(1)} collective-permute-done((bf16[400,768]{1,0:T(8,128)(2,1)S(1)}, bf16[400,768]{1,0:T(8,128)(2,1)S(1)}, u32[]{:S(2)}, u32[]{:S(2)}) %collective-permute-start.13) | collective-permute-done | bytes 614432 | tf_op jit(solution)/shard_map/ppermute | solution.py:42
  97.9 5.4 %collective-permute-start.20 = (f32[8,128]{1,0:T(8,128)S(1)}, f32[8,128]{1,0:T(8,128)S(1)}, u32[]{:S(2)}, u32[]{:S(2)}) collective-permute-start(f32[8,128]{1,0:T(8,128)S(1)} %add.334), channel_id=1, source_target_pairs={{0,2},{1,3},{2,0},{3,1},{4,6},{5,7},{6,4},{7,5},{8,10},{9,11},{10,... | collective-permute-start | bytes 12296 | tf_op jit(solution)/shard_map/ppermute | solution.py:42
  104.6 2.2 collective-permute-start.18
  108.6 5.8 %convolution_convert_fusion.q_ref.k_ref.v_ref = bf16[1536,1152]{1,0:T(8,128)(2,1)} fusion(bf16[768,1152]{1,0:T(8,128)(2,1)S(1)} %copy-done.57, bf16[768,768]{1,0:T(8,128)(2,1)S(1)} %copy-done.60, bf16[768,768]{1,0:T(8,128)(2,1)S(1)} %copy-done.16), kind=kOutput, calls=%fused_computation | convolution fusion | flops 2724397056 | bytes 7667712 | tf_op jit(solution)/shard_map/dot_general | solution.py:27
  114.3 29.6 %attention_forward.1 = (bf16[1536,384]{1,0:T(8,128)(2,1)}, f32[3,2,1536]{2,1,0:T(2,128)}) custom-call(s32[2]{0:T(128)} %add_clamp_fusion.counts_ref, bf16[1536,1152]{1,0:T(8,128)(2,1)} %convolution_convert_fusion.q_ref.k_ref.v_ref, bf16[1536,1152]{1,0:T(8,128)(2,1)} %convolution_convert_fusion.q_ref.k_ref.v_ref, ...), custom_call_target="tpu_custom_call" | custom-call | flops 1 | bytes 1 | tf_op jit(solution)/shard_map/attention_forward/pallas_call | solution.py:254
  144.6 14.8 %collective-permute-done.16.refs_2_ = bf16[960,768]{1,0:T(8,128)(2,1)} collective-permute-done((bf16[960,768]{1,0:T(8,128)(2,1)}, bf16[960,768]{1,0:T(8,128)(2,1)}, u32[]{:S(2)}, u32[]{:S(2)}) %collective-permute-start.16) | collective-permute-done | bytes 1474592 | tf_op jit(solution)/shard_map/ppermute | solution.py:42
  160.6 5.7 %place.3 = (bf16[1536,768]{1,0:T(8,128)(2,1)}, bf16[768,1536]{1,0:T(8,128)(2,1)}, bf16[768,768]{1,0:T(8,128)(2,1)}) custom-call(s32[1]{0:T(128)} %bitcast.24.p_ref, bf16[960,768]{1,0:T(8,128)(2,1)} %select_dynamic-update-slice_fusion.refs_0_, bf16[960,768]{1,0:T(8,128)(2,1)} %collective-permute-done.15.refs_1_, ...), custom_call_target="tpu_custom_call" | custom-call | tf_op jit(solution)/shard_map/place/pallas_call | solution.py:149
  171.8 2.5 collective-permute-done.22
  174.3 3.9 multiply_convert_fusion.2
  178.1 3.0 convolution_convert_fusion.4
  183.9 4.0 multiply_convert_fusion.3
  188.0 5.5 %convert_add_fusion.2 = f32[768,768]{1,0:T(8,128)} fusion(bf16[768,768]{1,0:T(8,128)(2,1)} %collective-permute-done.23, f32[768,768]{1,0:T(8,128)S(1)} %get-tuple-element.338, bf16[768,1536]{1,0:T(8,128)(2,1)S(1)} %get-tuple-element.341, bf16[1536,768]{1,0:T(8,128)(2,1)S(1)} %copy-done.55), kind=kOutput, calls=%fused_computation.69 | convolution fusion | flops 1813708800 | bytes 10616832 | tf_op jit(solution)/shard_map/dot_general | solution.py:27
  201.0 2.4 multiply_convert_fusion.4
  203.7 3.9 fusion.94
  207.7 4.0 multiply_convert_fusion.1
  211.7 2.3 add_convert_fusion.1
  214.0 4.2 multiply_convert_fusion
  218.3 2.0 convolution_convert_fusion.3
  225.3 2.0 fusion.95
  227.3 2.2 add_convert_fusion
  229.6 3.2 multiply_reduce_fusion
  232.8 2.8 fusion.32
  242.0 5.5 %collective-permute-start.31 = (bf16[384,768]{1,0:T(8,128)(2,1)}, bf16[384,768]{1,0:T(8,128)(2,1)}, u32[]{:S(2)}, u32[]{:S(2)}) collective-permute-start(bf16[384,768]{1,0:T(8,128)(2,1)} %get-tuple-element.280), channel_id=1, source_target_pairs={{0,1},{1,0},{2,5},{3,4},{4,3},{5,2},{6,7},{7,6},{8,9},{9,8},{10,13... | collective-permute-start | bytes 1769480 | tf_op jit(solution)/shard_map/ppermute | solution.py:42
  254.6 16.8 %attention_backward.3 = bf16[1536,384]{1,0:T(8,128)(2,1)} custom-call(s32[2]{0:T(128)} %add_clamp_fusion.counts_ref, bf16[1536,1152]{1,0:T(8,128)(2,1)} %convolution_convert_fusion.q_ref.k_ref.v_ref, bf16[1536,1152]{1,0:T(8,128)(2,1)} %convolution_convert_fusion.q_ref.k_ref.v_ref, bf16[1536,1152]{1,0:T(8,128)(2,1)} %convolution_convert_fusion.q_ref.k_ref.v_ref, ...), custom_call_target="tpu_custom_call" | custom-call | flops 1 | bytes 1 | tf_op jit(solution)/shard_map/attention_backward/pallas_call | solution.py:333
  274.2 5.3 %collective-permute-start.32 = (bf16[192,768]{1,0:T(8,128)(2,1)}, bf16[192,768]{1,0:T(8,128)(2,1)}, u32[]{:S(2)}, u32[]{:S(2)}) collective-permute-start(bf16[192,768]{1,0:T(8,128)(2,1)} %get-tuple-element.301), channel_id=1, source_target_pairs={{0,1},{1,0},{2,3},{3,2},{4,5},{5,4},{6,7},{7,6},{8,9},{9,8},{10,11... | collective-permute-start | bytes 884744 | tf_op jit(solution)/shard_map/ppermute | solution.py:42
  281.7 17.1 %attention_backward.4 = bf16[1536,384]{1,0:T(8,128)(2,1)} custom-call(s32[2]{0:T(128)} %add_clamp_fusion.counts_ref, bf16[1536,1152]{1,0:T(8,128)(2,1)} %convolution_convert_fusion.q_ref.k_ref.v_ref, bf16[1536,1152]{1,0:T(8,128)(2,1)} %convolution_convert_fusion.q_ref.k_ref.v_ref, bf16[1536,1152]{1,0:T(8,128)(2,1)} %convolution_convert_fusion.q_ref.k_ref.v_ref, ...), custom_call_target="tpu_custom_call" | custom-call | flops 1 | bytes 1 | tf_op jit(solution)/shard_map/attention_backward/pallas_call | solution.py:333
  298.8 4.0 fusion.37
  307.3 2.1 add_convert_fusion.3
  314.4 16.6 %attention_backward.5 = bf16[1536,384]{1,0:T(8,128)(2,1)} custom-call(s32[2]{0:T(128)} %add_clamp_fusion.counts_ref, bf16[1536,1152]{1,0:T(8,128)(2,1)} %convolution_convert_fusion.q_ref.k_ref.v_ref, bf16[1536,1152]{1,0:T(8,128)(2,1)} %convolution_convert_fusion.q_ref.k_ref.v_ref, bf16[1536,1152]{1,0:T(8,128)(2,1)} %convolution_convert_fusion.q_ref.k_ref.v_ref, ...), custom_call_target="tpu_custom_call" | custom-call | flops 1 | bytes 1 | tf_op jit(solution)/shard_map/attention_backward/pallas_call | solution.py:333
  331.1 3.5 convolution_convert_fusion.5
  334.7 3.3 fusion.10
  350.8 2.0 collective-permute-start.45
  353.0 6.0 %collective-permute-done.50 = bf16[48,2304]{1,0:T(8,128)(2,1)S(1)} collective-permute-done((bf16[48,2304]{1,0:T(8,128)(2,1)S(1)}, bf16[48,2304]{1,0:T(8,128)(2,1)S(1)}, u32[]{:S(2)}, u32[]{:S(2)}) %collective-permute-start.50) | collective-permute-done | bytes 221216 | tf_op jit(solution)/shard_map/ppermute | solution.py:42
  364.2 2.6 collective-permute-start.49
  366.9 4.3 collective-permute-start.48
  372.4 23.7 %collective-permute-done.48 = bf16[48,1152]{1,0:T(8,128)(2,1)S(1)} collective-permute-done((bf16[48,1152]{1,0:T(8,128)(2,1)S(1)}, bf16[48,1152]{1,0:T(8,128)(2,1)S(1)}, u32[]{:S(2)}, u32[]{:S(2)}) %collective-permute-start.48) | collective-permute-done | bytes 110624 | tf_op jit(solution)/shard_map/ppermute | solution.py:42
  396.1 3.0 collective-permute-start.54
  399.3 2.1 collective-permute-start.58
  401.4 3.4 collective-permute-done.55
  410.6 10.1 %collective-permute-done.57 = bf16[96,1152]{1,0:T(8,128)(2,1)S(1)} collective-permute-done((bf16[96,1152]{1,0:T(8,128)(2,1)S(1)}, bf16[96,1152]{1,0:T(8,128)(2,1)S(1)}, u32[]{:S(2)}, u32[]{:S(2)}) %collective-permute-start.57) | collective-permute-done | bytes 221216 | tf_op jit(solution)/shard_map/ppermute | solution.py:42
  (399 shorter events, 130.5 us)
Async XLA Ops:
  2.9 20.1 %collective-permute-start.2 = (bf16[288,768]{1,0:T(8,128)(2,1)}, bf16[288,768]{1,0:T(8,128)(2,1)}, u32[]{:S(2)}, u32[]{:S(2)}) collective-permute-start(bf16[288,768]{1,0:T(8,128)(2,1)} %pad_maximum_fusion.15), channel_id=1, source_target_pairs={{0,4},{1,5},{2,6},{3,7},{4,0},{5,1},{6,2},{7,3},{8,12},{9,13},{10,... | collective-permute-start | bytes 1327112 | tf_op jit(solution)/shard_map/ppermute | solution.py:42
  4.9 14.2 %collective-permute-start.5 = (f32[8,128]{1,0:T(8,128)S(1)}, f32[8,128]{1,0:T(8,128)S(1)}, u32[]{:S(2)}, u32[]{:S(2)}) collective-permute-start(f32[8,128]{1,0:T(8,128)S(1)} %broadcast_in_dim.82), channel_id=1, source_target_pairs={{0,4},{1,5},{2,6},{3,7},{4,0},{5,1},{6,2},{7,3},{8,12},{9,13},{10,... | collective-permute-start | bytes 12296 | tf_op jit(solution)/shard_map/ppermute | solution.py:42
  7.4 20.2 %collective-permute-start.4 = (bf16[400,768]{1,0:T(8,128)(2,1)}, bf16[400,768]{1,0:T(8,128)(2,1)}, u32[]{:S(2)}, u32[]{:S(2)}) collective-permute-start(bf16[400,768]{1,0:T(8,128)(2,1)} %fusion.49), channel_id=1, source_target_pairs={{0,4},{1,5},{2,6},{3,7},{4,0},{5,1},{6,2},{7,3},{8,12},{9,13},{10,... | collective-permute-start | bytes 1843208 | tf_op jit(solution)/shard_map/ppermute | solution.py:42
  8.6 14.3 %collective-permute-start.3 = (bf16[96,1280]{1,0:T(8,128)(2,1)S(1)}, bf16[96,1280]{1,0:T(8,128)(2,1)S(1)}, u32[]{:S(2)}, u32[]{:S(2)}) collective-permute-start(bf16[96,1280]{1,0:T(8,128)(2,1)S(1)} %bitcast.213), channel_id=1, source_target_pairs={{0,4},{1,5},{2,6},{3,7},{4,0},{5,1},{6,2},{7,3},{8,12},{9,13},{10,... | collective-permute-start | bytes 737288 | tf_op jit(solution)/shard_map/ppermute | solution.py:42
  11.1 20.8 %collective-permute-start = (bf16[384,768]{1,0:T(8,128)(2,1)}, bf16[384,768]{1,0:T(8,128)(2,1)}, u32[]{:S(2)}, u32[]{:S(2)}) collective-permute-start(bf16[384,768]{1,0:T(8,128)(2,1)} %get-tuple-element.286), channel_id=1, source_target_pairs={{0,0},{1,1},{2,4},{3,5},{4,2},{5,3},{6,6},{7,7},{8,8},{9,9},{10,12... | collective-permute-start | bytes 1769480 | tf_op jit(solution)/shard_map/ppermute | solution.py:42
  19.1 22.7 %collective-permute-start.1 = (bf16[384,768]{1,0:T(8,128)(2,1)}, bf16[384,768]{1,0:T(8,128)(2,1)S(1)}, u32[]{:S(2)}, u32[]{:S(2)}) collective-permute-start(bf16[384,768]{1,0:T(8,128)(2,1)} %get-tuple-element.287), channel_id=1, source_target_pairs={{0,1},{1,0},{2,5},{3,4},{4,3},{5,2},{6,7},{7,6},{8,9},{9,8},{10,13... | collective-permute-start | bytes 1769480 | tf_op jit(solution)/shard_map/ppermute | solution.py:42
  28.7 17.9 %collective-permute-start.6 = (bf16[400,768]{1,0:T(8,128)(2,1)S(1)}, bf16[400,768]{1,0:T(8,128)(2,1)S(1)}, u32[]{:S(2)}, u32[]{:S(2)}) collective-permute-start(bf16[400,768]{1,0:T(8,128)(2,1)S(1)} %get-tuple-element.261), channel_id=1, source_target_pairs={{0,8},{1,9},{2,10},{3,11},{4,12},{5,13},{6,14},{7,15},{8,0},{9,1},... | collective-permute-start | bytes 1843208 | tf_op jit(solution)/shard_map/ppermute | solution.py:42
  48.8 18.9 %collective-permute-start.10 = (bf16[192,1280]{1,0:T(8,128)(2,1)S(1)}, bf16[192,1280]{1,0:T(8,128)(2,1)S(1)}, u32[]{:S(2)}, u32[]{:S(2)}) collective-permute-start(bf16[192,1280]{1,0:T(8,128)(2,1)S(1)} %pad_maximum_fusion.14.refs_0_), channel_id=1, source_target_pairs={{0,16},{1,17},{2,18},{3,19},{4,20},{5,21},{6,22},{7,23},{8,24},{9,... | collective-permute-start | bytes 1474568 | tf_op jit(solution)/shard_map/ppermute | solution.py:42
  48.8 18.9 %collective-permute-start.11 = (bf16[192,1280]{1,0:T(8,128)(2,1)S(1)}, bf16[192,1280]{1,0:T(8,128)(2,1)S(1)}, u32[]{:S(2)}, u32[]{:S(2)}) collective-permute-start(bf16[192,1280]{1,0:T(8,128)(2,1)S(1)} %pad_maximum_fusion.14.refs_0_), channel_id=1, source_target_pairs={{0,24},{1,25},{2,26},{3,27},{4,28},{5,29},{6,30},{7,31},{8,16},{9,... | collective-permute-start | bytes 1474568 | tf_op jit(solution)/shard_map/ppermute | solution.py:42
  51.8 17.1 %collective-permute-start.9 = (bf16[192,1280]{1,0:T(8,128)(2,1)S(1)}, bf16[192,1280]{1,0:T(8,128)(2,1)S(1)}, u32[]{:S(2)}, u32[]{:S(2)}) collective-permute-start(bf16[192,1280]{1,0:T(8,128)(2,1)S(1)} %pad_maximum_fusion.14.refs_0_), channel_id=1, source_target_pairs={{0,8},{1,9},{2,10},{3,11},{4,12},{5,13},{6,14},{7,15},{8,0},{9,1},... | collective-permute-start | bytes 1474568 | tf_op jit(solution)/shard_map/ppermute | solution.py:42
  74.8 16.6 %collective-permute-start.12 = (bf16[768,768]{1,0:T(8,128)(2,1)S(1)}, bf16[768,768]{1,0:T(8,128)(2,1)S(1)}, u32[]{:S(2)}, u32[]{:S(2)}) collective-permute-start(bf16[768,768]{1,0:T(8,128)(2,1)S(1)} %fusion.24), channel_id=1, source_target_pairs={{0,4},{1,5},{2,6},{3,7},{4,0},{5,1},{6,2},{7,3},{8,12},{9,13},{10,... | collective-permute-start | bytes 3538952 | tf_op jit(solution)/shard_map/ppermute | solution.py:42
  75.1 16.3 %collective-permute-start.13 = (bf16[400,768]{1,0:T(8,128)(2,1)S(1)}, bf16[400,768]{1,0:T(8,128)(2,1)S(1)}, u32[]{:S(2)}, u32[]{:S(2)}) collective-permute-start(bf16[400,768]{1,0:T(8,128)(2,1)S(1)} %get-tuple-element.258), channel_id=1, source_target_pairs={{0,16},{1,17},{2,18},{3,19},{4,20},{5,21},{6,22},{7,23},{8,24},{9,... | collective-permute-start | bytes 1843208 | tf_op jit(solution)/shard_map/ppermute | solution.py:42
  92.4 52.2 %collective-permute-start.15 = (bf16[960,768]{1,0:T(8,128)(2,1)}, bf16[960,768]{1,0:T(8,128)(2,1)}, u32[]{:S(2)}, u32[]{:S(2)}) collective-permute-start(bf16[960,768]{1,0:T(8,128)(2,1)} %select_dynamic-update-slice_fusion.refs_0_), channel_id=1, source_target_pairs={{0,8},{1,9},{2,10},{3,11},{4,12},{5,13},{6,14},{7,15},{8,0},{9,1},... | collective-permute-start | bytes 4423688 | tf_op jit(solution)/shard_map/ppermute | solution.py:42
  93.9 65.5 %collective-permute-start.16 = (bf16[960,768]{1,0:T(8,128)(2,1)}, bf16[960,768]{1,0:T(8,128)(2,1)}, u32[]{:S(2)}, u32[]{:S(2)}) collective-permute-start(bf16[960,768]{1,0:T(8,128)(2,1)} %select_dynamic-update-slice_fusion.refs_0_), channel_id=1, source_target_pairs={{0,16},{1,17},{2,18},{3,19},{4,20},{5,21},{6,22},{7,23},{8,24},{9,... | collective-permute-start | bytes 4423688 | tf_op jit(solution)/shard_map/ppermute | solution.py:42
  94.4 65.0 %collective-permute-start.17 = (bf16[960,768]{1,0:T(8,128)(2,1)}, bf16[960,768]{1,0:T(8,128)(2,1)}, u32[]{:S(2)}, u32[]{:S(2)}) collective-permute-start(bf16[960,768]{1,0:T(8,128)(2,1)} %select_dynamic-update-slice_fusion.refs_0_), channel_id=1, source_target_pairs={{0,24},{1,25},{2,26},{3,27},{4,28},{5,29},{6,30},{7,31},{8,16},{9,... | collective-permute-start | bytes 4423688 | tf_op jit(solution)/shard_map/ppermute | solution.py:42
  97.9 9.0 %collective-permute-start.20 = (f32[8,128]{1,0:T(8,128)S(1)}, f32[8,128]{1,0:T(8,128)S(1)}, u32[]{:S(2)}, u32[]{:S(2)}) collective-permute-start(f32[8,128]{1,0:T(8,128)S(1)} %add.334), channel_id=1, source_target_pairs={{0,2},{1,3},{2,0},{3,1},{4,6},{5,7},{6,4},{7,5},{8,10},{9,11},{10,... | collective-permute-start | bytes 12296 | tf_op jit(solution)/shard_map/ppermute | solution.py:42
  104.6 39.9 %collective-permute-start.18 = (bf16[400,768]{1,0:T(8,128)(2,1)}, bf16[400,768]{1,0:T(8,128)(2,1)S(1)}, u32[]{:S(2)}, u32[]{:S(2)}) collective-permute-start(bf16[400,768]{1,0:T(8,128)(2,1)} %get-tuple-element.269), channel_id=1, source_target_pairs={{0,0},{1,1},{2,4},{3,5},{4,2},{5,3},{6,6},{7,7},{8,8},{9,9},{10,12... | collective-permute-start | bytes 1843208 | tf_op jit(solution)/shard_map/ppermute | solution.py:42
  106.8 37.7 %collective-permute-start.19 = (bf16[400,768]{1,0:T(8,128)(2,1)S(1)}, bf16[400,768]{1,0:T(8,128)(2,1)S(1)}, u32[]{:S(2)}, u32[]{:S(2)}) collective-permute-start(bf16[400,768]{1,0:T(8,128)(2,1)S(1)} %get-tuple-element.268), channel_id=1, source_target_pairs={{0,1},{1,0},{2,5},{3,4},{4,3},{5,2},{6,7},{7,6},{8,9},{9,8},{10,13... | collective-permute-start | bytes 1843208 | tf_op jit(solution)/shard_map/ppermute | solution.py:42
  220.3 9.2 %collective-permute-start.25 = (bf16[768,768]{1,0:T(8,128)(2,1)S(1)}, bf16[768,768]{1,0:T(8,128)(2,1)S(1)}, u32[]{:S(2)}, u32[]{:S(2)}) collective-permute-start(bf16[768,768]{1,0:T(8,128)(2,1)S(1)} %convolution_convert_fusion.3), channel_id=1, source_target_pairs={{0,4},{1,5},{2,6},{3,7},{4,0},{5,1},{6,2},{7,3},{8,12},{9,13},{10,... | collective-permute-start | bytes 3538952 | tf_op jit(solution)/shard_map/ppermute | solution.py:42
  221.8 20.2 %collective-permute-start.27 = (bf16[384,768]{1,0:T(8,128)(2,1)S(1)}, bf16[384,768]{1,0:T(8,128)(2,1)S(1)}, u32[]{:S(2)}, u32[]{:S(2)}) collective-permute-start(bf16[384,768]{1,0:T(8,128)(2,1)S(1)} %get-tuple-element.254), channel_id=1, source_target_pairs={{0,8},{1,9},{2,10},{3,11},{4,12},{5,13},{6,14},{7,15},{8,0},{9,1},... | collective-permute-start | bytes 1769480 | tf_op jit(solution)/shard_map/ppermute | solution.py:42
  222.3 27.7 %collective-permute-start.28 = (bf16[384,768]{1,0:T(8,128)(2,1)S(1)}, bf16[384,768]{1,0:T(8,128)(2,1)S(1)}, u32[]{:S(2)}, u32[]{:S(2)}) collective-permute-start(bf16[384,768]{1,0:T(8,128)(2,1)S(1)} %get-tuple-element.253), channel_id=1, source_target_pairs={{0,16},{1,17},{2,18},{3,19},{4,20},{5,21},{6,22},{7,23},{8,24},{9,... | collective-permute-start | bytes 1769480 | tf_op jit(solution)/shard_map/ppermute | solution.py:42
  223.5 28.0 %collective-permute-start.29 = (bf16[384,768]{1,0:T(8,128)(2,1)S(1)}, bf16[384,768]{1,0:T(8,128)(2,1)S(1)}, u32[]{:S(2)}, u32[]{:S(2)}) collective-permute-start(bf16[384,768]{1,0:T(8,128)(2,1)S(1)} %get-tuple-element.252), channel_id=1, source_target_pairs={{0,24},{1,25},{2,26},{3,27},{4,28},{5,29},{6,30},{7,31},{8,16},{9,... | collective-permute-start | bytes 1769480 | tf_op jit(solution)/shard_map/ppermute | solution.py:42
  236.9 15.1 %collective-permute-start.26 = (bf16[768,384]{1,0:T(8,128)(2,1)S(1)}, bf16[768,384]{1,0:T(8,128)(2,1)S(1)}, u32[]{:S(2)}, u32[]{:S(2)}) collective-permute-start(bf16[768,384]{1,0:T(8,128)(2,1)S(1)} %get-tuple-element.283), channel_id=1, source_target_pairs={{0,4},{1,5},{2,6},{3,7},{4,0},{5,1},{6,2},{7,3},{8,12},{9,13},{10,... | collective-permute-start | bytes 1769480 | tf_op jit(solution)/shard_map/ppermute | solution.py:42
  240.3 31.2 %collective-permute-start.30 = (bf16[384,768]{1,0:T(8,128)(2,1)}, bf16[384,768]{1,0:T(8,128)(2,1)S(1)}, u32[]{:S(2)}, u32[]{:S(2)}) collective-permute-start(bf16[384,768]{1,0:T(8,128)(2,1)} %get-tuple-element.281), channel_id=1, source_target_pairs={{0,0},{1,1},{2,4},{3,5},{4,2},{5,3},{6,6},{7,7},{8,8},{9,9},{10,12... | collective-permute-start | bytes 1769480 | tf_op jit(solution)/shard_map/ppermute | solution.py:42
  242.0 29.5 %collective-permute-start.31 = (bf16[384,768]{1,0:T(8,128)(2,1)}, bf16[384,768]{1,0:T(8,128)(2,1)}, u32[]{:S(2)}, u32[]{:S(2)}) collective-permute-start(bf16[384,768]{1,0:T(8,128)(2,1)} %get-tuple-element.280), channel_id=1, source_target_pairs={{0,1},{1,0},{2,5},{3,4},{4,3},{5,2},{6,7},{7,6},{8,9},{9,8},{10,13... | collective-permute-start | bytes 1769480 | tf_op jit(solution)/shard_map/ppermute | solution.py:42
  250.0 48.7 %collective-permute-start.33 = (bf16[192,2304]{1,0:T(8,128)(2,1)}, bf16[192,2304]{1,0:T(8,128)(2,1)}, u32[]{:S(2)}, u32[]{:S(2)}) collective-permute-start(bf16[192,2304]{1,0:T(8,128)(2,1)} %get-tuple-element.249), channel_id=1, source_target_pairs={{0,8},{1,9},{2,10},{3,11},{4,12},{5,13},{6,14},{7,15},{8,0},{9,1},... | collective-permute-start | bytes 2654216 | tf_op jit(solution)/shard_map/ppermute | solution.py:42
  251.5 47.3 %collective-permute-start.34 = (bf16[192,2304]{1,0:T(8,128)(2,1)}, bf16[192,2304]{1,0:T(8,128)(2,1)}, u32[]{:S(2)}, u32[]{:S(2)}) collective-permute-start(bf16[192,2304]{1,0:T(8,128)(2,1)} %get-tuple-element.250), channel_id=1, source_target_pairs={{0,16},{1,17},{2,18},{3,19},{4,20},{5,21},{6,22},{7,23},{8,24},{9,... | collective-permute-start | bytes 2654216 | tf_op jit(solution)/shard_map/ppermute | solution.py:42
  252.0 46.8 %collective-permute-start.35 = (bf16[192,2304]{1,0:T(8,128)(2,1)}, bf16[192,2304]{1,0:T(8,128)(2,1)}, u32[]{:S(2)}, u32[]{:S(2)}) collective-permute-start(bf16[192,2304]{1,0:T(8,128)(2,1)} %get-tuple-element.247), channel_id=1, source_target_pairs={{0,24},{1,25},{2,26},{3,27},{4,28},{5,29},{6,30},{7,31},{8,16},{9,... | collective-permute-start | bytes 2654216 | tf_op jit(solution)/shard_map/ppermute | solution.py:42
  274.2 24.6 %collective-permute-start.32 = (bf16[192,768]{1,0:T(8,128)(2,1)}, bf16[192,768]{1,0:T(8,128)(2,1)}, u32[]{:S(2)}, u32[]{:S(2)}) collective-permute-start(bf16[192,768]{1,0:T(8,128)(2,1)} %get-tuple-element.301), channel_id=1, source_target_pairs={{0,1},{1,0},{2,3},{3,2},{4,5},{5,4},{6,7},{7,6},{8,9},{9,8},{10,11... | collective-permute-start | bytes 884744 | tf_op jit(solution)/shard_map/ppermute | solution.py:42
  303.8 27.3 %collective-permute-start.38 = (bf16[192,768]{1,0:T(8,128)(2,1)}, bf16[192,768]{1,0:T(8,128)(2,1)}, u32[]{:S(2)}, u32[]{:S(2)}) collective-permute-start(bf16[192,768]{1,0:T(8,128)(2,1)} %get-tuple-element.276), channel_id=1, source_target_pairs={{0,8},{1,9},{2,10},{3,11},{4,12},{5,13},{6,14},{7,15},{8,0},{9,1},... | collective-permute-start | bytes 884744 | tf_op jit(solution)/shard_map/ppermute | solution.py:42
  305.1 25.9 %collective-permute-start.39 = (bf16[192,768]{1,0:T(8,128)(2,1)}, bf16[192,768]{1,0:T(8,128)(2,1)}, u32[]{:S(2)}, u32[]{:S(2)}) collective-permute-start(bf16[192,768]{1,0:T(8,128)(2,1)} %get-tuple-element.275), channel_id=1, source_target_pairs={{0,16},{1,17},{2,18},{3,19},{4,20},{5,21},{6,22},{7,23},{8,24},{9,... | collective-permute-start | bytes 884744 | tf_op jit(solution)/shard_map/ppermute | solution.py:42
  306.1 25.0 %collective-permute-start.40 = (bf16[192,768]{1,0:T(8,128)(2,1)}, bf16[192,768]{1,0:T(8,128)(2,1)}, u32[]{:S(2)}, u32[]{:S(2)}) collective-permute-start(bf16[192,768]{1,0:T(8,128)(2,1)} %get-tuple-element.274), channel_id=1, source_target_pairs={{0,24},{1,25},{2,26},{3,27},{4,28},{5,29},{6,30},{7,31},{8,16},{9,... | collective-permute-start | bytes 884744 | tf_op jit(solution)/shard_map/ppermute | solution.py:42
  310.2 20.8 %collective-permute-start.37 = (bf16[96,2304]{1,0:T(8,128)(2,1)}, bf16[96,2304]{1,0:T(8,128)(2,1)}, u32[]{:S(2)}, u32[]{:S(2)}) collective-permute-start(bf16[96,2304]{1,0:T(8,128)(2,1)} %get-tuple-element.290), channel_id=1, source_target_pairs={{0,1},{1,0},{2,3},{3,2},{4,5},{5,4},{6,7},{7,6},{8,9},{9,8},{10,11... | collective-permute-start | bytes 1327112 | tf_op jit(solution)/shard_map/ppermute | solution.py:42
  311.3 19.7 %collective-permute-start.36 = (bf16[96,768]{1,0:T(8,128)(2,1)S(1)}, bf16[96,768]{1,0:T(8,128)(2,1)S(1)}, u32[]{:S(2)}, u32[]{:S(2)}) collective-permute-start(bf16[96,768]{1,0:T(8,128)(2,1)S(1)} %get-tuple-element.323), channel_id=1, source_target_pairs={{0,2},{1,3},{2,0},{3,1},{4,6},{5,7},{6,4},{7,5},{8,10},{9,11},{10,... | collective-permute-start | bytes 442376 | tf_op jit(solution)/shard_map/ppermute | solution.py:42
  338.1 21.1 %collective-permute-start.46 = (bf16[768,768]{1,0:T(8,128)(2,1)S(1)}, bf16[768,768]{1,0:T(8,128)(2,1)S(1)}, u32[]{:S(2)}, u32[]{:S(2)}) collective-permute-start(bf16[768,768]{1,0:T(8,128)(2,1)S(1)} %slice.320), channel_id=1, source_target_pairs={{0,4},{1,5},{2,6},{3,7},{4,0},{5,1},{6,2},{7,3},{8,12},{9,13},{10,... | collective-permute-start | bytes 3538952 | tf_op jit(solution)/shard_map/ppermute | solution.py:42
  338.3 34.1 %collective-permute-start.52 = (bf16[96,768]{1,0:T(8,128)(2,1)S(1)}, bf16[96,768]{1,0:T(8,128)(2,1)S(1)}, u32[]{:S(2)}, u32[]{:S(2)}) collective-permute-start(bf16[96,768]{1,0:T(8,128)(2,1)S(1)} %add_convert_fusion.8), channel_id=1, source_target_pairs={{0,2},{1,3},{2,0},{3,1},{4,6},{5,7},{6,4},{7,5},{8,10},{9,11},{10,... | collective-permute-start | bytes 442376 | tf_op jit(solution)/shard_map/ppermute | solution.py:42
  342.9 9.9 %collective-permute-start.43 = (bf16[192,384]{1,0:T(8,128)(2,1)S(1)}, bf16[192,384]{1,0:T(8,128)(2,1)S(1)}, u32[]{:S(2)}, u32[]{:S(2)}) collective-permute-start(bf16[192,384]{1,0:T(8,128)(2,1)S(1)} %get-tuple-element.299), channel_id=1, source_target_pairs={{0,24},{1,25},{2,26},{3,27},{4,28},{5,29},{6,30},{7,31},{8,16},{9,... | collective-permute-start | bytes 442376 | tf_op jit(solution)/shard_map/ppermute | solution.py:42
  347.3 11.7 %collective-permute-start.50 = (bf16[48,2304]{1,0:T(8,128)(2,1)S(1)}, bf16[48,2304]{1,0:T(8,128)(2,1)S(1)}, u32[]{:S(2)}, u32[]{:S(2)}) collective-permute-start(bf16[48,2304]{1,0:T(8,128)(2,1)S(1)} %dynamic-slice_bitcast_fusion.10), channel_id=1, source_target_pairs={{0,2},{1,3},{2,0},{3,1},{4,6},{5,7},{6,4},{7,5},{8,10},{9,11},{10,... | collective-permute-start | bytes 663560 | tf_op jit(solution)/shard_map/ppermute | solution.py:42
  350.8 13.4 %collective-permute-start.45 = (bf16[96,768]{1,0:T(8,128)(2,1)S(1)}, bf16[96,768]{1,0:T(8,128)(2,1)S(1)}, u32[]{:S(2)}, u32[]{:S(2)}) collective-permute-start(bf16[96,768]{1,0:T(8,128)(2,1)S(1)} %get-tuple-element.321), channel_id=1, source_target_pairs={{0,1},{1,0},{2,3},{3,2},{4,5},{5,4},{6,7},{7,6},{8,9},{9,8},{10,11... | collective-permute-start | bytes 442376 | tf_op jit(solution)/shard_map/ppermute | solution.py:42
  352.9 11.2 %collective-permute-start.44 = (bf16[96,384]{1,0:T(8,128)(2,1)S(1)}, bf16[96,384]{1,0:T(8,128)(2,1)S(1)}, u32[]{:S(2)}, u32[]{:S(2)}) collective-permute-start(bf16[96,384]{1,0:T(8,128)(2,1)S(1)} %get-tuple-element.331), channel_id=1, source_target_pairs={{0,1},{1,0},{2,3},{3,2},{4,5},{5,4},{6,7},{7,6},{8,9},{9,8},{10,11... | collective-permute-start | bytes 221192 | tf_op jit(solution)/shard_map/ppermute | solution.py:42
  359.1 13.2 %collective-permute-start.51 = (bf16[48,2304]{1,0:T(8,128)(2,1)S(1)}, bf16[48,2304]{1,0:T(8,128)(2,1)S(1)}, u32[]{:S(2)}, u32[]{:S(2)}) collective-permute-start(bf16[48,2304]{1,0:T(8,128)(2,1)S(1)} %fusion.56), channel_id=1, source_target_pairs={{0,2},{1,3},{2,0},{3,1},{4,6},{5,7},{6,4},{7,5},{8,10},{9,11},{10,... | collective-permute-start | bytes 663560 | tf_op jit(solution)/shard_map/ppermute | solution.py:42
  362.7 33.4 %collective-permute-start.53 = (bf16[384,768]{1,0:T(8,128)(2,1)S(1)}, bf16[384,768]{1,0:T(8,128)(2,1)S(1)}, u32[]{:S(2)}, u32[]{:S(2)}) collective-permute-start(bf16[384,768]{1,0:T(8,128)(2,1)S(1)} %get-tuple-element.273), channel_id=1, source_target_pairs={{0,0},{1,1},{2,4},{3,5},{4,2},{5,3},{6,6},{7,7},{8,8},{9,9},{10,12... | collective-permute-start | bytes 1769480 | tf_op jit(solution)/shard_map/ppermute | solution.py:42
  366.9 29.1 %collective-permute-start.48 = (bf16[48,1152]{1,0:T(8,128)(2,1)S(1)}, bf16[48,1152]{1,0:T(8,128)(2,1)S(1)}, u32[]{:S(2)}, u32[]{:S(2)}) collective-permute-start(bf16[48,1152]{1,0:T(8,128)(2,1)S(1)} %get-tuple-element.329), channel_id=1, source_target_pairs={{0,2},{1,3},{2,0},{3,1},{4,6},{5,7},{6,4},{7,5},{8,10},{9,11},{10,... | collective-permute-start | bytes 331784 | tf_op jit(solution)/shard_map/ppermute | solution.py:42
  372.3 32.5 %collective-permute-start.56 = (bf16[384,768]{1,0:T(8,128)(2,1)S(1)}, bf16[384,768]{1,0:T(8,128)(2,1)S(1)}, u32[]{:S(2)}, u32[]{:S(2)}) collective-permute-start(bf16[384,768]{1,0:T(8,128)(2,1)S(1)} %get-tuple-element.272), channel_id=1, source_target_pairs={{0,1},{1,0},{2,5},{3,4},{4,3},{5,2},{6,7},{7,6},{8,9},{9,8},{10,13... | collective-permute-start | bytes 1769480 | tf_op jit(solution)/shard_map/ppermute | solution.py:42
  396.1 9.8 %collective-permute-start.54 = (bf16[48,1152]{1,0:T(8,128)(2,1)S(1)}, bf16[48,1152]{1,0:T(8,128)(2,1)S(1)}, u32[]{:S(2)}, u32[]{:S(2)}) collective-permute-start(bf16[48,1152]{1,0:T(8,128)(2,1)S(1)} %add_convert_fusion.11), channel_id=1, source_target_pairs={{0,2},{1,3},{2,0},{3,1},{4,6},{5,7},{6,4},{7,5},{8,10},{9,11},{10,... | collective-permute-start | bytes 331784 | tf_op jit(solution)/shard_map/ppermute | solution.py:42
  399.2 11.4 %collective-permute-start.59 = (bf16[192,768]{1,0:T(8,128)(2,1)S(1)}, bf16[192,768]{1,0:T(8,128)(2,1)S(1)}, u32[]{:S(2)}, u32[]{:S(2)}) collective-permute-start(bf16[192,768]{1,0:T(8,128)(2,1)S(1)} %pad_maximum_fusion.21), channel_id=1, source_target_pairs={{0,1},{1,0},{2,3},{3,2},{4,5},{5,4},{6,7},{7,6},{8,9},{9,8},{10,11... | collective-permute-start | bytes 884744 | tf_op jit(solution)/shard_map/ppermute | solution.py:42
  399.3 21.4 %collective-permute-start.58 = (bf16[96,2304]{1,0:T(8,128)(2,1)S(1)}, bf16[96,2304]{1,0:T(8,128)(2,1)S(1)}, u32[]{:S(2)}, u32[]{:S(2)}) collective-permute-start(bf16[96,2304]{1,0:T(8,128)(2,1)S(1)} %pad_maximum_fusion.16), channel_id=1, source_target_pairs={{0,1},{1,0},{2,3},{3,2},{4,5},{5,4},{6,7},{7,6},{8,9},{9,8},{10,11... | collective-permute-start | bytes 1327112 | tf_op jit(solution)/shard_map/ppermute | solution.py:42
  407.4 13.3 %collective-permute-start.57 = (bf16[96,1152]{1,0:T(8,128)(2,1)S(1)}, bf16[96,1152]{1,0:T(8,128)(2,1)S(1)}, u32[]{:S(2)}, u32[]{:S(2)}) collective-permute-start(bf16[96,1152]{1,0:T(8,128)(2,1)S(1)} %pad_maximum_fusion.23), channel_id=1, source_target_pairs={{0,1},{1,0},{2,3},{3,2},{4,5},{5,4},{6,7},{7,6},{8,9},{9,8},{10,11... | collective-permute-start | bytes 663560 | tf_op jit(solution)/shard_map/ppermute | solution.py:42
  (88 other events, 425.3 us)

commit v7 on v4

--- a/solution.py
+++ b/solution.py
@@ -442,6 +442,7 @@
     keep = lax.dynamic_index_in_dim(shard, c, 0, keepdims=False)
     send = lax.dynamic_index_in_dim(shard, 1 - c, 0, keepdims=False)
     qkv_shard = in_order(keep, across_cores(send), 0)
+    down_sources, *down_args = gathered_over_pairs(down_weight)
     qkv_pieces = gathered_over_pairs(qkv_shard)
 
     x_rows = turned(tokens).reshape(rows, width)
@@ -489,21 +490,17 @@
     got = across_cores(jnp.concatenate([send[:, :width], send[:, width:], out_weight], axis=0))
     up_shard = in_order(keep, jnp.concatenate([got[:own_rows], got[own_rows : 2 * own_rows]], axis=1), 0)
     out_shard = in_order(out_weight, got[2 * own_rows :], 0)
-    payload = jnp.concatenate(
-        [down_weight, up_shard[:, :width], up_shard[:, width:], out_shard], axis=0
-    )
-    down_rows = down_weight.shape[0]
+    payload = jnp.concatenate([up_shard[:, :width], up_shard[:, width:], out_shard], axis=0)
     payload_plan = (
-        (0, 0, down_rows, 0, width, 0),
-        (1, down_rows, pair_rows, 0, width, 0),
-        (1, down_rows + pair_rows, pair_rows, 0, width, width),
-        (2, down_rows + 2 * pair_rows, pair_rows, 0, width, 0),
+        (0, 0, pair_rows, 0, width, 0),
+        (0, pair_rows, pair_rows, 0, width, width),
+        (1, 2 * pair_rows, pair_rows, 0, width, 0),
     )
     depth_steps, plane_steps = sum_steps()
-    for step in plane_steps[1:]:
+    x_rows, payload, tally, down_sources = tied(x_rows, payload, tally, down_sources)
+    payload_first = halves_first(payload)
+    for step in depth_steps:
         tally = tally + step(tally)
-    x_rows, payload, tally = tied(x_rows, payload, tally)
-    payload_first = halves_first(payload)
 
     x_full = x_rows.astype(FULL)
     unit_one, inverse_one = norm_parts(x_full)
@@ -518,21 +515,24 @@
     norm_one = jnp.concatenate([norm_mine, across_cores(norm_mine)], axis=0)
     norm_one, tally, deal = tied(norm_one, tally, deal)
     deal = dealt(settled(*deal), 1)
-    tally = tally + depth_steps[0](tally)
+    tally = tally + plane_steps[1](tally)
     qkv = dot(norm_one, w_qkv, NN).astype(LOW)
     qkv, deal, tally, payload_first = tied(qkv, deal, tally, payload_first)
     payload_pieces = halves_second(payload_first)
     for level in range(2, levels):
         deal = dealt(settled(*deal), level)
-    for step in depth_steps[1:]:
-        tally = tally + step(tally)
     mixed, lse = attention_forward(counts, qkv, 512)
 
     sources, *place_args = payload_pieces
     mixed, sources, deal, tally = tied(mixed, sources, deal, tally)
+    for step in plane_steps[2:]:
+        tally = tally + step(tally)
     mixed_got = across_cores(mixed[rows:])
     goal = turned(settled(*deal))
-    w_down, w_up, w_out = placed((sources, *place_args), payload_plan)
+    w_up, w_out = placed((sources, *place_args), payload_plan)
+    (w_down,) = placed(
+        (down_sources, *down_args), ((0, 0, down_weight.shape[0], 0, width, 0),)
+    )
 
     attended = in_order(mixed[:rows], mixed_got, 1)
     middle = x_full + dot(attended, w_out, NN)

time: 441 us -> 446 us (1.011)
  waiting for transfers between devices: 118 us -> 98.4 us
  starting transfers between devices: 79 us -> 96 us
    ppermute x65 -> x68, waiting for transfers between devices: 118 us -> 98.4 us  [moved(): return lax.ppermute(value, AXES, links)]
    ppermute x65 -> x68, starting transfers between devices: 79 us -> 96 us  [moved(): return lax.ppermute(value, AXES, links)]
    pallas_call x2 -> x3, Pallas kernels: 8.58 us -> 10.1 us  [placed(): pl.pallas_call(functools.partial(place_kernel, segments=segments, layout=...]
  transfers between devices with their start and end apart: 65 -> 68, of which waited for: 22 -> 19; matrix products, arithmetic and copies ran while one was open for 19% -> 21% of each run, Pallas kernels for 20% -> 20%
where the time goes in v7:
time: 446 us; the launch traced here: 440 us
  waiting for transfers between devices  98.4 us (22%)
  starting transfers between devices  96 us (22%)
  Pallas kernels  89.9 us (20%)
  matrix products  64.8 us (15%)
  other arithmetic  58.7 us (13%)
  local copies, waits for them, and re-layouts  24.8 us (6%)
  between operations  7.26 us (2%)
    ppermute x68, waiting for transfers between devices, moved(): return lax.ppermute(value, AXES, links)  98.4 us
    ppermute x68, starting transfers between devices, moved(): return lax.ppermute(value, AXES, links)  96 us
    dot_general x20, matrix products, dot(): return lax.dot_general(left, right, form, preferred_element_type=FULL)  64.8 us
    pallas_call x3, Pallas kernels, attention_backward(): pl.pallas_call(functools.partial(backward_kernel, rows=rows, block=block,...  50.2 us
    pallas_call x1, Pallas kernels, attention_forward(): pl.pallas_call(functools.partial(forward_kernel, rows=rows, block=block),...  29.6 us
    pallas_call x3, Pallas kernels, placed(): pl.pallas_call(functools.partial(place_kernel, segments=segments, layout=...  10.1 us
  transfers between devices with their start and end apart: 68, of which 19 were waited for; matrix products, arithmetic and copies ran while one was open for 21% of the time, Pallas kernels for 20%

profile of v7, /device:TPU:0, one launch (start us, length us, event | category | flops | bytes accessed | tf_op | source)
XLA Modules:
  0.0 439.9 jit_solution(6633106579426654095)
XLA Ops:
  0.6 3.0 collective-permute-start.4
  21.9 2.5 collective-permute-start.10
  24.4 11.5 %collective-permute-done.1 = bf16[384,768]{1,0:T(8,128)(2,1)S(1)} collective-permute-done((bf16[384,768]{1,0:T(8,128)(2,1)}, bf16[384,768]{1,0:T(8,128)(2,1)S(1)}, u32[]{:S(2)}, u32[]{:S(2)}) %collective-permute-start.1) | collective-permute-done | bytes 589856 | tf_op jit(solution)/shard_map/ppermute | solution.py:42
  40.5 9.5 %collective-permute-done.8.refs_1_ = bf16[192,1280]{1,0:T(8,128)(2,1)S(1)} collective-permute-done((bf16[192,1280]{1,0:T(8,128)(2,1)S(1)}, bf16[192,1280]{1,0:T(8,128)(2,1)S(1)}, u32[]{:S(2)}, u32[]{:S(2)}) %collective-permute-start.8) | collective-permute-done | bytes 491552 | tf_op jit(solution)/shard_map/ppermute | solution.py:42
  50.0 2.3 collective-permute-done.9.refs_2_
  53.1 2.9 place.3
  58.3 3.5 collective-permute-start.11
  63.3 3.3 collective-permute-start.12
  68.2 7.6 %collective-permute-start.13 = (f32[8,128]{1,0:T(8,128)S(1)}, f32[8,128]{1,0:T(8,128)S(1)}, u32[]{:S(2)}, u32[]{:S(2)}) collective-permute-start(f32[8,128]{1,0:T(8,128)S(1)} %add.332), channel_id=1, source_target_pairs={{0,2},{1,3},{2,0},{3,1},{4,6},{5,7},{6,4},{7,5},{8,10},{9,11},{10,... | collective-permute-start | bytes 12296 | tf_op jit(solution)/shard_map/ppermute | solution.py:42
  80.8 4.8 %convolution_convert_fusion.q_ref.k_ref.v_ref = bf16[1536,1152]{1,0:T(8,128)(2,1)} fusion(bf16[1536,768]{1,0:T(8,128)(2,1)S(1)} %pad_maximum_fusion, bf16[768,1152]{1,0:T(8,128)(2,1)S(1)} %copy-done.52), kind=kOutput, calls=%fused_computation | convolution fusion | flops 2719678464 | bytes 7667712 | tf_op jit(solution)/shard_map/dot_general | solution.py:27
  85.7 3.4 collective-permute-done.16
  89.7 10.5 %collective-permute-done.15 = bf16[400,768]{1,0:T(8,128)(2,1)S(1)} collective-permute-done((bf16[400,768]{1,0:T(8,128)(2,1)S(1)}, bf16[400,768]{1,0:T(8,128)(2,1)S(1)}, u32[]{:S(2)}, u32[]{:S(2)}) %collective-permute-start.15) | collective-permute-done | bytes 614432 | tf_op jit(solution)/shard_map/ppermute | solution.py:42
  108.8 29.6 %attention_forward.1 = (bf16[1536,384]{1,0:T(8,128)(2,1)}, f32[3,2,1536]{2,1,0:T(2,128)}) custom-call(s32[2]{0:T(128)} %add_clamp_fusion.counts_ref, bf16[1536,1152]{1,0:T(8,128)(2,1)} %convolution_convert_fusion.q_ref.k_ref.v_ref, bf16[1536,1152]{1,0:T(8,128)(2,1)} %convolution_convert_fusion.q_ref.k_ref.v_ref, ...), custom_call_target="tpu_custom_call" | custom-call | flops 1 | bytes 1 | tf_op jit(solution)/shard_map/attention_forward/pallas_call | solution.py:277
  138.4 2.4 pad_maximum_fusion.2
  141.7 4.0 place.4
  151.2 3.2 place.5
  156.6 5.3 %multiply_convert_fusion.2 = (bf16[768,1536]{1,0:T(8,128)(2,1)S(1)}, f32[768,1536]{1,0:T(8,128)}) fusion(bf16[768,768]{1,0:T(8,128)(2,1)} %collective-permute-done.23, bf16[768,1536]{1,0:T(8,128)(2,1)S(1)} %copy-done.50), kind=kOutput, calls=%fused_computation.21 | convolution fusion | flops 1817837568 | bytes 10616832 | tf_op jit(solution)/shard_map/dot_general | solution.py:27
  162.0 3.0 convolution_convert_fusion.4
  166.4 6.9 %collective-permute-start.25 = (bf16[400,768]{1,0:T(8,128)(2,1)}, bf16[400,768]{1,0:T(8,128)(2,1)}, u32[]{:S(2)}, u32[]{:S(2)}) collective-permute-start(bf16[400,768]{1,0:T(8,128)(2,1)} %get-tuple-element.270), channel_id=1, source_target_pairs={{0,0},{1,1},{2,4},{3,5},{4,2},{5,3},{6,6},{7,7},{8,8},{9,9},{10,12... | collective-permute-start | bytes 1843208 | tf_op jit(solution)/shard_map/ppermute | solution.py:42
  176.6 2.4 collective-permute-done.27
  180.3 6.3 %multiply_convert_fusion.3 = (bf16[768,1536]{1,0:T(8,128)(2,1)S(1)}, f32[768,1536]{1,0:T(8,128)}) fusion(bf16[768,768]{1,0:T(8,128)(2,1)} %add_convert_fusion.2, bf16[768,1536]{1,0:T(8,128)(2,1)} %get-tuple-element.126), kind=kOutput, calls=%fused_computation.23 | convolution fusion | flops 1817837568 | bytes 10616832 | tf_op jit(solution)/shard_map/dot_general | solution.py:27
  186.7 8.7 %collective-permute-done.26 = bf16[400,768]{1,0:T(8,128)(2,1)} collective-permute-done((bf16[400,768]{1,0:T(8,128)(2,1)}, bf16[400,768]{1,0:T(8,128)(2,1)}, u32[]{:S(2)}, u32[]{:S(2)}) %collective-permute-start.26) | collective-permute-done | bytes 614432 | tf_op jit(solution)/shard_map/ppermute | solution.py:42
  196.9 4.7 %convert_add_fusion.2 = f32[768,768]{1,0:T(8,128)} fusion(bf16[768,768]{1,0:T(8,128)(2,1)} %collective-permute-done.24, f32[768,768]{1,0:T(8,128)S(1)} %get-tuple-element.346, bf16[768,1536]{1,0:T(8,128)(2,1)S(1)} %get-tuple-element.349, bf16[1536,768]{1,0:T(8,128)(2,1)S(1)} %copy-done.9), kind=kOutput, calls=%fused_computation.69 | convolution fusion | flops 1813708800 | bytes 10616832 | tf_op jit(solution)/shard_map/dot_general | solution.py:27
  209.2 2.4 multiply_convert_fusion.4
  211.7 3.9 fusion.94
  215.7 4.0 multiply_convert_fusion.1
  219.7 2.2 add_convert_fusion.1
  222.0 4.0 multiply_convert_fusion
  233.1 3.3 fusion.95
  236.4 3.3 add_convert_fusion
  239.8 3.2 multiply_reduce_fusion
  243.0 3.0 fusion.32
  252.3 4.1 collective-permute-start.35
  262.7 16.6 %attention_backward.3 = bf16[1536,384]{1,0:T(8,128)(2,1)} custom-call(s32[2]{0:T(128)} %add_clamp_fusion.counts_ref, bf16[1536,1152]{1,0:T(8,128)(2,1)} %convolution_convert_fusion.q_ref.k_ref.v_ref, bf16[1536,1152]{1,0:T(8,128)(2,1)} %convolution_convert_fusion.q_ref.k_ref.v_ref, bf16[1536,1152]{1,0:T(8,128)(2,1)} %convolution_convert_fusion.q_ref.k_ref.v_ref, ...), custom_call_target="tpu_custom_call" | custom-call | flops 1 | bytes 1 | tf_op jit(solution)/shard_map/attention_backward/pallas_call | solution.py:356
  282.0 4.5 %collective-permute-start.36 = (bf16[192,768]{1,0:T(8,128)(2,1)}, bf16[192,768]{1,0:T(8,128)(2,1)}, u32[]{:S(2)}, u32[]{:S(2)}) collective-permute-start(bf16[192,768]{1,0:T(8,128)(2,1)} %get-tuple-element.307), channel_id=1, source_target_pairs={{0,1},{1,0},{2,3},{3,2},{4,5},{5,4},{6,7},{7,6},{8,9},{9,8},{10,11... | collective-permute-start | bytes 884744 | tf_op jit(solution)/shard_map/ppermute | solution.py:42
  288.7 16.8 %attention_backward.4 = bf16[1536,384]{1,0:T(8,128)(2,1)} custom-call(s32[2]{0:T(128)} %add_clamp_fusion.counts_ref, bf16[1536,1152]{1,0:T(8,128)(2,1)} %convolution_convert_fusion.q_ref.k_ref.v_ref, bf16[1536,1152]{1,0:T(8,128)(2,1)} %convolution_convert_fusion.q_ref.k_ref.v_ref, bf16[1536,1152]{1,0:T(8,128)(2,1)} %convolution_convert_fusion.q_ref.k_ref.v_ref, ...), custom_call_target="tpu_custom_call" | custom-call | flops 1 | bytes 1 | tf_op jit(solution)/shard_map/attention_backward/pallas_call | solution.py:356
  305.6 4.0 fusion.37
  319.1 2.2 collective-permute-start.40
  323.6 16.8 %attention_backward.5 = bf16[1536,384]{1,0:T(8,128)(2,1)} custom-call(s32[2]{0:T(128)} %add_clamp_fusion.counts_ref, bf16[1536,1152]{1,0:T(8,128)(2,1)} %convolution_convert_fusion.q_ref.k_ref.v_ref, bf16[1536,1152]{1,0:T(8,128)(2,1)} %convolution_convert_fusion.q_ref.k_ref.v_ref, bf16[1536,1152]{1,0:T(8,128)(2,1)} %convolution_convert_fusion.q_ref.k_ref.v_ref, ...), custom_call_target="tpu_custom_call" | custom-call | flops 1 | bytes 1 | tf_op jit(solution)/shard_map/attention_backward/pallas_call | solution.py:356
  340.5 2.8 convolution_convert_fusion.5
  343.4 3.3 fusion.10
  371.9 25.9 %collective-permute-done.51 = bf16[48,2304]{1,0:T(8,128)(2,1)S(1)} collective-permute-done((bf16[48,2304]{1,0:T(8,128)(2,1)S(1)}, bf16[48,2304]{1,0:T(8,128)(2,1)S(1)}, u32[]{:S(2)}, u32[]{:S(2)}) %collective-permute-start.51) | collective-permute-done | bytes 221216 | tf_op jit(solution)/shard_map/ppermute | solution.py:42
  401.8 5.9 %collective-permute-done.56 = bf16[48,1152]{1,0:T(8,128)(2,1)S(1)} collective-permute-done((bf16[48,1152]{1,0:T(8,128)(2,1)S(1)}, bf16[48,1152]{1,0:T(8,128)(2,1)S(1)}, u32[]{:S(2)}, u32[]{:S(2)}) %collective-permute-start.56) | collective-permute-done | bytes 110624 | tf_op jit(solution)/shard_map/ppermute | solution.py:42
  410.6 2.2 collective-permute-start.60
  413.0 5.1 %collective-permute-done.60 = bf16[48,1152]{1,0:T(8,128)(2,1)S(1)} collective-permute-done((bf16[48,1152]{1,0:T(8,128)(2,1)S(1)}, bf16[48,1152]{1,0:T(8,128)(2,1)S(1)}, u32[]{:S(2)}, u32[]{:S(2)}) %collective-permute-start.60) | collective-permute-done | bytes 110624 | tf_op jit(solution)/shard_map/ppermute | solution.py:42
  419.3 2.5 collective-permute-start.63
  424.1 4.2 collective-permute-done.65
  429.6 2.2 collective-permute-start.66
  (396 shorter events, 142.9 us)
Async XLA Ops:
  0.6 37.4 %collective-permute-start.4 = (bf16[384,768]{1,0:T(8,128)(2,1)}, bf16[384,768]{1,0:T(8,128)(2,1)S(1)}, u32[]{:S(2)}, u32[]{:S(2)}) collective-permute-start(bf16[384,768]{1,0:T(8,128)(2,1)} %refs_0_), channel_id=1, source_target_pairs={{0,8},{1,9},{2,10},{3,11},{4,12},{5,13},{6,14},{7,15},{8,0},{9,1},... | collective-permute-start | bytes 1769480 | tf_op jit(solution)/shard_map/ppermute | solution.py:42
  3.7 36.0 %collective-permute-start.5 = (bf16[384,768]{1,0:T(8,128)(2,1)}, bf16[384,768]{1,0:T(8,128)(2,1)}, u32[]{:S(2)}, u32[]{:S(2)}) collective-permute-start(bf16[384,768]{1,0:T(8,128)(2,1)} %refs_0_), channel_id=1, source_target_pairs={{0,16},{1,17},{2,18},{3,19},{4,20},{5,21},{6,22},{7,23},{8,24},{9,... | collective-permute-start | bytes 1769480 | tf_op jit(solution)/shard_map/ppermute | solution.py:42
  5.2 34.5 %collective-permute-start.6 = (bf16[384,768]{1,0:T(8,128)(2,1)}, bf16[384,768]{1,0:T(8,128)(2,1)}, u32[]{:S(2)}, u32[]{:S(2)}) collective-permute-start(bf16[384,768]{1,0:T(8,128)(2,1)} %refs_0_), channel_id=1, source_target_pairs={{0,24},{1,25},{2,26},{3,27},{4,28},{5,29},{6,30},{7,31},{8,16},{9,... | collective-permute-start | bytes 1769480 | tf_op jit(solution)/shard_map/ppermute | solution.py:42
  19.4 16.5 %collective-permute-start.1 = (bf16[384,768]{1,0:T(8,128)(2,1)}, bf16[384,768]{1,0:T(8,128)(2,1)S(1)}, u32[]{:S(2)}, u32[]{:S(2)}) collective-permute-start(bf16[384,768]{1,0:T(8,128)(2,1)} %get-tuple-element.289), channel_id=1, source_target_pairs={{0,1},{1,0},{2,5},{3,4},{4,3},{5,2},{6,7},{7,6},{8,9},{9,8},{10,13... | collective-permute-start | bytes 1769480 | tf_op jit(solution)/shard_map/ppermute | solution.py:42
  21.9 18.5 %collective-permute-start.10 = (bf16[192,1280]{1,0:T(8,128)(2,1)S(1)}, bf16[192,1280]{1,0:T(8,128)(2,1)S(1)}, u32[]{:S(2)}, u32[]{:S(2)}) collective-permute-start(bf16[192,1280]{1,0:T(8,128)(2,1)S(1)} %pad_maximum_fusion.14.refs_0_), channel_id=1, source_target_pairs={{0,24},{1,25},{2,26},{3,27},{4,28},{5,29},{6,30},{7,31},{8,16},{9,... | collective-permute-start | bytes 1474568 | tf_op jit(solution)/shard_map/ppermute | solution.py:42
  35.9 14.1 %collective-permute-start.8 = (bf16[192,1280]{1,0:T(8,128)(2,1)S(1)}, bf16[192,1280]{1,0:T(8,128)(2,1)S(1)}, u32[]{:S(2)}, u32[]{:S(2)}) collective-permute-start(bf16[192,1280]{1,0:T(8,128)(2,1)S(1)} %pad_maximum_fusion.14.refs_0_), channel_id=1, source_target_pairs={{0,8},{1,9},{2,10},{3,11},{4,12},{5,13},{6,14},{7,15},{8,0},{9,1},... | collective-permute-start | bytes 1474568 | tf_op jit(solution)/shard_map/ppermute | solution.py:42
  38.1 14.2 %collective-permute-start.9 = (bf16[192,1280]{1,0:T(8,128)(2,1)S(1)}, bf16[192,1280]{1,0:T(8,128)(2,1)S(1)}, u32[]{:S(2)}, u32[]{:S(2)}) collective-permute-start(bf16[192,1280]{1,0:T(8,128)(2,1)S(1)} %pad_maximum_fusion.14.refs_0_), channel_id=1, source_target_pairs={{0,16},{1,17},{2,18},{3,19},{4,20},{5,21},{6,22},{7,23},{8,24},{9,... | collective-permute-start | bytes 1474568 | tf_op jit(solution)/shard_map/ppermute | solution.py:42
  58.3 20.0 %collective-permute-start.11 = (bf16[768,768]{1,0:T(8,128)(2,1)S(1)}, bf16[768,768]{1,0:T(8,128)(2,1)S(1)}, u32[]{:S(2)}, u32[]{:S(2)}) collective-permute-start(bf16[768,768]{1,0:T(8,128)(2,1)S(1)} %fusion.24), channel_id=1, source_target_pairs={{0,4},{1,5},{2,6},{3,7},{4,0},{5,1},{6,2},{7,3},{8,12},{9,13},{10,... | collective-permute-start | bytes 3538952 | tf_op jit(solution)/shard_map/ppermute | solution.py:42
  63.2 15.2 %collective-permute-start.14 = (bf16[400,768]{1,0:T(8,128)(2,1)S(1)}, bf16[400,768]{1,0:T(8,128)(2,1)S(1)}, u32[]{:S(2)}, u32[]{:S(2)}) collective-permute-start(bf16[400,768]{1,0:T(8,128)(2,1)S(1)} %fusion.52), channel_id=1, source_target_pairs={{0,4},{1,5},{2,6},{3,7},{4,0},{5,1},{6,2},{7,3},{8,12},{9,13},{10,... | collective-permute-start | bytes 1843208 | tf_op jit(solution)/shard_map/ppermute | solution.py:42
  68.2 10.0 %collective-permute-start.13 = (f32[8,128]{1,0:T(8,128)S(1)}, f32[8,128]{1,0:T(8,128)S(1)}, u32[]{:S(2)}, u32[]{:S(2)}) collective-permute-start(f32[8,128]{1,0:T(8,128)S(1)} %add.332), channel_id=1, source_target_pairs={{0,2},{1,3},{2,0},{3,1},{4,6},{5,7},{6,4},{7,5},{8,10},{9,11},{10,... | collective-permute-start | bytes 12296 | tf_op jit(solution)/shard_map/ppermute | solution.py:42
  75.9 13.8 %collective-permute-start.17 = (bf16[288,768]{1,0:T(8,128)(2,1)S(1)}, bf16[288,768]{1,0:T(8,128)(2,1)S(1)}, u32[]{:S(2)}, u32[]{:S(2)}) collective-permute-start(bf16[288,768]{1,0:T(8,128)(2,1)S(1)} %get-tuple-element.297), channel_id=1, source_target_pairs={{0,8},{1,9},{2,10},{3,11},{4,12},{5,13},{6,14},{7,15},{8,0},{9,1},... | collective-permute-start | bytes 1327112 | tf_op jit(solution)/shard_map/ppermute | solution.py:42
  76.8 12.9 %collective-permute-start.18 = (bf16[288,768]{1,0:T(8,128)(2,1)S(1)}, bf16[288,768]{1,0:T(8,128)(2,1)S(1)}, u32[]{:S(2)}, u32[]{:S(2)}) collective-permute-start(bf16[288,768]{1,0:T(8,128)(2,1)S(1)} %get-tuple-element.296), channel_id=1, source_target_pairs={{0,16},{1,17},{2,18},{3,19},{4,20},{5,21},{6,22},{7,23},{8,24},{9,... | collective-permute-start | bytes 1327112 | tf_op jit(solution)/shard_map/ppermute | solution.py:42
  78.5 10.7 %collective-permute-start.16 = (f32[8,128]{1,0:T(8,128)S(1)}, f32[8,128]{1,0:T(8,128)S(1)}, u32[]{:S(2)}, u32[]{:S(2)}) collective-permute-start(f32[8,128]{1,0:T(8,128)S(1)} %add.333), channel_id=1, source_target_pairs={{0,8},{1,9},{2,10},{3,11},{4,12},{5,13},{6,14},{7,15},{8,0},{9,1},... | collective-permute-start | bytes 12296 | tf_op jit(solution)/shard_map/ppermute | solution.py:42
  79.9 20.3 %collective-permute-start.15 = (bf16[400,768]{1,0:T(8,128)(2,1)S(1)}, bf16[400,768]{1,0:T(8,128)(2,1)S(1)}, u32[]{:S(2)}, u32[]{:S(2)}) collective-permute-start(bf16[400,768]{1,0:T(8,128)(2,1)S(1)} %get-tuple-element.263), channel_id=1, source_target_pairs={{0,8},{1,9},{2,10},{3,11},{4,12},{5,13},{6,14},{7,15},{8,0},{9,1},... | collective-permute-start | bytes 1843208 | tf_op jit(solution)/shard_map/ppermute | solution.py:42
  101.3 39.5 %collective-permute-start.20 = (bf16[576,768]{1,0:T(8,128)(2,1)}, bf16[576,768]{1,0:T(8,128)(2,1)}, u32[]{:S(2)}, u32[]{:S(2)}) collective-permute-start(bf16[576,768]{1,0:T(8,128)(2,1)} %pad_maximum_fusion.11), channel_id=1, source_target_pairs={{0,8},{1,9},{2,10},{3,11},{4,12},{5,13},{6,14},{7,15},{8,0},{9,1},... | collective-permute-start | bytes 2654216 | tf_op jit(solution)/shard_map/ppermute | solution.py:42
  103.1 37.8 %collective-permute-start.19 = (bf16[576,768]{1,0:T(8,128)(2,1)}, bf16[576,768]{1,0:T(8,128)(2,1)}, u32[]{:S(2)}, u32[]{:S(2)}) collective-permute-start(bf16[576,768]{1,0:T(8,128)(2,1)} %pad_maximum_fusion.10), channel_id=1, source_target_pairs={{0,16},{1,17},{2,18},{3,19},{4,20},{5,21},{6,22},{7,23},{8,24},{9,... | collective-permute-start | bytes 2654216 | tf_op jit(solution)/shard_map/ppermute | solution.py:42
  105.7 35.1 %collective-permute-start.21 = (bf16[400,768]{1,0:T(8,128)(2,1)}, bf16[400,768]{1,0:T(8,128)(2,1)}, u32[]{:S(2)}, u32[]{:S(2)}) collective-permute-start(bf16[400,768]{1,0:T(8,128)(2,1)} %get-tuple-element.260), channel_id=1, source_target_pairs={{0,16},{1,17},{2,18},{3,19},{4,20},{5,21},{6,22},{7,23},{8,24},{9,... | collective-permute-start | bytes 1843208 | tf_op jit(solution)/shard_map/ppermute | solution.py:42
  165.0 31.9 %collective-permute-start.24 = (bf16[768,768]{1,0:T(8,128)(2,1)}, bf16[768,768]{1,0:T(8,128)(2,1)}, u32[]{:S(2)}, u32[]{:S(2)}) collective-permute-start(bf16[768,768]{1,0:T(8,128)(2,1)} %convolution_convert_fusion.4), channel_id=1, source_target_pairs={{0,4},{1,5},{2,6},{3,7},{4,0},{5,1},{6,2},{7,3},{8,12},{9,13},{10,... | collective-permute-start | bytes 3538952 | tf_op jit(solution)/shard_map/ppermute | solution.py:42
  166.4 20.2 %collective-permute-start.25 = (bf16[400,768]{1,0:T(8,128)(2,1)}, bf16[400,768]{1,0:T(8,128)(2,1)}, u32[]{:S(2)}, u32[]{:S(2)}) collective-permute-start(bf16[400,768]{1,0:T(8,128)(2,1)} %get-tuple-element.270), channel_id=1, source_target_pairs={{0,0},{1,1},{2,4},{3,5},{4,2},{5,3},{6,6},{7,7},{8,8},{9,9},{10,12... | collective-permute-start | bytes 1843208 | tf_op jit(solution)/shard_map/ppermute | solution.py:42
  173.3 22.1 %collective-permute-start.26 = (bf16[400,768]{1,0:T(8,128)(2,1)}, bf16[400,768]{1,0:T(8,128)(2,1)}, u32[]{:S(2)}, u32[]{:S(2)}) collective-permute-start(bf16[400,768]{1,0:T(8,128)(2,1)} %get-tuple-element.271), channel_id=1, source_target_pairs={{0,1},{1,0},{2,5},{3,4},{4,3},{5,2},{6,7},{7,6},{8,9},{9,8},{10,13... | collective-permute-start | bytes 1843208 | tf_op jit(solution)/shard_map/ppermute | solution.py:42
  228.0 11.7 %collective-permute-start.29 = (bf16[768,768]{1,0:T(8,128)(2,1)S(1)}, bf16[768,768]{1,0:T(8,128)(2,1)S(1)}, u32[]{:S(2)}, u32[]{:S(2)}) collective-permute-start(bf16[768,768]{1,0:T(8,128)(2,1)S(1)} %convolution_convert_fusion.3), channel_id=1, source_target_pairs={{0,4},{1,5},{2,6},{3,7},{4,0},{5,1},{6,2},{7,3},{8,12},{9,13},{10,... | collective-permute-start | bytes 3538952 | tf_op jit(solution)/shard_map/ppermute | solution.py:42
  229.6 22.8 %collective-permute-start.31 = (bf16[384,768]{1,0:T(8,128)(2,1)S(1)}, bf16[384,768]{1,0:T(8,128)(2,1)S(1)}, u32[]{:S(2)}, u32[]{:S(2)}) collective-permute-start(bf16[384,768]{1,0:T(8,128)(2,1)S(1)} %get-tuple-element.256), channel_id=1, source_target_pairs={{0,8},{1,9},{2,10},{3,11},{4,12},{5,13},{6,14},{7,15},{8,0},{9,1},... | collective-permute-start | bytes 1769480 | tf_op jit(solution)/shard_map/ppermute | solution.py:42
  230.8 27.2 %collective-permute-start.32 = (bf16[384,768]{1,0:T(8,128)(2,1)S(1)}, bf16[384,768]{1,0:T(8,128)(2,1)S(1)}, u32[]{:S(2)}, u32[]{:S(2)}) collective-permute-start(bf16[384,768]{1,0:T(8,128)(2,1)S(1)} %get-tuple-element.255), channel_id=1, source_target_pairs={{0,16},{1,17},{2,18},{3,19},{4,20},{5,21},{6,22},{7,23},{8,24},{9,... | collective-permute-start | bytes 1769480 | tf_op jit(solution)/shard_map/ppermute | solution.py:42
  232.3 26.9 %collective-permute-start.33 = (bf16[384,768]{1,0:T(8,128)(2,1)S(1)}, bf16[384,768]{1,0:T(8,128)(2,1)S(1)}, u32[]{:S(2)}, u32[]{:S(2)}) collective-permute-start(bf16[384,768]{1,0:T(8,128)(2,1)S(1)} %get-tuple-element.254), channel_id=1, source_target_pairs={{0,24},{1,25},{2,26},{3,27},{4,28},{5,29},{6,30},{7,31},{8,16},{9,... | collective-permute-start | bytes 1769480 | tf_op jit(solution)/shard_map/ppermute | solution.py:42
  247.2 13.6 %collective-permute-start.30 = (bf16[768,384]{1,0:T(8,128)(2,1)S(1)}, bf16[768,384]{1,0:T(8,128)(2,1)S(1)}, u32[]{:S(2)}, u32[]{:S(2)}) collective-permute-start(bf16[768,384]{1,0:T(8,128)(2,1)S(1)} %get-tuple-element.285), channel_id=1, source_target_pairs={{0,4},{1,5},{2,6},{3,7},{4,0},{5,1},{6,2},{7,3},{8,12},{9,13},{10,... | collective-permute-start | bytes 1769480 | tf_op jit(solution)/shard_map/ppermute | solution.py:42
  250.6 28.6 %collective-permute-start.34 = (bf16[384,768]{1,0:T(8,128)(2,1)}, bf16[384,768]{1,0:T(8,128)(2,1)S(1)}, u32[]{:S(2)}, u32[]{:S(2)}) collective-permute-start(bf16[384,768]{1,0:T(8,128)(2,1)} %get-tuple-element.283), channel_id=1, source_target_pairs={{0,0},{1,1},{2,4},{3,5},{4,2},{5,3},{6,6},{7,7},{8,8},{9,9},{10,12... | collective-permute-start | bytes 1769480 | tf_op jit(solution)/shard_map/ppermute | solution.py:42
  252.3 26.9 %collective-permute-start.35 = (bf16[384,768]{1,0:T(8,128)(2,1)}, bf16[384,768]{1,0:T(8,128)(2,1)}, u32[]{:S(2)}, u32[]{:S(2)}) collective-permute-start(bf16[384,768]{1,0:T(8,128)(2,1)} %get-tuple-element.282), channel_id=1, source_target_pairs={{0,1},{1,0},{2,5},{3,4},{4,3},{5,2},{6,7},{7,6},{8,9},{9,8},{10,13... | collective-permute-start | bytes 1769480 | tf_op jit(solution)/shard_map/ppermute | solution.py:42
  258.0 47.5 %collective-permute-start.37 = (bf16[192,2304]{1,0:T(8,128)(2,1)}, bf16[192,2304]{1,0:T(8,128)(2,1)}, u32[]{:S(2)}, u32[]{:S(2)}) collective-permute-start(bf16[192,2304]{1,0:T(8,128)(2,1)} %get-tuple-element.251), channel_id=1, source_target_pairs={{0,8},{1,9},{2,10},{3,11},{4,12},{5,13},{6,14},{7,15},{8,0},{9,1},... | collective-permute-start | bytes 2654216 | tf_op jit(solution)/shard_map/ppermute | solution.py:42
  259.3 46.2 %collective-permute-start.38 = (bf16[192,2304]{1,0:T(8,128)(2,1)}, bf16[192,2304]{1,0:T(8,128)(2,1)}, u32[]{:S(2)}, u32[]{:S(2)}) collective-permute-start(bf16[192,2304]{1,0:T(8,128)(2,1)} %get-tuple-element.252), channel_id=1, source_target_pairs={{0,16},{1,17},{2,18},{3,19},{4,20},{5,21},{6,22},{7,23},{8,24},{9,... | collective-permute-start | bytes 2654216 | tf_op jit(solution)/shard_map/ppermute | solution.py:42
  260.8 44.7 %collective-permute-start.39 = (bf16[192,2304]{1,0:T(8,128)(2,1)}, bf16[192,2304]{1,0:T(8,128)(2,1)}, u32[]{:S(2)}, u32[]{:S(2)}) collective-permute-start(bf16[192,2304]{1,0:T(8,128)(2,1)} %get-tuple-element.249), channel_id=1, source_target_pairs={{0,24},{1,25},{2,26},{3,27},{4,28},{5,29},{6,30},{7,31},{8,16},{9,... | collective-permute-start | bytes 2654216 | tf_op jit(solution)/shard_map/ppermute | solution.py:42
  282.0 23.6 %collective-permute-start.36 = (bf16[192,768]{1,0:T(8,128)(2,1)}, bf16[192,768]{1,0:T(8,128)(2,1)}, u32[]{:S(2)}, u32[]{:S(2)}) collective-permute-start(bf16[192,768]{1,0:T(8,128)(2,1)} %get-tuple-element.307), channel_id=1, source_target_pairs={{0,1},{1,0},{2,3},{3,2},{4,5},{5,4},{6,7},{7,6},{8,9},{9,8},{10,11... | collective-permute-start | bytes 884744 | tf_op jit(solution)/shard_map/ppermute | solution.py:42
  310.7 29.7 %collective-permute-start.42 = (bf16[192,768]{1,0:T(8,128)(2,1)}, bf16[192,768]{1,0:T(8,128)(2,1)}, u32[]{:S(2)}, u32[]{:S(2)}) collective-permute-start(bf16[192,768]{1,0:T(8,128)(2,1)} %get-tuple-element.278), channel_id=1, source_target_pairs={{0,8},{1,9},{2,10},{3,11},{4,12},{5,13},{6,14},{7,15},{8,0},{9,1},... | collective-permute-start | bytes 884744 | tf_op jit(solution)/shard_map/ppermute | solution.py:42
  311.4 29.0 %collective-permute-start.43 = (bf16[192,768]{1,0:T(8,128)(2,1)}, bf16[192,768]{1,0:T(8,128)(2,1)}, u32[]{:S(2)}, u32[]{:S(2)}) collective-permute-start(bf16[192,768]{1,0:T(8,128)(2,1)} %get-tuple-element.277), channel_id=1, source_target_pairs={{0,16},{1,17},{2,18},{3,19},{4,20},{5,21},{6,22},{7,23},{8,24},{9,... | collective-permute-start | bytes 884744 | tf_op jit(solution)/shard_map/ppermute | solution.py:42
  313.4 27.1 %collective-permute-start.44 = (bf16[192,768]{1,0:T(8,128)(2,1)}, bf16[192,768]{1,0:T(8,128)(2,1)}, u32[]{:S(2)}, u32[]{:S(2)}) collective-permute-start(bf16[192,768]{1,0:T(8,128)(2,1)} %get-tuple-element.276), channel_id=1, source_target_pairs={{0,24},{1,25},{2,26},{3,27},{4,28},{5,29},{6,30},{7,31},{8,16},{9,... | collective-permute-start | bytes 884744 | tf_op jit(solution)/shard_map/ppermute | solution.py:42
  317.3 23.1 %collective-permute-start.41 = (bf16[96,2304]{1,0:T(8,128)(2,1)}, bf16[96,2304]{1,0:T(8,128)(2,1)}, u32[]{:S(2)}, u32[]{:S(2)}) collective-permute-start(bf16[96,2304]{1,0:T(8,128)(2,1)} %get-tuple-element.292), channel_id=1, source_target_pairs={{0,1},{1,0},{2,3},{3,2},{4,5},{5,4},{6,7},{7,6},{8,9},{9,8},{10,11... | collective-permute-start | bytes 1327112 | tf_op jit(solution)/shard_map/ppermute | solution.py:42
  319.1 21.3 %collective-permute-start.40 = (bf16[96,768]{1,0:T(8,128)(2,1)}, bf16[96,768]{1,0:T(8,128)(2,1)}, u32[]{:S(2)}, u32[]{:S(2)}) collective-permute-start(bf16[96,768]{1,0:T(8,128)(2,1)} %get-tuple-element.331), channel_id=1, source_target_pairs={{0,2},{1,3},{2,0},{3,1},{4,6},{5,7},{6,4},{7,5},{8,10},{9,11},{10,... | collective-permute-start | bytes 442376 | tf_op jit(solution)/shard_map/ppermute | solution.py:42
  346.8 14.7 %collective-permute-start.52 = (bf16[768,768]{1,0:T(8,128)(2,1)S(1)}, bf16[768,768]{1,0:T(8,128)(2,1)S(1)}, u32[]{:S(2)}, u32[]{:S(2)}) collective-permute-start(bf16[768,768]{1,0:T(8,128)(2,1)S(1)} %slice.333), channel_id=1, source_target_pairs={{0,4},{1,5},{2,6},{3,7},{4,0},{5,1},{6,2},{7,3},{8,12},{9,13},{10,... | collective-permute-start | bytes 3538952 | tf_op jit(solution)/shard_map/ppermute | solution.py:42
  348.5 22.3 %collective-permute-start.54 = (bf16[96,768]{1,0:T(8,128)(2,1)S(1)}, bf16[96,768]{1,0:T(8,128)(2,1)S(1)}, u32[]{:S(2)}, u32[]{:S(2)}) collective-permute-start(bf16[96,768]{1,0:T(8,128)(2,1)S(1)} %add_convert_fusion.9), channel_id=1, source_target_pairs={{0,2},{1,3},{2,0},{3,1},{4,6},{5,7},{6,4},{7,5},{8,10},{9,11},{10,... | collective-permute-start | bytes 442376 | tf_op jit(solution)/shard_map/ppermute | solution.py:42
  356.0 11.4 %collective-permute-start.50 = (bf16[48,2304]{1,0:T(8,128)(2,1)S(1)}, bf16[48,2304]{1,0:T(8,128)(2,1)S(1)}, u32[]{:S(2)}, u32[]{:S(2)}) collective-permute-start(bf16[48,2304]{1,0:T(8,128)(2,1)S(1)} %dynamic-slice_bitcast_fusion.10), channel_id=1, source_target_pairs={{0,2},{1,3},{2,0},{3,1},{4,6},{5,7},{6,4},{7,5},{8,10},{9,11},{10,... | collective-permute-start | bytes 663560 | tf_op jit(solution)/shard_map/ppermute | solution.py:42
  357.9 13.9 %collective-permute-start.49 = (bf16[96,768]{1,0:T(8,128)(2,1)S(1)}, bf16[96,768]{1,0:T(8,128)(2,1)S(1)}, u32[]{:S(2)}, u32[]{:S(2)}) collective-permute-start(bf16[96,768]{1,0:T(8,128)(2,1)S(1)} %get-tuple-element.329), channel_id=1, source_target_pairs={{0,1},{1,0},{2,3},{3,2},{4,5},{5,4},{6,7},{7,6},{8,9},{9,8},{10,11... | collective-permute-start | bytes 442376 | tf_op jit(solution)/shard_map/ppermute | solution.py:42
  359.9 11.9 %collective-permute-start.48 = (bf16[96,384]{1,0:T(8,128)(2,1)S(1)}, bf16[96,384]{1,0:T(8,128)(2,1)S(1)}, u32[]{:S(2)}, u32[]{:S(2)}) collective-permute-start(bf16[96,384]{1,0:T(8,128)(2,1)S(1)} %get-tuple-element.339), channel_id=1, source_target_pairs={{0,1},{1,0},{2,3},{3,2},{4,5},{5,4},{6,7},{7,6},{8,9},{9,8},{10,11... | collective-permute-start | bytes 221192 | tf_op jit(solution)/shard_map/ppermute | solution.py:42
  364.2 33.6 %collective-permute-start.55 = (bf16[384,768]{1,0:T(8,128)(2,1)S(1)}, bf16[384,768]{1,0:T(8,128)(2,1)S(1)}, u32[]{:S(2)}, u32[]{:S(2)}) collective-permute-start(bf16[384,768]{1,0:T(8,128)(2,1)S(1)} %get-tuple-element.275), channel_id=1, source_target_pairs={{0,0},{1,1},{2,4},{3,5},{4,2},{5,3},{6,6},{7,7},{8,8},{9,9},{10,12... | collective-permute-start | bytes 1769480 | tf_op jit(solution)/shard_map/ppermute | solution.py:42
  369.8 27.9 %collective-permute-start.51 = (bf16[48,2304]{1,0:T(8,128)(2,1)S(1)}, bf16[48,2304]{1,0:T(8,128)(2,1)S(1)}, u32[]{:S(2)}, u32[]{:S(2)}) collective-permute-start(bf16[48,2304]{1,0:T(8,128)(2,1)S(1)} %fusion.59), channel_id=1, source_target_pairs={{0,2},{1,3},{2,0},{3,1},{4,6},{5,7},{6,4},{7,5},{8,10},{9,11},{10,... | collective-permute-start | bytes 663560 | tf_op jit(solution)/shard_map/ppermute | solution.py:42
  370.8 31.0 %collective-permute-start.59 = (bf16[384,768]{1,0:T(8,128)(2,1)S(1)}, bf16[384,768]{1,0:T(8,128)(2,1)S(1)}, u32[]{:S(2)}, u32[]{:S(2)}) collective-permute-start(bf16[384,768]{1,0:T(8,128)(2,1)S(1)} %get-tuple-element.274), channel_id=1, source_target_pairs={{0,1},{1,0},{2,5},{3,4},{4,3},{5,2},{6,7},{7,6},{8,9},{9,8},{10,13... | collective-permute-start | bytes 1769480 | tf_op jit(solution)/shard_map/ppermute | solution.py:42
  397.8 11.1 %collective-permute-start.58 = (bf16[192,768]{1,0:T(8,128)(2,1)S(1)}, bf16[192,768]{1,0:T(8,128)(2,1)S(1)}, u32[]{:S(2)}, u32[]{:S(2)}) collective-permute-start(bf16[192,768]{1,0:T(8,128)(2,1)S(1)} %pad_maximum_fusion.20), channel_id=1, source_target_pairs={{0,1},{1,0},{2,3},{3,2},{4,5},{5,4},{6,7},{7,6},{8,9},{9,8},{10,11... | collective-permute-start | bytes 884744 | tf_op jit(solution)/shard_map/ppermute | solution.py:42
  398.5 9.1 %collective-permute-start.56 = (bf16[48,1152]{1,0:T(8,128)(2,1)S(1)}, bf16[48,1152]{1,0:T(8,128)(2,1)S(1)}, u32[]{:S(2)}, u32[]{:S(2)}) collective-permute-start(bf16[48,1152]{1,0:T(8,128)(2,1)S(1)} %get-tuple-element.337), channel_id=1, source_target_pairs={{0,2},{1,3},{2,0},{3,1},{4,6},{5,7},{6,4},{7,5},{8,10},{9,11},{10,... | collective-permute-start | bytes 331784 | tf_op jit(solution)/shard_map/ppermute | solution.py:42
  399.5 19.3 %collective-permute-start.61 = (bf16[96,2304]{1,0:T(8,128)(2,1)S(1)}, bf16[96,2304]{1,0:T(8,128)(2,1)S(1)}, u32[]{:S(2)}, u32[]{:S(2)}) collective-permute-start(bf16[96,2304]{1,0:T(8,128)(2,1)S(1)} %pad_maximum_fusion.16), channel_id=1, source_target_pairs={{0,1},{1,0},{2,3},{3,2},{4,5},{5,4},{6,7},{7,6},{8,9},{9,8},{10,11... | collective-permute-start | bytes 1327112 | tf_op jit(solution)/shard_map/ppermute | solution.py:42
  419.2 9.1 %collective-permute-start.64 = (bf16[96,2304]{1,0:T(8,128)(2,1)S(1)}, bf16[96,2304]{1,0:T(8,128)(2,1)S(1)}, u32[]{:S(2)}, u32[]{:S(2)}) collective-permute-start(bf16[96,2304]{1,0:T(8,128)(2,1)S(1)} %fusion.58), channel_id=1, source_target_pairs={{0,4},{1,5},{2,6},{3,7},{4,0},{5,1},{6,2},{7,3},{8,12},{9,13},{10,... | collective-permute-start | bytes 1327112 | tf_op jit(solution)/shard_map/ppermute | solution.py:42
  (85 other events, 545.4 us)

commit v8 on v4

--- a/solution.py
+++ b/solution.py
@@ -531,7 +531,7 @@
     sources, *place_args = payload_pieces
     mixed, sources, deal, tally = tied(mixed, sources, deal, tally)
     mixed_got = across_cores(mixed[rows:])
-    goal = turned(settled(*deal))
+    goal_moved = turned_parts(settled(*deal))
     w_down, w_up, w_out = placed((sources, *place_args), payload_plan)
 
     attended = in_order(mixed[:rows], mixed_got, 1)
@@ -546,6 +546,8 @@
 
     active_mine, slope_mine = expanded(norm_two)
     active_other, slope_other = expanded(norm_other)
+    active_other, slope_other, goal_moved = tied(active_other, slope_other, goal_moved)
+    goal = turned_settled(goal_moved)
     part_other = row_major(dot(active_other, w_down, NN).astype(LOW))
     part_mine = row_major(dot(active_mine, w_down, NN))
     output = middle + part_mine + across_cores(part_other).astype(FULL)

time: 441 us -> 439 us (level)
  waiting for transfers between devices: 118 us -> 104 us
  starting transfers between devices: 79 us -> 91.7 us
    ppermute x65, waiting for transfers between devices: 118 us -> 104 us  [moved(): return lax.ppermute(value, AXES, links)]
    ppermute x65, starting transfers between devices: 79 us -> 91.7 us  [moved(): return lax.ppermute(value, AXES, links)]
    unnamed x165 -> x171, local copies, waits for them, and re-layouts: 7.22 us -> 10.3 us
  transfers between devices with their start and end apart: 65 -> 65, of which waited for: 22 -> 23; matrix products, arithmetic and copies ran while one was open for 19% -> 19% of each run, Pallas kernels for 20% -> 20%
where the time goes in v8:
time: 439 us; the launch traced here: 433 us
  waiting for transfers between devices  104 us (24%)
  starting transfers between devices  91.7 us (21%)
  Pallas kernels  88.4 us (20%)
  matrix products  60.6 us (14%)
  other arithmetic  51.5 us (12%)
  local copies, waits for them, and re-layouts  29.1 us (7%)
  between operations  7.4 us (2%)
    ppermute x65, waiting for transfers between devices, moved(): return lax.ppermute(value, AXES, links)  104 us
    ppermute x65, starting transfers between devices, moved(): return lax.ppermute(value, AXES, links)  91.7 us
    dot_general x20, matrix products, dot(): return lax.dot_general(left, right, form, preferred_element_type=FULL)  60.6 us
    pallas_call x3, Pallas kernels, attention_backward(): pl.pallas_call(functools.partial(backward_kernel, rows=rows, block=block,...  50.2 us
    pallas_call x1, Pallas kernels, attention_forward(): pl.pallas_call(functools.partial(forward_kernel, rows=rows, block=block),...  29.6 us
    unnamed x171, local copies, waits for them, and re-layouts  10.3 us
  transfers between devices with their start and end apart: 65, of which 23 were waited for; matrix products, arithmetic and copies ran while one was open for 19% of the time, Pallas kernels for 20%

profile of v8, /device:TPU:0, one launch (start us, length us, event | category | flops | bytes accessed | tf_op | source)
XLA Modules:
  0.0 433.0 jit_solution(17958130899115112256)
XLA Ops:
  4.6 6.0 %collective-permute-start = (bf16[384,768]{1,0:T(8,128)(2,1)}, bf16[384,768]{1,0:T(8,128)(2,1)}, u32[]{:S(2)}, u32[]{:S(2)}) collective-permute-start(bf16[384,768]{1,0:T(8,128)(2,1)} %get-tuple-element.296), channel_id=1, source_target_pairs={{0,0},{1,1},{2,4},{3,5},{4,2},{5,3},{6,6},{7,7},{8,8},{9,9},{10,12... | collective-permute-start | bytes 1769480 | tf_op jit(solution)/shard_map/ppermute | solution.py:42
  10.5 2.6 collective-permute-start.1
  34.6 4.2 collective-permute-done.7.refs_1_
  38.8 9.4 %collective-permute-done.8.refs_2_ = bf16[192,1280]{1,0:T(8,128)(2,1)S(1)} collective-permute-done((bf16[192,1280]{1,0:T(8,128)(2,1)S(1)}, bf16[192,1280]{1,0:T(8,128)(2,1)S(1)}, u32[]{:S(2)}, u32[]{:S(2)}) %collective-permute-start.8) | collective-permute-done | bytes 491552 | tf_op jit(solution)/shard_map/ppermute | solution.py:42
  49.8 2.9 place.2
  60.6 4.9 %convolution_convert_fusion.q_ref.k_ref.v_ref = bf16[1536,1152]{1,0:T(8,128)(2,1)} fusion(bf16[1536,768]{1,0:T(8,128)(2,1)S(1)} %pad_maximum_fusion, bf16[768,1152]{1,0:T(8,128)(2,1)S(1)} %copy-done.68), kind=kOutput, calls=%fused_computation | convolution fusion | flops 2719678464 | bytes 7667712 | tf_op jit(solution)/shard_map/dot_general | solution.py:27
  65.7 9.8 %collective-permute-done.14.refs_1_ = bf16[480,768]{1,0:T(8,128)(2,1)S(1)} collective-permute-done((bf16[480,768]{1,0:T(8,128)(2,1)S(1)}, bf16[480,768]{1,0:T(8,128)(2,1)S(1)}, u32[]{:S(2)}, u32[]{:S(2)}) %collective-permute-start.14) | collective-permute-done | bytes 737312 | tf_op jit(solution)/shard_map/ppermute | solution.py:42
  75.5 12.2 %collective-permute-done.12 = bf16[400,768]{1,0:T(8,128)(2,1)S(1)} collective-permute-done((bf16[400,768]{1,0:T(8,128)(2,1)S(1)}, bf16[400,768]{1,0:T(8,128)(2,1)S(1)}, u32[]{:S(2)}, u32[]{:S(2)}) %collective-permute-start.12) | collective-permute-done | bytes 614432 | tf_op jit(solution)/shard_map/ppermute | solution.py:42
  96.2 2.2 collective-permute-start.19
  99.7 29.6 %attention_forward.1 = (bf16[1536,384]{1,0:T(8,128)(2,1)}, f32[3,2,1536]{2,1,0:T(2,128)}) custom-call(s32[2]{0:T(128)} %add_clamp_fusion.counts_ref, bf16[1536,1152]{1,0:T(8,128)(2,1)} %convolution_convert_fusion.q_ref.k_ref.v_ref, bf16[1536,1152]{1,0:T(8,128)(2,1)} %convolution_convert_fusion.q_ref.k_ref.v_ref, ...), custom_call_target="tpu_custom_call" | custom-call | flops 1 | bytes 1 | tf_op jit(solution)/shard_map/attention_forward/pallas_call | solution.py:277
  129.9 7.2 %collective-permute-done.18 = bf16[400,768]{1,0:T(8,128)(2,1)S(1)} collective-permute-done((bf16[400,768]{1,0:T(8,128)(2,1)}, bf16[400,768]{1,0:T(8,128)(2,1)S(1)}, u32[]{:S(2)}, u32[]{:S(2)}) %collective-permute-start.18) | collective-permute-done | bytes 614432 | tf_op jit(solution)/shard_map/ppermute | solution.py:42
  137.1 2.2 slice.207
  139.3 5.7 %place.3 = (bf16[1536,768]{1,0:T(8,128)(2,1)}, bf16[768,1536]{1,0:T(8,128)(2,1)}, bf16[768,768]{1,0:T(8,128)(2,1)}) custom-call(s32[1]{0:T(128)} %bitcast.7.p_ref, bf16[960,768]{1,0:T(8,128)(2,1)} %copy-done.1, bf16[480,768]{1,0:T(8,128)(2,1)} %copy-done.7, bf16[480,768]{1,0:T(8,128)(2,1)} %copy-done.8, bf16[960,768]{1,0:T(8,128)(2,1)} %collective-permute-done.16.refs_3_, ...), custom_call_target="tpu_custom_call" | custom-call | tf_op jit(solution)/shard_map/place/pallas_call | solution.py:172
  152.1 4.9 %fusion.4 = (bf16[768,1536]{1,0:T(8,128)(2,1)}, bf16[768,1536]{1,0:T(8,128)(2,1)S(1)}) fusion(bf16[768,768]{1,0:T(8,128)(2,1)S(1)} %collective-permute-done.21, bf16[768,1536]{1,0:T(8,128)(2,1)S(1)} %copy-done.63), kind=kOutput, calls=%fused_computation.11 | convolution fusion | flops 1824915456 | bytes 8257536 | tf_op jit(solution)/shard_map/dot_general | solution.py:27
  157.1 8.9 %collective-permute-done.23 = bf16[400,768]{1,0:T(8,128)(2,1)S(1)} collective-permute-done((bf16[400,768]{1,0:T(8,128)(2,1)S(1)}, bf16[400,768]{1,0:T(8,128)(2,1)S(1)}, u32[]{:S(2)}, u32[]{:S(2)}) %collective-permute-start.23) | collective-permute-done | bytes 614432 | tf_op jit(solution)/shard_map/ppermute | solution.py:42
  165.9 3.0 convolution_convert_fusion.4
  168.9 10.3 %collective-permute-start.24 = (bf16[768,768]{1,0:T(8,128)(2,1)}, bf16[768,768]{1,0:T(8,128)(2,1)}, u32[]{:S(2)}, u32[]{:S(2)}) collective-permute-start(bf16[768,768]{1,0:T(8,128)(2,1)} %convolution_convert_fusion.4), channel_id=1, source_target_pairs={{0,4},{1,5},{2,6},{3,7},{4,0},{5,1},{6,2},{7,3},{8,12},{9,13},{10,... | collective-permute-start | bytes 3538952 | tf_op jit(solution)/shard_map/ppermute | solution.py:42
  179.3 6.3 %multiply_convert_fusion.3 = (bf16[768,1536]{1,0:T(8,128)(2,1)S(1)}, f32[768,1536]{1,0:T(8,128)}) fusion(bf16[768,768]{1,0:T(8,128)(2,1)} %copy-done.19, bf16[768,1536]{1,0:T(8,128)(2,1)} %get-tuple-element.127), kind=kOutput, calls=%fused_computation.23 | convolution fusion | flops 1817837568 | bytes 10616832 | tf_op jit(solution)/shard_map/dot_general | solution.py:27
  188.2 4.7 %convert_add_fusion.2 = f32[768,768]{1,0:T(8,128)} fusion(bf16[768,768]{1,0:T(8,128)(2,1)} %collective-permute-done.24, f32[768,768]{1,0:T(8,128)S(1)} %get-tuple-element.348, bf16[768,1536]{1,0:T(8,128)(2,1)S(1)} %get-tuple-element.349, bf16[1536,768]{1,0:T(8,128)(2,1)S(1)} %copy-done.66), kind=kOutput, calls=%fused_computation.69 | convolution fusion | flops 1813708800 | bytes 10616832 | tf_op jit(solution)/shard_map/dot_general | solution.py:27
  200.4 2.4 multiply_convert_fusion.4
  203.0 3.9 fusion.94
  206.9 4.5 %multiply_convert_fusion.1 = bf16[768,1536]{1,0:T(8,128)(2,1)S(1)} fusion(bf16[768,768]{1,0:T(8,128)(2,1)S(1)} %multiply_convert_fusion.4, bf16[1536,768]{1,0:T(8,128)(2,1)S(1)} %copy-done.67, f32[768,1536]{1,0:T(8,128)S(1)} %bitcast.225), kind=kOutput, calls=%fused_computation.19 | convolution fusion | flops 1826095104 | bytes 10616832 | tf_op jit(solution)/shard_map/dot_general | solution.py:27
  211.4 2.2 add_convert_fusion.1
  213.7 2.0 multiply_convert_fusion
  222.7 2.1 fusion.95
  224.8 2.2 add_convert_fusion
  227.1 3.2 multiply_reduce_fusion
  230.3 3.0 fusion.32
  240.5 7.1 %collective-permute-start.32 = (bf16[384,768]{1,0:T(8,128)(2,1)}, bf16[384,768]{1,0:T(8,128)(2,1)}, u32[]{:S(2)}, u32[]{:S(2)}) collective-permute-start(bf16[384,768]{1,0:T(8,128)(2,1)} %get-tuple-element.290), channel_id=1, source_target_pairs={{0,1},{1,0},{2,5},{3,4},{4,3},{5,2},{6,7},{7,6},{8,9},{9,8},{10,13... | collective-permute-start | bytes 1769480 | tf_op jit(solution)/shard_map/ppermute | solution.py:42
  253.8 16.6 %attention_backward.3 = bf16[1536,384]{1,0:T(8,128)(2,1)} custom-call(s32[2]{0:T(128)} %add_clamp_fusion.counts_ref, bf16[1536,1152]{1,0:T(8,128)(2,1)} %convolution_convert_fusion.q_ref.k_ref.v_ref, bf16[1536,1152]{1,0:T(8,128)(2,1)} %convolution_convert_fusion.q_ref.k_ref.v_ref, bf16[1536,1152]{1,0:T(8,128)(2,1)} %convolution_convert_fusion.q_ref.k_ref.v_ref, ...), custom_call_target="tpu_custom_call" | custom-call | flops 1 | bytes 1 | tf_op jit(solution)/shard_map/attention_backward/pallas_call | solution.py:356
  273.1 6.4 %collective-permute-start.33 = (bf16[192,768]{1,0:T(8,128)(2,1)}, bf16[192,768]{1,0:T(8,128)(2,1)}, u32[]{:S(2)}, u32[]{:S(2)}) collective-permute-start(bf16[192,768]{1,0:T(8,128)(2,1)} %get-tuple-element.311), channel_id=1, source_target_pairs={{0,1},{1,0},{2,3},{3,2},{4,5},{5,4},{6,7},{7,6},{8,9},{9,8},{10,11... | collective-permute-start | bytes 884744 | tf_op jit(solution)/shard_map/ppermute | solution.py:42
  281.8 16.8 %attention_backward.4 = bf16[1536,384]{1,0:T(8,128)(2,1)} custom-call(s32[2]{0:T(128)} %add_clamp_fusion.counts_ref, bf16[1536,1152]{1,0:T(8,128)(2,1)} %convolution_convert_fusion.q_ref.k_ref.v_ref, bf16[1536,1152]{1,0:T(8,128)(2,1)} %convolution_convert_fusion.q_ref.k_ref.v_ref, bf16[1536,1152]{1,0:T(8,128)(2,1)} %convolution_convert_fusion.q_ref.k_ref.v_ref, ...), custom_call_target="tpu_custom_call" | custom-call | flops 1 | bytes 1 | tf_op jit(solution)/shard_map/attention_backward/pallas_call | solution.py:356
  298.6 4.0 fusion.37
  307.2 2.1 add_convert_fusion.3
  312.1 3.3 collective-permute-start.37
  317.7 16.8 %attention_backward.5 = bf16[1536,384]{1,0:T(8,128)(2,1)} custom-call(s32[2]{0:T(128)} %add_clamp_fusion.counts_ref, bf16[1536,1152]{1,0:T(8,128)(2,1)} %convolution_convert_fusion.q_ref.k_ref.v_ref, bf16[1536,1152]{1,0:T(8,128)(2,1)} %convolution_convert_fusion.q_ref.k_ref.v_ref, bf16[1536,1152]{1,0:T(8,128)(2,1)} %convolution_convert_fusion.q_ref.k_ref.v_ref, ...), custom_call_target="tpu_custom_call" | custom-call | flops 1 | bytes 1 | tf_op jit(solution)/shard_map/attention_backward/pallas_call | solution.py:356
  334.6 2.8 convolution_convert_fusion.5
  337.5 3.3 fusion.10
  349.5 2.9 collective-permute-start.47
  358.9 2.4 collective-permute-done.47
  363.3 2.2 collective-permute-start.56
  365.5 24.8 %collective-permute-done.48 = bf16[48,2304]{1,0:T(8,128)(2,1)S(1)} collective-permute-done((bf16[48,2304]{1,0:T(8,128)(2,1)S(1)}, bf16[48,2304]{1,0:T(8,128)(2,1)S(1)}, u32[]{:S(2)}, u32[]{:S(2)}) %collective-permute-start.48) | collective-permute-done | bytes 221216 | tf_op jit(solution)/shard_map/ppermute | solution.py:42
  390.5 2.4 collective-permute-start.54
  395.2 5.1 %collective-permute-done.53 = bf16[48,1152]{1,0:T(8,128)(2,1)S(1)} collective-permute-done((bf16[48,1152]{1,0:T(8,128)(2,1)S(1)}, bf16[48,1152]{1,0:T(8,128)(2,1)S(1)}, u32[]{:S(2)}, u32[]{:S(2)}) %collective-permute-start.53) | collective-permute-done | bytes 110624 | tf_op jit(solution)/shard_map/ppermute | solution.py:42
  403.1 2.8 collective-permute-start.57
  406.1 5.6 %collective-permute-done.57 = bf16[48,1152]{1,0:T(8,128)(2,1)S(1)} collective-permute-done((bf16[48,1152]{1,0:T(8,128)(2,1)S(1)}, bf16[48,1152]{1,0:T(8,128)(2,1)S(1)}, u32[]{:S(2)}, u32[]{:S(2)}) %collective-permute-start.57) | collective-permute-done | bytes 110624 | tf_op jit(solution)/shard_map/ppermute | solution.py:42
  417.2 4.1 collective-permute-done.62
  422.7 2.8 collective-permute-start.63
  (421 shorter events, 128.8 us)
Async XLA Ops:
  3.0 24.7 %collective-permute-start.2 = (bf16[288,768]{1,0:T(8,128)(2,1)}, bf16[288,768]{1,0:T(8,128)(2,1)}, u32[]{:S(2)}, u32[]{:S(2)}) collective-permute-start(bf16[288,768]{1,0:T(8,128)(2,1)} %pad_maximum_fusion.14), channel_id=1, source_target_pairs={{0,4},{1,5},{2,6},{3,7},{4,0},{5,1},{6,2},{7,3},{8,12},{9,13},{10,... | collective-permute-start | bytes 1327112 | tf_op jit(solution)/shard_map/ppermute | solution.py:42
  4.6 26.8 %collective-permute-start = (bf16[384,768]{1,0:T(8,128)(2,1)}, bf16[384,768]{1,0:T(8,128)(2,1)}, u32[]{:S(2)}, u32[]{:S(2)}) collective-permute-start(bf16[384,768]{1,0:T(8,128)(2,1)} %get-tuple-element.296), channel_id=1, source_target_pairs={{0,0},{1,1},{2,4},{3,5},{4,2},{5,3},{6,6},{7,7},{8,8},{9,9},{10,12... | collective-permute-start | bytes 1769480 | tf_op jit(solution)/shard_map/ppermute | solution.py:42
  10.5 21.8 %collective-permute-start.1 = (bf16[384,768]{1,0:T(8,128)(2,1)}, bf16[384,768]{1,0:T(8,128)(2,1)}, u32[]{:S(2)}, u32[]{:S(2)}) collective-permute-start(bf16[384,768]{1,0:T(8,128)(2,1)} %get-tuple-element.297), channel_id=1, source_target_pairs={{0,1},{1,0},{2,5},{3,4},{4,3},{5,2},{6,7},{7,6},{8,9},{9,8},{10,13... | collective-permute-start | bytes 1769480 | tf_op jit(solution)/shard_map/ppermute | solution.py:42
  24.6 14.2 %collective-permute-start.7 = (bf16[192,1280]{1,0:T(8,128)(2,1)S(1)}, bf16[192,1280]{1,0:T(8,128)(2,1)S(1)}, u32[]{:S(2)}, u32[]{:S(2)}) collective-permute-start(bf16[192,1280]{1,0:T(8,128)(2,1)S(1)} %pad_maximum_fusion.13.refs_0_), channel_id=1, source_target_pairs={{0,8},{1,9},{2,10},{3,11},{4,12},{5,13},{6,14},{7,15},{8,0},{9,1},... | collective-permute-start | bytes 1474568 | tf_op jit(solution)/shard_map/ppermute | solution.py:42
  26.2 22.0 %collective-permute-start.8 = (bf16[192,1280]{1,0:T(8,128)(2,1)S(1)}, bf16[192,1280]{1,0:T(8,128)(2,1)S(1)}, u32[]{:S(2)}, u32[]{:S(2)}) collective-permute-start(bf16[192,1280]{1,0:T(8,128)(2,1)S(1)} %pad_maximum_fusion.13.refs_0_), channel_id=1, source_target_pairs={{0,16},{1,17},{2,18},{3,19},{4,20},{5,21},{6,22},{7,23},{8,24},{9,... | collective-permute-start | bytes 1474568 | tf_op jit(solution)/shard_map/ppermute | solution.py:42
  27.7 20.5 %collective-permute-start.9 = (bf16[192,1280]{1,0:T(8,128)(2,1)S(1)}, bf16[192,1280]{1,0:T(8,128)(2,1)S(1)}, u32[]{:S(2)}, u32[]{:S(2)}) collective-permute-start(bf16[192,1280]{1,0:T(8,128)(2,1)S(1)} %pad_maximum_fusion.13.refs_0_), channel_id=1, source_target_pairs={{0,24},{1,25},{2,26},{3,27},{4,28},{5,29},{6,30},{7,31},{8,16},{9,... | collective-permute-start | bytes 1474568 | tf_op jit(solution)/shard_map/ppermute | solution.py:42
  56.0 19.4 %collective-permute-start.14 = (bf16[480,768]{1,0:T(8,128)(2,1)S(1)}, bf16[480,768]{1,0:T(8,128)(2,1)S(1)}, u32[]{:S(2)}, u32[]{:S(2)}) collective-permute-start(bf16[480,768]{1,0:T(8,128)(2,1)S(1)} %get-tuple-element.275), channel_id=1, source_target_pairs={{0,8},{1,9},{2,10},{3,11},{4,12},{5,13},{6,14},{7,15},{8,0},{9,1},... | collective-permute-start | bytes 2211848 | tf_op jit(solution)/shard_map/ppermute | solution.py:42
  56.5 18.9 %collective-permute-start.15 = (bf16[480,768]{1,0:T(8,128)(2,1)S(1)}, bf16[480,768]{1,0:T(8,128)(2,1)S(1)}, u32[]{:S(2)}, u32[]{:S(2)}) collective-permute-start(bf16[480,768]{1,0:T(8,128)(2,1)S(1)} %get-tuple-element.274), channel_id=1, source_target_pairs={{0,16},{1,17},{2,18},{3,19},{4,20},{5,21},{6,22},{7,23},{8,24},{9,... | collective-permute-start | bytes 2211848 | tf_op jit(solution)/shard_map/ppermute | solution.py:42
  59.4 28.3 %collective-permute-start.12 = (bf16[400,768]{1,0:T(8,128)(2,1)S(1)}, bf16[400,768]{1,0:T(8,128)(2,1)S(1)}, u32[]{:S(2)}, u32[]{:S(2)}) collective-permute-start(bf16[400,768]{1,0:T(8,128)(2,1)S(1)} %get-tuple-element.267), channel_id=1, source_target_pairs={{0,8},{1,9},{2,10},{3,11},{4,12},{5,13},{6,14},{7,15},{8,0},{9,1},... | collective-permute-start | bytes 1843208 | tf_op jit(solution)/shard_map/ppermute | solution.py:42
  89.0 48.1 %collective-permute-start.17 = (bf16[960,768]{1,0:T(8,128)(2,1)}, bf16[960,768]{1,0:T(8,128)(2,1)}, u32[]{:S(2)}, u32[]{:S(2)}) collective-permute-start(bf16[960,768]{1,0:T(8,128)(2,1)} %pad_maximum_fusion.2), channel_id=1, source_target_pairs={{0,8},{1,9},{2,10},{3,11},{4,12},{5,13},{6,14},{7,15},{8,0},{9,1},... | collective-permute-start | bytes 4423688 | tf_op jit(solution)/shard_map/ppermute | solution.py:42
  90.7 46.4 %collective-permute-start.16 = (bf16[960,768]{1,0:T(8,128)(2,1)}, bf16[960,768]{1,0:T(8,128)(2,1)}, u32[]{:S(2)}, u32[]{:S(2)}) collective-permute-start(bf16[960,768]{1,0:T(8,128)(2,1)} %pad_maximum_fusion.1), channel_id=1, source_target_pairs={{0,16},{1,17},{2,18},{3,19},{4,20},{5,21},{6,22},{7,23},{8,24},{9,... | collective-permute-start | bytes 4423688 | tf_op jit(solution)/shard_map/ppermute | solution.py:42
  93.3 43.8 %collective-permute-start.18 = (bf16[400,768]{1,0:T(8,128)(2,1)}, bf16[400,768]{1,0:T(8,128)(2,1)S(1)}, u32[]{:S(2)}, u32[]{:S(2)}) collective-permute-start(bf16[400,768]{1,0:T(8,128)(2,1)} %get-tuple-element.264), channel_id=1, source_target_pairs={{0,16},{1,17},{2,18},{3,19},{4,20},{5,21},{6,22},{7,23},{8,24},{9,... | collective-permute-start | bytes 1843208 | tf_op jit(solution)/shard_map/ppermute | solution.py:42
  96.2 33.1 %collective-permute-start.19 = (f32[8,128]{1,0:T(8,128)S(1)}, f32[8,128]{1,0:T(8,128)S(1)}, u32[]{:S(2)}, u32[]{:S(2)}) collective-permute-start(f32[8,128]{1,0:T(8,128)S(1)} %add.334), channel_id=1, source_target_pairs={{0,2},{1,3},{2,0},{3,1},{4,6},{5,7},{6,4},{7,5},{8,10},{9,11},{10,... | collective-permute-start | bytes 12296 | tf_op jit(solution)/shard_map/ppermute | solution.py:42
  151.1 14.8 %collective-permute-start.23 = (bf16[400,768]{1,0:T(8,128)(2,1)S(1)}, bf16[400,768]{1,0:T(8,128)(2,1)S(1)}, u32[]{:S(2)}, u32[]{:S(2)}) collective-permute-start(bf16[400,768]{1,0:T(8,128)(2,1)S(1)} %get-tuple-element.278), channel_id=1, source_target_pairs={{0,1},{1,0},{2,5},{3,4},{4,3},{5,2},{6,7},{7,6},{8,9},{9,8},{10,13... | collective-permute-start | bytes 1843208 | tf_op jit(solution)/shard_map/ppermute | solution.py:42
  168.9 16.9 %collective-permute-start.24 = (bf16[768,768]{1,0:T(8,128)(2,1)}, bf16[768,768]{1,0:T(8,128)(2,1)}, u32[]{:S(2)}, u32[]{:S(2)}) collective-permute-start(bf16[768,768]{1,0:T(8,128)(2,1)} %convolution_convert_fusion.4), channel_id=1, source_target_pairs={{0,4},{1,5},{2,6},{3,7},{4,0},{5,1},{6,2},{7,3},{8,12},{9,13},{10,... | collective-permute-start | bytes 3538952 | tf_op jit(solution)/shard_map/ppermute | solution.py:42
  202.8 8.6 %collective-permute-start.25 = (bf16[768,768]{1,0:T(8,128)(2,1)S(1)}, bf16[768,768]{1,0:T(8,128)(2,1)S(1)}, u32[]{:S(2)}, u32[]{:S(2)}) collective-permute-start(bf16[768,768]{1,0:T(8,128)(2,1)S(1)} %multiply_convert_fusion.4), channel_id=1, source_target_pairs={{0,4},{1,5},{2,6},{3,7},{4,0},{5,1},{6,2},{7,3},{8,12},{9,13},{10,... | collective-permute-start | bytes 3538952 | tf_op jit(solution)/shard_map/ppermute | solution.py:42
  217.7 9.3 %collective-permute-start.26 = (bf16[768,768]{1,0:T(8,128)(2,1)S(1)}, bf16[768,768]{1,0:T(8,128)(2,1)S(1)}, u32[]{:S(2)}, u32[]{:S(2)}) collective-permute-start(bf16[768,768]{1,0:T(8,128)(2,1)S(1)} %convolution_convert_fusion.3), channel_id=1, source_target_pairs={{0,4},{1,5},{2,6},{3,7},{4,0},{5,1},{6,2},{7,3},{8,12},{9,13},{10,... | collective-permute-start | bytes 3538952 | tf_op jit(solution)/shard_map/ppermute | solution.py:42
  219.2 20.4 %collective-permute-start.28 = (bf16[384,768]{1,0:T(8,128)(2,1)S(1)}, bf16[384,768]{1,0:T(8,128)(2,1)S(1)}, u32[]{:S(2)}, u32[]{:S(2)}) collective-permute-start(bf16[384,768]{1,0:T(8,128)(2,1)S(1)} %get-tuple-element.260), channel_id=1, source_target_pairs={{0,8},{1,9},{2,10},{3,11},{4,12},{5,13},{6,14},{7,15},{8,0},{9,1},... | collective-permute-start | bytes 1769480 | tf_op jit(solution)/shard_map/ppermute | solution.py:42
  220.8 28.4 %collective-permute-start.29 = (bf16[384,768]{1,0:T(8,128)(2,1)S(1)}, bf16[384,768]{1,0:T(8,128)(2,1)S(1)}, u32[]{:S(2)}, u32[]{:S(2)}) collective-permute-start(bf16[384,768]{1,0:T(8,128)(2,1)S(1)} %get-tuple-element.259), channel_id=1, source_target_pairs={{0,16},{1,17},{2,18},{3,19},{4,20},{5,21},{6,22},{7,23},{8,24},{9,... | collective-permute-start | bytes 1769480 | tf_op jit(solution)/shard_map/ppermute | solution.py:42
  222.3 28.4 %collective-permute-start.30 = (bf16[384,768]{1,0:T(8,128)(2,1)S(1)}, bf16[384,768]{1,0:T(8,128)(2,1)S(1)}, u32[]{:S(2)}, u32[]{:S(2)}) collective-permute-start(bf16[384,768]{1,0:T(8,128)(2,1)S(1)} %get-tuple-element.258), channel_id=1, source_target_pairs={{0,24},{1,25},{2,26},{3,27},{4,28},{5,29},{6,30},{7,31},{8,16},{9,... | collective-permute-start | bytes 1769480 | tf_op jit(solution)/shard_map/ppermute | solution.py:42
  234.5 17.7 %collective-permute-start.27 = (bf16[768,384]{1,0:T(8,128)(2,1)S(1)}, bf16[768,384]{1,0:T(8,128)(2,1)S(1)}, u32[]{:S(2)}, u32[]{:S(2)}) collective-permute-start(bf16[768,384]{1,0:T(8,128)(2,1)S(1)} %get-tuple-element.293), channel_id=1, source_target_pairs={{0,4},{1,5},{2,6},{3,7},{4,0},{5,1},{6,2},{7,3},{8,12},{9,13},{10,... | collective-permute-start | bytes 1769480 | tf_op jit(solution)/shard_map/ppermute | solution.py:42
  237.9 32.5 %collective-permute-start.31 = (bf16[384,768]{1,0:T(8,128)(2,1)}, bf16[384,768]{1,0:T(8,128)(2,1)S(1)}, u32[]{:S(2)}, u32[]{:S(2)}) collective-permute-start(bf16[384,768]{1,0:T(8,128)(2,1)} %get-tuple-element.291), channel_id=1, source_target_pairs={{0,0},{1,1},{2,4},{3,5},{4,2},{5,3},{6,6},{7,7},{8,8},{9,9},{10,12... | collective-permute-start | bytes 1769480 | tf_op jit(solution)/shard_map/ppermute | solution.py:42
  240.5 30.0 %collective-permute-start.32 = (bf16[384,768]{1,0:T(8,128)(2,1)}, bf16[384,768]{1,0:T(8,128)(2,1)}, u32[]{:S(2)}, u32[]{:S(2)}) collective-permute-start(bf16[384,768]{1,0:T(8,128)(2,1)} %get-tuple-element.290), channel_id=1, source_target_pairs={{0,1},{1,0},{2,5},{3,4},{4,3},{5,2},{6,7},{7,6},{8,9},{9,8},{10,13... | collective-permute-start | bytes 1769480 | tf_op jit(solution)/shard_map/ppermute | solution.py:42
  249.2 49.4 %collective-permute-start.34 = (bf16[192,2304]{1,0:T(8,128)(2,1)}, bf16[192,2304]{1,0:T(8,128)(2,1)}, u32[]{:S(2)}, u32[]{:S(2)}) collective-permute-start(bf16[192,2304]{1,0:T(8,128)(2,1)} %get-tuple-element.255), channel_id=1, source_target_pairs={{0,8},{1,9},{2,10},{3,11},{4,12},{5,13},{6,14},{7,15},{8,0},{9,1},... | collective-permute-start | bytes 2654216 | tf_op jit(solution)/shard_map/ppermute | solution.py:42
  250.8 47.8 %collective-permute-start.35 = (bf16[192,2304]{1,0:T(8,128)(2,1)}, bf16[192,2304]{1,0:T(8,128)(2,1)}, u32[]{:S(2)}, u32[]{:S(2)}) collective-permute-start(bf16[192,2304]{1,0:T(8,128)(2,1)} %get-tuple-element.256), channel_id=1, source_target_pairs={{0,16},{1,17},{2,18},{3,19},{4,20},{5,21},{6,22},{7,23},{8,24},{9,... | collective-permute-start | bytes 2654216 | tf_op jit(solution)/shard_map/ppermute | solution.py:42
  252.3 46.3 %collective-permute-start.36 = (bf16[192,2304]{1,0:T(8,128)(2,1)}, bf16[192,2304]{1,0:T(8,128)(2,1)}, u32[]{:S(2)}, u32[]{:S(2)}) collective-permute-start(bf16[192,2304]{1,0:T(8,128)(2,1)} %get-tuple-element.253), channel_id=1, source_target_pairs={{0,24},{1,25},{2,26},{3,27},{4,28},{5,29},{6,30},{7,31},{8,16},{9,... | collective-permute-start | bytes 2654216 | tf_op jit(solution)/shard_map/ppermute | solution.py:42
  273.1 25.5 %collective-permute-start.33 = (bf16[192,768]{1,0:T(8,128)(2,1)}, bf16[192,768]{1,0:T(8,128)(2,1)}, u32[]{:S(2)}, u32[]{:S(2)}) collective-permute-start(bf16[192,768]{1,0:T(8,128)(2,1)} %get-tuple-element.311), channel_id=1, source_target_pairs={{0,1},{1,0},{2,3},{3,2},{4,5},{5,4},{6,7},{7,6},{8,9},{9,8},{10,11... | collective-permute-start | bytes 884744 | tf_op jit(solution)/shard_map/ppermute | solution.py:42
  303.7 30.8 %collective-permute-start.39 = (bf16[192,768]{1,0:T(8,128)(2,1)}, bf16[192,768]{1,0:T(8,128)(2,1)}, u32[]{:S(2)}, u32[]{:S(2)}) collective-permute-start(bf16[192,768]{1,0:T(8,128)(2,1)} %get-tuple-element.286), channel_id=1, source_target_pairs={{0,8},{1,9},{2,10},{3,11},{4,12},{5,13},{6,14},{7,15},{8,0},{9,1},... | collective-permute-start | bytes 884744 | tf_op jit(solution)/shard_map/ppermute | solution.py:42
  303.8 30.7 %collective-permute-start.40 = (bf16[192,768]{1,0:T(8,128)(2,1)}, bf16[192,768]{1,0:T(8,128)(2,1)}, u32[]{:S(2)}, u32[]{:S(2)}) collective-permute-start(bf16[192,768]{1,0:T(8,128)(2,1)} %get-tuple-element.285), channel_id=1, source_target_pairs={{0,16},{1,17},{2,18},{3,19},{4,20},{5,21},{6,22},{7,23},{8,24},{9,... | collective-permute-start | bytes 884744 | tf_op jit(solution)/shard_map/ppermute | solution.py:42
  305.4 29.1 %collective-permute-start.41 = (bf16[192,768]{1,0:T(8,128)(2,1)}, bf16[192,768]{1,0:T(8,128)(2,1)}, u32[]{:S(2)}, u32[]{:S(2)}) collective-permute-start(bf16[192,768]{1,0:T(8,128)(2,1)} %get-tuple-element.284), channel_id=1, source_target_pairs={{0,24},{1,25},{2,26},{3,27},{4,28},{5,29},{6,30},{7,31},{8,16},{9,... | collective-permute-start | bytes 884744 | tf_op jit(solution)/shard_map/ppermute | solution.py:42
  310.3 24.2 %collective-permute-start.38 = (bf16[96,2304]{1,0:T(8,128)(2,1)}, bf16[96,2304]{1,0:T(8,128)(2,1)}, u32[]{:S(2)}, u32[]{:S(2)}) collective-permute-start(bf16[96,2304]{1,0:T(8,128)(2,1)} %get-tuple-element.300), channel_id=1, source_target_pairs={{0,1},{1,0},{2,3},{3,2},{4,5},{5,4},{6,7},{7,6},{8,9},{9,8},{10,11... | collective-permute-start | bytes 1327112 | tf_op jit(solution)/shard_map/ppermute | solution.py:42
  312.1 22.4 %collective-permute-start.37 = (bf16[96,768]{1,0:T(8,128)(2,1)}, bf16[96,768]{1,0:T(8,128)(2,1)}, u32[]{:S(2)}, u32[]{:S(2)}) collective-permute-start(bf16[96,768]{1,0:T(8,128)(2,1)} %get-tuple-element.333), channel_id=1, source_target_pairs={{0,2},{1,3},{2,0},{3,1},{4,6},{5,7},{6,4},{7,5},{8,10},{9,11},{10,... | collective-permute-start | bytes 442376 | tf_op jit(solution)/shard_map/ppermute | solution.py:42
  340.9 13.8 %collective-permute-start.49 = (bf16[768,768]{1,0:T(8,128)(2,1)S(1)}, bf16[768,768]{1,0:T(8,128)(2,1)S(1)}, u32[]{:S(2)}, u32[]{:S(2)}) collective-permute-start(bf16[768,768]{1,0:T(8,128)(2,1)S(1)} %slice.335), channel_id=1, source_target_pairs={{0,4},{1,5},{2,6},{3,7},{4,0},{5,1},{6,2},{7,3},{8,12},{9,13},{10,... | collective-permute-start | bytes 3538952 | tf_op jit(solution)/shard_map/ppermute | solution.py:42
  342.6 20.6 %collective-permute-start.51 = (bf16[96,768]{1,0:T(8,128)(2,1)S(1)}, bf16[96,768]{1,0:T(8,128)(2,1)S(1)}, u32[]{:S(2)}, u32[]{:S(2)}) collective-permute-start(bf16[96,768]{1,0:T(8,128)(2,1)S(1)} %add_convert_fusion.9), channel_id=1, source_target_pairs={{0,2},{1,3},{2,0},{3,1},{4,6},{5,7},{6,4},{7,5},{8,10},{9,11},{10,... | collective-permute-start | bytes 442376 | tf_op jit(solution)/shard_map/ppermute | solution.py:42
  342.9 9.5 %collective-permute-start.43 = (bf16[192,384]{1,0:T(8,128)(2,1)S(1)}, bf16[192,384]{1,0:T(8,128)(2,1)S(1)}, u32[]{:S(2)}, u32[]{:S(2)}) collective-permute-start(bf16[192,384]{1,0:T(8,128)(2,1)S(1)} %get-tuple-element.310), channel_id=1, source_target_pairs={{0,16},{1,17},{2,18},{3,19},{4,20},{5,21},{6,22},{7,23},{8,24},{9,... | collective-permute-start | bytes 442376 | tf_op jit(solution)/shard_map/ppermute | solution.py:42
  344.9 7.6 %collective-permute-start.44 = (bf16[192,384]{1,0:T(8,128)(2,1)S(1)}, bf16[192,384]{1,0:T(8,128)(2,1)S(1)}, u32[]{:S(2)}, u32[]{:S(2)}) collective-permute-start(bf16[192,384]{1,0:T(8,128)(2,1)S(1)} %get-tuple-element.309), channel_id=1, source_target_pairs={{0,24},{1,25},{2,26},{3,27},{4,28},{5,29},{6,30},{7,31},{8,16},{9,... | collective-permute-start | bytes 442376 | tf_op jit(solution)/shard_map/ppermute | solution.py:42
  349.5 11.8 %collective-permute-start.47 = (bf16[48,2304]{1,0:T(8,128)(2,1)S(1)}, bf16[48,2304]{1,0:T(8,128)(2,1)S(1)}, u32[]{:S(2)}, u32[]{:S(2)}) collective-permute-start(bf16[48,2304]{1,0:T(8,128)(2,1)S(1)} %dynamic-slice_bitcast_fusion.10), channel_id=1, source_target_pairs={{0,2},{1,3},{2,0},{3,1},{4,6},{5,7},{6,4},{7,5},{8,10},{9,11},{10,... | collective-permute-start | bytes 663560 | tf_op jit(solution)/shard_map/ppermute | solution.py:42
  352.4 13.0 %collective-permute-start.46 = (bf16[96,768]{1,0:T(8,128)(2,1)S(1)}, bf16[96,768]{1,0:T(8,128)(2,1)S(1)}, u32[]{:S(2)}, u32[]{:S(2)}) collective-permute-start(bf16[96,768]{1,0:T(8,128)(2,1)S(1)} %get-tuple-element.331), channel_id=1, source_target_pairs={{0,1},{1,0},{2,3},{3,2},{4,5},{5,4},{6,7},{7,6},{8,9},{9,8},{10,11... | collective-permute-start | bytes 442376 | tf_op jit(solution)/shard_map/ppermute | solution.py:42
  352.6 12.8 %collective-permute-start.45 = (bf16[96,384]{1,0:T(8,128)(2,1)S(1)}, bf16[96,384]{1,0:T(8,128)(2,1)S(1)}, u32[]{:S(2)}, u32[]{:S(2)}) collective-permute-start(bf16[96,384]{1,0:T(8,128)(2,1)S(1)} %get-tuple-element.341), channel_id=1, source_target_pairs={{0,1},{1,0},{2,3},{3,2},{4,5},{5,4},{6,7},{7,6},{8,9},{9,8},{10,11... | collective-permute-start | bytes 221192 | tf_op jit(solution)/shard_map/ppermute | solution.py:42
  357.4 32.9 %collective-permute-start.52 = (bf16[384,768]{1,0:T(8,128)(2,1)S(1)}, bf16[384,768]{1,0:T(8,128)(2,1)S(1)}, u32[]{:S(2)}, u32[]{:S(2)}) collective-permute-start(bf16[384,768]{1,0:T(8,128)(2,1)S(1)} %get-tuple-element.283), channel_id=1, source_target_pairs={{0,0},{1,1},{2,4},{3,5},{4,2},{5,3},{6,6},{7,7},{8,8},{9,9},{10,12... | collective-permute-start | bytes 1769480 | tf_op jit(solution)/shard_map/ppermute | solution.py:42
  362.5 27.8 %collective-permute-start.48 = (bf16[48,2304]{1,0:T(8,128)(2,1)S(1)}, bf16[48,2304]{1,0:T(8,128)(2,1)S(1)}, u32[]{:S(2)}, u32[]{:S(2)}) collective-permute-start(bf16[48,2304]{1,0:T(8,128)(2,1)S(1)} %fusion.56), channel_id=1, source_target_pairs={{0,2},{1,3},{2,0},{3,1},{4,6},{5,7},{6,4},{7,5},{8,10},{9,11},{10,... | collective-permute-start | bytes 663560 | tf_op jit(solution)/shard_map/ppermute | solution.py:42
  363.3 31.9 %collective-permute-start.56 = (bf16[384,768]{1,0:T(8,128)(2,1)S(1)}, bf16[384,768]{1,0:T(8,128)(2,1)S(1)}, u32[]{:S(2)}, u32[]{:S(2)}) collective-permute-start(bf16[384,768]{1,0:T(8,128)(2,1)S(1)} %get-tuple-element.282), channel_id=1, source_target_pairs={{0,1},{1,0},{2,5},{3,4},{4,3},{5,2},{6,7},{7,6},{8,9},{9,8},{10,13... | collective-permute-start | bytes 1769480 | tf_op jit(solution)/shard_map/ppermute | solution.py:42
  390.4 11.6 %collective-permute-start.55 = (bf16[192,768]{1,0:T(8,128)(2,1)S(1)}, bf16[192,768]{1,0:T(8,128)(2,1)S(1)}, u32[]{:S(2)}, u32[]{:S(2)}) collective-permute-start(bf16[192,768]{1,0:T(8,128)(2,1)S(1)} %pad_maximum_fusion.20), channel_id=1, source_target_pairs={{0,1},{1,0},{2,3},{3,2},{4,5},{5,4},{6,7},{7,6},{8,9},{9,8},{10,11... | collective-permute-start | bytes 884744 | tf_op jit(solution)/shard_map/ppermute | solution.py:42
  393.0 7.3 %collective-permute-start.53 = (bf16[48,1152]{1,0:T(8,128)(2,1)S(1)}, bf16[48,1152]{1,0:T(8,128)(2,1)S(1)}, u32[]{:S(2)}, u32[]{:S(2)}) collective-permute-start(bf16[48,1152]{1,0:T(8,128)(2,1)S(1)} %get-tuple-element.339), channel_id=1, source_target_pairs={{0,2},{1,3},{2,0},{3,1},{4,6},{5,7},{6,4},{7,5},{8,10},{9,11},{10,... | collective-permute-start | bytes 331784 | tf_op jit(solution)/shard_map/ppermute | solution.py:42
  393.5 18.9 %collective-permute-start.58 = (bf16[96,2304]{1,0:T(8,128)(2,1)S(1)}, bf16[96,2304]{1,0:T(8,128)(2,1)S(1)}, u32[]{:S(2)}, u32[]{:S(2)}) collective-permute-start(bf16[96,2304]{1,0:T(8,128)(2,1)S(1)} %pad_maximum_fusion.15), channel_id=1, source_target_pairs={{0,1},{1,0},{2,3},{3,2},{4,5},{5,4},{6,7},{7,6},{8,9},{9,8},{10,11... | collective-permute-start | bytes 1327112 | tf_op jit(solution)/shard_map/ppermute | solution.py:42
  403.1 8.6 %collective-permute-start.57 = (bf16[48,1152]{1,0:T(8,128)(2,1)S(1)}, bf16[48,1152]{1,0:T(8,128)(2,1)S(1)}, u32[]{:S(2)}, u32[]{:S(2)}) collective-permute-start(bf16[48,1152]{1,0:T(8,128)(2,1)S(1)} %add_convert_fusion.11), channel_id=1, source_target_pairs={{0,2},{1,3},{2,0},{3,1},{4,6},{5,7},{6,4},{7,5},{8,10},{9,11},{10,... | collective-permute-start | bytes 331784 | tf_op jit(solution)/shard_map/ppermute | solution.py:42
  412.8 8.6 %collective-permute-start.61 = (bf16[96,2304]{1,0:T(8,128)(2,1)S(1)}, bf16[96,2304]{1,0:T(8,128)(2,1)S(1)}, u32[]{:S(2)}, u32[]{:S(2)}) collective-permute-start(bf16[96,2304]{1,0:T(8,128)(2,1)S(1)} %fusion.55), channel_id=1, source_target_pairs={{0,4},{1,5},{2,6},{3,7},{4,0},{5,1},{6,2},{7,3},{8,12},{9,13},{10,... | collective-permute-start | bytes 1327112 | tf_op jit(solution)/shard_map/ppermute | solution.py:42
  412.9 8.4 %collective-permute-start.60 = (bf16[96,1152]{1,0:T(8,128)(2,1)S(1)}, bf16[96,1152]{1,0:T(8,128)(2,1)S(1)}, u32[]{:S(2)}, u32[]{:S(2)}) collective-permute-start(bf16[96,1152]{1,0:T(8,128)(2,1)S(1)} %pad_maximum_fusion.22), channel_id=1, source_target_pairs={{0,1},{1,0},{2,3},{3,2},{4,5},{5,4},{6,7},{7,6},{8,9},{9,8},{10,11... | collective-permute-start | bytes 663560 | tf_op jit(solution)/shard_map/ppermute | solution.py:42
  (97 other events, 534.9 us)

commit v9 on v8

--- a/solution.py
+++ b/solution.py
@@ -632,9 +632,7 @@
     late = depth_halved(added(late), low_bit)
     rest_own = added(rest_step)
     rest_got = across_depth(rest_own, high_bit)
-    late, early, rest_got, small, down_got, near = tied(
-        late, early, rest_got, small, down_got, input_moved[0]
-    )
+    late, early, small, near = tied(late, early, small, input_moved[0])
     down_own = depth_doubled(down_own, down_got, high_bit)
     down_got = across_depth(down_own, low_bit)
     qkv_step = depth_halved(jnp.concatenate([added(early), added(late)], axis=1), high_bit)

time: 439 us -> 442 us (level)
    unnamed x171 -> x169, local copies, waits for them, and re-layouts: 10.3 us -> 10.6 us
  transfers between devices with their start and end apart: 65 -> 65, of which waited for: 23 -> 24; matrix products, arithmetic and copies ran while one was open for 19% -> 21% of each run, Pallas kernels for 20% -> 20%
where the time goes in v9:
time: 442 us; the launch traced here: 436 us
  waiting for transfers between devices  108 us (24%)
  starting transfers between devices  90 us (20%)
  Pallas kernels  88.4 us (20%)
  matrix products  60.8 us (14%)
  other arithmetic  51.6 us (12%)
  local copies, waits for them, and re-layouts  29.3 us (7%)
  between operations  7.42 us (2%)
    ppermute x65, waiting for transfers between devices, moved(): return lax.ppermute(value, AXES, links)  108 us
    ppermute x65, starting transfers between devices, moved(): return lax.ppermute(value, AXES, links)  90 us
    dot_general x20, matrix products, dot(): return lax.dot_general(left, right, form, preferred_element_type=FULL)  60.8 us
    pallas_call x3, Pallas kernels, attention_backward(): pl.pallas_call(functools.partial(backward_kernel, rows=rows, block=block,...  50.2 us
    pallas_call x1, Pallas kernels, attention_forward(): pl.pallas_call(functools.partial(forward_kernel, rows=rows, block=block),...  29.6 us
    unnamed x169, local copies, waits for them, and re-layouts  10.6 us
  transfers between devices with their start and end apart: 65, of which 24 were waited for; matrix products, arithmetic and copies ran while one was open for 21% of the time, Pallas kernels for 20%

profile of v9, /device:TPU:0, one launch (start us, length us, event | category | flops | bytes accessed | tf_op | source)
XLA Modules:
  0.0 435.8 jit_solution(15263336762848138733)
XLA Ops:
  4.6 6.0 %collective-permute-start = (bf16[384,768]{1,0:T(8,128)(2,1)}, bf16[384,768]{1,0:T(8,128)(2,1)}, u32[]{:S(2)}, u32[]{:S(2)}) collective-permute-start(bf16[384,768]{1,0:T(8,128)(2,1)} %get-tuple-element.292), channel_id=1, source_target_pairs={{0,0},{1,1},{2,4},{3,5},{4,2},{5,3},{6,6},{7,7},{8,8},{9,9},{10,12... | collective-permute-start | bytes 1769480 | tf_op jit(solution)/shard_map/ppermute | solution.py:42
  10.5 2.6 collective-permute-start.1
  34.6 4.2 collective-permute-done.7.refs_1_
  38.8 9.4 %collective-permute-done.8.refs_2_ = bf16[192,1280]{1,0:T(8,128)(2,1)S(1)} collective-permute-done((bf16[192,1280]{1,0:T(8,128)(2,1)S(1)}, bf16[192,1280]{1,0:T(8,128)(2,1)S(1)}, u32[]{:S(2)}, u32[]{:S(2)}) %collective-permute-start.8) | collective-permute-done | bytes 491552 | tf_op jit(solution)/shard_map/ppermute | solution.py:42
  49.8 2.9 place.2
  60.7 4.9 %convolution_convert_fusion.q_ref.k_ref.v_ref = bf16[1536,1152]{1,0:T(8,128)(2,1)} fusion(bf16[1536,768]{1,0:T(8,128)(2,1)S(1)} %pad_maximum_fusion, bf16[768,1152]{1,0:T(8,128)(2,1)S(1)} %copy-done.67), kind=kOutput, calls=%fused_computation | convolution fusion | flops 2719678464 | bytes 7667712 | tf_op jit(solution)/shard_map/dot_general | solution.py:27
  65.7 9.8 %collective-permute-done.14.refs_1_ = bf16[480,768]{1,0:T(8,128)(2,1)S(1)} collective-permute-done((bf16[480,768]{1,0:T(8,128)(2,1)S(1)}, bf16[480,768]{1,0:T(8,128)(2,1)S(1)}, u32[]{:S(2)}, u32[]{:S(2)}) %collective-permute-start.14) | collective-permute-done | bytes 737312 | tf_op jit(solution)/shard_map/ppermute | solution.py:42
  75.5 12.2 %collective-permute-done.12 = bf16[400,768]{1,0:T(8,128)(2,1)S(1)} collective-permute-done((bf16[400,768]{1,0:T(8,128)(2,1)S(1)}, bf16[400,768]{1,0:T(8,128)(2,1)S(1)}, u32[]{:S(2)}, u32[]{:S(2)}) %collective-permute-start.12) | collective-permute-done | bytes 614432 | tf_op jit(solution)/shard_map/ppermute | solution.py:42
  96.3 2.2 collective-permute-start.19
  99.7 29.6 %attention_forward.1 = (bf16[1536,384]{1,0:T(8,128)(2,1)}, f32[3,2,1536]{2,1,0:T(2,128)}) custom-call(s32[2]{0:T(128)} %add_clamp_fusion.counts_ref, bf16[1536,1152]{1,0:T(8,128)(2,1)} %convolution_convert_fusion.q_ref.k_ref.v_ref, bf16[1536,1152]{1,0:T(8,128)(2,1)} %convolution_convert_fusion.q_ref.k_ref.v_ref, ...), custom_call_target="tpu_custom_call" | custom-call | flops 1 | bytes 1 | tf_op jit(solution)/shard_map/attention_forward/pallas_call | solution.py:277
  129.9 7.2 %collective-permute-done.18 = bf16[400,768]{1,0:T(8,128)(2,1)S(1)} collective-permute-done((bf16[400,768]{1,0:T(8,128)(2,1)}, bf16[400,768]{1,0:T(8,128)(2,1)S(1)}, u32[]{:S(2)}, u32[]{:S(2)}) %collective-permute-start.18) | collective-permute-done | bytes 614432 | tf_op jit(solution)/shard_map/ppermute | solution.py:42
  137.1 2.2 slice.207
  139.3 5.7 %place.3 = (bf16[1536,768]{1,0:T(8,128)(2,1)}, bf16[768,1536]{1,0:T(8,128)(2,1)}, bf16[768,768]{1,0:T(8,128)(2,1)}) custom-call(s32[1]{0:T(128)} %bitcast.7.p_ref, bf16[960,768]{1,0:T(8,128)(2,1)} %copy-done.1, bf16[480,768]{1,0:T(8,128)(2,1)} %copy-done.7, bf16[480,768]{1,0:T(8,128)(2,1)} %copy-done.8, bf16[960,768]{1,0:T(8,128)(2,1)} %collective-permute-done.16.refs_3_, ...), custom_call_target="tpu_custom_call" | custom-call | tf_op jit(solution)/shard_map/place/pallas_call | solution.py:172
  152.2 5.0 %fusion.4 = (bf16[768,1536]{1,0:T(8,128)(2,1)}, bf16[768,1536]{1,0:T(8,128)(2,1)S(1)}) fusion(bf16[768,768]{1,0:T(8,128)(2,1)S(1)} %collective-permute-done.21, bf16[768,1536]{1,0:T(8,128)(2,1)S(1)} %copy-done.62), kind=kOutput, calls=%fused_computation.11 | convolution fusion | flops 1824915456 | bytes 8257536 | tf_op jit(solution)/shard_map/dot_general | solution.py:27
  157.2 8.7 %collective-permute-done.23 = bf16[400,768]{1,0:T(8,128)(2,1)S(1)} collective-permute-done((bf16[400,768]{1,0:T(8,128)(2,1)S(1)}, bf16[400,768]{1,0:T(8,128)(2,1)S(1)}, u32[]{:S(2)}, u32[]{:S(2)}) %collective-permute-start.23) | collective-permute-done | bytes 614432 | tf_op jit(solution)/shard_map/ppermute | solution.py:42
  166.0 3.0 convolution_convert_fusion.4
  169.0 10.3 %collective-permute-start.24 = (bf16[768,768]{1,0:T(8,128)(2,1)}, bf16[768,768]{1,0:T(8,128)(2,1)}, u32[]{:S(2)}, u32[]{:S(2)}) collective-permute-start(bf16[768,768]{1,0:T(8,128)(2,1)} %convolution_convert_fusion.4), channel_id=1, source_target_pairs={{0,4},{1,5},{2,6},{3,7},{4,0},{5,1},{6,2},{7,3},{8,12},{9,13},{10,... | collective-permute-start | bytes 3538952 | tf_op jit(solution)/shard_map/ppermute | solution.py:42
  179.3 6.4 %multiply_convert_fusion.3 = (bf16[768,1536]{1,0:T(8,128)(2,1)S(1)}, f32[768,1536]{1,0:T(8,128)}) fusion(bf16[768,768]{1,0:T(8,128)(2,1)} %copy-done.19, bf16[768,1536]{1,0:T(8,128)(2,1)} %get-tuple-element.125), kind=kOutput, calls=%fused_computation.23 | convolution fusion | flops 1817837568 | bytes 10616832 | tf_op jit(solution)/shard_map/dot_general | solution.py:27
  188.2 4.7 %convert_add_fusion.2 = f32[768,768]{1,0:T(8,128)} fusion(bf16[768,768]{1,0:T(8,128)(2,1)} %collective-permute-done.24, f32[768,768]{1,0:T(8,128)S(1)} %get-tuple-element.344, bf16[768,1536]{1,0:T(8,128)(2,1)S(1)} %get-tuple-element.345, bf16[1536,768]{1,0:T(8,128)(2,1)S(1)} %copy-done.65), kind=kOutput, calls=%fused_computation.69 | convolution fusion | flops 1813708800 | bytes 10616832 | tf_op jit(solution)/shard_map/dot_general | solution.py:27
  200.4 2.4 multiply_convert_fusion.4
  203.0 3.9 fusion.94
  207.0 4.5 %multiply_convert_fusion.1 = bf16[768,1536]{1,0:T(8,128)(2,1)S(1)} fusion(bf16[768,768]{1,0:T(8,128)(2,1)S(1)} %multiply_convert_fusion.4, bf16[1536,768]{1,0:T(8,128)(2,1)S(1)} %copy-done.66, f32[768,1536]{1,0:T(8,128)S(1)} %bitcast.225), kind=kOutput, calls=%fused_computation.19 | convolution fusion | flops 1826095104 | bytes 10616832 | tf_op jit(solution)/shard_map/dot_general | solution.py:27
  211.5 2.2 add_convert_fusion.1
  213.7 2.0 multiply_convert_fusion
  215.8 2.0 convolution_convert_fusion.3
  222.8 2.1 fusion.95
  224.9 2.2 add_convert_fusion
  227.1 3.2 multiply_reduce_fusion
  230.3 3.0 fusion.32
  240.5 7.1 %collective-permute-start.32 = (bf16[384,768]{1,0:T(8,128)(2,1)}, bf16[384,768]{1,0:T(8,128)(2,1)}, u32[]{:S(2)}, u32[]{:S(2)}) collective-permute-start(bf16[384,768]{1,0:T(8,128)(2,1)} %get-tuple-element.286), channel_id=1, source_target_pairs={{0,1},{1,0},{2,5},{3,4},{4,3},{5,2},{6,7},{7,6},{8,9},{9,8},{10,13... | collective-permute-start | bytes 1769480 | tf_op jit(solution)/shard_map/ppermute | solution.py:42
  253.8 16.6 %attention_backward.3 = bf16[1536,384]{1,0:T(8,128)(2,1)} custom-call(s32[2]{0:T(128)} %add_clamp_fusion.counts_ref, bf16[1536,1152]{1,0:T(8,128)(2,1)} %convolution_convert_fusion.q_ref.k_ref.v_ref, bf16[1536,1152]{1,0:T(8,128)(2,1)} %convolution_convert_fusion.q_ref.k_ref.v_ref, bf16[1536,1152]{1,0:T(8,128)(2,1)} %convolution_convert_fusion.q_ref.k_ref.v_ref, ...), custom_call_target="tpu_custom_call" | custom-call | flops 1 | bytes 1 | tf_op jit(solution)/shard_map/attention_backward/pallas_call | solution.py:356
  273.2 6.4 %collective-permute-start.33 = (bf16[192,768]{1,0:T(8,128)(2,1)}, bf16[192,768]{1,0:T(8,128)(2,1)}, u32[]{:S(2)}, u32[]{:S(2)}) collective-permute-start(bf16[192,768]{1,0:T(8,128)(2,1)} %get-tuple-element.307), channel_id=1, source_target_pairs={{0,1},{1,0},{2,3},{3,2},{4,5},{5,4},{6,7},{7,6},{8,9},{9,8},{10,11... | collective-permute-start | bytes 884744 | tf_op jit(solution)/shard_map/ppermute | solution.py:42
  281.8 16.8 %attention_backward.4 = bf16[1536,384]{1,0:T(8,128)(2,1)} custom-call(s32[2]{0:T(128)} %add_clamp_fusion.counts_ref, bf16[1536,1152]{1,0:T(8,128)(2,1)} %convolution_convert_fusion.q_ref.k_ref.v_ref, bf16[1536,1152]{1,0:T(8,128)(2,1)} %convolution_convert_fusion.q_ref.k_ref.v_ref, bf16[1536,1152]{1,0:T(8,128)(2,1)} %convolution_convert_fusion.q_ref.k_ref.v_ref, ...), custom_call_target="tpu_custom_call" | custom-call | flops 1 | bytes 1 | tf_op jit(solution)/shard_map/attention_backward/pallas_call | solution.py:356
  298.6 4.0 fusion.37
  307.2 2.1 add_convert_fusion.3
  312.1 3.3 collective-permute-start.37
  317.7 16.8 %attention_backward.5 = bf16[1536,384]{1,0:T(8,128)(2,1)} custom-call(s32[2]{0:T(128)} %add_clamp_fusion.counts_ref, bf16[1536,1152]{1,0:T(8,128)(2,1)} %convolution_convert_fusion.q_ref.k_ref.v_ref, bf16[1536,1152]{1,0:T(8,128)(2,1)} %convolution_convert_fusion.q_ref.k_ref.v_ref, bf16[1536,1152]{1,0:T(8,128)(2,1)} %convolution_convert_fusion.q_ref.k_ref.v_ref, ...), custom_call_target="tpu_custom_call" | custom-call | flops 1 | bytes 1 | tf_op jit(solution)/shard_map/attention_backward/pallas_call | solution.py:356
  335.7 2.8 convolution_convert_fusion.5
  338.6 3.3 fusion.10
  355.9 6.8 %collective-permute-done.56 = bf16[48,2304]{1,0:T(8,128)(2,1)S(1)} collective-permute-done((bf16[48,2304]{1,0:T(8,128)(2,1)S(1)}, bf16[48,2304]{1,0:T(8,128)(2,1)S(1)}, u32[]{:S(2)}, u32[]{:S(2)}) %collective-permute-start.56) | collective-permute-done | bytes 221216 | tf_op jit(solution)/shard_map/ppermute | solution.py:42
  367.2 14.3 %collective-permute-done.57 = bf16[48,2304]{1,0:T(8,128)(2,1)S(1)} collective-permute-done((bf16[48,2304]{1,0:T(8,128)(2,1)S(1)}, bf16[48,2304]{1,0:T(8,128)(2,1)S(1)}, u32[]{:S(2)}, u32[]{:S(2)}) %collective-permute-start.57) | collective-permute-done | bytes 221216 | tf_op jit(solution)/shard_map/ppermute | solution.py:42
  384.7 3.9 collective-permute-start.50
  388.6 3.2 collective-permute-start.58
  391.8 15.5 %collective-permute-done.54 = bf16[384,768]{1,0:T(8,128)(2,1)S(1)} collective-permute-done((bf16[384,768]{1,0:T(8,128)(2,1)S(1)}, bf16[384,768]{1,0:T(8,128)(2,1)S(1)}, u32[]{:S(2)}, u32[]{:S(2)}) %collective-permute-start.54) | collective-permute-done | bytes 589856 | tf_op jit(solution)/shard_map/ppermute | solution.py:42
  411.2 2.3 collective-permute-done.58
  416.8 2.0 collective-permute-start.62
  420.0 4.1 collective-permute-done.62
  427.7 2.5 collective-permute-done.63
  (419 shorter events, 130.0 us)
Async XLA Ops:
  3.0 24.7 %collective-permute-start.2 = (bf16[288,768]{1,0:T(8,128)(2,1)}, bf16[288,768]{1,0:T(8,128)(2,1)}, u32[]{:S(2)}, u32[]{:S(2)}) collective-permute-start(bf16[288,768]{1,0:T(8,128)(2,1)} %pad_maximum_fusion.14), channel_id=1, source_target_pairs={{0,4},{1,5},{2,6},{3,7},{4,0},{5,1},{6,2},{7,3},{8,12},{9,13},{10,... | collective-permute-start | bytes 1327112 | tf_op jit(solution)/shard_map/ppermute | solution.py:42
  4.6 26.8 %collective-permute-start = (bf16[384,768]{1,0:T(8,128)(2,1)}, bf16[384,768]{1,0:T(8,128)(2,1)}, u32[]{:S(2)}, u32[]{:S(2)}) collective-permute-start(bf16[384,768]{1,0:T(8,128)(2,1)} %get-tuple-element.292), channel_id=1, source_target_pairs={{0,0},{1,1},{2,4},{3,5},{4,2},{5,3},{6,6},{7,7},{8,8},{9,9},{10,12... | collective-permute-start | bytes 1769480 | tf_op jit(solution)/shard_map/ppermute | solution.py:42
  10.5 21.8 %collective-permute-start.1 = (bf16[384,768]{1,0:T(8,128)(2,1)}, bf16[384,768]{1,0:T(8,128)(2,1)}, u32[]{:S(2)}, u32[]{:S(2)}) collective-permute-start(bf16[384,768]{1,0:T(8,128)(2,1)} %get-tuple-element.293), channel_id=1, source_target_pairs={{0,1},{1,0},{2,5},{3,4},{4,3},{5,2},{6,7},{7,6},{8,9},{9,8},{10,13... | collective-permute-start | bytes 1769480 | tf_op jit(solution)/shard_map/ppermute | solution.py:42
  24.6 14.2 %collective-permute-start.7 = (bf16[192,1280]{1,0:T(8,128)(2,1)S(1)}, bf16[192,1280]{1,0:T(8,128)(2,1)S(1)}, u32[]{:S(2)}, u32[]{:S(2)}) collective-permute-start(bf16[192,1280]{1,0:T(8,128)(2,1)S(1)} %pad_maximum_fusion.13.refs_0_), channel_id=1, source_target_pairs={{0,8},{1,9},{2,10},{3,11},{4,12},{5,13},{6,14},{7,15},{8,0},{9,1},... | collective-permute-start | bytes 1474568 | tf_op jit(solution)/shard_map/ppermute | solution.py:42
  26.2 22.0 %collective-permute-start.8 = (bf16[192,1280]{1,0:T(8,128)(2,1)S(1)}, bf16[192,1280]{1,0:T(8,128)(2,1)S(1)}, u32[]{:S(2)}, u32[]{:S(2)}) collective-permute-start(bf16[192,1280]{1,0:T(8,128)(2,1)S(1)} %pad_maximum_fusion.13.refs_0_), channel_id=1, source_target_pairs={{0,16},{1,17},{2,18},{3,19},{4,20},{5,21},{6,22},{7,23},{8,24},{9,... | collective-permute-start | bytes 1474568 | tf_op jit(solution)/shard_map/ppermute | solution.py:42
  27.7 20.5 %collective-permute-start.9 = (bf16[192,1280]{1,0:T(8,128)(2,1)S(1)}, bf16[192,1280]{1,0:T(8,128)(2,1)S(1)}, u32[]{:S(2)}, u32[]{:S(2)}) collective-permute-start(bf16[192,1280]{1,0:T(8,128)(2,1)S(1)} %pad_maximum_fusion.13.refs_0_), channel_id=1, source_target_pairs={{0,24},{1,25},{2,26},{3,27},{4,28},{5,29},{6,30},{7,31},{8,16},{9,... | collective-permute-start | bytes 1474568 | tf_op jit(solution)/shard_map/ppermute | solution.py:42
  56.0 19.4 %collective-permute-start.14 = (bf16[480,768]{1,0:T(8,128)(2,1)S(1)}, bf16[480,768]{1,0:T(8,128)(2,1)S(1)}, u32[]{:S(2)}, u32[]{:S(2)}) collective-permute-start(bf16[480,768]{1,0:T(8,128)(2,1)S(1)} %get-tuple-element.271), channel_id=1, source_target_pairs={{0,8},{1,9},{2,10},{3,11},{4,12},{5,13},{6,14},{7,15},{8,0},{9,1},... | collective-permute-start | bytes 2211848 | tf_op jit(solution)/shard_map/ppermute | solution.py:42
  56.6 18.9 %collective-permute-start.15 = (bf16[480,768]{1,0:T(8,128)(2,1)S(1)}, bf16[480,768]{1,0:T(8,128)(2,1)S(1)}, u32[]{:S(2)}, u32[]{:S(2)}) collective-permute-start(bf16[480,768]{1,0:T(8,128)(2,1)S(1)} %get-tuple-element.270), channel_id=1, source_target_pairs={{0,16},{1,17},{2,18},{3,19},{4,20},{5,21},{6,22},{7,23},{8,24},{9,... | collective-permute-start | bytes 2211848 | tf_op jit(solution)/shard_map/ppermute | solution.py:42
  59.4 28.3 %collective-permute-start.12 = (bf16[400,768]{1,0:T(8,128)(2,1)S(1)}, bf16[400,768]{1,0:T(8,128)(2,1)S(1)}, u32[]{:S(2)}, u32[]{:S(2)}) collective-permute-start(bf16[400,768]{1,0:T(8,128)(2,1)S(1)} %get-tuple-element.263), channel_id=1, source_target_pairs={{0,8},{1,9},{2,10},{3,11},{4,12},{5,13},{6,14},{7,15},{8,0},{9,1},... | collective-permute-start | bytes 1843208 | tf_op jit(solution)/shard_map/ppermute | solution.py:42
  89.0 48.1 %collective-permute-start.17 = (bf16[960,768]{1,0:T(8,128)(2,1)}, bf16[960,768]{1,0:T(8,128)(2,1)}, u32[]{:S(2)}, u32[]{:S(2)}) collective-permute-start(bf16[960,768]{1,0:T(8,128)(2,1)} %pad_maximum_fusion.2), channel_id=1, source_target_pairs={{0,8},{1,9},{2,10},{3,11},{4,12},{5,13},{6,14},{7,15},{8,0},{9,1},... | collective-permute-start | bytes 4423688 | tf_op jit(solution)/shard_map/ppermute | solution.py:42
  90.7 46.4 %collective-permute-start.16 = (bf16[960,768]{1,0:T(8,128)(2,1)}, bf16[960,768]{1,0:T(8,128)(2,1)}, u32[]{:S(2)}, u32[]{:S(2)}) collective-permute-start(bf16[960,768]{1,0:T(8,128)(2,1)} %pad_maximum_fusion.1), channel_id=1, source_target_pairs={{0,16},{1,17},{2,18},{3,19},{4,20},{5,21},{6,22},{7,23},{8,24},{9,... | collective-permute-start | bytes 4423688 | tf_op jit(solution)/shard_map/ppermute | solution.py:42
  93.3 43.8 %collective-permute-start.18 = (bf16[400,768]{1,0:T(8,128)(2,1)}, bf16[400,768]{1,0:T(8,128)(2,1)S(1)}, u32[]{:S(2)}, u32[]{:S(2)}) collective-permute-start(bf16[400,768]{1,0:T(8,128)(2,1)} %get-tuple-element.260), channel_id=1, source_target_pairs={{0,16},{1,17},{2,18},{3,19},{4,20},{5,21},{6,22},{7,23},{8,24},{9,... | collective-permute-start | bytes 1843208 | tf_op jit(solution)/shard_map/ppermute | solution.py:42
  96.3 33.1 %collective-permute-start.19 = (f32[8,128]{1,0:T(8,128)S(1)}, f32[8,128]{1,0:T(8,128)S(1)}, u32[]{:S(2)}, u32[]{:S(2)}) collective-permute-start(f32[8,128]{1,0:T(8,128)S(1)} %add.334), channel_id=1, source_target_pairs={{0,2},{1,3},{2,0},{3,1},{4,6},{5,7},{6,4},{7,5},{8,10},{9,11},{10,... | collective-permute-start | bytes 12296 | tf_op jit(solution)/shard_map/ppermute | solution.py:42
  151.1 14.8 %collective-permute-start.23 = (bf16[400,768]{1,0:T(8,128)(2,1)S(1)}, bf16[400,768]{1,0:T(8,128)(2,1)S(1)}, u32[]{:S(2)}, u32[]{:S(2)}) collective-permute-start(bf16[400,768]{1,0:T(8,128)(2,1)S(1)} %get-tuple-element.274), channel_id=1, source_target_pairs={{0,1},{1,0},{2,5},{3,4},{4,3},{5,2},{6,7},{7,6},{8,9},{9,8},{10,13... | collective-permute-start | bytes 1843208 | tf_op jit(solution)/shard_map/ppermute | solution.py:42
  169.0 16.9 %collective-permute-start.24 = (bf16[768,768]{1,0:T(8,128)(2,1)}, bf16[768,768]{1,0:T(8,128)(2,1)}, u32[]{:S(2)}, u32[]{:S(2)}) collective-permute-start(bf16[768,768]{1,0:T(8,128)(2,1)} %convolution_convert_fusion.4), channel_id=1, source_target_pairs={{0,4},{1,5},{2,6},{3,7},{4,0},{5,1},{6,2},{7,3},{8,12},{9,13},{10,... | collective-permute-start | bytes 3538952 | tf_op jit(solution)/shard_map/ppermute | solution.py:42
  202.9 8.6 %collective-permute-start.25 = (bf16[768,768]{1,0:T(8,128)(2,1)S(1)}, bf16[768,768]{1,0:T(8,128)(2,1)S(1)}, u32[]{:S(2)}, u32[]{:S(2)}) collective-permute-start(bf16[768,768]{1,0:T(8,128)(2,1)S(1)} %multiply_convert_fusion.4), channel_id=1, source_target_pairs={{0,4},{1,5},{2,6},{3,7},{4,0},{5,1},{6,2},{7,3},{8,12},{9,13},{10,... | collective-permute-start | bytes 3538952 | tf_op jit(solution)/shard_map/ppermute | solution.py:42
  217.8 9.3 %collective-permute-start.26 = (bf16[768,768]{1,0:T(8,128)(2,1)S(1)}, bf16[768,768]{1,0:T(8,128)(2,1)S(1)}, u32[]{:S(2)}, u32[]{:S(2)}) collective-permute-start(bf16[768,768]{1,0:T(8,128)(2,1)S(1)} %convolution_convert_fusion.3), channel_id=1, source_target_pairs={{0,4},{1,5},{2,6},{3,7},{4,0},{5,1},{6,2},{7,3},{8,12},{9,13},{10,... | collective-permute-start | bytes 3538952 | tf_op jit(solution)/shard_map/ppermute | solution.py:42
  219.3 20.4 %collective-permute-start.28 = (bf16[384,768]{1,0:T(8,128)(2,1)S(1)}, bf16[384,768]{1,0:T(8,128)(2,1)S(1)}, u32[]{:S(2)}, u32[]{:S(2)}) collective-permute-start(bf16[384,768]{1,0:T(8,128)(2,1)S(1)} %get-tuple-element.256), channel_id=1, source_target_pairs={{0,8},{1,9},{2,10},{3,11},{4,12},{5,13},{6,14},{7,15},{8,0},{9,1},... | collective-permute-start | bytes 1769480 | tf_op jit(solution)/shard_map/ppermute | solution.py:42
  220.8 28.4 %collective-permute-start.29 = (bf16[384,768]{1,0:T(8,128)(2,1)S(1)}, bf16[384,768]{1,0:T(8,128)(2,1)S(1)}, u32[]{:S(2)}, u32[]{:S(2)}) collective-permute-start(bf16[384,768]{1,0:T(8,128)(2,1)S(1)} %get-tuple-element.255), channel_id=1, source_target_pairs={{0,16},{1,17},{2,18},{3,19},{4,20},{5,21},{6,22},{7,23},{8,24},{9,... | collective-permute-start | bytes 1769480 | tf_op jit(solution)/shard_map/ppermute | solution.py:42
  222.4 28.4 %collective-permute-start.30 = (bf16[384,768]{1,0:T(8,128)(2,1)S(1)}, bf16[384,768]{1,0:T(8,128)(2,1)S(1)}, u32[]{:S(2)}, u32[]{:S(2)}) collective-permute-start(bf16[384,768]{1,0:T(8,128)(2,1)S(1)} %get-tuple-element.254), channel_id=1, source_target_pairs={{0,24},{1,25},{2,26},{3,27},{4,28},{5,29},{6,30},{7,31},{8,16},{9,... | collective-permute-start | bytes 1769480 | tf_op jit(solution)/shard_map/ppermute | solution.py:42
  234.6 17.7 %collective-permute-start.27 = (bf16[768,384]{1,0:T(8,128)(2,1)S(1)}, bf16[768,384]{1,0:T(8,128)(2,1)S(1)}, u32[]{:S(2)}, u32[]{:S(2)}) collective-permute-start(bf16[768,384]{1,0:T(8,128)(2,1)S(1)} %get-tuple-element.289), channel_id=1, source_target_pairs={{0,4},{1,5},{2,6},{3,7},{4,0},{5,1},{6,2},{7,3},{8,12},{9,13},{10,... | collective-permute-start | bytes 1769480 | tf_op jit(solution)/shard_map/ppermute | solution.py:42
  238.0 32.5 %collective-permute-start.31 = (bf16[384,768]{1,0:T(8,128)(2,1)}, bf16[384,768]{1,0:T(8,128)(2,1)S(1)}, u32[]{:S(2)}, u32[]{:S(2)}) collective-permute-start(bf16[384,768]{1,0:T(8,128)(2,1)} %get-tuple-element.287), channel_id=1, source_target_pairs={{0,0},{1,1},{2,4},{3,5},{4,2},{5,3},{6,6},{7,7},{8,8},{9,9},{10,12... | collective-permute-start | bytes 1769480 | tf_op jit(solution)/shard_map/ppermute | solution.py:42
  240.5 29.9 %collective-permute-start.32 = (bf16[384,768]{1,0:T(8,128)(2,1)}, bf16[384,768]{1,0:T(8,128)(2,1)}, u32[]{:S(2)}, u32[]{:S(2)}) collective-permute-start(bf16[384,768]{1,0:T(8,128)(2,1)} %get-tuple-element.286), channel_id=1, source_target_pairs={{0,1},{1,0},{2,5},{3,4},{4,3},{5,2},{6,7},{7,6},{8,9},{9,8},{10,13... | collective-permute-start | bytes 1769480 | tf_op jit(solution)/shard_map/ppermute | solution.py:42
  249.2 49.4 %collective-permute-start.34 = (bf16[192,2304]{1,0:T(8,128)(2,1)}, bf16[192,2304]{1,0:T(8,128)(2,1)}, u32[]{:S(2)}, u32[]{:S(2)}) collective-permute-start(bf16[192,2304]{1,0:T(8,128)(2,1)} %get-tuple-element.251), channel_id=1, source_target_pairs={{0,8},{1,9},{2,10},{3,11},{4,12},{5,13},{6,14},{7,15},{8,0},{9,1},... | collective-permute-start | bytes 2654216 | tf_op jit(solution)/shard_map/ppermute | solution.py:42
  250.8 47.8 %collective-permute-start.35 = (bf16[192,2304]{1,0:T(8,128)(2,1)}, bf16[192,2304]{1,0:T(8,128)(2,1)}, u32[]{:S(2)}, u32[]{:S(2)}) collective-permute-start(bf16[192,2304]{1,0:T(8,128)(2,1)} %get-tuple-element.252), channel_id=1, source_target_pairs={{0,16},{1,17},{2,18},{3,19},{4,20},{5,21},{6,22},{7,23},{8,24},{9,... | collective-permute-start | bytes 2654216 | tf_op jit(solution)/shard_map/ppermute | solution.py:42
  252.3 46.3 %collective-permute-start.36 = (bf16[192,2304]{1,0:T(8,128)(2,1)}, bf16[192,2304]{1,0:T(8,128)(2,1)}, u32[]{:S(2)}, u32[]{:S(2)}) collective-permute-start(bf16[192,2304]{1,0:T(8,128)(2,1)} %get-tuple-element.249), channel_id=1, source_target_pairs={{0,24},{1,25},{2,26},{3,27},{4,28},{5,29},{6,30},{7,31},{8,16},{9,... | collective-permute-start | bytes 2654216 | tf_op jit(solution)/shard_map/ppermute | solution.py:42
  273.2 25.5 %collective-permute-start.33 = (bf16[192,768]{1,0:T(8,128)(2,1)}, bf16[192,768]{1,0:T(8,128)(2,1)}, u32[]{:S(2)}, u32[]{:S(2)}) collective-permute-start(bf16[192,768]{1,0:T(8,128)(2,1)} %get-tuple-element.307), channel_id=1, source_target_pairs={{0,1},{1,0},{2,3},{3,2},{4,5},{5,4},{6,7},{7,6},{8,9},{9,8},{10,11... | collective-permute-start | bytes 884744 | tf_op jit(solution)/shard_map/ppermute | solution.py:42
  303.7 30.8 %collective-permute-start.39 = (bf16[192,768]{1,0:T(8,128)(2,1)}, bf16[192,768]{1,0:T(8,128)(2,1)}, u32[]{:S(2)}, u32[]{:S(2)}) collective-permute-start(bf16[192,768]{1,0:T(8,128)(2,1)} %get-tuple-element.282), channel_id=1, source_target_pairs={{0,8},{1,9},{2,10},{3,11},{4,12},{5,13},{6,14},{7,15},{8,0},{9,1},... | collective-permute-start | bytes 884744 | tf_op jit(solution)/shard_map/ppermute | solution.py:42
  303.8 30.7 %collective-permute-start.40 = (bf16[192,768]{1,0:T(8,128)(2,1)}, bf16[192,768]{1,0:T(8,128)(2,1)}, u32[]{:S(2)}, u32[]{:S(2)}) collective-permute-start(bf16[192,768]{1,0:T(8,128)(2,1)} %get-tuple-element.281), channel_id=1, source_target_pairs={{0,16},{1,17},{2,18},{3,19},{4,20},{5,21},{6,22},{7,23},{8,24},{9,... | collective-permute-start | bytes 884744 | tf_op jit(solution)/shard_map/ppermute | solution.py:42
  305.4 29.2 %collective-permute-start.41 = (bf16[192,768]{1,0:T(8,128)(2,1)}, bf16[192,768]{1,0:T(8,128)(2,1)}, u32[]{:S(2)}, u32[]{:S(2)}) collective-permute-start(bf16[192,768]{1,0:T(8,128)(2,1)} %get-tuple-element.280), channel_id=1, source_target_pairs={{0,24},{1,25},{2,26},{3,27},{4,28},{5,29},{6,30},{7,31},{8,16},{9,... | collective-permute-start | bytes 884744 | tf_op jit(solution)/shard_map/ppermute | solution.py:42
  310.3 24.2 %collective-permute-start.38 = (bf16[96,2304]{1,0:T(8,128)(2,1)}, bf16[96,2304]{1,0:T(8,128)(2,1)}, u32[]{:S(2)}, u32[]{:S(2)}) collective-permute-start(bf16[96,2304]{1,0:T(8,128)(2,1)} %get-tuple-element.296), channel_id=1, source_target_pairs={{0,1},{1,0},{2,3},{3,2},{4,5},{5,4},{6,7},{7,6},{8,9},{9,8},{10,11... | collective-permute-start | bytes 1327112 | tf_op jit(solution)/shard_map/ppermute | solution.py:42
  312.1 22.4 %collective-permute-start.37 = (bf16[96,768]{1,0:T(8,128)(2,1)}, bf16[96,768]{1,0:T(8,128)(2,1)}, u32[]{:S(2)}, u32[]{:S(2)}) collective-permute-start(bf16[96,768]{1,0:T(8,128)(2,1)} %get-tuple-element.329), channel_id=1, source_target_pairs={{0,2},{1,3},{2,0},{3,1},{4,6},{5,7},{6,4},{7,5},{8,10},{9,11},{10,... | collective-permute-start | bytes 442376 | tf_op jit(solution)/shard_map/ppermute | solution.py:42
  335.6 13.3 %collective-permute-start.52 = (bf16[96,768]{1,0:T(8,128)(2,1)S(1)}, bf16[96,768]{1,0:T(8,128)(2,1)S(1)}, u32[]{:S(2)}, u32[]{:S(2)}) collective-permute-start(bf16[96,768]{1,0:T(8,128)(2,1)S(1)} %add_convert_fusion.8), channel_id=1, source_target_pairs={{0,2},{1,3},{2,0},{3,1},{4,6},{5,7},{6,4},{7,5},{8,10},{9,11},{10,... | collective-permute-start | bytes 442376 | tf_op jit(solution)/shard_map/ppermute | solution.py:42
  342.0 20.8 %collective-permute-start.47 = (bf16[768,768]{1,0:T(8,128)(2,1)S(1)}, bf16[768,768]{1,0:T(8,128)(2,1)S(1)}, u32[]{:S(2)}, u32[]{:S(2)}) collective-permute-start(bf16[768,768]{1,0:T(8,128)(2,1)S(1)} %slice.335), channel_id=1, source_target_pairs={{0,4},{1,5},{2,6},{3,7},{4,0},{5,1},{6,2},{7,3},{8,12},{9,13},{10,... | collective-permute-start | bytes 3538952 | tf_op jit(solution)/shard_map/ppermute | solution.py:42
  344.2 39.3 %collective-permute-start.46 = (bf16[96,768]{1,0:T(8,128)(2,1)S(1)}, bf16[96,768]{1,0:T(8,128)(2,1)S(1)}, u32[]{:S(2)}, u32[]{:S(2)}) collective-permute-start(bf16[96,768]{1,0:T(8,128)(2,1)S(1)} %get-tuple-element.327), channel_id=1, source_target_pairs={{0,1},{1,0},{2,3},{3,2},{4,5},{5,4},{6,7},{7,6},{8,9},{9,8},{10,11... | collective-permute-start | bytes 442376 | tf_op jit(solution)/shard_map/ppermute | solution.py:42
  345.9 7.6 %collective-permute-start.43 = (bf16[192,384]{1,0:T(8,128)(2,1)S(1)}, bf16[192,384]{1,0:T(8,128)(2,1)S(1)}, u32[]{:S(2)}, u32[]{:S(2)}) collective-permute-start(bf16[192,384]{1,0:T(8,128)(2,1)S(1)} %get-tuple-element.306), channel_id=1, source_target_pairs={{0,16},{1,17},{2,18},{3,19},{4,20},{5,21},{6,22},{7,23},{8,24},{9,... | collective-permute-start | bytes 442376 | tf_op jit(solution)/shard_map/ppermute | solution.py:42
  351.7 10.9 %collective-permute-start.56 = (bf16[48,2304]{1,0:T(8,128)(2,1)S(1)}, bf16[48,2304]{1,0:T(8,128)(2,1)S(1)}, u32[]{:S(2)}, u32[]{:S(2)}) collective-permute-start(bf16[48,2304]{1,0:T(8,128)(2,1)S(1)} %dynamic-slice_bitcast_fusion.10), channel_id=1, source_target_pairs={{0,2},{1,3},{2,0},{3,1},{4,6},{5,7},{6,4},{7,5},{8,10},{9,11},{10,... | collective-permute-start | bytes 663560 | tf_op jit(solution)/shard_map/ppermute | solution.py:42
  353.5 38.3 %collective-permute-start.53 = (bf16[192,768]{1,0:T(8,128)(2,1)S(1)}, bf16[192,768]{1,0:T(8,128)(2,1)S(1)}, u32[]{:S(2)}, u32[]{:S(2)}) collective-permute-start(bf16[192,768]{1,0:T(8,128)(2,1)S(1)} %pad_maximum_fusion.20), channel_id=1, source_target_pairs={{0,1},{1,0},{2,3},{3,2},{4,5},{5,4},{6,7},{7,6},{8,9},{9,8},{10,11... | collective-permute-start | bytes 884744 | tf_op jit(solution)/shard_map/ppermute | solution.py:42
  355.3 28.2 %collective-permute-start.45 = (bf16[96,384]{1,0:T(8,128)(2,1)S(1)}, bf16[96,384]{1,0:T(8,128)(2,1)S(1)}, u32[]{:S(2)}, u32[]{:S(2)}) collective-permute-start(bf16[96,384]{1,0:T(8,128)(2,1)S(1)} %get-tuple-element.337), channel_id=1, source_target_pairs={{0,1},{1,0},{2,3},{3,2},{4,5},{5,4},{6,7},{7,6},{8,9},{9,8},{10,11... | collective-permute-start | bytes 221192 | tf_op jit(solution)/shard_map/ppermute | solution.py:42
  362.7 18.8 %collective-permute-start.57 = (bf16[48,2304]{1,0:T(8,128)(2,1)S(1)}, bf16[48,2304]{1,0:T(8,128)(2,1)S(1)}, u32[]{:S(2)}, u32[]{:S(2)}) collective-permute-start(bf16[48,2304]{1,0:T(8,128)(2,1)S(1)} %fusion.56), channel_id=1, source_target_pairs={{0,2},{1,3},{2,0},{3,1},{4,6},{5,7},{6,4},{7,5},{8,10},{9,11},{10,... | collective-permute-start | bytes 663560 | tf_op jit(solution)/shard_map/ppermute | solution.py:42
  365.7 17.7 %collective-permute-start.49 = (bf16[384,768]{1,0:T(8,128)(2,1)S(1)}, bf16[384,768]{1,0:T(8,128)(2,1)S(1)}, u32[]{:S(2)}, u32[]{:S(2)}) collective-permute-start(bf16[384,768]{1,0:T(8,128)(2,1)S(1)} %get-tuple-element.279), channel_id=1, source_target_pairs={{0,0},{1,1},{2,4},{3,5},{4,2},{5,3},{6,6},{7,7},{8,8},{9,9},{10,12... | collective-permute-start | bytes 1769480 | tf_op jit(solution)/shard_map/ppermute | solution.py:42
  382.7 24.6 %collective-permute-start.54 = (bf16[384,768]{1,0:T(8,128)(2,1)S(1)}, bf16[384,768]{1,0:T(8,128)(2,1)S(1)}, u32[]{:S(2)}, u32[]{:S(2)}) collective-permute-start(bf16[384,768]{1,0:T(8,128)(2,1)S(1)} %get-tuple-element.278), channel_id=1, source_target_pairs={{0,1},{1,0},{2,5},{3,4},{4,3},{5,2},{6,7},{7,6},{8,9},{9,8},{10,13... | collective-permute-start | bytes 1769480 | tf_op jit(solution)/shard_map/ppermute | solution.py:42
  383.4 8.4 %collective-permute-start.51 = (f32[8,768]{1,0:T(8,128)S(1)}, f32[8,768]{1,0:T(8,128)S(1)}, u32[]{:S(2)}, u32[]{:S(2)}) collective-permute-start(f32[8,768]{1,0:T(8,128)S(1)} %fusion.85), channel_id=1, source_target_pairs={{0,8},{1,9},{2,10},{3,11},{4,12},{5,13},{6,14},{7,15},{8,0},{9,1},... | collective-permute-start | bytes 73736 | tf_op jit(solution)/shard_map/ppermute | solution.py:42
  384.7 22.6 %collective-permute-start.50 = (bf16[48,1152]{1,0:T(8,128)(2,1)S(1)}, bf16[48,1152]{1,0:T(8,128)(2,1)S(1)}, u32[]{:S(2)}, u32[]{:S(2)}) collective-permute-start(bf16[48,1152]{1,0:T(8,128)(2,1)S(1)} %get-tuple-element.335), channel_id=1, source_target_pairs={{0,2},{1,3},{2,0},{3,1},{4,6},{5,7},{6,4},{7,5},{8,10},{9,11},{10,... | collective-permute-start | bytes 331784 | tf_op jit(solution)/shard_map/ppermute | solution.py:42
  388.6 24.8 %collective-permute-start.58 = (bf16[96,2304]{1,0:T(8,128)(2,1)S(1)}, bf16[96,2304]{1,0:T(8,128)(2,1)S(1)}, u32[]{:S(2)}, u32[]{:S(2)}) collective-permute-start(bf16[96,2304]{1,0:T(8,128)(2,1)S(1)} %pad_maximum_fusion.15), channel_id=1, source_target_pairs={{0,1},{1,0},{2,3},{3,2},{4,5},{5,4},{6,7},{7,6},{8,9},{9,8},{10,11... | collective-permute-start | bytes 1327112 | tf_op jit(solution)/shard_map/ppermute | solution.py:42
  415.5 8.6 %collective-permute-start.61 = (bf16[96,2304]{1,0:T(8,128)(2,1)S(1)}, bf16[96,2304]{1,0:T(8,128)(2,1)S(1)}, u32[]{:S(2)}, u32[]{:S(2)}) collective-permute-start(bf16[96,2304]{1,0:T(8,128)(2,1)S(1)} %fusion.55), channel_id=1, source_target_pairs={{0,4},{1,5},{2,6},{3,7},{4,0},{5,1},{6,2},{7,3},{8,12},{9,13},{10,... | collective-permute-start | bytes 1327112 | tf_op jit(solution)/shard_map/ppermute | solution.py:42
  415.7 8.4 %collective-permute-start.60 = (bf16[96,1152]{1,0:T(8,128)(2,1)S(1)}, bf16[96,1152]{1,0:T(8,128)(2,1)S(1)}, u32[]{:S(2)}, u32[]{:S(2)}) collective-permute-start(bf16[96,1152]{1,0:T(8,128)(2,1)S(1)} %pad_maximum_fusion.22), channel_id=1, source_target_pairs={{0,1},{1,0},{2,3},{3,2},{4,5},{5,4},{6,7},{7,6},{8,9},{9,8},{10,11... | collective-permute-start | bytes 663560 | tf_op jit(solution)/shard_map/ppermute | solution.py:42
  416.8 7.2 %collective-permute-start.62 = (f32[8,768]{1,0:T(8,128)S(1)}, f32[8,768]{1,0:T(8,128)S(1)}, u32[]{:S(2)}, u32[]{:S(2)}) collective-permute-start(f32[8,768]{1,0:T(8,128)S(1)} %add.386), channel_id=1, source_target_pairs={{0,1},{1,0},{2,3},{3,2},{4,5},{5,4},{6,7},{7,6},{8,9},{9,8},{10,11... | collective-permute-start | bytes 73736 | tf_op jit(solution)/shard_map/ppermute | solution.py:42
  (96 other events, 530.8 us)
